TPU v7x, 32 devices: a whole 2x2x4 slice. The times are simulated.
32 devices in a mesh: expert: 8 (over z, core), shard: 4 (over y, x).
Axes of the slice: x: 2, y: 2, z: 4, core: 2. Of those that a mesh axis runs over, the one named last changes fastest.
Arguments:
- layer_input: bfloat16 [16384, 1536], P(('expert', 'shard')), may hold values from -6 to 6
- out_cotangent: bfloat16 [16384, 1536], P(('expert', 'shard')), may hold values from -6 to 6
- parents: int32 [128], P(('expert', 'shard')), may hold values from 0 to 2, as said below
- routes: int32 [16384, 8], P(('expert', 'shard')), may hold values from 0 to 15, all different within a row; in each aligned block of 512 rows (0 to 511, 512 to 1023, ...) at most 320 rows name the same one
- norm1_gain: bfloat16 [1536], P('shard'), may hold values from 0.099609375 to 1.8984375
- qkv_weight: bfloat16 [1536, 2560], P('shard'), may hold values from -0.15625 to 0.15625
- out_weight: bfloat16 [1536, 1536], P('shard'), may hold values from -0.875 to 0.875
- norm2_gain: bfloat16 [1536], P('shard'), may hold values from 0.099609375 to 1.8984375
- router_weight: bfloat16 [1536, 16], P('shard'), may hold values from -0.078125 to 0.078125
- gate_weight: bfloat16 [16, 1536, 512], P('expert', 'shard'), may hold values from -0.15625 to 0.15625
- up_weight: bfloat16 [16, 1536, 512], P('expert', 'shard'), may hold values from -0.15625 to 0.15625
- down_weight: bfloat16 [16, 512, 1536], P('expert', None, 'shard'), may hold values from -0.75 to 0.75
Outputs:
- output: bfloat16 [16384, 1536], P(('expert', 'shard'))
- input_grad: bfloat16 [16384, 1536], P(('expert', 'shard'))
- grad_norm1_gain: float32 [1536], P('shard')
- grad_qkv_weight: float32 [1536, 2560], P('shard')
- grad_out_weight: float32 [1536, 1536], P('shard')
- grad_norm2_gain: float32 [1536], P('shard')
- grad_router_weight: float32 [1536, 16], P('shard')
- grad_gate_weight: float32 [16, 1536, 512], P('expert', 'shard')
- grad_up_weight: float32 [16, 1536, 512], P('expert', 'shard')
- grad_down_weight: float32 [16, 512, 1536], P('expert', None, 'shard')
Inputs may be any that keep to these rules, and one draw needn't show every extreme that they name: `parents`: within each tree's block of 4 entries, entry s names a segment before s, entry 0 names 0, and the last entry names its predecessor. `routes`: each row names 8 different experts; in the rows of one device each expert is named by at most 320 rows, a bound that some block reaches.
All inputs are finite; a program needn't handle non-finite values.
Results may differ from a plain program's by a relative error of at most 0.02.
Values may be sent and summed in bfloat16 or wider, within the bound.
No kernel may reach another device: no remote copies, remote signals or barrier semaphores. Data moves between devices by JAX's collectives and lax.ppermute only.
A program may use at most 320 MiB of HBM per device.

v0:
```python
from functools import partial

import jax
import jax.numpy as jnp
from jax import lax
from jax.sharding import PartitionSpec as P

HEADS = 24
KV_HEADS = 8
HEAD_DIM = 64
TOP = 8
SEG = 128


EPSILON = 1e-06
THETA = 10000.0
NEGATIVE = -1e30


def tree_tables(parents, seg_len):
    seg_count = parents.shape[0]
    seg_ids = jnp.arange(seg_count, dtype=jnp.int32)

    def follow(step_index, state_pair):
        pointer, ancestry = state_pair
        landed = pointer[:, None] == seg_ids[None, :]
        ancestry = jnp.maximum(ancestry, landed.astype(jnp.float32))
        pointer = jnp.sum(jnp.where(landed, parents[None, :], 0), axis=1)
        return (pointer, ancestry)

    start_state = (seg_ids, jnp.zeros((seg_count, seg_count), jnp.float32))
    pointer, ancestry = lax.fori_loop(0, seg_count, follow, start_state)
    depth = jnp.sum(ancestry, axis=1) - 1.0
    row_count = seg_count * seg_len
    token_ids = jnp.arange(row_count, dtype=jnp.int32)
    offsets = (token_ids % seg_len).astype(jnp.float32)
    positions = jnp.repeat(depth, seg_len) * seg_len + offsets
    reach = jnp.repeat(jnp.repeat(ancestry, seg_len, axis=0), seg_len, axis=1)
    allowed = (reach > 0.5) & (token_ids[None, :] <= token_ids[:, None])
    return (allowed, positions)


def rope_tables(positions, head_size):
    half_size = head_size // 2
    frequency = THETA ** (-(jnp.arange(half_size, dtype=jnp.float32) * 2.0) / head_size)
    angles = positions[:, None] * frequency[None, :]
    cosine = jnp.cos(angles)
    sine = jnp.sin(angles)
    return (jnp.concatenate([cosine, cosine], axis=1), jnp.concatenate([sine, sine], axis=1))


def turn_half(values):
    half_size = values.shape[-1] // 2
    return jnp.concatenate([-values[..., half_size:], values[..., :half_size]], axis=-1)


def rotate(values, cosine, sine):
    return values * cosine[:, None, :] + turn_half(values) * sine[:, None, :]


def unrotate(grads, cosine, sine):
    return grads * cosine[:, None, :] - turn_half(grads * sine[:, None, :])


def place_rows(routes, expert_count, capacity):
    token_count, top_count = routes.shape
    flat_routes = routes.reshape(-1)
    hot_table = (flat_routes[:, None] == jnp.arange(expert_count, dtype=jnp.int32)[None, :]).astype(
        jnp.int32
    )
    earlier = jnp.cumsum(hot_table, axis=0) - hot_table
    slots = jnp.sum(earlier * hot_table, axis=1)
    table = jnp.full((expert_count, capacity), token_count * top_count, jnp.int32)
    table = table.at[flat_routes, slots].set(jnp.arange(token_count * top_count, dtype=jnp.int32))
    return (slots.reshape(token_count, top_count), table)


def inverse_rms(values):
    return lax.rsqrt(jnp.mean(values * values, axis=1, keepdims=True) + EPSILON)


def masked_scores(query_head, key_head, allowed, scaling):
    scores = (
        jnp.einsum("tgd,sd->gts", query_head, key_head, preferred_element_type=jnp.float32)
        * scaling
    )
    return jnp.where(allowed[None], scores, NEGATIVE)


def attend_forward(allowed, scaling, inputs_three):
    query_head, key_head, value_head = inputs_three
    scores = masked_scores(query_head, key_head, allowed, scaling)
    highest = jnp.max(scores, axis=2, keepdims=True)
    powers = jnp.exp(scores - highest)
    totals = jnp.sum(powers, axis=2, keepdims=True)
    probs = (powers / totals).astype(jnp.bfloat16)
    mixed = jnp.einsum("gts,sd->tgd", probs, value_head, preferred_element_type=jnp.float32)
    return (mixed, (highest + jnp.log(totals))[..., 0])


def attend_backward(allowed, scaling, inputs_five):
    query_head, key_head, value_head, grad_head, log_total = inputs_five
    scores = masked_scores(query_head, key_head, allowed, scaling)
    probs = jnp.exp(scores - log_total[..., None])
    grad_probs = jnp.einsum(
        "tgd,sd->gts", grad_head, value_head, preferred_element_type=jnp.float32
    )
    centre = jnp.sum(probs * grad_probs, axis=2, keepdims=True)
    grad_scores = (probs * (grad_probs - centre)).astype(jnp.bfloat16)
    grad_query = (
        jnp.einsum("gts,sd->tgd", grad_scores, key_head, preferred_element_type=jnp.float32)
        * scaling
    )
    grad_key = (
        jnp.einsum("gts,tgd->sd", grad_scores, query_head, preferred_element_type=jnp.float32)
        * scaling
    )
    grad_value = jnp.einsum(
        "gts,tgd->sd", probs.astype(jnp.bfloat16), grad_head, preferred_element_type=jnp.float32
    )
    return (grad_query, grad_key, grad_value)


def expert_forward(arrived, gate_full, up_full, down_full):
    gate_in = jnp.einsum("lrd,ldf->lrf", arrived, gate_full, preferred_element_type=jnp.float32)
    up_in = jnp.einsum("lrd,ldf->lrf", arrived, up_full, preferred_element_type=jnp.float32)
    sigma = jax.nn.sigmoid(gate_in)
    active = gate_in * sigma
    hidden_mid = (active * up_in).astype(jnp.bfloat16)
    produced = jnp.einsum(
        "lrf,lfd->lrd", hidden_mid, down_full, preferred_element_type=jnp.float32
    ).astype(jnp.bfloat16)
    return (gate_in, up_in, sigma, active, hidden_mid, produced)


def expert_backward(arrived, grad_arrived, kept, gate_back, up_back, down_back):
    gate_in, up_in, sigma, active, hidden_mid = kept
    grad_mid = jnp.einsum(
        "lrd,lfd->lrf", grad_arrived, down_back, preferred_element_type=jnp.float32
    )
    grad_down = jnp.einsum(
        "lrf,lrd->lfd", hidden_mid, grad_arrived, preferred_element_type=jnp.float32
    )
    grad_gate_in = (grad_mid * up_in * sigma * (1.0 + gate_in * (1.0 - sigma))).astype(jnp.bfloat16)
    grad_up_in = (grad_mid * active).astype(jnp.bfloat16)
    grad_gate = jnp.einsum(
        "lrd,lrf->ldf", arrived, grad_gate_in, preferred_element_type=jnp.float32
    )
    grad_up = jnp.einsum("lrd,lrf->ldf", arrived, grad_up_in, preferred_element_type=jnp.float32)
    grad_taken = jnp.einsum(
        "lrf,ldf->lrd", grad_gate_in, gate_back, preferred_element_type=jnp.float32
    )
    grad_taken = (
        grad_taken
        + jnp.einsum("lrf,ldf->lrd", grad_up_in, up_back, preferred_element_type=jnp.float32)
    ).astype(jnp.bfloat16)
    return (grad_gate, grad_up, grad_down, grad_taken)


def backward_weights(
    norm1_gain,
    qkv_weight,
    out_weight,
    norm2_gain,
    router_weight,
    gate_weight,
    up_weight,
    down_weight,
):
    expert_set = (
        lax.all_gather(gate_weight, "shard", axis=1, tiled=True),
        lax.all_gather(up_weight, "shard", axis=1, tiled=True),
        lax.all_gather(down_weight, "shard", axis=2, tiled=True),
    )
    attn_set = (
        lax.all_gather(norm1_gain, "shard", axis=0, tiled=True),
        lax.all_gather(qkv_weight, "shard", axis=0, tiled=True),
        lax.all_gather(out_weight, "shard", axis=0, tiled=True),
        lax.all_gather(norm2_gain, "shard", axis=0, tiled=True),
        lax.all_gather(router_weight, "shard", axis=0, tiled=True),
    )
    return tuple(attn_set) + tuple(expert_set)


def per_device(
    layer_input,
    out_cotangent,
    parents,
    routes,
    norm1_gain,
    qkv_weight,
    out_weight,
    norm2_gain,
    router_weight,
    gate_weight,
    up_weight,
    down_weight,
):
    gain_one, mixer, projector, gain_two, router = (
        lax.all_gather(norm1_gain, "shard", axis=0, tiled=True),
        lax.all_gather(qkv_weight, "shard", axis=0, tiled=True),
        lax.all_gather(out_weight, "shard", axis=0, tiled=True),
        lax.all_gather(norm2_gain, "shard", axis=0, tiled=True),
        lax.all_gather(router_weight, "shard", axis=0, tiled=True),
    )
    gate_full, up_full, down_full = (
        lax.all_gather(gate_weight, "shard", axis=1, tiled=True),
        lax.all_gather(up_weight, "shard", axis=1, tiled=True),
        lax.all_gather(down_weight, "shard", axis=2, tiled=True),
    )
    token_count = layer_input.shape[0]
    width = layer_input.shape[1]
    groups = HEADS // KV_HEADS
    query_width = HEADS * HEAD_DIM
    key_width = KV_HEADS * HEAD_DIM
    scaling = HEAD_DIM ** (-0.5)
    allowed, positions = tree_tables(parents, SEG)
    cosine, sine = rope_tables(positions, HEAD_DIM)
    activity = layer_input.astype(jnp.float32)
    scale_one = inverse_rms(activity)
    normed_one = activity * scale_one
    hidden_one = (normed_one * gain_one.astype(jnp.float32)[None, :]).astype(jnp.bfloat16)
    mixed = jnp.dot(hidden_one, mixer, preferred_element_type=jnp.float32)
    query = rotate(
        mixed[:, :query_width].reshape(token_count, HEADS, HEAD_DIM), cosine, sine
    ).astype(jnp.bfloat16)
    keys_rot = rotate(
        mixed[:, query_width : query_width + key_width].reshape(token_count, KV_HEADS, HEAD_DIM),
        cosine,
        sine,
    ).astype(jnp.bfloat16)
    values = (
        mixed[:, query_width + key_width :]
        .reshape(token_count, KV_HEADS, HEAD_DIM)
        .astype(jnp.bfloat16)
    )
    query_heads = jnp.transpose(
        query.reshape(token_count, KV_HEADS, groups, HEAD_DIM), (1, 0, 2, 3)
    )
    key_heads = jnp.transpose(keys_rot, (1, 0, 2))
    value_heads = jnp.transpose(values, (1, 0, 2))
    attended, log_total = lax.map(
        partial(attend_forward, allowed, scaling), (query_heads, key_heads, value_heads)
    )
    attended = (
        jnp.transpose(attended, (1, 0, 2, 3)).reshape(token_count, query_width).astype(jnp.bfloat16)
    )
    resid = activity + jnp.dot(attended, projector, preferred_element_type=jnp.float32)
    scale_two = inverse_rms(resid)
    normed_two = resid * scale_two
    hidden_two = (normed_two * gain_two.astype(jnp.float32)[None, :]).astype(jnp.bfloat16)
    logits = jnp.dot(hidden_two, router, preferred_element_type=jnp.float32)
    expert_count = router.shape[1]
    route_hot = routes[:, :, None] == jnp.arange(expert_count, dtype=jnp.int32)[None, None, :]
    chosen = jnp.sum(jnp.where(route_hot, logits[:, None, :], 0.0), axis=2)
    chosen_top = jnp.max(chosen, axis=1, keepdims=True)
    chosen_powers = jnp.exp(chosen - chosen_top)
    gates = chosen_powers / jnp.sum(chosen_powers, axis=1, keepdims=True)
    capacity = token_count * TOP * 5 // (expert_count * 4)
    owner_count = lax.axis_size("expert")
    local_count = gate_full.shape[0]
    slots, table = place_rows(routes, expert_count, capacity)
    send_table = jnp.transpose(
        table.reshape(owner_count, local_count, capacity), (1, 0, 2)
    ).reshape(local_count, owner_count * capacity)
    padded = jnp.concatenate([hidden_two, jnp.zeros((1, width), jnp.bfloat16)], axis=0)
    outgoing = padded[send_table // TOP]
    upstream = out_cotangent.astype(jnp.float32)
    weighted = (
        (gates[:, :, None] * upstream[:, None, :])
        .astype(jnp.bfloat16)
        .reshape(token_count * TOP, width)
    )
    weighted = jnp.concatenate([weighted, jnp.zeros((1, width), jnp.bfloat16)], axis=0)
    grad_outgoing = weighted[send_table]
    arrived = lax.all_to_all(outgoing, "expert", split_axis=1, concat_axis=1, tiled=True)
    gate_in, up_in, sigma, active, hidden_mid, produced = expert_forward(
        arrived, gate_full, up_full, down_full
    )
    returned = lax.all_to_all(produced, "expert", split_axis=1, concat_axis=1, tiled=True)
    grad_arrived = lax.all_to_all(grad_outgoing, "expert", split_axis=1, concat_axis=1, tiled=True)
    back_set = backward_weights(
        norm1_gain,
        qkv_weight,
        out_weight,
        norm2_gain,
        router_weight,
        gate_weight,
        up_weight,
        down_weight,
    )
    grad_gate, grad_up, grad_down, grad_taken = expert_backward(
        arrived,
        grad_arrived,
        (gate_in, up_in, sigma, active, hidden_mid),
        back_set[5],
        back_set[6],
        back_set[7],
    )
    grad_back = lax.all_to_all(grad_taken, "expert", split_axis=1, concat_axis=1, tiled=True)
    gain_one_back, mixer_back, projector_back, gain_two_back, router_back = (
        back_set[0],
        back_set[1],
        back_set[2],
        back_set[3],
        back_set[4],
    )
    location = (
        routes % local_count * (owner_count * capacity) + routes // local_count * capacity + slots
    )
    picked = returned.reshape(-1, width)[location]
    output = resid + jnp.sum(gates[:, :, None] * picked, axis=1)
    grad_gates = jnp.sum(upstream[:, None, :] * picked, axis=2)
    grad_hidden_two = jnp.sum(grad_back.reshape(-1, width)[location], axis=1, dtype=jnp.float32)
    mean_gate = jnp.sum(gates * grad_gates, axis=1, keepdims=True)
    grad_chosen = gates * (grad_gates - mean_gate)
    grad_logits = jnp.sum(jnp.where(route_hot, grad_chosen[:, :, None], 0.0), axis=1)
    grad_hidden_two = grad_hidden_two + jnp.dot(
        grad_logits, router_back.astype(jnp.float32).T, precision=lax.Precision.HIGHEST
    )
    grad_router = jnp.dot(
        hidden_two.astype(jnp.float32).T, grad_logits, precision=lax.Precision.HIGHEST
    )
    grad_gain_two = jnp.sum(grad_hidden_two * normed_two, axis=0)
    grad_normed_two = grad_hidden_two * gain_two_back.astype(jnp.float32)[None, :]
    grad_resid = upstream + scale_two * (
        grad_normed_two - normed_two * jnp.mean(grad_normed_two * normed_two, axis=1, keepdims=True)
    )
    grad_branch = grad_resid.astype(jnp.bfloat16)
    grad_projector = jnp.dot(attended.T, grad_branch, preferred_element_type=jnp.float32)
    grad_attended = jnp.dot(
        grad_branch, projector_back.T, preferred_element_type=jnp.float32
    ).astype(jnp.bfloat16)
    grad_heads = jnp.transpose(
        grad_attended.reshape(token_count, KV_HEADS, groups, HEAD_DIM), (1, 0, 2, 3)
    )
    grad_query, grad_key, grad_value = lax.map(
        partial(attend_backward, allowed, scaling),
        (query_heads, key_heads, value_heads, grad_heads, log_total),
    )
    grad_query = jnp.transpose(grad_query, (1, 0, 2, 3)).reshape(token_count, HEADS, HEAD_DIM)
    grad_key = jnp.transpose(grad_key, (1, 0, 2))
    grad_value = jnp.transpose(grad_value, (1, 0, 2))
    grad_mixed = jnp.concatenate(
        [
            unrotate(grad_query, cosine, sine).reshape(token_count, query_width),
            unrotate(grad_key, cosine, sine).reshape(token_count, key_width),
            grad_value.reshape(token_count, key_width),
        ],
        axis=1,
    ).astype(jnp.bfloat16)
    grad_mixer = jnp.dot(hidden_one.T, grad_mixed, preferred_element_type=jnp.float32)
    grad_hidden_one = jnp.dot(grad_mixed, mixer_back.T, preferred_element_type=jnp.float32)
    grad_gain_one = jnp.sum(grad_hidden_one * normed_one, axis=0)
    grad_normed_one = grad_hidden_one * gain_one_back.astype(jnp.float32)[None, :]
    grad_input = grad_resid + scale_one * (
        grad_normed_one - normed_one * jnp.mean(grad_normed_one * normed_one, axis=1, keepdims=True)
    )
    shares = (
        lax.psum_scatter(
            grad_gain_one.astype(jnp.bfloat16), "shard", scatter_dimension=0, tiled=True
        ).astype(jnp.float32),
        lax.psum_scatter(
            grad_mixer.astype(jnp.bfloat16), "shard", scatter_dimension=0, tiled=True
        ).astype(jnp.float32),
        lax.psum_scatter(
            grad_projector.astype(jnp.bfloat16), "shard", scatter_dimension=0, tiled=True
        ).astype(jnp.float32),
        lax.psum_scatter(
            grad_gain_two.astype(jnp.bfloat16), "shard", scatter_dimension=0, tiled=True
        ).astype(jnp.float32),
        lax.psum_scatter(
            grad_router.astype(jnp.bfloat16), "shard", scatter_dimension=0, tiled=True
        ).astype(jnp.float32),
    )
    totals = (
        lax.psum(shares[0].astype(jnp.bfloat16), "expert").astype(jnp.float32),
        lax.psum(shares[1].astype(jnp.bfloat16), "expert").astype(jnp.float32),
        lax.psum(shares[2].astype(jnp.bfloat16), "expert").astype(jnp.float32),
        lax.psum(shares[3].astype(jnp.bfloat16), "expert").astype(jnp.float32),
        lax.psum(shares[4].astype(jnp.bfloat16), "expert").astype(jnp.float32),
    )
    expert_shares = (
        lax.psum_scatter(
            grad_gate.astype(jnp.bfloat16), "shard", scatter_dimension=1, tiled=True
        ).astype(jnp.float32),
        lax.psum_scatter(
            grad_up.astype(jnp.bfloat16), "shard", scatter_dimension=1, tiled=True
        ).astype(jnp.float32),
        lax.psum_scatter(
            grad_down.astype(jnp.bfloat16), "shard", scatter_dimension=2, tiled=True
        ).astype(jnp.float32),
    )
    return (
        output.astype(jnp.bfloat16),
        grad_input.astype(jnp.bfloat16),
        totals[0],
        totals[1],
        totals[2],
        totals[3],
        totals[4],
        expert_shares[0],
        expert_shares[1],
        expert_shares[2],
    )


def solution(mesh):
    return jax.shard_map(
        per_device,
        mesh=mesh,
        in_specs=(
            P(("expert", "shard"), None),
            P(("expert", "shard"), None),
            P(("expert", "shard")),
            P(("expert", "shard"), None),
            P("shard"),
            P("shard", None),
            P("shard", None),
            P("shard"),
            P("shard", None),
            P("expert", "shard", None),
            P("expert", "shard", None),
            P("expert", None, "shard"),
        ),
        out_specs=(
            P(("expert", "shard"), None),
            P(("expert", "shard"), None),
            P("shard"),
            P("shard", None),
            P("shard", None),
            P("shard"),
            P("shard", None),
            P("expert", "shard", None),
            P("expert", "shard", None),
            P("expert", None, "shard"),
        ),
        check_vma=False,
    )
```

profile of v0, /device:TPU:0, one launch (start us, length us, event | category | flops | bytes accessed | tf_op | source)
XLA Modules:
  0.0 2060.4 jit_solution(1354389074873814163)
XLA Ops:
  12.7 9.5 all-gather.1
  22.3 8.1 all-gather
  30.8 4.6 reduce-window.6
  36.7 15.8 scatter_custom_fusion
  52.8 43.1 %all-gather.8.cloned.1.call-done = bf16[1536,2560]{1,0:T(8,128)(2,1)} async-done(((bf16[384,2560]{1,0:T(8,128)(2,1)}), bf16[1536,2560]{1,0:T(8,128)(2,1)}) %all-gather.8.cloned.1.call-update) | async-done | bytes 7864336 | tf_op jit(solution)/shard_map/all_gather | solution.py:201
  96.0 6.6 fusion.102
  106.7 2.7 copy.157
  117.5 45.7 %while.44 = (s32[]{:T(128)}, bf16[8,512,3,64]{1,3,2,0:T(8,128)(2,1)}, f32[8,3,512]{2,1,0:T(4,128)}, bf16[8,512,64]{1,2,0:T(8,128)(2,1)}, bf16[8,512,64]{1,2,0:T(...) while((s32[]{:T(128)}, ...), condition=%wide.region_8.9_spmd.clone.clone, body=%wide.region_5.8_spmd.clone.sunk.clone | while | flops 211286528 | bytes 11262041 | solution.py:242
  120.1 2.6 fusion.209
  125.8 2.6 fusion.209
  137.2 2.6 fusion.209
  142.9 2.6 fusion.209
  148.6 2.6 fusion.209
  160.0 2.6 fusion.209
  163.2 5.3 multiply_reduce_fusion.2
  171.7 23.8 %gather_fusion = bf16[5120,1536]{1,0:T(8,128)(2,1)} fusion(bf16[513,1536]{1,0:T(8,128)(2,1)S(1)} %concatenate.44, s32[5120]{0:T(1024)S(1)} %broadcast_clamp_fusion.1), kind=kCustom, calls=%fused_computation | custom fusion | bytes 31477760 | tf_op jit(solution)/shard_map/gather | solution.py:267
  195.5 29.3 %copy.165 = bf16[2,2560,1536]{2,0,1:T(2,128)(2,1)} copy(bf16[2,2560,1536]{2,1,0:T(8,128)(2,1)} %bitcast.310) | data formatting | bytes 31457280 | tf_op jit(solution)/shard_map/gather | solution.py:267
  224.8 5.6 all-to-all-start
  232.3 8.7 all_gather.36
  245.1 3.8 fusion.68
  249.0 5.6 concatenate.46
  254.6 37.5 %gather_fusion.2 = bf16[5120,1536]{1,0:T(8,128)(2,1)} fusion(bf16[4097,1536]{1,0:T(8,128)(2,1)} %concatenate.46, s32[5120]{0:T(1024)S(1)} %broadcast_clamp_fusion), kind=kCustom, calls=%fused_computation.2 | custom fusion | bytes 31477760 | tf_op jit(solution)/shard_map/gather | solution.py:275
  292.1 29.3 %copy.175 = bf16[2,2560,1536]{2,0,1:T(2,128)(2,1)} copy(bf16[2,2560,1536]{2,1,0:T(8,128)(2,1)} %bitcast.311) | data formatting | bytes 31457280 | tf_op jit(solution)/shard_map/gather | solution.py:275
  321.3 250.3 %all-to-all-done = bf16[2,2560,1536]{2,0,1:T(2,128)(2,1)} async-done(((bf16[2,2560,1536]{2,0,1:T(2,128)(2,1)}), bf16[2,2560,1536]{2,0,1:T(2,128)(2,1)}, u32[]{:S(2)}, u32[]{:S(2)}) %all-to-all-start) | async-done | bytes 15728672 | tf_op jit(solution)/shard_map/all_to_all | solution.py:276
  571.6 5.6 all-to-all-start.2
  579.1 38.9 %copy.182 = bf16[2,2560,1536]{1,2,0:T(8,128)(2,1)} copy(bf16[2,2560,1536]{2,0,1:T(2,128)(2,1)} %all-to-all-done) | data formatting | bytes 31457280 | tf_op jit(solution)/shard_map/all_to_all | solution.py:276
  618.1 6.3 all-gather.14.cloned.1.call-done
  624.4 15.1 fusion.129
  639.4 30.7 %all-gather.12.cloned.1.call-done = bf16[2,1536,512]{2,1,0:T(8,128)(2,1)} async-done(((bf16[2,384,512]{2,1,0:T(8,128)(2,1)}), bf16[2,1536,512]{2,1,0:T(8,128)(2,1)}) %all-gather.12.cloned.1.call-update) | async-done | bytes 3145744 | tf_op jit(solution)/shard_map/all_gather | solution.py:207
  670.1 15.2 fusion.128
  685.2 30.4 %all-gather.16.cloned.1.call-done = bf16[2,512,1536]{2,1,0:T(8,128)(2,1)} async-done(((bf16[2,512,384]{2,1,0:T(8,128)(2,1)}), bf16[2,512,1536]{2,1,0:T(8,128)(2,1)}) %all-gather.16.cloned.1.call-update) | async-done | bytes 3145744 | tf_op jit(solution)/shard_map/all_gather | solution.py:209
  715.6 202.8 %all-to-all-done.2 = bf16[2,2560,1536]{2,0,1:T(2,128)(2,1)} async-done(((bf16[2,2560,1536]{2,0,1:T(2,128)(2,1)}), bf16[2,2560,1536]{2,0,1:T(2,128)(2,1)}, u32[]{:S(2)}, u32[]{:S(2)}) %all-to-all-start.2) | async-done | bytes 15728672 | tf_op jit(solution)/shard_map/all_to_all | solution.py:281
  918.4 25.5 %multiply_convert_fusion = (bf16[2,2560,512]{2,1,0:T(8,128)(2,1)}, bf16[2,2560,512]{2,1,0:T(8,128)(2,1)}, bf16[2,2560,512]{2,1,0:T(8,128)(2,1)}) fusion(f32[2,2560,512]{2,1,0:T(8,128)} %fusion.128, f32[2,2560,512]{2,1,0:T(8,128)} %fusion.129, bf16[2,512,1536]{2,1,0:T(8,128)(2,1)} %all-gather.16.cloned.1.call-done, bf16[2,2560,1536]{2,0,1:T(2,128)(2,1)} %all-to-all-done.2), kind=kOutput, calls=%fused_computation.91 | convolution fusion | flops 8092385280 | bytes 55574528 | tf_op jit(solution)/shard_map/lrd,lfd->lrf/dot_general | solution.py:138
  943.9 13.6 convolution_convert_fusion
  957.5 29.3 %copy.168 = bf16[2,2560,1536]{2,0,1:T(2,128)(2,1)} copy(bf16[2,2560,1536]{2,1,0:T(8,128)(2,1)} %convolution_convert_fusion) | data formatting | bytes 31457280 | tf_op jit(solution)/shard_map/convert_element_type | solution.py:132
  986.7 5.9 all-to-all-start.1
  992.6 17.7 fusion.130
  1010.3 21.7 %add_convert_fusion = bf16[2,2560,1536]{2,1,0:T(8,128)(2,1)} fusion(f32[2,2560,1536]{2,1,0:T(8,128)} %fusion.130, bf16[2,2560,512]{2,1,0:T(8,128)(2,1)} %get-tuple-element.251, bf16[2,1536,512]{2,1,0:T(8,128)(2,1)S(1)} %copy-done.54), kind=kOutput, calls=%fused_computation.79 | convolution fusion | flops 8068792320 | bytes 55574528 | tf_op jit(solution)/shard_map/lrf,ldf->lrd/dot_general | solution.py:155
  1032.0 29.3 %copy.177 = bf16[2,2560,1536]{2,0,1:T(2,128)(2,1)} copy(bf16[2,2560,1536]{2,1,0:T(8,128)(2,1)} %add_convert_fusion) | data formatting | bytes 31457280 | tf_op jit(solution)/shard_map/convert_element_type | solution.py:156
  1061.3 272.5 %all-to-all-done.1 = bf16[2,2560,1536]{2,0,1:T(2,128)(2,1)} async-done(((bf16[2,2560,1536]{2,0,1:T(2,128)(2,1)}), bf16[2,2560,1536]{2,0,1:T(2,128)(2,1)}, u32[]{:S(2)}, u32[]{:S(2)}) %all-to-all-start.1) | async-done | bytes 15728672 | tf_op jit(solution)/shard_map/all_to_all | solution.py:280
  1333.8 5.6 all-to-all-start.3
  1339.5 15.7 fusion.78
  1355.2 7.1 copy.193
  1365.0 14.3 convolution_convert_fusion.3
  1379.4 14.7 convolution_convert_fusion.4
  1395.5 15.3 copy.169
  1410.8 32.9 %gather_fusion.1 = bf16[4096,1536]{1,0:T(8,128)(2,1)} fusion(bf16[5120,1536]{1,0:T(8,128)(2,1)} %bitcast.309, s32[4096]{0:T(1024)S(1)} %broadcast_clamp_fusion.2), kind=kCustom, calls=%fused_computation.1 | custom fusion | bytes 25182208 | tf_op jit(solution)/shard_map/gather | solution.py:311
  1443.7 17.2 fusion.67
  1461.9 218.7 %all-to-all-done.3 = bf16[2,2560,1536]{2,0,1:T(2,128)(2,1)} async-done(((bf16[2,2560,1536]{2,0,1:T(2,128)(2,1)}), bf16[2,2560,1536]{2,0,1:T(2,128)(2,1)}, u32[]{:S(2)}, u32[]{:S(2)}) %all-to-all-start.3) | async-done | bytes 15728672 | tf_op jit(solution)/shard_map/all_to_all | solution.py:300
  1680.6 15.0 copy.178
  1695.6 32.8 %gather_fusion.3 = bf16[4096,1536]{1,0:T(8,128)(2,1)} fusion(bf16[5120,1536]{1,0:T(8,128)(2,1)} %bitcast.308, s32[4096]{0:T(1024)S(1)} %broadcast_clamp_fusion.2), kind=kCustom, calls=%fused_computation.3 | custom fusion | bytes 25182208 | tf_op jit(solution)/shard_map/gather | solution.py:314
  1728.6 10.9 convert_reduce_fusion
  1744.3 3.8 convolution_convert_fusion.5
  1750.7 5.8 convolution_convert_fusion.2
  1758.4 87.0 %while.45 = (s32[]{:T(128)}, f32[8,512,3,64]{1,3,2,0:T(8,128)S(1)}, f32[8,512,64]{1,2,0:T(8,128)}, bf16[8,512,64]{1,2,0:T(8,128)(2,1)}, bf16[8,512,64]{1,2,0:T(8...) while((s32[]{:T(128)}, f32[8,512,3,64]{1,3,2,0:T(8,128)S(1)}, ...), condition=%wide.region_25.26_spmd.clone.clone, body=%wide.region_23.25_spmd.clone.sunk.clone | while | flops 511048192 | bytes 25793648 | solution.py:337
  1850.7 8.2 convolution_convert_fusion.1
  1863.4 3.1 reshape.500
  1873.5 67.0 %reduce-scatter.11.cloned.1.call-done = bf16[384,2560]{1,0:T(8,128)(2,1)} async-done(((bf16[1536,2560]{1,0:T(8,128)(2,1)}), bf16[384,2560]{1,0:T(8,128)(2,1)}) %reduce-scatter.11.cloned.1.call-update) | async-done | bytes 1966096 | tf_op jit(solution)/shard_map/reduce_scatter | solution.py:363
  1940.5 11.1 fusion.87
  1951.6 9.1 all-reduce.6
  1960.8 4.4 fusion.86
  1968.7 29.3 %all-reduce.4 = (bf16[384]{0:T(512)(128)(2,1)S(1)}, bf16[384]{0:T(512)(128)(2,1)S(1)}, bf16[384,16]{0,1:T(8,128)(2,1)S(1)}) all-reduce(bf16[384]{0:T(512)(128)(2,1)S(1)} %dynamic-slice.1, bf16[384]{0:T(512)(128)(2,1)S(1)} %dynamic-slice.3, bf16[384,16]{0,1:T(8,128)(2,1)S(1)} %copy.192), channel_id=1, replica_groups=mesh['expert'=8,'shard'=4] {'expert'}, use_global_device_ids=true, to_apply=%region_29.30 | all-reduce | flops 6912 | bytes 27648 | tf_op jit(solution)/shard_map/psum | solution.py:377
  1999.8 47.9 %all-reduce.9.cloned.1.call-done = (bf16[384,2560]{1,0:T(8,128)(2,1)}, bf16[384,1536]{1,0:T(8,128)(2,1)}) async-done(((bf16[384,2560]{1,0:T(8,128)(2,1)}, bf16[384,1536]{1,0:T(8,128)(2,1)}), (bf16[384,2560]{1,0:T(8,128)(2,1)}, bf16[384,1536]{1,0:T(8,128)(2,1)})) %all-reduce.9.cloned.1.call-update) | async-done | bytes 3145744 | tf_op jit(solution)/shard_map/psum | solution.py:378
  2047.7 4.0 convert_element_type.195
  (367 shorter events, 185.5 us)
Async XLA Ops:
  7.2 3.5 copy-start.50
  7.2 3.5 copy-start.51
  7.2 3.5 copy-start.13
  7.2 88.8 %all-gather.8.cloned.1.call-start = ((), (), s32[]{:S(2)}) async-start(), calls=%async_computation.10 | async-start | bytes 9830400 | tf_op jit(solution)/shard_map/all_gather | solution.py:201
  8.0 3.2 copy-start.57
  8.0 155.2 %all-gather.10.cloned.1.call-start = ((), (), s32[]{:S(2)}) async-start(), calls=%async_computation.11 | async-start | bytes 5898240 | tf_op jit(solution)/shard_map/all_gather | solution.py:202
  8.9 27.3 %copy-start.11 = (s32[512,8]{1,0:T(8,128)}, s32[512,8]{1,0:T(8,128)S(1)}, u32[]{:S(2)}) copy-start(s32[512,8]{1,0:T(8,128)S(1)} %copy.161) | copy-start | bytes 49156
  9.2 27.3 %copy-start.53 = (s32[2]{0:T(128)S(1)}, s32[2]{0:T(128)}, u32[]{:S(2)}) copy-start(s32[2]{0:T(128)} %constant.173) | copy-start | bytes 28
  9.2 27.4 %copy-start.52 = (s32[2]{0:T(128)S(1)}, s32[2]{0:T(128)}, u32[]{:S(2)}) copy-start(s32[2]{0:T(128)} %constant.170) | copy-start | bytes 28
  11.1 91.5 %copy-start.48 = (f32[512]{0:T(512)}, f32[512]{0:T(512)S(1)}, u32[]{:S(2)}) copy-start(f32[512]{0:T(512)S(1)} %add_rsqrt_fusion.1) | copy-start | bytes 6148
  22.3 146.2 %copy-start.37 = (f32[1536]{0:T(1024)}, f32[1536]{0:T(1024)S(1)}, u32[]{:S(2)}) copy-start(f32[1536]{0:T(1024)S(1)} %reshape.490) | copy-start | bytes 18436
  30.4 72.3 %copy-start.43 = (f32[1536]{0:T(1024)}, f32[1536]{0:T(1024)S(1)}, u32[]{:S(2)}) copy-start(f32[1536]{0:T(1024)S(1)} %reshape.489) | copy-start | bytes 18436
  30.7 84.8 %copy-start.18 = (f32[512,64]{0,1:T(8,128)}, f32[512,64]{0,1:T(8,128)S(1)}, u32[]{:S(2)}) copy-start(f32[512,64]{0,1:T(8,128)S(1)} %pad_maximum_fusion.4) | copy-start | bytes 393220
  30.7 84.8 %copy-start.20 = (f32[512,64]{0,1:T(8,128)}, f32[512,64]{0,1:T(8,128)S(1)}, u32[]{:S(2)}) copy-start(f32[512,64]{0,1:T(8,128)S(1)} %pad_maximum_fusion.5) | copy-start | bytes 393220
  36.4 66.2 %copy-start.33 = (s32[4096]{0:T(1024)}, s32[4096]{0:T(1024)S(1)}, u32[]{:S(2)}) copy-start(s32[4096]{0:T(1024)S(1)} %fusion.110) | copy-start | bytes 49156
  117.5 45.7 %copy-start.14 = (bf16[512,1536]{1,0:T(8,128)(2,1)S(1)}, bf16[512,1536]{1,0:T(8,128)(2,1)}, u32[]{:S(2)}) copy-start(bf16[512,1536]{1,0:T(8,128)(2,1)} %param.18) | copy-start | bytes 4718596
  163.2 5.3 copy-start.31
  168.5 1.7 copy-start.2
  168.5 2.0 copy-start.41
  224.8 346.8 %all-to-all-start = ((bf16[2,2560,1536]{2,0,1:T(2,128)(2,1)}), bf16[2,2560,1536]{2,0,1:T(2,128)(2,1)}, u32[]{:S(2)}, u32[]{:S(2)}) async-start(bf16[2,2560,1536]{2,0,1:T(2,128)(2,1)} %copy.165), calls=%async_computation | async-start | bytes 31457280 | tf_op jit(solution)/shard_map/all_to_all | solution.py:276
  230.4 1.9 copy-start.47
  232.3 16.6 copy-start
  243.7 5.3 copy-start.39
  245.0 4.0 copy-start.22
  571.6 346.8 %all-to-all-start.2 = ((bf16[2,2560,1536]{2,0,1:T(2,128)(2,1)}), bf16[2,2560,1536]{2,0,1:T(2,128)(2,1)}, u32[]{:S(2)}, u32[]{:S(2)}) async-start(bf16[2,2560,1536]{2,0,1:T(2,128)(2,1)} %copy.175), calls=%async_computation.2 | async-start | bytes 31457280 | tf_op jit(solution)/shard_map/all_to_all | solution.py:281
  577.2 47.1 %all-gather.14.cloned.1.call-start = ((), (), s32[]{:S(2)}) async-start(), calls=%async_computation.13 | async-start | bytes 3932160 | tf_op jit(solution)/shard_map/all_gather | solution.py:208
  578.0 92.1 %all-gather.12.cloned.1.call-start = ((), (), s32[]{:S(2)}) async-start(), calls=%async_computation.12 | async-start | bytes 3932160 | tf_op jit(solution)/shard_map/all_gather | solution.py:207
  578.6 137.1 %all-gather.16.cloned.1.call-start = ((), (), s32[]{:S(2)}) async-start(), calls=%async_computation.14 | async-start | bytes 3932160 | tf_op jit(solution)/shard_map/all_gather | solution.py:209
  715.6 228.3 %copy-start.55 = (bf16[2,512,1536]{2,1,0:T(8,128)(2,1)S(1)}, bf16[2,512,1536]{2,1,0:T(8,128)(2,1)}, u32[]{:S(2)}) copy-start(bf16[2,512,1536]{2,1,0:T(8,128)(2,1)} %all-gather.16.cloned.1.call-done) | copy-start | bytes 9437188
  986.7 347.1 %all-to-all-start.1 = ((bf16[2,2560,1536]{2,0,1:T(2,128)(2,1)}), bf16[2,2560,1536]{2,0,1:T(2,128)(2,1)}, u32[]{:S(2)}, u32[]{:S(2)}) async-start(bf16[2,2560,1536]{2,0,1:T(2,128)(2,1)} %copy.168), calls=%async_computation.1 | async-start | bytes 31457280 | tf_op jit(solution)/shard_map/all_to_all | solution.py:280
  992.6 17.7 copy-start.54
  1333.8 346.8 %all-to-all-start.3 = ((bf16[2,2560,1536]{2,0,1:T(2,128)(2,1)}), bf16[2,2560,1536]{2,0,1:T(2,128)(2,1)}, u32[]{:S(2)}, u32[]{:S(2)}) async-start(bf16[2,2560,1536]{2,0,1:T(2,128)(2,1)} %copy.177), calls=%async_computation.3 | async-start | bytes 31457280 | tf_op jit(solution)/shard_map/all_to_all | solution.py:300
  1339.4 523.9 %reduce-scatter.21.cloned.1.call-start = ((), (), s32[]{:S(2)}) async-start(), calls=%async_computation.20 | async-start | bytes 3932160
  1364.9 503.6 %reduce-scatter.17.cloned.1.call-start = ((), (), s32[]{:S(2)}) async-start(), calls=%async_computation.18 | async-start | bytes 3932160 | tf_op jit(solution)/shard_map/reduce_scatter | solution.py:387
  1379.3 491.7 %reduce-scatter.15.cloned.1.call-start = ((), (), s32[]{:S(2)}) async-start(), calls=%async_computation.17 | async-start | bytes 3932160 | tf_op jit(solution)/shard_map/reduce_scatter | solution.py:384
  1394.1 479.4 %reduce-scatter.13.cloned.1.call-start = ((), (), s32[]{:S(2)}) async-start(), calls=%async_computation.16 | async-start | bytes 5898240 | tf_op jit(solution)/shard_map/reduce_scatter | solution.py:366
  1410.8 32.9 %copy-start.1 = (f32[512,1536]{1,0:T(8,128)S(1)}, f32[512,1536]{1,0:T(8,128)}, u32[]{:S(2)}) copy-start(f32[512,1536]{1,0:T(8,128)} %copy-done) | copy-start | bytes 9437188
  1410.8 32.9 %copy-start.23 = (f32[512,8]{1,0:T(8,128)S(1)}, f32[512,8]{1,0:T(8,128)}, u32[]{:S(2)}) copy-start(f32[512,8]{1,0:T(8,128)} %copy-done.22) | copy-start | bytes 49156
  1695.6 32.8 %copy-start.27 = (f32[512,8]{0,1:T(8,128)S(1)}, f32[512,8]{0,1:T(8,128)}, u32[]{:S(2)}) copy-start(f32[512,8]{0,1:T(8,128)} %copy-done.26) | copy-start | bytes 49156
  1695.6 32.8 %copy-start.40 = (f32[512]{0:T(512)S(1)}, f32[512]{0:T(512)}, u32[]{:S(2)}) copy-start(f32[512]{0:T(512)} %copy-done.39) | copy-start | bytes 6148
  1695.6 32.8 %copy-start.46 = (f32[512]{0:T(512)S(1)}, f32[512]{0:T(512)}, u32[]{:S(2)}) copy-start(f32[512]{0:T(512)} %copy-done.45) | copy-start | bytes 6148
  1695.6 32.9 %copy-start.36 = (s32[512,8]{0,1:T(8,128)S(1)}, s32[512,8]{0,1:T(8,128)}, u32[]{:S(2)}) copy-start(s32[512,8]{0,1:T(8,128)} %param.21) | copy-start | bytes 49156
  1728.6 10.9 copy-start.3
  1728.6 10.9 copy-start.30
  1728.6 10.9 copy-start.38
  1728.6 10.9 copy-start.42
  1739.6 2.4 copy-start.9
  1739.6 2.4 copy-start.16
  1739.6 4.7 slice-start
  1742.0 2.3 slice-start.1
  1744.3 6.4 copy-start.7
  1756.5 1.9 copy-start.6
  1756.5 1.9 copy-start.32
  1756.5 184.0 %reduce-scatter.11.cloned.1.call-start = ((), (), s32[]{:S(2)}) async-start(), calls=%async_computation.15 | async-start | bytes 9830400 | tf_op jit(solution)/shard_map/reduce_scatter | solution.py:363
  1758.4 87.0 %copy-start.21 = (f32[512,64]{0,1:T(8,128)S(1)}, f32[512,64]{0,1:T(8,128)}, u32[]{:S(2)}) copy-start(f32[512,64]{0,1:T(8,128)} %copy-done.20) | copy-start | bytes 393220
  1848.6 1.9 copy-start.15
  1848.6 1.9 copy-start.44
  1848.6 1.9 copy-start.49
  1848.6 2.0 copy-start.56
  1858.9 3.2 copy-start.58
  1859.0 108.8 %reduce-scatter.19.cloned.1.call-start = ((), (), s32[]{:S(2)}) async-start(), calls=%async_computation.19 | async-start | bytes 491520
  1862.0 185.7 %all-reduce.9.cloned.1.call-start = ((), (), s32[]{:S(2)}) async-start(), calls=%async_computation.21 | async-start | bytes 6291456 | tf_op jit(solution)/shard_map/psum | solution.py:378
  1940.5 20.3 copy-start.8
  2047.7 4.1 copy-start.25
  (13 other events, 12.9 us)
Sparse Core Ops, SparseCore 0:
  9.9 86.0 all-gather.7
  97.8 57.0 all-gather.9
  579.9 44.4 all-gather.13
  626.1 43.9 all-gather.11
  671.7 43.8 all-gather.15
  1365.0 44.3 reduce-scatter.20
  1412.4 43.9 reduce-scatter.16
  1459.3 43.9 reduce-scatter.14
  1756.6 55.0 reduce-scatter.12
  1859.1 81.3 reduce-scatter.10
  1943.3 24.4 reduce-scatter.18
  1970.0 77.5 all-reduce.8
where the time goes:
time: 2070 us; the launch traced here: 2060 us
  waiting for transfers between devices  1180 us (57%)
  local copies, waits for them, and re-layouts  383 us (19%)
  matrix products  308 us (15%)
  other arithmetic  89.6 us (4%)
  blocking collectives  64.7 us (3%)
  starting transfers between devices  23.2 us (1%)
    all_to_all x1, waiting for transfers between devices, per_device(): lax.all_to_all(produced, 'expert', split_axis=1, concat_axis=1, tiled=True)  273 us
    all_to_all x1, waiting for transfers between devices, per_device(): lax.all_to_all(outgoing, 'expert', split_axis=1, concat_axis=1, tiled=True)  250 us
    all_to_all x1, waiting for transfers between devices, per_device(): lax.all_to_all(grad_taken, 'expert', split_axis=1, concat_axis=1, tiled=T...  219 us
    all_to_all x1, waiting for transfers between devices, per_device(): lax.all_to_all(grad_outgoing, 'expert', split_axis=1, concat_axis=1, tile...  203 us
    reduce_scatter x1, waiting for transfers between devices, per_device(): lax.psum_scatter(grad_mixer.astype(jnp.bfloat16), 'shard', scatter_dimens...  67 us
    gather x2, local copies, waits for them, and re-layouts, per_device(): grad_outgoing = weighted[send_table]  66.8 us
    gather x2, local copies, waits for them, and re-layouts, per_device(): outgoing = padded[send_table // TOP]  53.1 us
    psum x1, waiting for transfers between devices, per_device(): lax.psum(shares[1].astype(jnp.bfloat16), 'expert').astype(jnp.float32)  47.9 us
  transfers between devices with their start and end apart: 16, of which 11 were waited for; matrix products, arithmetic and copies ran while one was open for 31% of the time, Pallas kernels for 0%

commit v1 on v0

v1 whole, which is shorter than its diff:
```python
import jax
import jax.numpy as jnp
from jax import lax
from jax.experimental import pallas as pl
from jax.experimental.pallas import tpu as pltpu
from jax.sharding import PartitionSpec as P

HEADS = 24
KV_HEADS = 8
HEAD_DIM = 64
SEG = 128

EPSILON = 1e-06
THETA = 10000.0
NEGATIVE = -1e30

NT = (((1,), (1,)), ((), ()))
NN = (((1,), (0,)), ((), ()))
TN = (((0,), (0,)), ((), ()))
def dot(left, right, dims):
    return lax.dot_general(left, right, dims, preferred_element_type=jnp.float32)

def turned(values):
    lane = lax.broadcasted_iota(jnp.int32, values.shape, 1)
    first = lane % HEAD_DIM < HEAD_DIM // 2
    ahead = pltpu.roll(values, 128 - HEAD_DIM // 2, 1)
    behind = pltpu.roll(values, HEAD_DIM // 2, 1)
    return jnp.where(first, -ahead, behind)


def tree_tables(parents):
    segs = parents.shape[0]
    ids = jnp.arange(segs, dtype=jnp.int32)
    pointer = ids
    ancestry = jnp.zeros((segs, segs), jnp.bool_)
    for _ in range(segs):
        landed = pointer[:, None] == ids[None, :]
        ancestry = ancestry | landed
        pointer = jnp.sum(jnp.where(landed, parents[None, :], 0), axis=1)
    depth = jnp.sum(ancestry.astype(jnp.float32), axis=1) - 1.0
    token_ids = jnp.arange(segs * SEG, dtype=jnp.int32)
    positions = jnp.repeat(depth, SEG) * SEG + (token_ids % SEG).astype(jnp.float32)
    reach = jnp.repeat(jnp.repeat(ancestry.astype(jnp.float32), SEG, axis=0), SEG, axis=1)
    allowed = (reach > 0.5) & (token_ids[None, :] <= token_ids[:, None])
    half = HEAD_DIM // 2
    frequency = THETA ** (-(jnp.arange(half, dtype=jnp.float32) * 2.0) / HEAD_DIM)
    angles = positions[:, None] * frequency[None, :]
    cosine, sine = jnp.cos(angles), jnp.sin(angles)
    return (
        jnp.where(allowed, 0.0, NEGATIVE),
        jnp.concatenate([cosine] * 4, axis=1),
        jnp.concatenate([sine] * 4, axis=1),
    )


def inverse_rms(values):
    return lax.rsqrt(jnp.mean(values * values, axis=1, keepdims=True) + EPSILON)


def swap_core(value):
    count = lax.axis_size("expert")
    return lax.ppermute(value, "expert", [(i, i ^ 1) for i in range(count)])


def next_chip(value):
    count = lax.axis_size("expert")
    return lax.ppermute(value, "expert", [(i, (i + 2) % count) for i in range(count)])


def across(value, mask):
    return lax.ppermute(value, "shard", [(i, i ^ mask) for i in range(4)])


def after(value, *earlier):
    return lax.optimization_barrier((value,) + earlier)[0]


def gather_first(block, on_lanes=False):
    if lax.axis_size("shard") != 4:
        if on_lanes:
            return [lax.all_gather(block, "shard", axis=block.ndim - 1, tiled=True)[None]]
        return [lax.all_gather(block, "shard", axis=0, tiled=False)]
    return [block[None], across(block, 1)[None], across(block, 2)[None]]


def gather_second(pieces, split):
    if len(pieces) == 1:
        return pieces
    axis = split + 1
    half = pieces[1].shape[axis] // 2
    first = lax.slice_in_dim(pieces[2], 0, half, axis=axis)
    last = lax.slice_in_dim(pieces[1], half, 2 * half, axis=axis)
    return pieces + [across(first, 1), across(last, 2)]


def gather_small(value):
    if lax.axis_size("shard") != 4:
        return lax.all_gather(value, "shard", axis=1, tiled=True)
    me = lax.axis_index("shard")
    parts = [value, across(value, 1), across(value, 2), across(value, 3)]
    odd = me % 2 == 1
    parts = [jnp.where(odd, parts[i ^ 1], parts[i]) for i in range(4)]
    high = me >= 2
    parts = [jnp.where(high, parts[i ^ 2], parts[i]) for i in range(4)]
    return jnp.concatenate(parts, axis=1)


def shard_order():
    shards = lax.axis_size("shard")
    me = lax.axis_index("shard")
    core = lax.axis_index("expert") % 2
    if shards != 4:
        return jnp.concatenate([jnp.arange(shards, dtype=jnp.int32), core[None].astype(jnp.int32)])
    return jnp.stack([me, me ^ 1, me ^ 2, me ^ 3, me ^ 3, core]).astype(jnp.int32)


def add_low(*terms):
    total = terms[0].astype(jnp.float32)
    for term in terms[1:]:
        total = total + term.astype(jnp.float32)
    return total.astype(jnp.bfloat16)


def reduce_first(blocks):
    if lax.axis_size("shard") != 4:
        return (lax.psum_scatter(blocks, "shard", scatter_dimension=0, tiled=False),)
    me = lax.axis_index("shard")
    own, beside, above, far = (
        lax.dynamic_index_in_dim(blocks, me ^ r, 0, keepdims=False) for r in range(4)
    )
    half = own.shape[0] // 2
    from_x = across(jnp.concatenate([far[:half], beside[:half]]), 1)
    from_y = across(jnp.concatenate([far[half:], above[half:]]), 2)
    return own, beside[half:], above[:half], from_x, from_y


def reduce_second(state):
    if len(state) == 1:
        return state
    own, beside, above, from_x, from_y = state
    half = own.shape[0] // 2
    last_x = across(add_low(beside, from_y[:half]), 1)
    last_y = across(add_low(above, from_x[:half]), 2)
    return own, from_x[half:], from_y[half:], last_x, last_y


def reduce_last(state, dtype=jnp.bfloat16):
    if len(state) == 1:
        return state[0].astype(dtype)
    own, from_x, from_y, last_x, last_y = (v.astype(jnp.float32) for v in state)
    half = own.shape[0] // 2
    return jnp.concatenate([own[:half] + from_x + last_y, own[half:] + last_x + from_y]).astype(dtype)


def reduce_chips(value):
    count = lax.axis_size("expert")
    mask = 2
    while mask < count:
        value = add_low(value, lax.ppermute(value, "expert", [(i, i ^ mask) for i in range(count)]))
        mask *= 2
    return value


def piece_copies(pieces, order_ref, target, sem, axis, split, base=0, stride=None, window=None):
    copies = []
    slot = 0
    block = pieces[0].shape[1:]
    stride = block[axis] if stride is None else stride
    align = 128 if axis == len(block) - 1 else 16
    for piece in pieces:
        for c in range(piece.shape[0]):
            shape = piece.shape[1:]
            start = [0] * len(shape)
            if slot == 4 and shape[split] < block[split]:
                start[split] = block[split] - shape[split]
            start[axis] = pl.multiple_of(order_ref[slot] * stride + base + start[axis], align)
            index = tuple(pl.ds(first, size) for first, size in zip(start, shape))
            source = piece.at[c]
            if window is not None:
                cols = shape[-1] // 2
                source = source.at[:, window * cols : (window + 1) * cols]
                index = index[:-1] + (slice(None),)
            copies.append(pltpu.make_async_copy(source, target.at[index], sem))
            slot += 1
    return copies


def attend_kernel(count, call, order_ref, group_ref, hidden_ref, cos_ref, sin_ref, bias_ref, *rest):
    mine, other = rest[:count], rest[count : 2 * count]
    att_ref, q_ref, k_ref, v_ref, lse_ref, weight_ref, sems = rest[-7:]
    step = pl.program_id(0)
    first = piece_copies(mine, order_ref, weight_ref.at[0], sems.at[0], 0, 0, window=call)
    second = piece_copies(other, order_ref, weight_ref.at[1], sems.at[1], 0, 0, window=call)

    @pl.when(step == 0)
    def _():
        for copy in first + second:
            copy.start()
        for copy in first:
            copy.wait()

    @pl.when(step == 1)
    def _():
        for copy in second:
            copy.wait()

    hidden = hidden_ref[...]
    cosine, sine = cos_ref[...], sin_ref[...]
    mixed = dot(hidden, weight_ref[step], NN)
    low = jnp.bfloat16
    for p in range(3):
        part = mixed[:, 128 * p : 128 * p + 128]
        q_ref[:, 128 * p : 128 * p + 128] = (part * cosine + turned(part) * sine).astype(low)
    part = mixed[:, 384:512]
    k_ref[...] = (part * cosine + turned(part) * sine).astype(low)
    v_ref[...] = mixed[:, 512:640].astype(low)
    scaling = HEAD_DIM ** (-0.5)
    tokens = hidden.shape[0]
    for seg in range(tokens // SEG):
        rows = pl.ds(seg * SEG, SEG)
        span = (seg + 1) * SEG
        bias = bias_ref[rows, :span]
        outs = []
        logs = []
        for h in range(6):
            kv = h // 3
            keys = k_ref[:span, HEAD_DIM * kv : HEAD_DIM * (kv + 1)]
            vals = v_ref[:span, HEAD_DIM * kv : HEAD_DIM * (kv + 1)]
            query = q_ref[rows, HEAD_DIM * h : HEAD_DIM * (h + 1)]
            scores = dot(query, keys, NT) * scaling + bias
            highest = jnp.max(scores, axis=1, keepdims=True)
            powers = jnp.exp(scores - highest)
            total = jnp.sum(powers, axis=1, keepdims=True)
            probs = (powers * (1.0 / total)).astype(low)
            outs.append(dot(probs, vals, NN))
            logs.append(highest + jnp.log(total))
        att_ref[rows, :] = jnp.concatenate(outs, axis=1).astype(low)
        lse_ref[rows, :] = jnp.concatenate(logs + [logs[-1]] * 2, axis=1)


def attend(hidden, mixer_p, call, order, groups, cosine, sine, bias, kept):
    tokens, width = hidden.shape
    low = jnp.bfloat16
    whole = lambda a: pl.BlockSpec(a.shape, lambda j, o, g: (0, 0))
    anywhere = pl.BlockSpec(memory_space=pl.ANY)
    col = lambda w: pl.BlockSpec((tokens, w), lambda j, o, g: (0, g[j]))
    shape = lambda w: jax.ShapeDtypeStruct((tokens, w), low)
    operands = [order, groups, hidden, cosine, sine, bias, *mixer_p]
    in_specs = [whole(hidden), whole(cosine), whole(sine), whole(bias)]
    in_specs += [anywhere] * len(mixer_p)
    aliases = {}
    if kept is not None:
        aliases = {len(operands) + i: i for i in range(5)}
        operands += list(kept)
        in_specs += [anywhere] * 5
    cols = mixer_p[0].shape[-1] // 2
    return pl.pallas_call(
        lambda *refs: attend_kernel(len(mixer_p) // 2, call, *refs),
        grid_spec=pltpu.PrefetchScalarGridSpec(
            num_scalar_prefetch=2,
            grid=(2,),
            in_specs=in_specs,
            out_specs=[col(384), col(384), col(128), col(128)]
            + [pl.BlockSpec((None, tokens, 8), lambda j, o, g: (g[j], 0, 0))],
            scratch_shapes=[pltpu.VMEM((2, width, cols), low), pltpu.SemaphoreType.DMA((2,))],
        ),
        out_shape=[shape(1536), shape(1536), shape(512), shape(512)]
        + [jax.ShapeDtypeStruct((4, tokens, 8), jnp.float32)],
        input_output_aliases=aliases,
        compiler_params=pltpu.CompilerParams(vmem_limit_bytes=40 * 2**20),
        cost_estimate=pl.CostEstimate(flops=16 * 10**9, bytes_accessed=8 * 10**6, transcendentals=0),
        name="attend",
    )(*operands)


def projector_copies(count, pieces, order_ref, target, sem):
    rows = pieces[0].shape[1]
    slots = order_ref.shape[0] - 1
    core = order_ref[slots]
    copies = piece_copies(pieces[:count], order_ref, target, sem, 0, 0, core * rows, 2 * rows)
    return copies + piece_copies(
        pieces[count:], order_ref, target, sem, 0, 0, (1 - core) * rows, 2 * rows
    )


def attend_back_kernel(mine, counts, call, group_ref, order_ref, branch_ref, hidden_ref, q_ref, k_ref, v_ref, lse_ref, cos_ref, sin_ref, bias_ref, *rest):
    first, second = counts
    pieces, mixer_p = rest[:first], rest[first : first + second]
    wide_ref, input_ref, proj_ref, weight_ref, mixed_ref, grad_ref, dk_ref, dv_ref, sems = rest[first + second :]
    step = pl.program_id(0)
    load = projector_copies(mine, pieces, order_ref, proj_ref, sems.at[0])
    half = second // 2
    more = [
        piece_copies(mixer_p[c * half : (c + 1) * half], order_ref, weight_ref.at[c], sems.at[1 + c], 0, 0, window=call)
        for c in range(2)
    ]

    @pl.when(step == 0)
    def _():
        for copy in load + more[0] + more[1]:
            copy.start()
        for copy in load:
            copy.wait()

    group = group_ref[step]
    low = jnp.bfloat16
    rows = pl.ds(pl.multiple_of(group * 384, 128), 384)
    grad_ref[...] = dot(branch_ref[...], proj_ref[rows, :], NT).astype(low)
    cosine, sine = cos_ref[...], sin_ref[...]
    scaling = HEAD_DIM ** (-0.5)
    tokens = branch_ref.shape[0]
    for seg in reversed(range(tokens // SEG)):
        rows = pl.ds(seg * SEG, SEG)
        span = (seg + 1) * SEG
        bias = bias_ref[rows, :span]
        gqs = []
        gks = []
        gvs = []
        for kv in range(2):
            keys = k_ref[:span, HEAD_DIM * kv : HEAD_DIM * (kv + 1)]
            vals = v_ref[:span, HEAD_DIM * kv : HEAD_DIM * (kv + 1)]
            gscore = []
            probs_all = []
            queries = []
            grads = []
            for h in range(3 * kv, 3 * kv + 3):
                query = q_ref[rows, HEAD_DIM * h : HEAD_DIM * (h + 1)]
                grad = grad_ref[rows, HEAD_DIM * h : HEAD_DIM * (h + 1)]
                scores = dot(query, keys, NT) * scaling + bias
                probs = jnp.exp(scores - lse_ref[rows, h : h + 1])
                gprobs = dot(grad, vals, NT)
                centre = jnp.sum(probs * gprobs, axis=1, keepdims=True)
                gs = (probs * (gprobs - centre)).astype(low)
                gqs.append(dot(gs, keys, NN) * scaling)
                gscore.append(gs)
                probs_all.append(probs.astype(low))
                queries.append(query)
                grads.append(grad)
            gks.append(dot(jnp.concatenate(gscore, 0), jnp.concatenate(queries, 0), TN) * scaling)
            gvs.append(dot(jnp.concatenate(probs_all, 0), jnp.concatenate(grads, 0), TN))
        gq = jnp.concatenate(gqs, axis=1)
        cos_rows, sin_rows = cosine[seg * SEG : span], sine[seg * SEG : span]
        for p in range(3):
            part = gq[:, 128 * p : 128 * p + 128]
            mixed_ref[rows, 128 * p : 128 * p + 128] = (
                part * cos_rows - turned(part * sin_rows)
            ).astype(low)
        gk = jnp.concatenate(gks, axis=1)
        gv = jnp.concatenate(gvs, axis=1)
        if span == tokens:
            dk_ref[...] = gk
            dv_ref[...] = gv
        else:
            dk_ref[:span, :] += gk
            dv_ref[:span, :] += gv
    gk = dk_ref[...]
    mixed_ref[:, 384:512] = (gk * cosine - turned(gk * sine)).astype(low)
    mixed_ref[:, 512:640] = dv_ref[...].astype(low)
    for c in range(2):

        @pl.when(step == c)
        def _():
            for copy in more[c]:
                copy.wait()

    wide_ref[...] = dot(hidden_ref[...], mixed_ref[...], TN).astype(low)
    part = dot(mixed_ref[...], weight_ref[step], NT)

    @pl.when(step == 0)
    def _():
        input_ref[...] = part

    @pl.when(step > 0)
    def _():
        input_ref[...] += part


def attend_back(call, branch, hidden, proj, mixer_p, order, groups, q, k, v, lse, cosine, sine, bias):
    tokens, width = branch.shape
    low = jnp.bfloat16
    whole = lambda a: pl.BlockSpec(a.shape, lambda j, g, o: (0, 0))
    col = lambda w: pl.BlockSpec((tokens, w), lambda j, g, o: (0, g[j]))
    cols = mixer_p[0].shape[-1] // 2
    mine = len(mixer_p) // 2
    return pl.pallas_call(
        lambda *refs: attend_back_kernel(mine, (len(proj), len(mixer_p)), call, *refs),
        grid_spec=pltpu.PrefetchScalarGridSpec(
            num_scalar_prefetch=2,
            grid=(2,),
            in_specs=[whole(branch), whole(hidden), col(384), col(128), col(128)]
            + [pl.BlockSpec((None, tokens, 8), lambda j, g, o: (g[j], 0, 0))]
            + [whole(cosine), whole(sine), whole(bias)]
            + [pl.BlockSpec(memory_space=pl.ANY)] * (len(proj) + len(mixer_p)),
            out_specs=[
                pl.BlockSpec((None, width, cols), lambda j, g, o: (j, 0, 0)),
                pl.BlockSpec((tokens, width), lambda j, g, o: (0, 0)),
            ],
            scratch_shapes=[
                pltpu.VMEM((width, width), low),
                pltpu.VMEM((2, width, cols), low),
                pltpu.VMEM((tokens, cols), low),
                pltpu.VMEM((tokens, 384), low),
                pltpu.VMEM((tokens, 128), jnp.float32),
                pltpu.VMEM((tokens, 128), jnp.float32),
                pltpu.SemaphoreType.DMA((3,)),
            ],
        ),
        out_shape=[
            jax.ShapeDtypeStruct((2, width, cols), low),
            jax.ShapeDtypeStruct((tokens, width), jnp.float32),
        ],
        compiler_params=pltpu.CompilerParams(vmem_limit_bytes=50 * 2**20),
        cost_estimate=pl.CostEstimate(flops=20 * 10**9, bytes_accessed=8 * 10**6, transcendentals=0),
        name="attend_back",
    )(groups, order, branch, hidden, q, k, v, lse, cosine, sine, bias, *proj, *mixer_p)


def project_kernel(mine, count, order_ref, left_ref, *rest):
    pieces = rest[:count]
    out_ref, weight_ref, sem = rest[count:]
    copies = projector_copies(mine, pieces, order_ref, weight_ref, sem)
    for copy in copies:
        copy.start()
    for copy in copies:
        copy.wait()
    out_ref[...] = dot(left_ref[...], weight_ref[...], NN)


def project(left, proj, mine, order):
    tokens, width = left.shape
    return pl.pallas_call(
        lambda *refs: project_kernel(mine, len(proj), *refs),
        grid_spec=pltpu.PrefetchScalarGridSpec(
            num_scalar_prefetch=1,
            grid=(1,),
            in_specs=[pl.BlockSpec((tokens, width), lambda i, o: (0, 0))]
            + [pl.BlockSpec(memory_space=pl.ANY)] * len(proj),
            out_specs=pl.BlockSpec((tokens, width), lambda i, o: (0, 0)),
            scratch_shapes=[pltpu.VMEM((width, width), jnp.bfloat16), pltpu.SemaphoreType.DMA],
        ),
        out_shape=jax.ShapeDtypeStruct((tokens, width), jnp.float32),
        compiler_params=pltpu.CompilerParams(vmem_limit_bytes=40 * 2**20),
        cost_estimate=pl.CostEstimate(flops=5 * 10**9, bytes_accessed=8 * 10**6, transcendentals=0),
        name="project",
    )(order, left, *proj)


TILE = 256


def extra_rows(expert_count):
    return 8 if expert_count <= 24 else 16


def with_table(rows, table):
    tokens, width = rows.shape
    expert_count = table.shape[1]
    extra = extra_rows(expert_count)
    tiles = tokens // TILE
    high = table.astype(jnp.bfloat16)
    rest = (table - high.astype(jnp.float32)).astype(jnp.bfloat16)
    both = jnp.stack([high.T, rest.T], axis=1)
    both = both.reshape(expert_count // extra, extra, 2, tiles, TILE)
    both = jnp.transpose(both, (3, 1, 0, 2, 4)).reshape(tiles, extra, -1)
    both = jnp.pad(both, ((0, 0), (0, 0), (0, width - both.shape[2])))
    return jnp.concatenate([rows.reshape(tiles, TILE, width), both], axis=1).reshape(-1, width)


def table_of(rows, tokens, expert_count):
    extra = extra_rows(expert_count)
    tiles = tokens // TILE
    both = rows.reshape(tiles, TILE + extra, -1)[:, TILE:, : expert_count // extra * 2 * TILE]
    both = both.reshape(tiles, extra, expert_count // extra, 2, TILE)
    return jnp.transpose(jnp.sum(both.astype(jnp.float32), axis=3), (0, 3, 2, 1)).reshape(tokens, -1)


def rows_of(rows, tokens):
    tiles = tokens // TILE
    return rows.reshape(tiles, rows.shape[0] // tiles, -1)[:, :TILE].reshape(tokens, -1)


def expert_kernel(counts, expert_count, order_ref, place_ref, xa_ref, xb_ref, u_ref, *rest):
    pieces, more = counts
    sides_p, downs_p = rest[:pieces], rest[pieces : 2 * pieces]
    rest = rest[2 * pieces + more :]
    (gta_ref, gtb_ref, out_ref, x_ref, mid_ref, sides_ref, ws_ref, wd_ref, sems) = rest
    low = jnp.bfloat16
    extra = extra_rows(expert_count)
    step = pl.program_id(0)
    half = pl.num_programs(0) // 2
    load = piece_copies(sides_p, order_ref, ws_ref, sems.at[0], 1, 0)
    load_down = piece_copies(downs_p, order_ref, wd_ref, sems.at[1], 2, 0)

    @pl.when(step == 0)
    def _():
        for copy in load + load_down:
            copy.start()

    first = step < half
    table = jnp.where(first, xa_ref[TILE:, :], xb_ref[TILE:, :])

    @pl.when(first)
    def _():
        x_ref[...] = xa_ref[:TILE, :]

    @pl.when(jnp.logical_not(first))
    def _():
        x_ref[...] = xb_ref[:TILE, :]

    @pl.when(step == 0)
    def _():
        for copy in load + load_down:
            copy.wait()

    rows, cots = x_ref[...], u_ref[...]
    row = lax.broadcasted_iota(jnp.int32, (extra, 128), 0)
    lane = lax.broadcasted_iota(jnp.int32, (extra, 128), 1)
    expert = place_ref[2] * 2 + lane
    picks = []
    for block in range(expert_count // extra):
        hit = (lane < 2) & (row == expert - block * extra)
        picks.append(jnp.where(hit, 1.0, 0.0).astype(low))
    gates_wide = None
    for block, pick in enumerate(picks):
        for part in range(2):
            at = (2 * block + part) * TILE
            value = dot(table[:, at : at + TILE], pick, TN)
            gates_wide = value if gates_wide is None else gates_wide + value
    out = None
    taken = None
    sums = []
    for l in range(2):
        gates = gates_wide[:, l : l + 1]
        gate_in = dot(rows, ws_ref[2 * l], NN)
        up_in = dot(rows, ws_ref[2 * l + 1], NN)
        back = dot(cots, wd_ref[l], NT)
        sigma = 1.0 / (1.0 + jnp.exp(-gate_in))
        active = gate_in * sigma
        mid = active * up_in
        sums.append(jnp.sum(mid * back, axis=1, keepdims=True))
        mid_low = (mid * gates).astype(low)
        mid_ref[l] = mid_low
        part = dot(mid_low, wd_ref[l], NN)
        out = part if out is None else out + part
        back = back * gates
        grad_gate = (back * up_in * sigma * (1.0 + gate_in * (1.0 - sigma))).astype(low)
        grad_up = (back * active).astype(low)
        sides_ref[2 * l] = grad_gate
        sides_ref[2 * l + 1] = grad_up
        part = dot(grad_gate, ws_ref[2 * l], NT) + dot(grad_up, ws_ref[2 * l + 1], NT)
        taken = part if taken is None else taken + part
    out_ref[...] = out.astype(low)
    taken_low = taken.astype(low)
    wide = lax.broadcasted_iota(jnp.int32, (TILE, 128), 1)
    sums = jnp.where(wide == 0, sums[0], jnp.where(wide == 1, sums[1], 0.0))
    high = sums.astype(low)
    parts = (high, (sums - high.astype(jnp.float32)).astype(low))
    columns = [dot(pick, value, NT).astype(low) for pick in picks for value in parts]
    left = rows.shape[1] - TILE * len(columns)
    if left:
        columns.append(jnp.zeros((extra, left), low))
    columns = jnp.concatenate(columns, axis=1)

    @pl.when(first)
    def _():
        gta_ref[:TILE, :] = taken_low
        gta_ref[TILE:, :] = columns

    @pl.when(jnp.logical_not(first))
    def _():
        gtb_ref[:TILE, :] = taken_low
        gtb_ref[TILE:, :] = columns


def expert_chunk(order, place, xa, xb, cots, sides, downs, expert_count, kept):
    total, width = cots.shape
    devices = lax.axis_size("expert")
    tokens = total // devices
    hidden = sides[0].shape[-1]
    half = tokens // TILE
    steps = 2 * half
    low = jnp.bfloat16
    tall = TILE + extra_rows(expert_count)
    first = pl.BlockSpec((tall, width), lambda i, o, p: (jnp.minimum(i, half - 1), 0))
    second = pl.BlockSpec((tall, width), lambda i, o, p: (jnp.maximum(i - half, 0), 0))
    where = lambda i, p: jnp.where(i < half, p[0] * half + i, p[1] * half + i - half)
    anywhere = pl.BlockSpec(memory_space=pl.ANY)
    big_row = pl.BlockSpec((TILE, width), lambda i, o, p: (where(i, p), 0))
    big = lambda n: pl.BlockSpec((n, TILE, hidden), lambda i, o, p: (0, where(i, p), 0))
    single = jax.ShapeDtypeStruct((half * tall, width), low)
    shapes = [jax.ShapeDtypeStruct((total, width), low)] * 2
    shapes += [jax.ShapeDtypeStruct((n, total, hidden), low) for n in (2, 4)]
    operands = [order, place, xa, xb, cots, *sides, *downs]
    in_specs = [first, second, big_row] + [anywhere] * (2 * len(sides))
    aliases = {}
    more = 0
    if kept is not None:
        more = len(shapes)
        aliases = {len(operands) + i: 2 + i for i in range(more)}
        operands += list(kept)
        in_specs += [anywhere] * more
    res = pl.pallas_call(
        lambda *refs: expert_kernel((len(sides), more), expert_count, *refs),
        grid_spec=pltpu.PrefetchScalarGridSpec(
            num_scalar_prefetch=2,
            grid=(steps,),
            in_specs=in_specs,
            out_specs=[first, second, big_row, big_row, big(2), big(4)],
            scratch_shapes=[
                pltpu.VMEM((4, width, hidden), low),
                pltpu.VMEM((2, hidden, width), low),
                pltpu.SemaphoreType.DMA((2,)),
            ],
        ),
        out_shape=[single] * 2 + shapes,
        input_output_aliases=aliases,
        compiler_params=pltpu.CompilerParams(vmem_limit_bytes=58 * 2**20),
        cost_estimate=pl.CostEstimate(flops=27 * 10**9, bytes_accessed=8 * 10**6, transcendentals=0),
        name="expert_chunk",
    )(*operands)
    return res[:2], res[2:]


def wide_grad_kernel(on_rows, left_ref, right_ref, out_ref, acc_ref):
    step = pl.program_id(1)
    value = dot(left_ref[...], right_ref[...], TN)

    @pl.when(step == 0)
    def _():
        acc_ref[...] = value

    @pl.when(step > 0)
    def _():
        acc_ref[...] += value

    @pl.when(step == pl.num_programs(1) - 1)
    def _():
        rows, cols = out_ref.shape[-2:]
        for j in range(out_ref.shape[0]):
            if on_rows:
                part = acc_ref[j * rows : (j + 1) * rows, :]
            else:
                part = acc_ref[:, j * cols : (j + 1) * cols]
            out_ref[j] = part.astype(out_ref.dtype)


def weight_grad(left, right, parts, on_rows):
    count = left.shape[0] if left.ndim == 3 else right.shape[0]
    total, size_m = left.shape[-2:]
    size_n = right.shape[-1]
    block = 1024
    spec = lambda a: (
        pl.BlockSpec((None, block, a.shape[-1]), lambda l, k: (l, k, 0))
        if a.ndim == 3
        else pl.BlockSpec((block, a.shape[-1]), lambda l, k: (k, 0))
    )
    shape = (size_m // parts, size_n) if on_rows else (size_m, size_n // parts)
    return pl.pallas_call(
        lambda *refs: wide_grad_kernel(on_rows, *refs),
        grid=(count, total // block),
        in_specs=[spec(left), spec(right)],
        out_specs=pl.BlockSpec((parts, None) + shape, lambda l, k: (0, l, 0, 0)),
        out_shape=jax.ShapeDtypeStruct((parts, count) + shape, jnp.bfloat16),
        scratch_shapes=[pltpu.VMEM((size_m, size_n), jnp.float32)],
        compiler_params=pltpu.CompilerParams(vmem_limit_bytes=48 * 2**20),
        cost_estimate=pl.CostEstimate(flops=20 * 10**9, bytes_accessed=8 * 10**6, transcendentals=0),
        name="weight_grad",
    )(left, right)


def per_device(
    layer_input,
    out_cotangent,
    parents,
    routes,
    norm1_gain,
    qkv_weight,
    out_weight,
    norm2_gain,
    router_weight,
    gate_weight,
    up_weight,
    down_weight,
):
    low = jnp.bfloat16
    shards = lax.axis_size("shard")
    tokens, width = layer_input.shape
    expert_count = router_weight.shape[1]
    local_count = gate_weight.shape[0]
    chips = lax.axis_size("expert") // 2
    me = lax.axis_index("expert")
    core = me % 2
    order = shard_order()
    queries = HEADS * HEAD_DIM

    by_group = [
        jnp.concatenate(
            [
                qkv_weight[:, 384 * g : 384 * (g + 1)],
                qkv_weight[:, queries + 128 * g : queries + 128 * (g + 1)],
                qkv_weight[:, queries + 512 + 128 * g : queries + 512 + 128 * (g + 1)],
            ],
            axis=1,
        )
        for g in range(4)
    ]
    half_columns = lambda g, h: jnp.concatenate([by_group[g], by_group[h]], axis=1)
    block = jnp.where(core == 0, half_columns(0, 2), half_columns(1, 3))
    small = jnp.concatenate([router_weight, norm1_gain[:, None], norm2_gain[:, None]], axis=1).T
    small = gather_small(small)
    mixer_first = gather_first(block)
    mine = gather_second(mixer_first, 0)
    mixer_p = mine + [swap_core(p) for p in mine]
    router = small[:expert_count].T
    gain_one = small[expert_count].astype(jnp.float32)[None, :]
    gain_two = small[expert_count + 1].astype(jnp.float32)[None, :]
    block = lax.dynamic_slice_in_dim(out_weight, core * (out_weight.shape[0] // 2), out_weight.shape[0] // 2, 0)
    project_first = gather_first(after(block, *mine))
    sides = jnp.stack([gate_weight, up_weight], axis=1).reshape(4, -1, gate_weight.shape[2])
    sides_first = gather_first(after(sides, *mine))

    cots = lax.all_gather(out_cotangent, "expert", axis=0, tiled=True)

    bias, cosine, sine = tree_tables(parents)
    activity = layer_input.astype(jnp.float32)
    scale_one = inverse_rms(activity)
    normed_one = activity * scale_one
    hidden_one = (normed_one * gain_one).astype(low)
    saved = None
    groups = []
    for call in range(2):
        groups.append(jnp.stack([2 * call + core, 2 * call + 1 - core]).astype(jnp.int32))
        saved = attend(hidden_one, mixer_p, call, order, groups[call], cosine, sine, bias, saved)
        if call == 0:
            project_first, saved = lax.optimization_barrier((project_first, saved))
            proj = gather_second(project_first, 0)
            near = swap_core(jnp.concatenate(proj[:3], axis=0))
    proj, near, sides_first, saved = lax.optimization_barrier((proj, near, sides_first, saved))
    far = [swap_core(p) for p in proj[3:]]
    sides_p = gather_second(sides_first, 0)
    downs_first = gather_first(after(down_weight, *far), True)
    proj = proj + [near] + far
    attended, query, keys, values, log_total = saved
    resid = activity + project(attended, proj, len(mixer_p) // 2, order)
    scale_two = inverse_rms(resid)
    normed_two = resid * scale_two
    hidden_two = (normed_two * gain_two).astype(low)
    logits = jnp.dot(hidden_two, router, preferred_element_type=jnp.float32)
    routed = jnp.any(
        routes[:, :, None] == jnp.arange(expert_count, dtype=jnp.int32)[None, None, :], axis=1
    )
    masked = jnp.where(routed, logits, NEGATIVE)
    powers = jnp.exp(masked - jnp.max(masked, axis=1, keepdims=True))
    gates = powers / jnp.sum(powers, axis=1, keepdims=True)
    upstream = out_cotangent.astype(jnp.float32)

    downs_p = gather_second(downs_first, 0)
    rows = [with_table(hidden_two, gates)]
    rows.append(next_chip(rows[0]))
    beside = swap_core(rows[0])
    rows[0], rows[1], beside = lax.optimization_barrier((rows[0], rows[1], beside))
    kept = total = None
    for step in range(chips):
        ahead = next_chip(rows[step + 1]) if step + 2 < chips else None
        beside_next = swap_core(rows[step + 1]) if step + 1 < chips else None
        here = rows[step]
        if step > 1:
            here, total = lax.optimization_barrier((here, total))
        sent = next_chip(total) if step > 1 else None
        place = jnp.stack([(me - 2 * step) % (2 * chips), (me - 2 * step) % (2 * chips) ^ 1, me])
        parts, kept = expert_chunk(
            order, place.astype(jnp.int32), here, beside, cots, sides_p, downs_p, expert_count, kept
        )
        parts, kept, ahead, beside, sent = lax.optimization_barrier((parts, kept, ahead, beside_next, sent))
        if ahead is not None:
            rows.append(ahead)
        pair = (parts[0], swap_core(parts[1]))
        if step == 0:
            last = pair
        else:
            total = add_low(*pair, *(() if sent is None else (sent,)))
    out_all, all_rows, all_mid, all_sides = kept
    all_rows, total = lax.optimization_barrier((all_rows, total))
    sent = next_chip(total)
    wide_sides = weight_grad(all_rows, all_sides, shards, True)
    sent, wide_sides = lax.optimization_barrier((sent, wide_sides))
    sides_state = reduce_first(wide_sides)
    final = sum(v.astype(jnp.float32) for v in (*last, sent))
    grad_hidden_two = rows_of(final, tokens)
    grad_gates = table_of(final, tokens, expert_count)
    branch_out = lax.psum_scatter(after(out_all, final), "expert", scatter_dimension=0, tiled=True)

    mean_gate = jnp.sum(gates * grad_gates, axis=1, keepdims=True)
    grad_logits = gates * (grad_gates - mean_gate)
    grad_hidden_two = grad_hidden_two + jnp.dot(
        grad_logits, router.astype(jnp.float32).T, precision=lax.Precision.HIGHEST
    )
    grad_router = jnp.dot(
        hidden_two.astype(jnp.float32).T, grad_logits, precision=lax.Precision.HIGHEST
    )
    grad_gain_two = jnp.sum(grad_hidden_two * normed_two, axis=0)
    grad_normed_two = grad_hidden_two * gain_two
    grad_resid = upstream + scale_two * (
        grad_normed_two - normed_two * jnp.mean(grad_normed_two * normed_two, axis=1, keepdims=True)
    )
    grad_branch = grad_resid.astype(low)

    def spread_sum(blocks):
        return reduce_chips(reduce_last(reduce_second(reduce_first(blocks))))

    grad_projector = jnp.dot(attended.T, grad_branch, preferred_element_type=jnp.float32).astype(low)
    halves = grad_projector.reshape(shards, 2, -1, width)
    mine = lax.dynamic_index_in_dim(halves, core, 1, keepdims=False)
    other = lax.dynamic_index_in_dim(halves, 1 - core, 1, keepdims=False)
    half_projector = (mine, swap_core(other))

    def small_sum(value):
        value = add_low(value, swap_core(value))
        if shards == 4:
            value = add_low(value, across(value, 1))
            value = add_low(value, across(value, 2))
        else:
            value = lax.psum(value, "shard")
        value = reduce_chips(value)
        size = width // shards
        return lax.dynamic_slice_in_dim(value, lax.axis_index("shard") * size, size, 1).astype(jnp.float32)

    first_small = jnp.concatenate([grad_router, grad_gain_two[:, None]], axis=1).T.astype(low)

    finals = []
    parts = []
    for call in range(2):
        wide, part = attend_back(
            call, grad_branch, hidden_one, proj, mixer_p, order, groups[call],
            query, keys, values, log_total, cosine, sine, bias,
        )
        parts.append(part)
        if call == 0:
            grad_branch, wide, sides_state, first_small, half_projector = lax.optimization_barrier(
                (grad_branch, wide, sides_state, first_small, half_projector)
            )
            sides_state = reduce_second(sides_state)
        wide = wide.reshape(2, shards, -1, wide.shape[-1])
        finals.append((wide[0], swap_core(wide[1])))
    parts, finals[0], sides_state, all_mid = lax.optimization_barrier((parts, finals[0], sides_state, all_mid))
    wide_down = weight_grad(all_mid, cots, shards, False)
    down_state = reduce_second(reduce_first(wide_down))
    finals = [spread_sum(add_low(*v)) for v in finals]
    finals = [(v, swap_core(v)) for v in finals]
    grad_hidden_one = parts[0] + parts[1]
    first_small = small_sum(first_small)
    mine = spread_sum(add_low(*half_projector))
    other = swap_core(mine)
    grad_projector = jnp.where(
        core == 0, jnp.concatenate([mine, other]), jnp.concatenate([other, mine])
    ).astype(jnp.float32)
    grad_sides = reduce_last(sides_state, jnp.float32)
    grad_sides = grad_sides.reshape(2, 2, *grad_sides.shape[1:])
    grad_gate, grad_up = grad_sides[:, 0], grad_sides[:, 1]
    grad_down = reduce_last(down_state, jnp.float32)
    output = (resid + after(branch_out, wide_down).astype(jnp.float32)).astype(low)
    grad_gain_one = jnp.sum(grad_hidden_one * normed_one, axis=0)
    grad_normed_one = grad_hidden_one * gain_one
    grad_input = grad_resid + scale_one * (
        grad_normed_one - normed_one * jnp.mean(grad_normed_one * normed_one, axis=1, keepdims=True)
    )
    last_small = small_sum(grad_gain_one[None].astype(low))
    ordered = []
    for mine, other in finals:
        ordered.append(jnp.where(core == 0, mine, other))
        ordered.append(jnp.where(core == 0, other, mine))
    grad_mixer = jnp.concatenate(
        [g[:, :384] for g in ordered] + [g[:, 384:512] for g in ordered] + [g[:, 512:] for g in ordered],
        axis=1,
    ).astype(jnp.float32)
    return (
        output,
        grad_input.astype(low),
        last_small[0],
        grad_mixer,
        grad_projector,
        first_small[expert_count],
        first_small[:expert_count].T,
        grad_gate,
        grad_up,
        grad_down,
    )


def solution(mesh):
    return jax.shard_map(
        per_device,
        mesh=mesh,
        in_specs=(
            P(("expert", "shard"), None),
            P(("expert", "shard"), None),
            P(("expert", "shard")),
            P(("expert", "shard"), None),
            P("shard"),
            P("shard", None),
            P("shard", None),
            P("shard"),
            P("shard", None),
            P("expert", "shard", None),
            P("expert", "shard", None),
            P("expert", None, "shard"),
        ),
        out_specs=(
            P(("expert", "shard"), None),
            P(("expert", "shard"), None),
            P("shard"),
            P("shard", None),
            P("shard", None),
            P("shard"),
            P("shard", None),
            P("expert", "shard", None),
            P("expert", "shard", None),
            P("expert", None, "shard"),
        ),
        check_vma=False,
    )
```

time: 2070 us -> 733 us (0.35)
  waiting for transfers between devices: 1180 us -> 231 us
  local copies, waits for them, and re-layouts: 383 us -> 41.6 us
  Pallas kernels: 0 us -> 307 us
  matrix products: 308 us -> 9.28 us
  blocking collectives: 64.7 us -> 0 us
  starting transfers between devices: 23.2 us -> 63.3 us
  other arithmetic: 89.6 us -> 60.9 us
    all_to_all x4 -> x0, waiting for transfers between devices: 944 us -> none  [the longest x1 273 us: per_device(): lax.all_to_all(produced, 'expert', split_axis=1, concat_axis=1, tiled=True)]
    pallas_call x0 -> x11, Pallas kernels: none -> 307 us  [the longest x4 127 us: expert_chunk(): pl.pallas_call(lambda *refs: expert_kernel((len(sides), more), expert_cou...]
    dot_general x71 -> x1, matrix products: 299 us -> 5.17 us  [per_device(): jnp.dot(grad_logits, router.astype(jnp.float32).T, precision=lax.Precisio...]
    ppermute x0 -> x83, waiting for transfers between devices: none -> 230 us  [the longest x43 108 us: across(): return lax.ppermute(value, 'shard', [(i, i ^ mask) for i in range(4)])]
    gather x6 -> x0, local copies, waits for them, and re-layouts: 186 us -> none  [the longest x2 66.8 us: per_device(): grad_outgoing = weighted[send_table]]
    all_gather x5 -> x1, waiting for transfers between devices: 110 us -> 0.01 us  [per_device(): cots = lax.all_gather(out_cotangent, 'expert', axis=0, tiled=True)]
    all_to_all x3 -> x0, local copies, waits for them, and re-layouts: 69.3 us -> none  [the longest x1 38.9 us: per_device(): lax.all_to_all(outgoing, 'expert', split_axis=1, concat_axis=1, tiled=True)]
    reduce_scatter x4 -> x1, waiting for transfers between devices: 67 us -> 0.01 us  [per_device(): lax.psum_scatter(after(out_all, final), 'expert', scatter_dimension=0, ti...]
  transfers between devices with their start and end apart: 16 -> 85, of which waited for: 11 -> 37; matrix products, arithmetic and copies ran while one was open for 31% -> 11% of each run, Pallas kernels for 0% -> 42%
where the time goes in v1:
time: 733 us; the launch traced here: 729 us
  Pallas kernels  307 us (42%)
  waiting for transfers between devices  231 us (32%)
  starting transfers between devices  63.3 us (9%)
  other arithmetic  60.9 us (8%)
  local copies, waits for them, and re-layouts  41.6 us (6%)
  between operations  16.3 us (2%)
  matrix products  9.28 us (1%)
    pallas_call x4, Pallas kernels, expert_chunk(): pl.pallas_call(lambda *refs: expert_kernel((len(sides), more), expert_cou...  127 us
    ppermute x43, waiting for transfers between devices, across(): return lax.ppermute(value, 'shard', [(i, i ^ mask) for i in range(4)])  108 us
    ppermute x10, waiting for transfers between devices, reduce_chips(): lax.ppermute(value, 'expert', [(i, i ^ mask) for i in range(count)])  68.3 us
    pallas_call x2, Pallas kernels, attend_back(): pl.pallas_call(lambda *refs: attend_back_kernel(mine, (len(proj), len(mix...  65.4 us
    pallas_call x2, Pallas kernels, weight_grad(): pl.pallas_call(lambda *refs: wide_grad_kernel(on_rows, *refs), grid=(coun...  61.1 us
    pallas_call x2, Pallas kernels, attend(): pl.pallas_call(lambda *refs: attend_kernel(len(mixer_p) // 2, call, *refs...  49.7 us
    ppermute x43, starting transfers between devices, across(): return lax.ppermute(value, 'shard', [(i, i ^ mask) for i in range(4)])  48.8 us
    ppermute x6, waiting for transfers between devices, next_chip(): lax.ppermute(value, 'expert', [(i, (i + 2) % count) for i in range(count)])  36.5 us
  transfers between devices with their start and end apart: 85, of which 37 were waited for; matrix products, arithmetic and copies ran while one was open for 11% of the time, Pallas kernels for 42%

profile of v1, /device:TPU:0, one launch (start us, length us, event | category | flops | bytes accessed | tf_op | source)
XLA Modules:
  0.0 729.3 jit_solution(604253033274403463)
XLA Ops:
  10.5 2.9 collective-permute-start
  15.1 2.0 collective-permute-start.7
  27.3 10.3 %collective-permute-done.1 = bf16[384,1280]{1,0:T(8,128)(2,1)} collective-permute-done((bf16[384,1280]{1,0:T(8,128)(2,1)}, bf16[384,1280]{1,0:T(8,128)(2,1)}, u32[]{:S(2)}, u32[]{:S(2)}) %collective-permute-start.1) | collective-permute-done | bytes 983072 | tf_op jit(solution)/shard_map/ppermute | solution.py:71
  37.6 1.9 slice.552
  39.6 1.8 slice.553
  41.4 1.9 collective-permute-start.3
  44.3 6.7 collective-permute-done.2.refs_9_.refs_22_
  50.9 2.2 collective-permute-done.3.refs_10_.refs_23_
  53.2 3.0 fusion.6.refs_2_.refs_3_
  59.3 24.7 %attend.2 = (bf16[512,1536]{1,0:T(8,128)(2,1)S(1)}, bf16[512,1536]{1,0:T(8,128)(2,1)}, bf16[512,512]{1,0:T(8,128)(2,1)S(1)}, bf16[512,512]{1,0:T(8,128)(2,1)S(1)}, f32[4,512,8]{2,1,0:T(8,128)S(1)}) custom-call(s32[6]{0:T(128)S(1)} %stack.100.refs_0_.refs_1_, s32[2]{0:T(128)S(1)} %get-tuple-element.353.refs_1_.refs_0_, ...), custom_call_target="tpu_custom_call" | custom-call | flops 16000000000 | bytes 8000000 | tf_op jit(solution)/shard_map/attend/pallas_call | solution.py:257
  90.4 24.9 %attend.3 = (bf16[512,1536]{1,0:T(8,128)(2,1)S(1)}, bf16[512,1536]{1,0:T(8,128)(2,1)}, bf16[512,512]{1,0:T(8,128)(2,1)S(1)}, bf16[512,512]{1,0:T(8,128)(2,1)S(1)}, f32[4,512,8]{2,1,0:T(8,128)S(1)}) custom-call(s32[6]{0:T(128)S(1)} %stack.100.refs_0_.refs_1_, ...), custom_call_target="tpu_custom_call", output_to_operand_aliasing={{0}: (16, {}), {1}: (17, {}), {2}: (18, {}), {3}: (19, {}),... | custom-call | flops 16000000000 | bytes 8000000 | tf_op jit(solution)/shard_map/attend/pallas_call | solution.py:257
  115.4 13.4 %collective-permute-done.14.refs_5_.refs_14_ = bf16[1,96,1536]{2,1,0:T(8,128)(2,1)S(1)} collective-permute-done((bf16[1,96,1536]{2,1,0:T(8,128)(2,1)S(1)}, bf16[1,96,1536]{2,1,0:T(8,128)(2,1)S(1)}, u32[]{:S(2)}, u32[]{:S(2)}) %collective-permute-start.14) | collective-permute-done | bytes 294944 | tf_op jit(solution)/shard_map/ppermute | solution.py:71
  131.1 4.2 project.1
  141.9 2.1 slice.436
  144.8 14.8 %collective-permute-done.26 = bf16[2,512,384]{2,1,0:T(8,128)(2,1)S(1)} collective-permute-done((bf16[2,512,384]{2,1,0:T(8,128)(2,1)S(1)}, bf16[2,512,384]{2,1,0:T(8,128)(2,1)S(1)}, u32[]{:S(2)}, u32[]{:S(2)}) %collective-permute-start.26) | collective-permute-done | bytes 786464 | tf_op jit(solution)/shard_map/ppermute | solution.py:71
  162.4 15.3 %collective-permute-done.21.refs_2_ = bf16[528,1536]{1,0:T(8,128)(2,1)S(1)} collective-permute-done((bf16[528,1536]{1,0:T(8,128)(2,1)}, bf16[528,1536]{1,0:T(8,128)(2,1)S(1)}, u32[]{:S(2)}, u32[]{:S(2)}) %collective-permute-start.21) | collective-permute-done | bytes 1622048 | tf_op jit(solution)/shard_map/ppermute | solution.py:67
  181.2 4.5 collective-permute-done.27.refs_13_
  185.7 3.6 collective-permute-done.28.refs_14_
  189.3 32.0 %expert_chunk.4 = (bf16[528,1536]{1,0:T(8,128)(2,1)}, bf16[528,1536]{1,0:T(8,128)(2,1)}, bf16[4096,1536]{1,0:T(8,128)(2,1)}, bf16[4096,1536]{1,0:T(8,128)(2,1)},...) custom-call(s32[6]{0:T(128)} %copy-done.7, s32[3]{0:T(128)} %get-tuple-element.357.refs_1_, ...), custom_call_target="tpu_custom_call" | custom-call | flops 27000000512 | bytes 8000000 | tf_op jit(solution)/shard_map/expert_chunk/pallas_call | solution.py:602
  221.4 31.7 %expert_chunk.5 = (bf16[528,1536]{1,0:T(8,128)(2,1)}, bf16[528,1536]{1,0:T(8,128)(2,1)}, bf16[4096,1536]{1,0:T(8,128)(2,1)}, bf16[4096,1536]{1,0:T(8,128)(2,1)},...) custom-call(s32[6]{0:T(128)} %copy-done.7, ...), custom_call_target="tpu_custom_call", output_to_operand_aliasing={{2}: (15, {}), {3}: (16, {}), {4}: (17, {}), {5}: (18, {})} | custom-call | flops 27000000512 | bytes 8000000 | tf_op jit(solution)/shard_map/expert_chunk/pallas_call | solution.py:602
  253.1 6.1 collective-permute-done.31.refs_2_
  259.7 4.8 collective-permute-done.33
  266.4 31.9 %expert_chunk.6 = (bf16[528,1536]{1,0:T(8,128)(2,1)}, bf16[528,1536]{1,0:T(8,128)(2,1)}, bf16[4096,1536]{1,0:T(8,128)(2,1)}, bf16[4096,1536]{1,0:T(8,128)(2,1)},...) custom-call(s32[6]{0:T(128)} %copy-done.7, ...), custom_call_target="tpu_custom_call", output_to_operand_aliasing={{2}: (15, {}), {3}: (16, {}), {4}: (17, {}), {5}: (18, {})} | custom-call | flops 27000000512 | bytes 8000000 | tf_op jit(solution)/shard_map/expert_chunk/pallas_call | solution.py:602
  298.3 7.4 %collective-permute-done.35 = bf16[528,1536]{1,0:T(8,128)(2,1)S(1)} collective-permute-done((bf16[528,1536]{1,0:T(8,128)(2,1)S(1)}, bf16[528,1536]{1,0:T(8,128)(2,1)S(1)}, u32[]{:S(2)}, u32[]{:S(2)}) %collective-permute-start.35) | collective-permute-done | bytes 1622048 | tf_op jit(solution)/shard_map/ppermute | solution.py:67
  305.7 3.7 collective-permute-done.36
  309.4 2.0 add_convert_fusion.3
  311.5 31.6 %expert_chunk.7 = (bf16[528,1536]{1,0:T(8,128)(2,1)}, bf16[528,1536]{1,0:T(8,128)(2,1)}, bf16[4096,1536]{1,0:T(8,128)(2,1)}, bf16[4096,1536]{1,0:T(8,128)(2,1)},...) custom-call(s32[6]{0:T(128)} %copy-done.7, ...), custom_call_target="tpu_custom_call", output_to_operand_aliasing={{2}: (15, {}), {3}: (16, {}), {4}: (17, {}), {5}: (18, {})} | custom-call | flops 27000000512 | bytes 8000000 | tf_op jit(solution)/shard_map/expert_chunk/pallas_call | solution.py:602
  343.2 7.7 %collective-permute-done.37 = bf16[528,1536]{1,0:T(8,128)(2,1)} collective-permute-done((bf16[528,1536]{1,0:T(8,128)(2,1)S(1)}, bf16[528,1536]{1,0:T(8,128)(2,1)}, u32[]{:S(2)}, u32[]{:S(2)}) %collective-permute-start.37) | collective-permute-done | bytes 1622048 | tf_op jit(solution)/shard_map/ppermute | solution.py:67
  351.4 5.6 collective-permute-done.39
  357.0 3.0 add_convert_fusion.2
  360.1 40.6 %weight_grad.2 = bf16[4,4,384,512]{3,2,1,0:T(8,128)(2,1)} custom-call(bf16[4096,1536]{1,0:T(8,128)(2,1)} %get-tuple-element.229.refs_0_, bf16[4,4096,512]{2,1,0:T(8,128)(2,1)} %get-tuple-element.230.refs_1_), custom_call_target="tpu_custom_call" | custom-call | flops 20000000000 | bytes 8000000 | tf_op jit(solution)/shard_map/weight_grad/pallas_call | solution.py:658
  401.3 1.9 slice.556
  403.2 5.2 multiply_reduce_fusion
  408.4 4.9 dynamic-slice_bitcast_fusion.4
  419.6 2.9 convolution_convert_fusion
  422.5 2.7 dynamic-slice_bitcast_fusion
  426.6 32.9 %attend_back.2 = (bf16[2,1536,640]{2,1,0:T(8,128)(2,1)}, f32[512,1536]{1,0:T(8,128)}) custom-call(s32[2]{0:T(128)S(1)} %get-tuple-element.353.refs_1_.refs_0_, s32[6]{0:T(128)S(1)} %copy-done.8, bf16[512,1536]{1,0:T(8,128)(2,1)} %copy-done.46, bf16[512,1536]{1,0:T(8,128)(2,1)} %fusion.6.refs_2_.refs_3_, bf16[512,1536]{1,0:T(8,128)(2,1)} %get-tuple-element.233.refs_4_, ...), custom_call_target="tpu_custom_call" | custom-call | flops 20000000000 | bytes 8000000 | tf_op jit(solution)/shard_map/attend_back/pallas_call | solution.py:385
  459.5 2.8 dynamic-slice_bitcast_fusion.2
  463.0 3.8 fusion.76
  466.8 2.4 add_convert_fusion.7
  470.0 2.4 add_convert_fusion
  475.0 32.5 %attend_back.3 = (bf16[2,1536,640]{2,1,0:T(8,128)(2,1)}, f32[512,1536]{1,0:T(8,128)}) custom-call(s32[2]{0:T(128)S(1)} %get-tuple-element.354.refs_1_.refs_0_, s32[6]{0:T(128)S(1)} %copy-done.8, bf16[512,1536]{1,0:T(8,128)(2,1)} %copy-done.46, bf16[512,1536]{1,0:T(8,128)(2,1)} %fusion.6.refs_2_.refs_3_, bf16[512,1536]{1,0:T(8,128)(2,1)} %get-tuple-element.233.refs_4_, ...), custom_call_target="tpu_custom_call" | custom-call | flops 20000000000 | bytes 8000000 | tf_op jit(solution)/shard_map/attend_back/pallas_call | solution.py:385
  509.5 2.7 collective-permute-done.75
  513.5 3.2 collective-permute-done.76
  519.1 5.1 collective-permute-done.77
  525.0 16.5 %collective-permute-done.68 = bf16[96,1536]{1,0:T(8,128)(2,1)S(1)} collective-permute-done((bf16[96,1536]{1,0:T(8,128)(2,1)S(1)}, bf16[96,1536]{1,0:T(8,128)(2,1)S(1)}, u32[]{:S(2)}, u32[]{:S(2)}) %collective-permute-start.68) | collective-permute-done | bytes 294944 | tf_op jit(solution)/shard_map/ppermute | solution.py:71
  541.7 4.5 collective-permute-start.71
  551.2 16.9 %collective-permute-done.71 = bf16[192,1536]{1,0:T(8,128)(2,1)S(1)} collective-permute-done((bf16[192,1536]{1,0:T(8,128)(2,1)S(1)}, bf16[192,1536]{1,0:T(8,128)(2,1)S(1)}, u32[]{:S(2)}, u32[]{:S(2)}) %collective-permute-start.71) | collective-permute-done | bytes 589856 | tf_op jit(solution)/shard_map/ppermute | solution.py:159
  569.1 2.0 collective-permute-start.72
  572.3 2.0 add_convert_fusion.1
  582.3 20.4 %weight_grad.3 = bf16[4,2,512,384]{3,2,1,0:T(8,128)(2,1)S(1)} custom-call(bf16[2,4096,512]{2,1,0:T(8,128)(2,1)} %get-tuple-element.249.refs_0_, bf16[4096,1536]{1,0:T(8,128)(2,1)} %all-gather.2.cloned.1.call-done.refs_4_.refs_1_), custom_call_target="tpu_custom_call" | custom-call | flops 20000000000 | bytes 8000000 | tf_op jit(solution)/shard_map/weight_grad/pallas_call | solution.py:658
  605.3 2.0 slice_bitcast_fusion
  609.0 2.1 collective-permute-done.48
  611.8 3.0 collective-permute-done.49
  615.4 3.0 collective-permute-done.50
  619.5 3.6 collective-permute-done.51
  630.5 6.8 collective-permute-done.62
  639.8 16.4 %collective-permute-done.53 = bf16[192,640]{1,0:T(8,128)(2,1)S(1)} collective-permute-done((bf16[192,640]{1,0:T(8,128)(2,1)S(1)}, bf16[192,640]{1,0:T(8,128)(2,1)S(1)}, u32[]{:S(2)}, u32[]{:S(2)}) %collective-permute-start.53) | collective-permute-done | bytes 245792 | tf_op jit(solution)/shard_map/ppermute | solution.py:71
  664.7 10.9 %collective-permute-done.56 = bf16[384,640]{1,0:T(8,128)(2,1)S(1)} collective-permute-done((bf16[384,640]{1,0:T(8,128)(2,1)S(1)}, bf16[384,640]{1,0:T(8,128)(2,1)S(1)}, u32[]{:S(2)}, u32[]{:S(2)}) %collective-permute-start.56) | collective-permute-done | bytes 491552 | tf_op jit(solution)/shard_map/ppermute | solution.py:159
  678.1 6.6 collective-permute-done.64
  685.4 18.3 %collective-permute-done.57 = bf16[384,640]{1,0:T(8,128)(2,1)S(1)} collective-permute-done((bf16[384,640]{1,0:T(8,128)(2,1)S(1)}, bf16[384,640]{1,0:T(8,128)(2,1)S(1)}, u32[]{:S(2)}, u32[]{:S(2)}) %collective-permute-start.57) | collective-permute-done | bytes 491552 | tf_op jit(solution)/shard_map/ppermute | solution.py:159
  705.3 3.6 collective-permute-done.65
  711.5 2.4 convert_element_type.624
  713.9 8.3 %fusion.11 = (bf16[512,1536]{1,0:T(8,128)(2,1)}, bf16[512,1536]{1,0:T(8,128)(2,1)}) fusion(bf16[512,1536]{1,0:T(8,128)(2,1)S(1)} %copy-done.30, f32[512]{0:T(512)S(1)} %broadcast_multiply_fusion, f32[1536]{0:T(1024)S(1)} %copy-done.61, f32[512]{0:T(512)S(1)} %copy-done.67, f32[512,1536]{1,0:T(8,128)} %get-tuple-element.251, ...), kind=kLoop, calls=%fused_computation.24 | loop fusion | flops 14942208 | bytes 20467712 | tf_op jit(solution)/shard_map/convert_element_type | solution.py:878
  (439 shorter events, 110.2 us)
Async XLA Ops:
  7.2 182.1 %all-gather.2.cloned.1.call-start = ((), (), s32[]{:S(2)}) async-start(), calls=%async_computation.1 | async-start | bytes 14155776 | tf_op jit(solution)/shard_map/all_gather | solution.py:722
  7.9 705.9 %reduce-scatter.2.cloned.1.call-start = ((), (), s32[]{:S(2)}) async-start(), calls=%async_computation.2 | async-start | bytes 14155776 | tf_op jit(solution)/shard_map/reduce_scatter | solution.py:791
  10.5 29.1 %collective-permute-start = (bf16[384,1280]{1,0:T(8,128)(2,1)}, bf16[384,1280]{1,0:T(8,128)(2,1)}, u32[]{:S(2)}, u32[]{:S(2)}) collective-permute-start(bf16[384,1280]{1,0:T(8,128)(2,1)} %broadcast_select_fusion), channel_id=1, source_target_pairs={{0,1},{1,0},{2,3},{3,2},{4,5},{5,4},{6,7},{7,6},{8,9},{9,8},{10,11... | collective-permute-start | bytes 2949128 | tf_op jit(solution)/shard_map/ppermute | solution.py:71
  13.5 24.1 %collective-permute-start.1 = (bf16[384,1280]{1,0:T(8,128)(2,1)}, bf16[384,1280]{1,0:T(8,128)(2,1)}, u32[]{:S(2)}, u32[]{:S(2)}) collective-permute-start(bf16[384,1280]{1,0:T(8,128)(2,1)} %broadcast_select_fusion), channel_id=1, source_target_pairs={{0,2},{1,3},{2,0},{3,1},{4,6},{5,7},{6,4},{7,5},{8,10},{9,11},{10,... | collective-permute-start | bytes 2949128 | tf_op jit(solution)/shard_map/ppermute | solution.py:71
  15.0 28.5 %collective-permute-start.6 = (bf16[18,384]{1,0:T(8,128)(2,1)S(1)}, bf16[18,384]{1,0:T(8,128)(2,1)S(1)}, u32[]{:S(2)}, u32[]{:S(2)}) collective-permute-start(bf16[18,384]{1,0:T(8,128)(2,1)S(1)} %maximum_bitcast_fusion.2), channel_id=1, source_target_pairs={{0,3},{1,2},{2,1},{3,0},{4,7},{5,6},{6,5},{7,4},{8,11},{9,10},{10,... | collective-permute-start | bytes 41480 | tf_op jit(solution)/shard_map/ppermute | solution.py:71
  15.1 28.5 %collective-permute-start.7 = (bf16[18,384]{1,0:T(8,128)(2,1)S(1)}, bf16[18,384]{1,0:T(8,128)(2,1)S(1)}, u32[]{:S(2)}, u32[]{:S(2)}) collective-permute-start(bf16[18,384]{1,0:T(8,128)(2,1)S(1)} %maximum_bitcast_fusion.2), channel_id=1, source_target_pairs={{0,2},{1,3},{2,0},{3,1},{4,6},{5,7},{6,4},{7,5},{8,10},{9,11},{10,... | collective-permute-start | bytes 41480 | tf_op jit(solution)/shard_map/ppermute | solution.py:71
  17.1 27.0 %collective-permute-start.8 = (bf16[18,384]{1,0:T(8,128)(2,1)S(1)}, bf16[18,384]{1,0:T(8,128)(2,1)S(1)}, u32[]{:S(2)}, u32[]{:S(2)}) collective-permute-start(bf16[18,384]{1,0:T(8,128)(2,1)S(1)} %maximum_bitcast_fusion.2), channel_id=1, source_target_pairs={{0,1},{1,0},{2,3},{3,2},{4,5},{5,4},{6,7},{7,6},{8,9},{9,8},{10,11... | collective-permute-start | bytes 41480 | tf_op jit(solution)/shard_map/ppermute | solution.py:71
  41.4 11.7 %collective-permute-start.3 = (bf16[1,192,1280]{2,1,0:T(8,128)(2,1)}, bf16[1,192,1280]{2,1,0:T(8,128)(2,1)}, u32[]{:S(2)}, u32[]{:S(2)}) collective-permute-start(bf16[1,192,1280]{2,1,0:T(8,128)(2,1)} %slice.553), channel_id=1, source_target_pairs={{0,2},{1,3},{2,0},{3,1},{4,6},{5,7},{6,4},{7,5},{8,10},{9,11},{10,... | collective-permute-start | bytes 1474568 | tf_op jit(solution)/shard_map/ppermute | solution.py:71
  43.5 12.7 %collective-permute-start.9 = (bf16[1,384,1280]{2,1,0:T(8,128)(2,1)S(1)}, bf16[1,384,1280]{2,1,0:T(8,128)(2,1)S(1)}, u32[]{:S(2)}, u32[]{:S(2)}) collective-permute-start(bf16[1,384,1280]{2,1,0:T(8,128)(2,1)S(1)} %broadcast_select_fusion.1.refs_6_.refs_19_), channel_id=1, source_target_pairs={{0,4},{4,0},{8,12},{12,8},{16,20},{20,16},{24,28},{28,24},{1,5},{5... | collective-permute-start | bytes 2949128 | tf_op jit(solution)/shard_map/ppermute | solution.py:62
  43.6 13.9 %collective-permute-start.10 = (bf16[1,384,1280]{2,1,0:T(8,128)(2,1)}, bf16[1,384,1280]{2,1,0:T(8,128)(2,1)S(1)}, u32[]{:S(2)}, u32[]{:S(2)}) collective-permute-start(bf16[1,384,1280]{2,1,0:T(8,128)(2,1)} %bitcast.17.refs_7_.refs_20_), channel_id=1, source_target_pairs={{0,4},{4,0},{8,12},{12,8},{16,20},{20,16},{24,28},{28,24},{1,5},{5... | collective-permute-start | bytes 2949128 | tf_op jit(solution)/shard_map/ppermute | solution.py:62
  44.1 15.2 %collective-permute-start.11 = (bf16[1,384,1280]{2,1,0:T(8,128)(2,1)}, bf16[1,384,1280]{2,1,0:T(8,128)(2,1)S(1)}, u32[]{:S(2)}, u32[]{:S(2)}) collective-permute-start(bf16[1,384,1280]{2,1,0:T(8,128)(2,1)} %bitcast.18.refs_8_.refs_21_), channel_id=1, source_target_pairs={{0,4},{4,0},{8,12},{12,8},{16,20},{20,16},{24,28},{28,24},{1,5},{5... | collective-permute-start | bytes 2949128 | tf_op jit(solution)/shard_map/ppermute | solution.py:62
  56.2 27.9 %collective-permute-start.4 = (bf16[192,1536]{1,0:T(8,128)(2,1)S(1)}, bf16[192,1536]{1,0:T(8,128)(2,1)S(1)}, u32[]{:S(2)}, u32[]{:S(2)}) collective-permute-start(bf16[192,1536]{1,0:T(8,128)(2,1)S(1)} %constant_dynamic-slice_fusion.2), channel_id=1, source_target_pairs={{0,1},{1,0},{2,3},{3,2},{4,5},{5,4},{6,7},{7,6},{8,9},{9,8},{10,11... | collective-permute-start | bytes 1769480 | tf_op jit(solution)/shard_map/ppermute | solution.py:71
  57.5 26.6 %collective-permute-start.5 = (bf16[192,1536]{1,0:T(8,128)(2,1)S(1)}, bf16[192,1536]{1,0:T(8,128)(2,1)S(1)}, u32[]{:S(2)}, u32[]{:S(2)}) collective-permute-start(bf16[192,1536]{1,0:T(8,128)(2,1)S(1)} %constant_dynamic-slice_fusion.2), channel_id=1, source_target_pairs={{0,2},{1,3},{2,0},{3,1},{4,6},{5,7},{6,4},{7,5},{8,10},{9,11},{10,... | collective-permute-start | bytes 1769480 | tf_op jit(solution)/shard_map/ppermute | solution.py:71
  84.3 44.7 %collective-permute-start.16 = (bf16[3,192,1536]{2,1,0:T(8,128)(2,1)S(1)}, bf16[3,192,1536]{2,1,0:T(8,128)(2,1)S(1)}, u32[]{:S(2)}, u32[]{:S(2)}) collective-permute-start(bf16[3,192,1536]{2,1,0:T(8,128)(2,1)S(1)} %pad_maximum_fusion.1), channel_id=1, source_target_pairs={{0,4},{4,0},{8,12},{12,8},{16,20},{20,16},{24,28},{28,24},{1,5},{5... | collective-permute-start | bytes 5308424 | tf_op jit(solution)/shard_map/ppermute | solution.py:62
  86.1 42.8 %collective-permute-start.17 = (bf16[4,384,512]{2,1,0:T(8,128)(2,1)S(1)}, bf16[4,384,512]{2,1,0:T(8,128)(2,1)S(1)}, u32[]{:S(2)}, u32[]{:S(2)}) collective-permute-start(bf16[4,384,512]{2,1,0:T(8,128)(2,1)S(1)} %bitcast.286), channel_id=1, source_target_pairs={{0,1},{1,0},{2,3},{3,2},{4,5},{5,4},{6,7},{7,6},{8,9},{9,8},{10,11... | collective-permute-start | bytes 4718600 | tf_op jit(solution)/shard_map/ppermute | solution.py:71
  86.6 42.4 %collective-permute-start.18 = (bf16[4,384,512]{2,1,0:T(8,128)(2,1)S(1)}, bf16[4,384,512]{2,1,0:T(8,128)(2,1)}, u32[]{:S(2)}, u32[]{:S(2)}) collective-permute-start(bf16[4,384,512]{2,1,0:T(8,128)(2,1)S(1)} %bitcast.287), channel_id=1, source_target_pairs={{0,2},{1,3},{2,0},{3,1},{4,6},{5,7},{6,4},{7,5},{8,10},{9,11},{10,... | collective-permute-start | bytes 4718600 | tf_op jit(solution)/shard_map/ppermute | solution.py:71
  87.2 41.6 %collective-permute-start.14 = (bf16[1,96,1536]{2,1,0:T(8,128)(2,1)S(1)}, bf16[1,96,1536]{2,1,0:T(8,128)(2,1)S(1)}, u32[]{:S(2)}, u32[]{:S(2)}) collective-permute-start(bf16[1,96,1536]{2,1,0:T(8,128)(2,1)S(1)} %slice.432), channel_id=1, source_target_pairs={{0,1},{1,0},{2,3},{3,2},{4,5},{5,4},{6,7},{7,6},{8,9},{9,8},{10,11... | collective-permute-start | bytes 884744 | tf_op jit(solution)/shard_map/ppermute | solution.py:71
  88.7 40.3 %collective-permute-start.15 = (bf16[1,96,1536]{2,1,0:T(8,128)(2,1)S(1)}, bf16[1,96,1536]{2,1,0:T(8,128)(2,1)S(1)}, u32[]{:S(2)}, u32[]{:S(2)}) collective-permute-start(bf16[1,96,1536]{2,1,0:T(8,128)(2,1)S(1)} %slice.433), channel_id=1, source_target_pairs={{0,2},{1,3},{2,0},{3,1},{4,6},{5,7},{6,4},{7,5},{8,10},{9,11},{10,... | collective-permute-start | bytes 884744 | tf_op jit(solution)/shard_map/ppermute | solution.py:71
  138.2 39.5 %collective-permute-start.21 = (bf16[528,1536]{1,0:T(8,128)(2,1)}, bf16[528,1536]{1,0:T(8,128)(2,1)S(1)}, u32[]{:S(2)}, u32[]{:S(2)}) collective-permute-start(bf16[528,1536]{1,0:T(8,128)(2,1)} %bitcast.45.refs_2_), channel_id=1, source_target_pairs={{0,8},{4,12},{8,16},{12,20},{16,24},{20,28},{24,0},{28,4},{1,9},{5... | collective-permute-start | bytes 4866056 | tf_op jit(solution)/shard_map/ppermute | solution.py:67
  139.7 41.4 %collective-permute-start.22 = (bf16[528,1536]{1,0:T(8,128)(2,1)}, bf16[528,1536]{1,0:T(8,128)(2,1)}, u32[]{:S(2)}, u32[]{:S(2)}) collective-permute-start(bf16[528,1536]{1,0:T(8,128)(2,1)} %bitcast.45.refs_2_), channel_id=1, source_target_pairs={{0,4},{4,0},{8,12},{12,8},{16,20},{20,16},{24,28},{28,24},{1,5},{5... | collective-permute-start | bytes 4866056 | tf_op jit(solution)/shard_map/ppermute | solution.py:62
  139.7 20.0 %collective-permute-start.26 = (bf16[2,512,384]{2,1,0:T(8,128)(2,1)S(1)}, bf16[2,512,384]{2,1,0:T(8,128)(2,1)S(1)}, u32[]{:S(2)}, u32[]{:S(2)}) collective-permute-start(bf16[2,512,384]{2,1,0:T(8,128)(2,1)S(1)} %copy-done.75), channel_id=1, source_target_pairs={{0,2},{1,3},{2,0},{3,1},{4,6},{5,7},{6,4},{7,5},{8,10},{9,11},{10,... | collective-permute-start | bytes 2359304 | tf_op jit(solution)/shard_map/ppermute | solution.py:71
  140.6 20.4 %collective-permute-start.25 = (bf16[2,512,384]{2,1,0:T(8,128)(2,1)S(1)}, bf16[2,512,384]{2,1,0:T(8,128)(2,1)S(1)}, u32[]{:S(2)}, u32[]{:S(2)}) collective-permute-start(bf16[2,512,384]{2,1,0:T(8,128)(2,1)S(1)} %copy-done.75), channel_id=1, source_target_pairs={{0,1},{1,0},{2,3},{3,2},{4,5},{5,4},{6,7},{7,6},{8,9},{9,8},{10,11... | collective-permute-start | bytes 2359304 | tf_op jit(solution)/shard_map/ppermute | solution.py:71
  144.0 37.1 %collective-permute-start.23 = (bf16[1,2,384,512]{3,2,1,0:T(8,128)(2,1)}, bf16[1,2,384,512]{3,2,1,0:T(8,128)(2,1)}, u32[]{:S(2)}, u32[]{:S(2)}) collective-permute-start(bf16[1,2,384,512]{3,2,1,0:T(8,128)(2,1)} %slice.436), channel_id=1, source_target_pairs={{0,1},{1,0},{2,3},{3,2},{4,5},{5,4},{6,7},{7,6},{8,9},{9,8},{10,11... | collective-permute-start | bytes 2359304 | tf_op jit(solution)/shard_map/ppermute | solution.py:71
  159.6 21.6 %collective-permute-start.24 = (bf16[1,2,384,512]{3,2,1,0:T(8,128)(2,1)S(1)}, bf16[1,2,384,512]{3,2,1,0:T(8,128)(2,1)}, u32[]{:S(2)}, u32[]{:S(2)}) collective-permute-start(bf16[1,2,384,512]{3,2,1,0:T(8,128)(2,1)S(1)} %slice.437), channel_id=1, source_target_pairs={{0,2},{1,3},{2,0},{3,1},{4,6},{5,7},{6,4},{7,5},{8,10},{9,11},{10,... | collective-permute-start | bytes 2359304 | tf_op jit(solution)/shard_map/ppermute | solution.py:71
  161.0 24.7 %collective-permute-start.27 = (bf16[1,1,512,384]{3,2,1,0:T(8,128)(2,1)S(1)}, bf16[1,1,512,384]{3,2,1,0:T(8,128)(2,1)}, u32[]{:S(2)}, u32[]{:S(2)}) collective-permute-start(bf16[1,1,512,384]{3,2,1,0:T(8,128)(2,1)S(1)} %slice.554), channel_id=1, source_target_pairs={{0,1},{1,0},{2,3},{3,2},{4,5},{5,4},{6,7},{7,6},{8,9},{9,8},{10,11... | collective-permute-start | bytes 1179656 | tf_op jit(solution)/shard_map/ppermute | solution.py:71
  181.1 40.2 %collective-permute-start.29 = (bf16[528,1536]{1,0:T(8,128)(2,1)}, bf16[528,1536]{1,0:T(8,128)(2,1)}, u32[]{:S(2)}, u32[]{:S(2)}) collective-permute-start(bf16[528,1536]{1,0:T(8,128)(2,1)} %copy-done.73), channel_id=1, source_target_pairs={{0,8},{4,12},{8,16},{12,20},{16,24},{20,28},{24,0},{28,4},{1,9},{5... | collective-permute-start | bytes 4866056 | tf_op jit(solution)/shard_map/ppermute | solution.py:67
  181.1 40.2 %collective-permute-start.30 = (bf16[528,1536]{1,0:T(8,128)(2,1)}, bf16[528,1536]{1,0:T(8,128)(2,1)}, u32[]{:S(2)}, u32[]{:S(2)}) collective-permute-start(bf16[528,1536]{1,0:T(8,128)(2,1)} %copy-done.73), channel_id=1, source_target_pairs={{0,4},{4,0},{8,12},{12,8},{16,20},{20,16},{24,28},{28,24},{1,5},{5... | collective-permute-start | bytes 4866056 | tf_op jit(solution)/shard_map/ppermute | solution.py:62
  221.3 37.9 %collective-permute-start.31 = (bf16[528,1536]{1,0:T(8,128)(2,1)}, bf16[528,1536]{1,0:T(8,128)(2,1)}, u32[]{:S(2)}, u32[]{:S(2)}) collective-permute-start(bf16[528,1536]{1,0:T(8,128)(2,1)} %collective-permute-done.29.refs_2_), channel_id=1, source_target_pairs={{0,8},{4,12},{8,16},{12,20},{16,24},{20,28},{24,0},{28,4},{1,9},{5... | collective-permute-start | bytes 4866056 | tf_op jit(solution)/shard_map/ppermute | solution.py:67
  221.4 37.9 %collective-permute-start.32 = (bf16[528,1536]{1,0:T(8,128)(2,1)}, bf16[528,1536]{1,0:T(8,128)(2,1)S(1)}, u32[]{:S(2)}, u32[]{:S(2)}) collective-permute-start(bf16[528,1536]{1,0:T(8,128)(2,1)} %collective-permute-done.29.refs_2_), channel_id=1, source_target_pairs={{0,4},{4,0},{8,12},{12,8},{16,20},{20,16},{24,28},{28,24},{1,5},{5... | collective-permute-start | bytes 4866056 | tf_op jit(solution)/shard_map/ppermute | solution.py:62
  259.2 39.1 %collective-permute-start.34 = (bf16[528,1536]{1,0:T(8,128)(2,1)}, bf16[528,1536]{1,0:T(8,128)(2,1)}, u32[]{:S(2)}, u32[]{:S(2)}) collective-permute-start(bf16[528,1536]{1,0:T(8,128)(2,1)} %collective-permute-done.31.refs_2_), channel_id=1, source_target_pairs={{0,4},{4,0},{8,12},{12,8},{16,20},{20,16},{24,28},{28,24},{1,5},{5... | collective-permute-start | bytes 4866056 | tf_op jit(solution)/shard_map/ppermute | solution.py:62
  266.4 39.3 %collective-permute-start.35 = (bf16[528,1536]{1,0:T(8,128)(2,1)S(1)}, bf16[528,1536]{1,0:T(8,128)(2,1)S(1)}, u32[]{:S(2)}, u32[]{:S(2)}) collective-permute-start(bf16[528,1536]{1,0:T(8,128)(2,1)S(1)} %add_convert_fusion.4), channel_id=1, source_target_pairs={{0,8},{4,12},{8,16},{12,20},{16,24},{20,28},{24,0},{28,4},{1,9},{5... | collective-permute-start | bytes 4866056 | tf_op jit(solution)/shard_map/ppermute | solution.py:67
  311.4 39.4 %collective-permute-start.37 = (bf16[528,1536]{1,0:T(8,128)(2,1)S(1)}, bf16[528,1536]{1,0:T(8,128)(2,1)}, u32[]{:S(2)}, u32[]{:S(2)}) collective-permute-start(bf16[528,1536]{1,0:T(8,128)(2,1)S(1)} %add_convert_fusion.3), channel_id=1, source_target_pairs={{0,8},{4,12},{8,16},{12,20},{16,24},{20,28},{24,0},{28,4},{1,9},{5... | collective-permute-start | bytes 4866056 | tf_op jit(solution)/shard_map/ppermute | solution.py:67
  350.9 49.8 %collective-permute-start.38 = (bf16[528,1536]{1,0:T(8,128)(2,1)}, bf16[528,1536]{1,0:T(8,128)(2,1)S(1)}, u32[]{:S(2)}, u32[]{:S(2)}) collective-permute-start(bf16[528,1536]{1,0:T(8,128)(2,1)} %get-tuple-element.223), channel_id=1, source_target_pairs={{0,4},{4,0},{8,12},{12,8},{16,20},{20,16},{24,28},{28,24},{1,5},{5... | collective-permute-start | bytes 4866056 | tf_op jit(solution)/shard_map/ppermute | solution.py:62
  360.0 40.7 %collective-permute-start.40 = (bf16[528,1536]{1,0:T(8,128)(2,1)S(1)}, bf16[528,1536]{1,0:T(8,128)(2,1)S(1)}, u32[]{:S(2)}, u32[]{:S(2)}) collective-permute-start(bf16[528,1536]{1,0:T(8,128)(2,1)S(1)} %add_convert_fusion.2), channel_id=1, source_target_pairs={{0,8},{4,12},{8,16},{12,20},{16,24},{20,28},{24,0},{28,4},{1,9},{5... | collective-permute-start | bytes 4866056 | tf_op jit(solution)/shard_map/ppermute | solution.py:67
  414.6 48.4 %collective-permute-start.41 = (bf16[4,384,512]{2,1,0:T(8,128)(2,1)}, bf16[4,384,512]{2,1,0:T(8,128)(2,1)}, u32[]{:S(2)}, u32[]{:S(2)}) collective-permute-start(bf16[4,384,512]{2,1,0:T(8,128)(2,1)} %pad_maximum_fusion.3), channel_id=1, source_target_pairs={{0,1},{1,0},{2,3},{3,2},{4,5},{5,4},{6,7},{7,6},{8,9},{9,8},{10,11... | collective-permute-start | bytes 4718600 | tf_op jit(solution)/shard_map/ppermute | solution.py:71
  417.6 45.4 %collective-permute-start.42 = (bf16[4,384,512]{2,1,0:T(8,128)(2,1)}, bf16[4,384,512]{2,1,0:T(8,128)(2,1)}, u32[]{:S(2)}, u32[]{:S(2)}) collective-permute-start(bf16[4,384,512]{2,1,0:T(8,128)(2,1)} %pad_maximum_fusion.4), channel_id=1, source_target_pairs={{0,2},{1,3},{2,0},{3,1},{4,6},{5,7},{6,4},{7,5},{8,10},{9,11},{10,... | collective-permute-start | bytes 4718600 | tf_op jit(solution)/shard_map/ppermute | solution.py:71
  425.2 37.8 %collective-permute-start.43 = (bf16[4,192,1536]{2,1,0:T(8,128)(2,1)}, bf16[4,192,1536]{2,1,0:T(8,128)(2,1)}, u32[]{:S(2)}, u32[]{:S(2)}) collective-permute-start(bf16[4,192,1536]{2,1,0:T(8,128)(2,1)} %get-tuple-element.280), channel_id=1, source_target_pairs={{0,4},{4,0},{8,12},{12,8},{16,20},{20,16},{24,28},{28,24},{1,5},{5... | collective-permute-start | bytes 7077896 | tf_op jit(solution)/shard_map/ppermute | solution.py:62
  466.8 104.2 %collective-permute-start.44 = (bf16[4,384,640]{2,1,0:T(8,128)(2,1)}, bf16[4,384,640]{2,1,0:T(8,128)(2,1)}, u32[]{:S(2)}, u32[]{:S(2)}) collective-permute-start(bf16[4,384,640]{2,1,0:T(8,128)(2,1)} %bitcast.70), channel_id=1, source_target_pairs={{0,4},{4,0},{8,12},{12,8},{16,20},{20,16},{24,28},{28,24},{1,5},{5... | collective-permute-start | bytes 5898248 | tf_op jit(solution)/shard_map/ppermute | solution.py:62
  469.2 101.8 %collective-permute-start.45 = (bf16[2,384,512]{2,1,0:T(8,128)(2,1)}, bf16[2,384,512]{2,1,0:T(8,128)(2,1)S(1)}, u32[]{:S(2)}, u32[]{:S(2)}) collective-permute-start(bf16[2,384,512]{2,1,0:T(8,128)(2,1)} %add_convert_fusion.7), channel_id=1, source_target_pairs={{0,1},{1,0},{2,3},{3,2},{4,5},{5,4},{6,7},{7,6},{8,9},{9,8},{10,11... | collective-permute-start | bytes 2359304 | tf_op jit(solution)/shard_map/ppermute | solution.py:71
  472.5 45.2 %collective-permute-start.67 = (bf16[192,1536]{1,0:T(8,128)(2,1)S(1)}, bf16[192,1536]{1,0:T(8,128)(2,1)S(1)}, u32[]{:S(2)}, u32[]{:S(2)}) collective-permute-start(bf16[192,1536]{1,0:T(8,128)(2,1)S(1)} %pad_maximum_fusion.8), channel_id=1, source_target_pairs={{0,1},{1,0},{2,3},{3,2},{4,5},{5,4},{6,7},{7,6},{8,9},{9,8},{10,11... | collective-permute-start | bytes 1769480 | tf_op jit(solution)/shard_map/ppermute | solution.py:71
  473.9 44.0 %collective-permute-start.69 = (bf16[192,1536]{1,0:T(8,128)(2,1)S(1)}, bf16[192,1536]{1,0:T(8,128)(2,1)S(1)}, u32[]{:S(2)}, u32[]{:S(2)}) collective-permute-start(bf16[192,1536]{1,0:T(8,128)(2,1)S(1)} %pad_maximum_fusion.9), channel_id=1, source_target_pairs={{0,2},{1,3},{2,0},{3,1},{4,6},{5,7},{6,4},{7,5},{8,10},{9,11},{10,... | collective-permute-start | bytes 1769480 | tf_op jit(solution)/shard_map/ppermute | solution.py:71
  475.0 32.5 %collective-permute-start.74 = (bf16[17,1536]{1,0:T(8,128)(2,1)S(1)}, bf16[17,1536]{1,0:T(8,128)(2,1)S(1)}, u32[]{:S(2)}, u32[]{:S(2)}) collective-permute-start(bf16[17,1536]{1,0:T(8,128)(2,1)S(1)} %maximum_bitcast_fusion), channel_id=1, source_target_pairs={{0,4},{4,0},{8,12},{12,8},{16,20},{20,16},{24,28},{28,24},{1,5},{5... | collective-permute-start | bytes 156680 | tf_op jit(solution)/shard_map/ppermute | solution.py:62
  516.7 54.4 %collective-permute-start.46 = (bf16[2,384,512]{2,1,0:T(8,128)(2,1)S(1)}, bf16[2,384,512]{2,1,0:T(8,128)(2,1)S(1)}, u32[]{:S(2)}, u32[]{:S(2)}) collective-permute-start(bf16[2,384,512]{2,1,0:T(8,128)(2,1)S(1)} %add_convert_fusion.6), channel_id=1, source_target_pairs={{0,2},{1,3},{2,0},{3,1},{4,6},{5,7},{6,4},{7,5},{8,10},{9,11},{10,... | collective-permute-start | bytes 2359304 | tf_op jit(solution)/shard_map/ppermute | solution.py:71
  518.0 23.5 %collective-permute-start.68 = (bf16[96,1536]{1,0:T(8,128)(2,1)S(1)}, bf16[96,1536]{1,0:T(8,128)(2,1)S(1)}, u32[]{:S(2)}, u32[]{:S(2)}) collective-permute-start(bf16[96,1536]{1,0:T(8,128)(2,1)S(1)} %get-tuple-element.298), channel_id=1, source_target_pairs={{0,2},{1,3},{2,0},{3,1},{4,6},{5,7},{6,4},{7,5},{8,10},{9,11},{10,... | collective-permute-start | bytes 884744 | tf_op jit(solution)/shard_map/ppermute | solution.py:71
  524.2 17.3 %collective-permute-start.70 = (bf16[96,1536]{1,0:T(8,128)(2,1)S(1)}, bf16[96,1536]{1,0:T(8,128)(2,1)S(1)}, u32[]{:S(2)}, u32[]{:S(2)}) collective-permute-start(bf16[96,1536]{1,0:T(8,128)(2,1)S(1)} %get-tuple-element.299), channel_id=1, source_target_pairs={{0,1},{1,0},{2,3},{3,2},{4,5},{5,4},{6,7},{7,6},{8,9},{9,8},{10,11... | collective-permute-start | bytes 884744 | tf_op jit(solution)/shard_map/ppermute | solution.py:71
  541.7 26.3 %collective-permute-start.71 = (bf16[192,1536]{1,0:T(8,128)(2,1)S(1)}, bf16[192,1536]{1,0:T(8,128)(2,1)S(1)}, u32[]{:S(2)}, u32[]{:S(2)}) collective-permute-start(bf16[192,1536]{1,0:T(8,128)(2,1)S(1)} %pad_maximum_fusion.10), channel_id=1, source_target_pairs={{0,8},{4,12},{8,0},{12,4},{16,24},{20,28},{24,16},{28,20},{1,9},{5... | collective-permute-start | bytes 1769480 | tf_op jit(solution)/shard_map/ppermute | solution.py:159
  550.0 29.1 %collective-permute-start.59 = (bf16[4,384,640]{2,1,0:T(8,128)(2,1)S(1)}, bf16[4,384,640]{2,1,0:T(8,128)(2,1)S(1)}, u32[]{:S(2)}, u32[]{:S(2)}) collective-permute-start(bf16[4,384,640]{2,1,0:T(8,128)(2,1)S(1)} %bitcast.285), channel_id=1, source_target_pairs={{0,4},{4,0},{8,12},{12,8},{16,20},{20,16},{24,28},{28,24},{1,5},{5... | collective-permute-start | bytes 5898248 | tf_op jit(solution)/shard_map/ppermute | solution.py:62
  569.1 55.2 %collective-permute-start.72 = (bf16[192,1536]{1,0:T(8,128)(2,1)}, bf16[192,1536]{1,0:T(8,128)(2,1)}, u32[]{:S(2)}, u32[]{:S(2)}) collective-permute-start(bf16[192,1536]{1,0:T(8,128)(2,1)} %add_convert_fusion.9), channel_id=1, source_target_pairs={{0,16},{4,20},{8,24},{12,28},{16,0},{20,4},{24,8},{28,12},{1,17},{... | collective-permute-start | bytes 1769480 | tf_op jit(solution)/shard_map/ppermute | solution.py:159
  572.3 35.1 %collective-permute-start.47 = (bf16[1,1536]{1,0:T(2,128)(2,1)S(1)}, bf16[1,1536]{1,0:T(2,128)(2,1)S(1)}, u32[]{:S(2)}, u32[]{:S(2)}) collective-permute-start(bf16[1,1536]{1,0:T(2,128)(2,1)S(1)} %convert_element_type.563), channel_id=1, source_target_pairs={{0,4},{4,0},{8,12},{12,8},{16,20},{20,16},{24,28},{28,24},{1,5},{5... | collective-permute-start | bytes 9224 | tf_op jit(solution)/shard_map/ppermute | solution.py:62
  575.3 51.8 %collective-permute-start.52 = (bf16[384,640]{1,0:T(8,128)(2,1)}, bf16[384,640]{1,0:T(8,128)(2,1)}, u32[]{:S(2)}, u32[]{:S(2)}) collective-permute-start(bf16[384,640]{1,0:T(8,128)(2,1)} %pad_maximum_fusion.11), channel_id=1, source_target_pairs={{0,1},{1,0},{2,3},{3,2},{4,5},{5,4},{6,7},{7,6},{8,9},{9,8},{10,11... | collective-permute-start | bytes 1474568 | tf_op jit(solution)/shard_map/ppermute | solution.py:71
  577.6 51.1 %collective-permute-start.54 = (bf16[384,640]{1,0:T(8,128)(2,1)}, bf16[384,640]{1,0:T(8,128)(2,1)}, u32[]{:S(2)}, u32[]{:S(2)}) collective-permute-start(bf16[384,640]{1,0:T(8,128)(2,1)} %pad_maximum_fusion.12), channel_id=1, source_target_pairs={{0,2},{1,3},{2,0},{3,1},{4,6},{5,7},{6,4},{7,5},{8,10},{9,11},{10,... | collective-permute-start | bytes 1474568 | tf_op jit(solution)/shard_map/ppermute | solution.py:71
  581.3 48.5 %collective-permute-start.60 = (bf16[384,640]{1,0:T(8,128)(2,1)}, bf16[384,640]{1,0:T(8,128)(2,1)}, u32[]{:S(2)}, u32[]{:S(2)}) collective-permute-start(bf16[384,640]{1,0:T(8,128)(2,1)} %pad_maximum_fusion.14), channel_id=1, source_target_pairs={{0,1},{1,0},{2,3},{3,2},{4,5},{5,4},{6,7},{7,6},{8,9},{9,8},{10,11... | collective-permute-start | bytes 1474568 | tf_op jit(solution)/shard_map/ppermute | solution.py:71
  623.1 14.2 %collective-permute-start.62 = (bf16[384,640]{1,0:T(8,128)(2,1)S(1)}, bf16[384,640]{1,0:T(8,128)(2,1)S(1)}, u32[]{:S(2)}, u32[]{:S(2)}) collective-permute-start(bf16[384,640]{1,0:T(8,128)(2,1)S(1)} %pad_maximum_fusion.15), channel_id=1, source_target_pairs={{0,2},{1,3},{2,0},{3,1},{4,6},{5,7},{6,4},{7,5},{8,10},{9,11},{10,... | collective-permute-start | bytes 1474568 | tf_op jit(solution)/shard_map/ppermute | solution.py:71
  624.2 51.5 %collective-permute-start.79 = (bf16[2,512,384]{2,1,0:T(8,128)(2,1)S(1)}, bf16[2,512,384]{2,1,0:T(8,128)(2,1)S(1)}, u32[]{:S(2)}, u32[]{:S(2)}) collective-permute-start(bf16[2,512,384]{2,1,0:T(8,128)(2,1)S(1)} %pad_maximum_fusion.6), channel_id=1, source_target_pairs={{0,1},{1,0},{2,3},{3,2},{4,5},{5,4},{6,7},{7,6},{8,9},{9,8},{10,11... | collective-permute-start | bytes 2359304 | tf_op jit(solution)/shard_map/ppermute | solution.py:71
  627.1 48.7 %collective-permute-start.81 = (bf16[2,512,384]{2,1,0:T(8,128)(2,1)S(1)}, bf16[2,512,384]{2,1,0:T(8,128)(2,1)S(1)}, u32[]{:S(2)}, u32[]{:S(2)}) collective-permute-start(bf16[2,512,384]{2,1,0:T(8,128)(2,1)S(1)} %pad_maximum_fusion.7), channel_id=1, source_target_pairs={{0,2},{1,3},{2,0},{3,1},{4,6},{5,7},{6,4},{7,5},{8,10},{9,11},{10,... | collective-permute-start | bytes 2359304 | tf_op jit(solution)/shard_map/ppermute | solution.py:71
  628.7 30.9 %collective-permute-start.73 = (bf16[192,1536]{1,0:T(8,128)(2,1)S(1)}, bf16[192,1536]{1,0:T(8,128)(2,1)S(1)}, u32[]{:S(2)}, u32[]{:S(2)}) collective-permute-start(bf16[192,1536]{1,0:T(8,128)(2,1)S(1)} %add_convert_fusion.8), channel_id=1, source_target_pairs={{0,4},{4,0},{8,12},{12,8},{16,20},{20,16},{24,28},{28,24},{1,5},{5... | collective-permute-start | bytes 1769480 | tf_op jit(solution)/shard_map/ppermute | solution.py:62
  629.9 26.4 %collective-permute-start.53 = (bf16[192,640]{1,0:T(8,128)(2,1)S(1)}, bf16[192,640]{1,0:T(8,128)(2,1)S(1)}, u32[]{:S(2)}, u32[]{:S(2)}) collective-permute-start(bf16[192,640]{1,0:T(8,128)(2,1)S(1)} %get-tuple-element.310), channel_id=1, source_target_pairs={{0,2},{1,3},{2,0},{3,1},{4,6},{5,7},{6,4},{7,5},{8,10},{9,11},{10,... | collective-permute-start | bytes 737288 | tf_op jit(solution)/shard_map/ppermute | solution.py:71
  637.3 19.5 %collective-permute-start.55 = (bf16[192,640]{1,0:T(8,128)(2,1)S(1)}, bf16[192,640]{1,0:T(8,128)(2,1)S(1)}, u32[]{:S(2)}, u32[]{:S(2)}) collective-permute-start(bf16[192,640]{1,0:T(8,128)(2,1)S(1)} %get-tuple-element.311), channel_id=1, source_target_pairs={{0,1},{1,0},{2,3},{3,2},{4,5},{5,4},{6,7},{7,6},{8,9},{9,8},{10,11... | collective-permute-start | bytes 737288 | tf_op jit(solution)/shard_map/ppermute | solution.py:71
  659.5 16.0 %collective-permute-start.56 = (bf16[384,640]{1,0:T(8,128)(2,1)S(1)}, bf16[384,640]{1,0:T(8,128)(2,1)S(1)}, u32[]{:S(2)}, u32[]{:S(2)}) collective-permute-start(bf16[384,640]{1,0:T(8,128)(2,1)S(1)} %pad_maximum_fusion.13), channel_id=1, source_target_pairs={{0,8},{4,12},{8,0},{12,4},{16,24},{20,28},{24,16},{28,20},{1,9},{5... | collective-permute-start | bytes 1474568 | tf_op jit(solution)/shard_map/ppermute | solution.py:159
  664.1 20.6 %collective-permute-start.64 = (bf16[384,640]{1,0:T(8,128)(2,1)S(1)}, bf16[384,640]{1,0:T(8,128)(2,1)S(1)}, u32[]{:S(2)}, u32[]{:S(2)}) collective-permute-start(bf16[384,640]{1,0:T(8,128)(2,1)S(1)} %pad_maximum_fusion.16), channel_id=1, source_target_pairs={{0,8},{4,12},{8,0},{12,4},{16,24},{20,28},{24,16},{28,20},{1,9},{5... | collective-permute-start | bytes 1474568 | tf_op jit(solution)/shard_map/ppermute | solution.py:159
  675.7 27.9 %collective-permute-start.57 = (bf16[384,640]{1,0:T(8,128)(2,1)S(1)}, bf16[384,640]{1,0:T(8,128)(2,1)S(1)}, u32[]{:S(2)}, u32[]{:S(2)}) collective-permute-start(bf16[384,640]{1,0:T(8,128)(2,1)S(1)} %add_convert_fusion.13), channel_id=1, source_target_pairs={{0,16},{4,20},{8,24},{12,28},{16,0},{20,4},{24,8},{28,12},{1,17},{... | collective-permute-start | bytes 1474568 | tf_op jit(solution)/shard_map/ppermute | solution.py:159
  676.0 27.8 %collective-permute-start.80 = (bf16[1,512,384]{2,1,0:T(8,128)(2,1)S(1)}, bf16[1,512,384]{2,1,0:T(8,128)(2,1)S(1)}, u32[]{:S(2)}, u32[]{:S(2)}) collective-permute-start(bf16[1,512,384]{2,1,0:T(8,128)(2,1)S(1)} %get-tuple-element.286), channel_id=1, source_target_pairs={{0,2},{1,3},{2,0},{3,1},{4,6},{5,7},{6,4},{7,5},{8,10},{9,11},{10,... | collective-permute-start | bytes 1179656 | tf_op jit(solution)/shard_map/ppermute | solution.py:71
  676.6 27.2 %collective-permute-start.82 = (bf16[1,512,384]{2,1,0:T(8,128)(2,1)S(1)}, bf16[1,512,384]{2,1,0:T(8,128)(2,1)S(1)}, u32[]{:S(2)}, u32[]{:S(2)}) collective-permute-start(bf16[1,512,384]{2,1,0:T(8,128)(2,1)S(1)} %get-tuple-element.287), channel_id=1, source_target_pairs={{0,1},{1,0},{2,3},{3,2},{4,5},{5,4},{6,7},{7,6},{8,9},{9,8},{10,11... | collective-permute-start | bytes 1179656 | tf_op jit(solution)/shard_map/ppermute | solution.py:71
  684.9 24.1 %collective-permute-start.65 = (bf16[384,640]{1,0:T(8,128)(2,1)S(1)}, bf16[384,640]{1,0:T(8,128)(2,1)S(1)}, u32[]{:S(2)}, u32[]{:S(2)}) collective-permute-start(bf16[384,640]{1,0:T(8,128)(2,1)S(1)} %add_convert_fusion.11), channel_id=1, source_target_pairs={{0,16},{4,20},{8,24},{12,28},{16,0},{20,4},{24,8},{28,12},{1,17},{... | collective-permute-start | bytes 1474568 | tf_op jit(solution)/shard_map/ppermute | solution.py:159
  (98 other events, 1635.6 us)
Sparse Core Ops, SparseCore 0:
  9.7 119.4 all-gather.1
  425.5 140.8 reduce-scatter.1

commit v2 on v1

--- a/solution.py
+++ b/solution.py
@@ -141,7 +141,7 @@
     half = own.shape[0] // 2
     last_x = across(add_low(beside, from_y[:half]), 1)
     last_y = across(add_low(above, from_x[:half]), 2)
-    return own, from_x[half:], from_y[half:], last_x, last_y
+    return own, from_x, from_y, last_x, last_y
 
 
 def reduce_last(state, dtype=jnp.bfloat16):
@@ -149,15 +149,25 @@
         return state[0].astype(dtype)
     own, from_x, from_y, last_x, last_y = (v.astype(jnp.float32) for v in state)
     half = own.shape[0] // 2
-    return jnp.concatenate([own[:half] + from_x + last_y, own[half:] + last_x + from_y]).astype(dtype)
+    low_half, high_half = own[:half] + from_x[half:] + last_y, own[half:] + last_x + from_y[half:]
+    return jnp.concatenate([low_half, high_half]).astype(dtype)
 
 
 def reduce_chips(value):
     count = lax.axis_size("expert")
-    mask = 2
-    while mask < count:
-        value = add_low(value, lax.ppermute(value, "expert", [(i, i ^ mask) for i in range(count)]))
-        mask *= 2
+    me = lax.axis_index("expert")
+    masks = [1 << i for i in range(1, count.bit_length() - 1)]
+    swap = lambda v, mask: lax.ppermute(v, "expert", [(i, i ^ mask) for i in range(count)])
+    for mask in masks:
+        half = value.shape[0] // 2
+        upper = (me & mask) != 0
+        keep = jnp.where(upper, value[half:], value[:half])
+        send = jnp.where(upper, value[:half], value[half:])
+        value = add_low(keep, swap(send, mask))
+    for mask in reversed(masks):
+        other = swap(value, mask)
+        upper = (me & mask) != 0
+        value = jnp.concatenate([jnp.where(upper, other, value), jnp.where(upper, value, other)])
     return value
 
 
@@ -208,32 +218,29 @@
     cosine, sine = cos_ref[...], sin_ref[...]
     mixed = dot(hidden, weight_ref[step], NN)
     low = jnp.bfloat16
+    scaling = HEAD_DIM ** (-0.5)
     for p in range(3):
         part = mixed[:, 128 * p : 128 * p + 128]
-        q_ref[:, 128 * p : 128 * p + 128] = (part * cosine + turned(part) * sine).astype(low)
+        turned_part = (part * cosine + turned(part) * sine).astype(low)
+        q_ref[:, 128 * p : 128 * p + 128] = turned_part * scaling
     part = mixed[:, 384:512]
     k_ref[...] = (part * cosine + turned(part) * sine).astype(low)
     v_ref[...] = mixed[:, 512:640].astype(low)
-    scaling = HEAD_DIM ** (-0.5)
     tokens = hidden.shape[0]
     for seg in range(tokens // SEG):
         rows = pl.ds(seg * SEG, SEG)
         span = (seg + 1) * SEG
         bias = bias_ref[rows, :span]
-        outs = []
-        logs = []
-        for h in range(6):
-            kv = h // 3
-            keys = k_ref[:span, HEAD_DIM * kv : HEAD_DIM * (kv + 1)]
-            vals = v_ref[:span, HEAD_DIM * kv : HEAD_DIM * (kv + 1)]
-            query = q_ref[rows, HEAD_DIM * h : HEAD_DIM * (h + 1)]
-            scores = dot(query, keys, NT) * scaling + bias
-            highest = jnp.max(scores, axis=1, keepdims=True)
-            powers = jnp.exp(scores - highest)
-            total = jnp.sum(powers, axis=1, keepdims=True)
-            probs = (powers * (1.0 / total)).astype(low)
-            outs.append(dot(probs, vals, NN))
-            logs.append(highest + jnp.log(total))
+        keys = [k_ref[:span, HEAD_DIM * kv : HEAD_DIM * (kv + 1)] for kv in range(2)]
+        vals = [v_ref[:span, HEAD_DIM * kv : HEAD_DIM * (kv + 1)] for kv in range(2)]
+        queries = [q_ref[rows, HEAD_DIM * h : HEAD_DIM * (h + 1)] for h in range(6)]
+        scores = [dot(queries[h], keys[h // 3], NT) + bias for h in range(6)]
+        highest = [jnp.max(v, axis=1, keepdims=True) for v in scores]
+        powers = [jnp.exp(v - m) for v, m in zip(scores, highest)]
+        totals = [jnp.sum(v, axis=1, keepdims=True) for v in powers]
+        probs = [(v * (1.0 / t)).astype(low) for v, t in zip(powers, totals)]
+        outs = [dot(v, vals[h // 3], NN) for h, v in enumerate(probs)]
+        logs = [m + jnp.log(t) for m, t in zip(highest, totals)]
         att_ref[rows, :] = jnp.concatenate(outs, axis=1).astype(low)
         lse_ref[rows, :] = jnp.concatenate(logs + [logs[-1]] * 2, axis=1)
 
@@ -242,9 +249,9 @@
     tokens, width = hidden.shape
     low = jnp.bfloat16
     whole = lambda a: pl.BlockSpec(a.shape, lambda j, o, g: (0, 0))
-    anywhere = pl.BlockSpec(memory_space=pl.ANY)
+    anywhere = pl.BlockSpec(memory_space=pltpu.HBM)
     col = lambda w: pl.BlockSpec((tokens, w), lambda j, o, g: (0, g[j]))
-    shape = lambda w: jax.ShapeDtypeStruct((tokens, w), low)
+    shape = lambda w: pltpu.HBM((tokens, w), low)
     operands = [order, groups, hidden, cosine, sine, bias, *mixer_p]
     in_specs = [whole(hidden), whole(cosine), whole(sine), whole(bias)]
     in_specs += [anywhere] * len(mixer_p)
@@ -265,10 +272,10 @@
             scratch_shapes=[pltpu.VMEM((2, width, cols), low), pltpu.SemaphoreType.DMA((2,))],
         ),
         out_shape=[shape(1536), shape(1536), shape(512), shape(512)]
-        + [jax.ShapeDtypeStruct((4, tokens, 8), jnp.float32)],
+        + [pltpu.HBM((4, tokens, 8), jnp.float32)],
         input_output_aliases=aliases,
         compiler_params=pltpu.CompilerParams(vmem_limit_bytes=40 * 2**20),
-        cost_estimate=pl.CostEstimate(flops=16 * 10**9, bytes_accessed=8 * 10**6, transcendentals=0),
+        cost_estimate=pl.CostEstimate(flops=48 * 10**9, bytes_accessed=8 * 10**6, transcendentals=0),
         name="attend",
     )(*operands)
 
@@ -283,10 +290,27 @@
     )
 
 
+def row_to_column(row, lane):
+    low = jnp.bfloat16
+    pick = (lax.broadcasted_iota(jnp.int32, (8, 128), 1) == lane) & (
+        lax.broadcasted_iota(jnp.int32, (8, 128), 0) == 0
+    )
+    pick = pick.astype(jnp.float32).astype(low)
+    rows = jnp.broadcast_to(row, (8, row.shape[1]))
+    high = rows.astype(low)
+    rest = (rows - high.astype(jnp.float32)).astype(low)
+    return (dot(high, pick, TN) + dot(rest, pick, TN)).astype(low)
+
+
 def attend_back_kernel(mine, counts, call, group_ref, order_ref, branch_ref, hidden_ref, q_ref, k_ref, v_ref, lse_ref, cos_ref, sin_ref, bias_ref, *rest):
     first, second = counts
     pieces, mixer_p = rest[:first], rest[first : first + second]
-    wide_ref, input_ref, proj_ref, weight_ref, mixed_ref, grad_ref, dk_ref, dv_ref, sems = rest[first + second :]
+    rest = rest[first + second :]
+    if call:
+        part_ref, x_ref, resid_ref, gain_ref = rest[:4]
+        rest = rest[4:]
+    wide_refs, input_ref = rest[:2], rest[2]
+    proj_ref, weight_ref, mixed_ref, grad_ref, dk_ref, dv_ref, total_ref, sems = rest[3:]
     step = pl.program_id(0)
     load = projector_copies(mine, pieces, order_ref, proj_ref, sems.at[0])
     half = second // 2
@@ -313,31 +337,21 @@
         rows = pl.ds(seg * SEG, SEG)
         span = (seg + 1) * SEG
         bias = bias_ref[rows, :span]
-        gqs = []
-        gks = []
-        gvs = []
-        for kv in range(2):
-            keys = k_ref[:span, HEAD_DIM * kv : HEAD_DIM * (kv + 1)]
-            vals = v_ref[:span, HEAD_DIM * kv : HEAD_DIM * (kv + 1)]
-            gscore = []
-            probs_all = []
-            queries = []
-            grads = []
-            for h in range(3 * kv, 3 * kv + 3):
-                query = q_ref[rows, HEAD_DIM * h : HEAD_DIM * (h + 1)]
-                grad = grad_ref[rows, HEAD_DIM * h : HEAD_DIM * (h + 1)]
-                scores = dot(query, keys, NT) * scaling + bias
-                probs = jnp.exp(scores - lse_ref[rows, h : h + 1])
-                gprobs = dot(grad, vals, NT)
-                centre = jnp.sum(probs * gprobs, axis=1, keepdims=True)
-                gs = (probs * (gprobs - centre)).astype(low)
-                gqs.append(dot(gs, keys, NN) * scaling)
-                gscore.append(gs)
-                probs_all.append(probs.astype(low))
-                queries.append(query)
-                grads.append(grad)
-            gks.append(dot(jnp.concatenate(gscore, 0), jnp.concatenate(queries, 0), TN) * scaling)
-            gvs.append(dot(jnp.concatenate(probs_all, 0), jnp.concatenate(grads, 0), TN))
+        part = lambda ref, r, h: ref[r, HEAD_DIM * h : HEAD_DIM * (h + 1)]
+        keys = [part(k_ref, pl.ds(0, span), kv) for kv in range(2)]
+        vals = [part(v_ref, pl.ds(0, span), kv) for kv in range(2)]
+        queries = [part(q_ref, rows, h) for h in range(6)]
+        grads = [part(grad_ref, rows, h) for h in range(6)]
+        scores = [dot(queries[h], keys[h // 3], NT) + bias for h in range(6)]
+        gprobs = [dot(grads[h], vals[h // 3], NT) for h in range(6)]
+        probs = [jnp.exp(v - lse_ref[rows, h : h + 1]) for h, v in enumerate(scores)]
+        centres = [jnp.sum(p * g, axis=1, keepdims=True) for p, g in zip(probs, gprobs)]
+        gscore = [(p * (g - c)).astype(low) for p, g, c in zip(probs, gprobs, centres)]
+        probs = [p.astype(low) for p in probs]
+        gqs = [dot(v, keys[h // 3], NN) * scaling for h, v in enumerate(gscore)]
+        three = lambda values, kv: jnp.concatenate(values[3 * kv : 3 * kv + 3], 0)
+        gks = [dot(three(gscore, kv), three(queries, kv), TN) for kv in range(2)]
+        gvs = [dot(three(probs, kv), three(grads, kv), TN) for kv in range(2)]
         gq = jnp.concatenate(gqs, axis=1)
         cos_rows, sin_rows = cosine[seg * SEG : span], sine[seg * SEG : span]
         for p in range(3):
@@ -363,25 +377,54 @@
             for copy in more[c]:
                 copy.wait()
 
-    wide_ref[...] = dot(hidden_ref[...], mixed_ref[...], TN).astype(low)
+    wide = dot(hidden_ref[...], mixed_ref[...], TN).astype(low)
     part = dot(mixed_ref[...], weight_ref[step], NT)
+    for c in range(2):
+
+        @pl.when(step == c)
+        def _():
+            wide_refs[c][:, :640] = wide
+
+    if not call:
+
+        @pl.when(step == 0)
+        def _():
+            input_ref[...] = part
+
+        @pl.when(step > 0)
+        def _():
+            input_ref[...] += part
+
+        return
 
     @pl.when(step == 0)
     def _():
-        input_ref[...] = part
+        total_ref[...] = part + part_ref[...]
 
     @pl.when(step > 0)
     def _():
-        input_ref[...] += part
-
-
-def attend_back(call, branch, hidden, proj, mixer_p, order, groups, q, k, v, lse, cosine, sine, bias):
+        value = x_ref[...].astype(jnp.float32)
+        scale = lax.rsqrt(jnp.mean(value * value, axis=1, keepdims=True) + EPSILON)
+        normed = value * scale
+        grad = total_ref[...] + part
+        product = grad * normed
+        gains = row_to_column(jnp.sum(product, axis=0, keepdims=True), 0)
+        for ref in wide_refs:
+            ref[:, 640:] = gains
+        grad = grad * gain_ref[...]
+        mean = jnp.mean(grad * normed, axis=1, keepdims=True)
+        input_ref[...] = (resid_ref[...] + scale * (grad - normed * mean)).astype(low)
+
+
+def attend_back(call, branch, hidden, proj, mixer_p, order, groups, q, k, v, lse, cosine, sine, bias, *more):
     tokens, width = branch.shape
     low = jnp.bfloat16
     whole = lambda a: pl.BlockSpec(a.shape, lambda j, g, o: (0, 0))
     col = lambda w: pl.BlockSpec((tokens, w), lambda j, g, o: (0, g[j]))
     cols = mixer_p[0].shape[-1] // 2
     mine = len(mixer_p) // 2
+    wide = jax.ShapeDtypeStruct((width, cols + 128 * call), low)
+    given = jax.ShapeDtypeStruct((tokens, width), low if call else jnp.float32)
     return pl.pallas_call(
         lambda *refs: attend_back_kernel(mine, (len(proj), len(mixer_p)), call, *refs),
         grid_spec=pltpu.PrefetchScalarGridSpec(
@@ -390,11 +433,9 @@
             in_specs=[whole(branch), whole(hidden), col(384), col(128), col(128)]
             + [pl.BlockSpec((None, tokens, 8), lambda j, g, o: (g[j], 0, 0))]
             + [whole(cosine), whole(sine), whole(bias)]
-            + [pl.BlockSpec(memory_space=pl.ANY)] * (len(proj) + len(mixer_p)),
-            out_specs=[
-                pl.BlockSpec((None, width, cols), lambda j, g, o: (j, 0, 0)),
-                pl.BlockSpec((tokens, width), lambda j, g, o: (0, 0)),
-            ],
+            + [pl.BlockSpec(memory_space=pltpu.HBM)] * (len(proj) + len(mixer_p))
+            + [whole(value) for value in more],
+            out_specs=[whole(wide), whole(wide), whole(given)],
             scratch_shapes=[
                 pltpu.VMEM((width, width), low),
                 pltpu.VMEM((2, width, cols), low),
@@ -402,93 +443,294 @@
                 pltpu.VMEM((tokens, 384), low),
                 pltpu.VMEM((tokens, 128), jnp.float32),
                 pltpu.VMEM((tokens, 128), jnp.float32),
+                pltpu.VMEM((tokens, width) if call else (8, 128), jnp.float32),
                 pltpu.SemaphoreType.DMA((3,)),
             ],
         ),
-        out_shape=[
-            jax.ShapeDtypeStruct((2, width, cols), low),
-            jax.ShapeDtypeStruct((tokens, width), jnp.float32),
-        ],
-        compiler_params=pltpu.CompilerParams(vmem_limit_bytes=50 * 2**20),
-        cost_estimate=pl.CostEstimate(flops=20 * 10**9, bytes_accessed=8 * 10**6, transcendentals=0),
+        out_shape=[wide, wide, given],
+        compiler_params=pltpu.CompilerParams(vmem_limit_bytes=58 * 2**20),
+        cost_estimate=pl.CostEstimate(flops=60 * 10**9, bytes_accessed=8 * 10**6, transcendentals=0),
         name="attend_back",
-    )(groups, order, branch, hidden, q, k, v, lse, cosine, sine, bias, *proj, *mixer_p)
-
-
-def project_kernel(mine, count, order_ref, left_ref, *rest):
+    )(groups, order, branch, hidden, q, k, v, lse, cosine, sine, bias, *proj, *mixer_p, *more)
+
+
+TILE = 256
+
+
+def extra_rows(expert_count):
+    return 8 if expert_count <= 24 else 16
+
+
+def table_picks(expert_count):
+    extra = extra_rows(expert_count)
+    row = lax.broadcasted_iota(jnp.int32, (extra, 128), 0)
+    lane = lax.broadcasted_iota(jnp.int32, (extra, 128), 1)
+    return [
+        (lane == row + block * extra).astype(jnp.float32).astype(jnp.bfloat16)
+        for block in range(expert_count // extra)
+    ]
+
+
+def table_rows(values, picks, width):
+    low = jnp.bfloat16
+    high = values.astype(low)
+    parts = (high, (values - high.astype(jnp.float32)).astype(low))
+    rows = [dot(pick, value, NT).astype(low) for pick in picks for value in parts]
+    left = width - TILE * len(rows)
+    if left:
+        rows.append(jnp.zeros((picks[0].shape[0], left), low))
+    return jnp.concatenate(rows, axis=1)
+
+
+def table_values(rows, picks):
+    total = None
+    for block, pick in enumerate(picks):
+        for part in range(2):
+            at = (2 * block + part) * TILE
+            value = dot(rows[:, at : at + TILE], pick, TN)
+            total = value if total is None else total + value
+    return total
+
+
+def project_kernel(mine, count, expert_count, order_ref, left_ref, x_ref, routes_ref, gain_ref, router_ref, *rest):
     pieces = rest[:count]
-    out_ref, weight_ref, sem = rest[count:]
+    resid_ref, gates_ref, rows_ref, weight_ref, sem = rest[count:]
     copies = projector_copies(mine, pieces, order_ref, weight_ref, sem)
-    for copy in copies:
-        copy.start()
-    for copy in copies:
-        copy.wait()
-    out_ref[...] = dot(left_ref[...], weight_ref[...], NN)
-
-
-def project(left, proj, mine, order):
+
+    @pl.when(pl.program_id(0) == 0)
+    def _():
+        for copy in copies:
+            copy.start()
+        for copy in copies:
+            copy.wait()
+
+    low = jnp.bfloat16
+    resid = x_ref[...].astype(jnp.float32) + dot(left_ref[...], weight_ref[...], NN)
+    resid_ref[...] = resid
+    scale = lax.rsqrt(jnp.mean(resid * resid, axis=1, keepdims=True) + EPSILON)
+    hidden = (resid * scale * gain_ref[...]).astype(low)
+    rows_ref[:TILE, :] = hidden
+    logits = dot(hidden, router_ref[...], NT)
+    lane = lax.broadcasted_iota(jnp.int32, logits.shape, 1)
+    routed = lane == routes_ref[:, 0:1]
+    for k in range(1, routes_ref.shape[1]):
+        routed = routed | (lane == routes_ref[:, k : k + 1])
+    logits = jnp.where(routed, logits, NEGATIVE)
+    powers = jnp.exp(logits - jnp.max(logits, axis=1, keepdims=True))
+    gates = powers / jnp.sum(powers, axis=1, keepdims=True)
+    gates_ref[...] = gates
+    rows_ref[TILE:, :] = table_rows(gates, table_picks(expert_count), hidden.shape[1])
+
+
+def project(left, x, routes, gain, router, expert_count, proj, mine, order):
     tokens, width = left.shape
+    tall = TILE + extra_rows(expert_count)
+    tile = lambda w, h=TILE: pl.BlockSpec((h, w), lambda i, o: (i, 0))
+    whole = lambda a: pl.BlockSpec(a.shape, lambda i, o: (0, 0))
     return pl.pallas_call(
-        lambda *refs: project_kernel(mine, len(proj), *refs),
+        lambda *refs: project_kernel(mine, len(proj), expert_count, *refs),
         grid_spec=pltpu.PrefetchScalarGridSpec(
             num_scalar_prefetch=1,
-            grid=(1,),
-            in_specs=[pl.BlockSpec((tokens, width), lambda i, o: (0, 0))]
-            + [pl.BlockSpec(memory_space=pl.ANY)] * len(proj),
-            out_specs=pl.BlockSpec((tokens, width), lambda i, o: (0, 0)),
+            grid=(tokens // TILE,),
+            in_specs=[tile(width), tile(width), tile(routes.shape[1]), whole(gain), whole(router)]
+            + [pl.BlockSpec(memory_space=pltpu.HBM)] * len(proj),
+            out_specs=[tile(width), tile(128), tile(width, tall)],
             scratch_shapes=[pltpu.VMEM((width, width), jnp.bfloat16), pltpu.SemaphoreType.DMA],
         ),
-        out_shape=jax.ShapeDtypeStruct((tokens, width), jnp.float32),
+        out_shape=[
+            jax.ShapeDtypeStruct((tokens, width), jnp.float32),
+            jax.ShapeDtypeStruct((tokens, 128), jnp.float32),
+            jax.ShapeDtypeStruct((tokens // TILE * tall, width), jnp.bfloat16),
+        ],
         compiler_params=pltpu.CompilerParams(vmem_limit_bytes=40 * 2**20),
-        cost_estimate=pl.CostEstimate(flops=5 * 10**9, bytes_accessed=8 * 10**6, transcendentals=0),
+        cost_estimate=pl.CostEstimate(flops=30 * 10**9, bytes_accessed=8 * 10**6, transcendentals=0),
         name="project",
-    )(order, left, *proj)
-
-
-TILE = 256
-
-
-def extra_rows(expert_count):
-    return 8 if expert_count <= 24 else 16
-
-
-def with_table(rows, table):
-    tokens, width = rows.shape
-    expert_count = table.shape[1]
-    extra = extra_rows(expert_count)
-    tiles = tokens // TILE
-    high = table.astype(jnp.bfloat16)
-    rest = (table - high.astype(jnp.float32)).astype(jnp.bfloat16)
-    both = jnp.stack([high.T, rest.T], axis=1)
-    both = both.reshape(expert_count // extra, extra, 2, tiles, TILE)
-    both = jnp.transpose(both, (3, 1, 0, 2, 4)).reshape(tiles, extra, -1)
-    both = jnp.pad(both, ((0, 0), (0, 0), (0, width - both.shape[2])))
-    return jnp.concatenate([rows.reshape(tiles, TILE, width), both], axis=1).reshape(-1, width)
-
-
-def table_of(rows, tokens, expert_count):
-    extra = extra_rows(expert_count)
-    tiles = tokens // TILE
-    both = rows.reshape(tiles, TILE + extra, -1)[:, TILE:, : expert_count // extra * 2 * TILE]
-    both = both.reshape(tiles, extra, expert_count // extra, 2, TILE)
-    return jnp.transpose(jnp.sum(both.astype(jnp.float32), axis=3), (0, 3, 2, 1)).reshape(tokens, -1)
-
-
-def rows_of(rows, tokens):
-    tiles = tokens // TILE
-    return rows.reshape(tiles, rows.shape[0] // tiles, -1)[:, :TILE].reshape(tokens, -1)
+    )(order, left, x, routes, gain, router, *proj)
+
+
+def turn_kernel(expert_count, order_ref, a_ref, b_ref, c_ref, rows_ref, gates_ref, resid_ref, cot_ref, left_ref, gain_ref, router_ref,
+                branch_ref, grad_ref, mine_ref, other_ref, low_ref, small_ref, gains_ref):
+    low = jnp.bfloat16
+    step = pl.program_id(0)
+    total = a_ref[...].astype(jnp.float32) + b_ref[...].astype(jnp.float32) + c_ref[...].astype(jnp.float32)
+    gates = gates_ref[...]
+    grad_gates = table_values(total[TILE:, :].astype(low), table_picks(expert_count))
+    mean = jnp.sum(gates * grad_gates, axis=1, keepdims=True)
+    grad_logits = gates * (grad_gates - mean)
+    high = grad_logits.astype(low)
+    rest = (grad_logits - high.astype(jnp.float32)).astype(low)
+    grad = total[:TILE, :] + dot(high, router_ref[...], NN) + dot(rest, router_ref[...], NN)
+    resid = resid_ref[...]
+    scale = lax.rsqrt(jnp.mean(resid * resid, axis=1, keepdims=True) + EPSILON)
+    normed = resid * scale
+    hidden = rows_ref[:TILE, :]
+    small = dot(hidden, jnp.concatenate([high, rest], axis=1), TN)
+    small = small[:, :128] + small[:, 128:]
+    gains = jnp.sum(grad * normed, axis=0, keepdims=True)
+    grad = grad * gain_ref[...]
+    mean = jnp.mean(grad * normed, axis=1, keepdims=True)
+    grad = cot_ref[...].astype(jnp.float32) + scale * (grad - normed * mean)
+    grad_ref[...] = grad
+    branch = grad.astype(low)
+    branch_ref[...] = branch
+    low_ref[pl.ds(pl.multiple_of(step * TILE, TILE), TILE), :] = branch
+
+    @pl.when(step == 0)
+    def _():
+        small_ref[...] = small
+        gains_ref[...] = gains
+
+    @pl.when(step > 0)
+    def _():
+        small_ref[...] += small
+        gains_ref[...] += gains
+
+    @pl.when(step == pl.num_programs(0) - 1)
+    def _():
+        core = order_ref[order_ref.shape[0] - 1]
+        half = low_ref.shape[1] // 2
+        left = left_ref[...]
+        small = small_ref[...].astype(low) + row_to_column(gains_ref[...], expert_count)
+        for ref, which in ((mine_ref, core), (other_ref, 1 - core)):
+            part = low_ref[:, pl.ds(pl.multiple_of(which * half, 128), half)]
+            ref[:, :half] = dot(left, part, TN).astype(low)
+            ref[:, half:] = small
+
+
+def turn(expert_count, order, a, b, c, rows, gates, resid, cots, left, gain, router):
+    tokens, width = left.shape
+    tall = TILE + extra_rows(expert_count)
+    tile = lambda w, h=TILE: pl.BlockSpec((h, w), lambda i, o: (i, 0))
+    whole = lambda a: pl.BlockSpec(a.shape, lambda i, o: (0, 0))
+    half = jax.ShapeDtypeStruct((width, width // 2 + 128), jnp.bfloat16)
+    return pl.pallas_call(
+        lambda *refs: turn_kernel(expert_count, *refs),
+        grid_spec=pltpu.PrefetchScalarGridSpec(
+            num_scalar_prefetch=1,
+            grid=(tokens // TILE,),
+            in_specs=[tile(width, tall)] * 4 + [tile(128), tile(width), tile(width), whole(left)]
+            + [whole(gain), whole(router)],
+            out_specs=[tile(width), tile(width), whole(half), whole(half)],
+            scratch_shapes=[
+                pltpu.VMEM((tokens, width), jnp.bfloat16),
+                pltpu.VMEM((width, 128), jnp.float32),
+                pltpu.VMEM((1, width), jnp.float32),
+            ],
+        ),
+        out_shape=[
+            jax.ShapeDtypeStruct((tokens, width), jnp.bfloat16),
+            jax.ShapeDtypeStruct((tokens, width), jnp.float32),
+            half,
+            half,
+        ],
+        compiler_params=pltpu.CompilerParams(vmem_limit_bytes=58 * 2**20),
+        cost_estimate=pl.CostEstimate(flops=30 * 10**9, bytes_accessed=8 * 10**6, transcendentals=0),
+        name="turn",
+    )(order, a, b, c, rows, gates, resid, cots, left, gain, router)
+
+
+def fold_kernel(pairs, table_ref, *refs):
+    x_ref, y_ref, own_ref, beside_ref, above_ref = refs[2 * pairs :]
+    places = ((x_ref, 0, 2), (y_ref, 2, 4), (own_ref, 4, 6), (beside_ref, 6, 7), (above_ref, 7, 8))
+    step = pl.program_id(0)
+    at = 0
+    for i in range(pairs):
+        left, right = refs[2 * i][...], refs[2 * i + 1][...]
+        value = (left.astype(jnp.float32) + right.astype(jnp.float32)).astype(jnp.bfloat16)
+        columns = slice(at, at + value.shape[1])
+        at += value.shape[1]
+        for ref, low, high in places:
+
+            @pl.when((step >= low) & (step < high))
+            def _():
+                ref[:, columns] = value
+
+
+def fold(*operands):
+    if lax.axis_size("shard") != 4:
+        parts = [add_low(operands[i], operands[i + 1]) for i in range(0, len(operands), 2)]
+        blocks = jnp.concatenate(parts, axis=1)
+        return reduce_first(blocks.reshape(lax.axis_size("shard"), -1, blocks.shape[1]))
+    me = lax.axis_index("shard")
+    rows = operands[0].shape[0] // 8
+    where = [(3, 0), (1, 0), (3, 1), (2, 1), (0, 0), (0, 1), (1, 1), (2, 0)]
+    table = jnp.stack([(me ^ r) * 2 + half for r, half in where]).astype(jnp.int32)
+    columns = sum(v.shape[1] for v in operands[::2])
+    given = lambda n: jax.ShapeDtypeStruct((n * rows, columns), jnp.bfloat16)
+    place = lambda low, count: pl.BlockSpec((rows, columns), lambda i, t: (jnp.clip(i - low, 0, count - 1), 0))
+    x, y, own, beside, above = pl.pallas_call(
+        lambda *refs: fold_kernel(len(operands) // 2, *refs),
+        grid_spec=pltpu.PrefetchScalarGridSpec(
+            num_scalar_prefetch=1,
+            grid=(8,),
+            in_specs=[pl.BlockSpec((rows, v.shape[1]), lambda i, t: (t[i], 0)) for v in operands],
+            out_specs=[place(0, 2), place(2, 2), place(4, 2), place(6, 1), place(7, 1)],
+        ),
+        out_shape=[given(2), given(2), given(2), given(1), given(1)],
+        cost_estimate=pl.CostEstimate(flops=10**9, bytes_accessed=4 * 10**6, transcendentals=0),
+        name="fold",
+    )(table, *operands)
+    return own, beside, above, across(x, 1), across(y, 2)
+
+
+def finish_kernel(order_ref, one_mine, one_other, two_mine, two_other, mixer_ref, proj_ref, router_ref, second_ref, first_ref):
+    lower = order_ref[order_ref.shape[0] - 1] == 0
+    wide = jnp.float32
+    half = proj_ref.shape[1] // 2
+    groups = []
+    for mine, other in ((one_mine, one_other), (two_mine, two_other)):
+        a, b = mine[:, :640].astype(wide), other[:, :640].astype(wide)
+        groups += [jnp.where(lower, a, b), jnp.where(lower, b, a)]
+    for g, value in enumerate(groups):
+        mixer_ref[:, 384 * g : 384 * (g + 1)] = value[:, :384]
+        mixer_ref[:, 1536 + 128 * g : 1536 + 128 * (g + 1)] = value[:, 384:512]
+        mixer_ref[:, 2048 + 128 * g : 2048 + 128 * (g + 1)] = value[:, 512:]
+    a, b = one_mine[:, 640 : 640 + half].astype(wide), one_other[:, 640 : 640 + half].astype(wide)
+    proj_ref[:, :half] = jnp.where(lower, a, b)
+    proj_ref[:, half:] = jnp.where(lower, b, a)
+    experts = router_ref.shape[0]
+    size = (experts + 8, 128)
+    pick = lax.broadcasted_iota(jnp.int32, size, 0) == lax.broadcasted_iota(jnp.int32, size, 1)
+    pick = pick.astype(wide).astype(jnp.bfloat16)
+    rows = dot(pick, one_mine[:, 640 + half :], NT)
+    router_ref[...] = rows[:experts, :]
+    second_ref[...] = rows[experts : experts + 1, :]
+    first_ref[...] = dot(pick, two_mine[:, 640:], NT)[:1, :]
+
+
+def finish(expert_count, order, one, two):
+    rows = one[0].shape[0]
+    block = 128 if rows % 128 == 0 else rows
+    tall = [jax.ShapeDtypeStruct((rows, w), jnp.float32) for w in (2560, 1536)]
+    flat = [jax.ShapeDtypeStruct((h, rows), jnp.float32) for h in (expert_count, 1, 1)]
+    spec = lambda a: pl.BlockSpec((block, a.shape[1]), lambda i, o: (i, 0))
+    flat_spec = lambda a: pl.BlockSpec((a.shape[0], block), lambda i, o: (0, i))
+    operands = [*one, *two]
+    return pl.pallas_call(
+        finish_kernel,
+        grid_spec=pltpu.PrefetchScalarGridSpec(
+            num_scalar_prefetch=1,
+            grid=(rows // block,),
+            in_specs=[spec(v) for v in operands],
+            out_specs=[spec(v) for v in tall] + [flat_spec(v) for v in flat],
+        ),
+        out_shape=tall + flat,
+        cost_estimate=pl.CostEstimate(flops=10**9, bytes_accessed=4 * 10**6, transcendentals=0),
+        name="finish",
+    )(order, *operands)
 
 
 def expert_kernel(counts, expert_count, order_ref, place_ref, xa_ref, xb_ref, u_ref, *rest):
     pieces, more = counts
-    sides_p, downs_p = rest[:pieces], rest[pieces : 2 * pieces]
-    rest = rest[2 * pieces + more :]
-    (gta_ref, gtb_ref, out_ref, x_ref, mid_ref, sides_ref, ws_ref, wd_ref, sems) = rest
+    gates_p, ups_p, downs_p = (rest[i * pieces : (i + 1) * pieces] for i in range(3))
+    rest = rest[3 * pieces + more :]
+    (gta_ref, gtb_ref, out_ref, x_ref, mid_ref, sides_ref, wg_ref, wu_ref, wd_ref, sems) = rest
     low = jnp.bfloat16
     extra = extra_rows(expert_count)
     step = pl.program_id(0)
     half = pl.num_programs(0) // 2
-    load = piece_copies(sides_p, order_ref, ws_ref, sems.at[0], 1, 0)
+    load = piece_copies(gates_p, order_ref, wg_ref, sems.at[0], 1, 0)
+    load += piece_copies(ups_p, order_ref, wu_ref, sems.at[0], 1, 0)
     load_down = piece_copies(downs_p, order_ref, wd_ref, sems.at[1], 2, 0)
 
     @pl.when(step == 0)
@@ -531,8 +773,8 @@
     sums = []
     for l in range(2):
         gates = gates_wide[:, l : l + 1]
-        gate_in = dot(rows, ws_ref[2 * l], NN)
-        up_in = dot(rows, ws_ref[2 * l + 1], NN)
+        gate_in = dot(rows, wg_ref[l], NN)
+        up_in = dot(rows, wu_ref[l], NN)
         back = dot(cots, wd_ref[l], NT)
         sigma = 1.0 / (1.0 + jnp.exp(-gate_in))
         active = gate_in * sigma
@@ -547,7 +789,7 @@
         grad_up = (back * active).astype(low)
         sides_ref[2 * l] = grad_gate
         sides_ref[2 * l + 1] = grad_up
-        part = dot(grad_gate, ws_ref[2 * l], NT) + dot(grad_up, ws_ref[2 * l + 1], NT)
+        part = dot(grad_gate, wg_ref[l], NT) + dot(grad_up, wu_ref[l], NT)
         taken = part if taken is None else taken + part
     out_ref[...] = out.astype(low)
     taken_low = taken.astype(low)
@@ -572,11 +814,11 @@
         gtb_ref[TILE:, :] = columns
 
 
-def expert_chunk(order, place, xa, xb, cots, sides, downs, expert_count, kept):
+def expert_chunk(order, place, xa, xb, cots, gates, ups, downs, expert_count, kept):
     total, width = cots.shape
     devices = lax.axis_size("expert")
     tokens = total // devices
-    hidden = sides[0].shape[-1]
+    hidden = gates[0].shape[-1]
     half = tokens // TILE
     steps = 2 * half
     low = jnp.bfloat16
@@ -584,14 +826,14 @@
     first = pl.BlockSpec((tall, width), lambda i, o, p: (jnp.minimum(i, half - 1), 0))
     second = pl.BlockSpec((tall, width), lambda i, o, p: (jnp.maximum(i - half, 0), 0))
     where = lambda i, p: jnp.where(i < half, p[0] * half + i, p[1] * half + i - half)
-    anywhere = pl.BlockSpec(memory_space=pl.ANY)
+    anywhere = pl.BlockSpec(memory_space=pltpu.HBM)
     big_row = pl.BlockSpec((TILE, width), lambda i, o, p: (where(i, p), 0))
     big = lambda n: pl.BlockSpec((n, TILE, hidden), lambda i, o, p: (0, where(i, p), 0))
     single = jax.ShapeDtypeStruct((half * tall, width), low)
     shapes = [jax.ShapeDtypeStruct((total, width), low)] * 2
     shapes += [jax.ShapeDtypeStruct((n, total, hidden), low) for n in (2, 4)]
-    operands = [order, place, xa, xb, cots, *sides, *downs]
-    in_specs = [first, second, big_row] + [anywhere] * (2 * len(sides))
+    operands = [order, place, xa, xb, cots, *gates, *ups, *downs]
+    in_specs = [first, second, big_row] + [anywhere] * (3 * len(gates))
     aliases = {}
     more = 0
     if kept is not None:
@@ -600,14 +842,15 @@
         operands += list(kept)
         in_specs += [anywhere] * more
     res = pl.pallas_call(
-        lambda *refs: expert_kernel((len(sides), more), expert_count, *refs),
+        lambda *refs: expert_kernel((len(gates), more), expert_count, *refs),
         grid_spec=pltpu.PrefetchScalarGridSpec(
             num_scalar_prefetch=2,
             grid=(steps,),
             in_specs=in_specs,
             out_specs=[first, second, big_row, big_row, big(2), big(4)],
             scratch_shapes=[
-                pltpu.VMEM((4, width, hidden), low),
+                pltpu.VMEM((2, width, hidden), low),
+                pltpu.VMEM((2, width, hidden), low),
                 pltpu.VMEM((2, hidden, width), low),
                 pltpu.SemaphoreType.DMA((2,)),
             ],
@@ -615,7 +858,7 @@
         out_shape=[single] * 2 + shapes,
         input_output_aliases=aliases,
         compiler_params=pltpu.CompilerParams(vmem_limit_bytes=58 * 2**20),
-        cost_estimate=pl.CostEstimate(flops=27 * 10**9, bytes_accessed=8 * 10**6, transcendentals=0),
+        cost_estimate=pl.CostEstimate(flops=81 * 10**9, bytes_accessed=8 * 10**6, transcendentals=0),
         name="expert_chunk",
     )(*operands)
     return res[:2], res[2:]
@@ -663,9 +906,85 @@
         out_shape=jax.ShapeDtypeStruct((parts, count) + shape, jnp.bfloat16),
         scratch_shapes=[pltpu.VMEM((size_m, size_n), jnp.float32)],
         compiler_params=pltpu.CompilerParams(vmem_limit_bytes=48 * 2**20),
-        cost_estimate=pl.CostEstimate(flops=20 * 10**9, bytes_accessed=8 * 10**6, transcendentals=0),
+        cost_estimate=pl.CostEstimate(flops=60 * 10**9, bytes_accessed=8 * 10**6, transcendentals=0),
         name="weight_grad",
     )(left, right)
+
+
+def sorted_grad_kernel(on_rows, half, order_ref, left_ref, right_ref, own_ref, beside_ref, above_ref, x_ref, y_ref, acc_ref):
+    index, step = pl.program_id(0), pl.program_id(1)
+    value = dot(left_ref[...], right_ref[...], TN)
+
+    @pl.when(step == 0)
+    def _():
+        acc_ref[...] = value
+
+    @pl.when(step > 0)
+    def _():
+        acc_ref[...] += value
+
+    def block(r):
+        rows, cols = own_ref.shape
+        size = rows if on_rows else cols
+        place = pl.ds(pl.multiple_of(order_ref[r] * size, 128), size)
+        part = acc_ref[place, :] if on_rows else acc_ref[:, place]
+        return part.astype(own_ref.dtype)
+
+    last = step == pl.num_programs(1) - 1
+
+    @pl.when(last)
+    def _():
+        own_ref[...] = block(0)
+
+    @pl.when(last & (index < half))
+    def _():
+        x_ref[0] = block(3)
+        x_ref[1] = block(1)
+        above_ref[...] = block(2)
+
+    @pl.when(last & (index >= half))
+    def _():
+        y_ref[0] = block(3)
+        y_ref[1] = block(2)
+        beside_ref[...] = block(1)
+
+
+def grad_exchange(left, right, order, on_rows, pick=0, stride=1):
+    shards = lax.axis_size("shard")
+    if shards != 4:
+        return reduce_first(weight_grad(left, right[pick::stride] if right.ndim == 3 else right, shards, on_rows))
+    count = left.shape[0] if left.ndim == 3 else right.shape[0] // stride
+    half = count // 2
+    total, size_m = left.shape[-2:]
+    size_n = right.shape[-1]
+    block = 1024
+    spec = lambda a: (
+        pl.BlockSpec((None, block, a.shape[-1]), lambda l, k, o: (l * stride + pick, k, 0))
+        if a.ndim == 3
+        else pl.BlockSpec((block, a.shape[-1]), lambda l, k, o: (k, 0))
+    )
+    shape = (size_m // 4, size_n) if on_rows else (size_m, size_n // 4)
+    early = lambda l: jnp.minimum(l, half - 1)
+    late = lambda l: jnp.maximum(l - half, 0)
+    one = lambda f: pl.BlockSpec((None,) + shape, lambda l, k, o: (f(l), 0, 0))
+    two = lambda f: pl.BlockSpec((2, None) + shape, lambda l, k, o: (0, f(l), 0, 0))
+    low = lambda *lead: jax.ShapeDtypeStruct(lead + shape, jnp.bfloat16)
+    own, beside, above, x, y = pl.pallas_call(
+        lambda *refs: sorted_grad_kernel(on_rows, half, *refs),
+        grid_spec=pltpu.PrefetchScalarGridSpec(
+            num_scalar_prefetch=1,
+            grid=(count, total // block),
+            in_specs=[spec(left), spec(right)],
+            out_specs=[one(lambda l: l), one(late), one(early), two(early), two(late)],
+            scratch_shapes=[pltpu.VMEM((size_m, size_n), jnp.float32)],
+        ),
+        out_shape=[low(count), low(half), low(half), low(2, half), low(2, half)],
+        compiler_params=pltpu.CompilerParams(vmem_limit_bytes=48 * 2**20),
+        cost_estimate=pl.CostEstimate(flops=60 * 10**9, bytes_accessed=8 * 10**6, transcendentals=0),
+        name="weight_grad",
+    )(order, left, right)
+    merged = lambda v: v.reshape((2 * half,) + shape)
+    return own, beside, above, across(merged(x), 1), across(merged(y), 2)
 
 
 def per_device(
@@ -709,23 +1028,22 @@
     small = jnp.concatenate([router_weight, norm1_gain[:, None], norm2_gain[:, None]], axis=1).T
     small = gather_small(small)
     mixer_first = gather_first(block)
+    router = jnp.pad(small[:expert_count], ((0, 128 - expert_count), (0, 0)))
+    gain_one = small[expert_count].astype(jnp.float32)[None, :]
+    gain_two = small[expert_count + 1].astype(jnp.float32)[None, :]
+    activity = layer_input.astype(jnp.float32)
+    hidden_one = (activity * inverse_rms(activity) * gain_one).astype(low)
+    bias, cosine, sine = tree_tables(parents)
+    mixer_first, hidden_one, bias, cosine, sine = lax.optimization_barrier(
+        (mixer_first, hidden_one, bias, cosine, sine)
+    )
     mine = gather_second(mixer_first, 0)
     mixer_p = mine + [swap_core(p) for p in mine]
-    router = small[:expert_count].T
-    gain_one = small[expert_count].astype(jnp.float32)[None, :]
-    gain_two = small[expert_count + 1].astype(jnp.float32)[None, :]
     block = lax.dynamic_slice_in_dim(out_weight, core * (out_weight.shape[0] // 2), out_weight.shape[0] // 2, 0)
     project_first = gather_first(after(block, *mine))
-    sides = jnp.stack([gate_weight, up_weight], axis=1).reshape(4, -1, gate_weight.shape[2])
-    sides_first = gather_first(after(sides, *mine))
 
     cots = lax.all_gather(out_cotangent, "expert", axis=0, tiled=True)
 
-    bias, cosine, sine = tree_tables(parents)
-    activity = layer_input.astype(jnp.float32)
-    scale_one = inverse_rms(activity)
-    normed_one = activity * scale_one
-    hidden_one = (normed_one * gain_one).astype(low)
     saved = None
     groups = []
     for call in range(2):
@@ -735,27 +1053,22 @@
             project_first, saved = lax.optimization_barrier((project_first, saved))
             proj = gather_second(project_first, 0)
             near = swap_core(jnp.concatenate(proj[:3], axis=0))
-    proj, near, sides_first, saved = lax.optimization_barrier((proj, near, sides_first, saved))
+            gates_first = gather_first(after(gate_weight, project_first))
+    proj, near, gates_first, saved = lax.optimization_barrier((proj, near, gates_first, saved))
     far = [swap_core(p) for p in proj[3:]]
-    sides_p = gather_second(sides_first, 0)
-    downs_first = gather_first(after(down_weight, *far), True)
+    ups_first = gather_first(after(up_weight, proj))
     proj = proj + [near] + far
     attended, query, keys, values, log_total = saved
-    resid = activity + project(attended, proj, len(mixer_p) // 2, order)
-    scale_two = inverse_rms(resid)
-    normed_two = resid * scale_two
-    hidden_two = (normed_two * gain_two).astype(low)
-    logits = jnp.dot(hidden_two, router, preferred_element_type=jnp.float32)
-    routed = jnp.any(
-        routes[:, :, None] == jnp.arange(expert_count, dtype=jnp.int32)[None, None, :], axis=1
-    )
-    masked = jnp.where(routed, logits, NEGATIVE)
-    powers = jnp.exp(masked - jnp.max(masked, axis=1, keepdims=True))
-    gates = powers / jnp.sum(powers, axis=1, keepdims=True)
-    upstream = out_cotangent.astype(jnp.float32)
-
+    resid, gates, sent_rows = project(
+        attended, layer_input, routes, gain_two, router, expert_count, proj, len(mixer_p) // 2, order
+    )
+    ups_first, sent_rows = lax.optimization_barrier((ups_first, sent_rows))
+    gates_p = gather_second(gates_first, 0)
+    ups_first, down_block = lax.optimization_barrier((ups_first, after(down_weight, *gates_p)))
+    downs_first = gather_first(down_block, True)
+    ups_p = gather_second(ups_first, 0)
     downs_p = gather_second(downs_first, 0)
-    rows = [with_table(hidden_two, gates)]
+    rows = [sent_rows]
     rows.append(next_chip(rows[0]))
     beside = swap_core(rows[0])
     rows[0], rows[1], beside = lax.optimization_barrier((rows[0], rows[1], beside))
@@ -769,7 +1082,7 @@
         sent = next_chip(total) if step > 1 else None
         place = jnp.stack([(me - 2 * step) % (2 * chips), (me - 2 * step) % (2 * chips) ^ 1, me])
         parts, kept = expert_chunk(
-            order, place.astype(jnp.int32), here, beside, cots, sides_p, downs_p, expert_count, kept
+            order, place.astype(jnp.int32), here, beside, cots, gates_p, ups_p, downs_p, expert_count, kept
         )
         parts, kept, ahead, beside, sent = lax.optimization_barrier((parts, kept, ahead, beside_next, sent))
         if ahead is not None:
@@ -782,105 +1095,66 @@
     out_all, all_rows, all_mid, all_sides = kept
     all_rows, total = lax.optimization_barrier((all_rows, total))
     sent = next_chip(total)
-    wide_sides = weight_grad(all_rows, all_sides, shards, True)
-    sent, wide_sides = lax.optimization_barrier((sent, wide_sides))
-    sides_state = reduce_first(wide_sides)
-    final = sum(v.astype(jnp.float32) for v in (*last, sent))
-    grad_hidden_two = rows_of(final, tokens)
-    grad_gates = table_of(final, tokens, expert_count)
-    branch_out = lax.psum_scatter(after(out_all, final), "expert", scatter_dimension=0, tiled=True)
-
-    mean_gate = jnp.sum(gates * grad_gates, axis=1, keepdims=True)
-    grad_logits = gates * (grad_gates - mean_gate)
-    grad_hidden_two = grad_hidden_two + jnp.dot(
-        grad_logits, router.astype(jnp.float32).T, precision=lax.Precision.HIGHEST
-    )
-    grad_router = jnp.dot(
-        hidden_two.astype(jnp.float32).T, grad_logits, precision=lax.Precision.HIGHEST
-    )
-    grad_gain_two = jnp.sum(grad_hidden_two * normed_two, axis=0)
-    grad_normed_two = grad_hidden_two * gain_two
-    grad_resid = upstream + scale_two * (
-        grad_normed_two - normed_two * jnp.mean(grad_normed_two * normed_two, axis=1, keepdims=True)
-    )
-    grad_branch = grad_resid.astype(low)
-
-    def spread_sum(blocks):
-        return reduce_chips(reduce_last(reduce_second(reduce_first(blocks))))
-
-    grad_projector = jnp.dot(attended.T, grad_branch, preferred_element_type=jnp.float32).astype(low)
-    halves = grad_projector.reshape(shards, 2, -1, width)
-    mine = lax.dynamic_index_in_dim(halves, core, 1, keepdims=False)
-    other = lax.dynamic_index_in_dim(halves, 1 - core, 1, keepdims=False)
-    half_projector = (mine, swap_core(other))
-
-    def small_sum(value):
-        value = add_low(value, swap_core(value))
-        if shards == 4:
-            value = add_low(value, across(value, 1))
-            value = add_low(value, across(value, 2))
-        else:
-            value = lax.psum(value, "shard")
-        value = reduce_chips(value)
-        size = width // shards
-        return lax.dynamic_slice_in_dim(value, lax.axis_index("shard") * size, size, 1).astype(jnp.float32)
-
-    first_small = jnp.concatenate([grad_router, grad_gain_two[:, None]], axis=1).T.astype(low)
-
-    finals = []
-    parts = []
-    for call in range(2):
-        wide, part = attend_back(
-            call, grad_branch, hidden_one, proj, mixer_p, order, groups[call],
-            query, keys, values, log_total, cosine, sine, bias,
-        )
-        parts.append(part)
-        if call == 0:
-            grad_branch, wide, sides_state, first_small, half_projector = lax.optimization_barrier(
-                (grad_branch, wide, sides_state, first_small, half_projector)
-            )
-            sides_state = reduce_second(sides_state)
-        wide = wide.reshape(2, shards, -1, wide.shape[-1])
-        finals.append((wide[0], swap_core(wide[1])))
-    parts, finals[0], sides_state, all_mid = lax.optimization_barrier((parts, finals[0], sides_state, all_mid))
-    wide_down = weight_grad(all_mid, cots, shards, False)
-    down_state = reduce_second(reduce_first(wide_down))
-    finals = [spread_sum(add_low(*v)) for v in finals]
-    finals = [(v, swap_core(v)) for v in finals]
-    grad_hidden_one = parts[0] + parts[1]
-    first_small = small_sum(first_small)
-    mine = spread_sum(add_low(*half_projector))
-    other = swap_core(mine)
-    grad_projector = jnp.where(
-        core == 0, jnp.concatenate([mine, other]), jnp.concatenate([other, mine])
-    ).astype(jnp.float32)
-    grad_sides = reduce_last(sides_state, jnp.float32)
-    grad_sides = grad_sides.reshape(2, 2, *grad_sides.shape[1:])
-    grad_gate, grad_up = grad_sides[:, 0], grad_sides[:, 1]
+    gate_state = grad_exchange(all_rows, all_sides, order, True, 0, 2)
+    gate_done, all_rows = lax.optimization_barrier((gate_state[0], all_rows))
+    gate_state = (gate_done,) + gate_state[1:]
+    up_state = grad_exchange(all_rows, all_sides, order, True, 1, 2)
+    sent, up_done, gate_state = lax.optimization_barrier((sent, up_state[0], gate_state))
+    up_state = (up_done,) + up_state[1:]
+    branch_out = lax.psum_scatter(after(out_all, sent), "expert", scatter_dimension=0, tiled=True)
+    grad_branch, grad_resid, out_mine, out_other = turn(
+        expert_count, order, *last, sent, sent_rows, gates, resid, out_cotangent, attended, gain_two, router
+    )
+    grad_branch, up_state, out_other = lax.optimization_barrier((grad_branch, up_state, out_other))
+    gate_state, up_state = reduce_second(gate_state), reduce_second(up_state)
+    out_sent = swap_core(out_other)
+    backward = lambda call, branch, *more: attend_back(
+        call, branch, hidden_one, proj, mixer_p, order, groups[call],
+        query, keys, values, log_total, cosine, sine, bias, *more,
+    )
+    wide, other, part = backward(0, grad_branch)
+    grad_branch, wide, other, part, out_mine, out_sent, gate_state, up_state = lax.optimization_barrier(
+        (grad_branch, wide, other, part, out_mine, out_sent, gate_state, up_state)
+    )
+    state_one = fold(wide, swap_core(other), out_mine, out_sent)
+    grad_branch, folded = lax.optimization_barrier((grad_branch, state_one[0]))
+    state_one = (folded,) + state_one[1:]
+    wide, other, grad_input = backward(1, grad_branch, part, layer_input, grad_resid, gain_one)
+    wide, other, grad_input, state_one, all_mid = lax.optimization_barrier(
+        (wide, other, grad_input, state_one, all_mid)
+    )
+    state_one = reduce_second(state_one)
+    sent = swap_core(other)
+    down_state = grad_exchange(all_mid, cots, order, False)
+    kernel_done, state_one, sent, gate_state, up_state = lax.optimization_barrier(
+        (down_state[0], state_one, sent, gate_state, up_state)
+    )
+    down_state = (kernel_done,) + down_state[1:]
+    one = reduce_last(state_one)
+    wide, one = lax.optimization_barrier((wide, one))
+    state_two = fold(wide, sent)
+    state_two = reduce_second(state_two)
+    two = reduce_last(state_two)
+    two, down_state = lax.optimization_barrier((two, down_state))
+    down_state = reduce_second(down_state)
+    one = reduce_chips(one)
+    two = reduce_chips(two)
+    grad_gate = reduce_last(gate_state, jnp.float32)
+    grad_up = reduce_last(up_state, jnp.float32)
     grad_down = reduce_last(down_state, jnp.float32)
-    output = (resid + after(branch_out, wide_down).astype(jnp.float32)).astype(low)
-    grad_gain_one = jnp.sum(grad_hidden_one * normed_one, axis=0)
-    grad_normed_one = grad_hidden_one * gain_one
-    grad_input = grad_resid + scale_one * (
-        grad_normed_one - normed_one * jnp.mean(grad_normed_one * normed_one, axis=1, keepdims=True)
-    )
-    last_small = small_sum(grad_gain_one[None].astype(low))
-    ordered = []
-    for mine, other in finals:
-        ordered.append(jnp.where(core == 0, mine, other))
-        ordered.append(jnp.where(core == 0, other, mine))
-    grad_mixer = jnp.concatenate(
-        [g[:, :384] for g in ordered] + [g[:, 384:512] for g in ordered] + [g[:, 512:] for g in ordered],
-        axis=1,
-    ).astype(jnp.float32)
+    output = (resid + branch_out.astype(jnp.float32)).astype(low)
+    two, output, grad_gate, grad_up = lax.optimization_barrier((two, output, grad_gate, grad_up))
+    grad_mixer, grad_projector, grad_router, grad_gain_two, grad_gain_one = finish(
+        expert_count, order, (one, swap_core(one)), (two, swap_core(two))
+    )
     return (
         output,
-        grad_input.astype(low),
-        last_small[0],
+        grad_input,
+        grad_gain_one[0],
         grad_mixer,
         grad_projector,
-        first_small[expert_count],
-        first_small[:expert_count].T,
+        grad_gain_two[0],
+        grad_router.T,
         grad_gate,
         grad_up,
         grad_down,

time: 733 us -> 651 us (0.89)
  waiting for transfers between devices: 231 us -> 170 us
  local copies, waits for them, and re-layouts: 41.6 us -> 28.4 us
  Pallas kernels: 307 us -> 318 us
  other arithmetic: 60.9 us -> 50.1 us
  matrix products: 9.28 us -> 0 us
    pallas_call x7 -> x12, Pallas kernels: 192 us -> 236 us  [the longest x4 127 us: expert_chunk(): pl.pallas_call(lambda *refs: expert_kernel((len(gates), more), expert_cou...]
    pallas_call x2, Pallas kernels: 49.7 us -> 25 us  [attend(): pl.pallas_call(lambda *refs: attend_kernel(len(mixer_p) // 2, call, *refs...]
    ppermute x10 -> x8, waiting for transfers between devices: 68.3 us -> 44.7 us  [reduce_chips(): lax.ppermute(v, 'expert', [(i, i ^ mask) for i in range(count)])]
    ppermute x43, waiting for transfers between devices: 108 us -> 88.6 us  [across(): return lax.ppermute(value, 'shard', [(i, i ^ mask) for i in range(4)])]
    slice x12 -> x0, local copies, waits for them, and re-layouts: 15.7 us -> none  [the longest x1 4.9 us: reduce_first(): from_y = across(jnp.concatenate([far[half:], above[half:]]), 2)]
    ppermute x6, waiting for transfers between devices: 36.5 us -> 21.3 us  [next_chip(): lax.ppermute(value, 'expert', [(i, (i + 2) % count) for i in range(count)])]
    unnamed x178 -> x186, local copies, waits for them, and re-layouts: 9.64 us -> 20.7 us
    convert_element_type x10 -> x4, other arithmetic: 16.7 us -> 5.98 us  [the longest x1 3.11 us: per_device(): output = (resid + branch_out.astype(jnp.float32)).astype(low)]
  transfers between devices with their start and end apart: 85 -> 80, of which waited for: 37 -> 34; matrix products, arithmetic and copies ran while one was open for 11% -> 9% of each run, Pallas kernels for 42% -> 48%
where the time goes in v2:
time: 651 us; the launch traced here: 646 us
  Pallas kernels  318 us (49%)
  waiting for transfers between devices  170 us (26%)
  starting transfers between devices  64.4 us (10%)
  other arithmetic  50.1 us (8%)
  local copies, waits for them, and re-layouts  28.4 us (4%)
  between operations  15.8 us (2%)
    pallas_call x4, Pallas kernels, expert_chunk(): pl.pallas_call(lambda *refs: expert_kernel((len(gates), more), expert_cou...  127 us
    ppermute x43, waiting for transfers between devices, across(): return lax.ppermute(value, 'shard', [(i, i ^ mask) for i in range(4)])  88.6 us
    pallas_call x3, Pallas kernels, grad_exchange(): pl.pallas_call(lambda *refs: sorted_grad_kernel(on_rows, half, *refs), gr...  62.5 us
    pallas_call x2, Pallas kernels, attend_back(): pl.pallas_call(lambda *refs: attend_back_kernel(mine, (len(proj), len(mix...  56.9 us
    ppermute x43, starting transfers between devices, across(): return lax.ppermute(value, 'shard', [(i, i ^ mask) for i in range(4)])  49.1 us
    ppermute x8, waiting for transfers between devices, reduce_chips(): lax.ppermute(v, 'expert', [(i, i ^ mask) for i in range(count)])  44.7 us
    pallas_call x2, Pallas kernels, attend(): pl.pallas_call(lambda *refs: attend_kernel(len(mixer_p) // 2, call, *refs...  25 us
    ppermute x6, waiting for transfers between devices, next_chip(): lax.ppermute(value, 'expert', [(i, (i + 2) % count) for i in range(count)])  21.3 us
  transfers between devices with their start and end apart: 80, of which 34 were waited for; matrix products, arithmetic and copies ran while one was open for 9% of the time, Pallas kernels for 48%

profile of v2, /device:TPU:0, one launch (start us, length us, event | category | flops | bytes accessed | tf_op | source)
XLA Modules:
  0.0 646.5 jit_solution(8812882899041431100)
XLA Ops:
  8.0 1.7 slice_dynamic-update-slice_fusion.1
  15.3 1.7 slice_dynamic-update-slice_fusion.8
  17.0 2.4 broadcast_select_fusion
  19.3 3.0 collective-permute-start
  24.6 2.0 collective-permute-start.3
  31.3 2.1 broadcast_in_dim.111
  36.1 10.3 %collective-permute-done.2 = bf16[18,384]{1,0:T(8,128)(2,1)} collective-permute-done((bf16[18,384]{1,0:T(8,128)(2,1)}, bf16[18,384]{1,0:T(8,128)(2,1)}, u32[]{:S(2)}, u32[]{:S(2)}) %collective-permute-start.2) | collective-permute-done | bytes 13856 | tf_op jit(solution)/shard_map/ppermute | solution.py:71
  48.2 2.2 fusion.2.refs_2_.refs_3_
  55.3 11.3 %collective-permute-done.5.refs_9_.refs_22_ = bf16[1,192,1280]{2,1,0:T(8,128)(2,1)} collective-permute-done((bf16[1,192,1280]{2,1,0:T(8,128)(2,1)S(1)}, bf16[1,192,1280]{2,1,0:T(8,128)(2,1)}, u32[]{:S(2)}, u32[]{:S(2)}) %collective-permute-start.5) | collective-permute-done | bytes 491552 | tf_op jit(solution)/shard_map/ppermute | solution.py:71
  73.8 12.3 %attend.2 = (bf16[512,1536]{1,0:T(8,128)(2,1)}, bf16[512,1536]{1,0:T(8,128)(2,1)}, bf16[512,512]{1,0:T(8,128)(2,1)}, bf16[512,512]{1,0:T(8,128)(2,1)}, f32[4,512,8]{2,1,0:T(8,128)}) custom-call(s32[6]{0:T(128)S(1)} %stack.130.refs_0_.refs_1_.order_ref, s32[2]{0:T(128)S(1)} %pad_add_fusion.1.refs_1_.refs_0_, bf16[512,1536]{1,0:T(8,128)(2,1)S(1)} %copy-done.6, ...), custom_call_target="tpu_custom_call" | custom-call | flops 48000000000 | bytes 8000000 | tf_op jit(solution)/shard_map/attend/pallas_call | solution.py:264
  88.8 1.6 collective-permute-start.15
  90.8 12.7 %attend.3 = (bf16[512,1536]{1,0:T(8,128)(2,1)}, bf16[512,1536]{1,0:T(8,128)(2,1)}, bf16[512,512]{1,0:T(8,128)(2,1)}, bf16[512,512]{1,0:T(8,128)(2,1)}, f32[4,512,8]{2,1,0:T(8,128)}) custom-call(s32[6]{0:T(128)S(1)} %stack.130.refs_0_.refs_1_.order_ref, ...), custom_call_target="tpu_custom_call", output_to_operand_aliasing={{0}: (16, {}), {1}: (17, {}), {2}: (18, {}), {3}: (19, {}),... | custom-call | flops 48000000000 | bytes 8000000 | tf_op jit(solution)/shard_map/attend/pallas_call | solution.py:264
  103.5 8.5 %collective-permute-done.14.refs_9_.refs_14_ = bf16[1,96,1536]{2,1,0:T(8,128)(2,1)S(1)} collective-permute-done((bf16[1,96,1536]{2,1,0:T(8,128)(2,1)S(1)}, bf16[1,96,1536]{2,1,0:T(8,128)(2,1)S(1)}, u32[]{:S(2)}, u32[]{:S(2)}) %collective-permute-start.14) | collective-permute-done | bytes 294944 | tf_op jit(solution)/shard_map/ppermute | solution.py:71
  113.0 1.6 collective-permute-start.19
  116.6 7.9 %project.1 = (f32[512,1536]{1,0:T(8,128)S(1)}, f32[512,128]{1,0:T(8,128)S(1)}, bf16[528,1536]{1,0:T(8,128)(2,1)}) custom-call(s32[6]{0:T(128)S(1)} %stack.130.refs_0_.refs_1_.order_ref, bf16[512,1536]{1,0:T(8,128)(2,1)S(1)} %copy-done.28, bf16[512,1536]{1,0:T(8,128)(2,1)S(1)} %copy-done.2, s32[512,8]{1,0:T(8,128)S(1)} %copy.39.refs_3_, ...), custom_call_target="tpu_custom_call" | custom-call | flops 30000001024 | bytes 8000000 | tf_op jit(solution)/shard_map/project/pallas_call | solution.py:530
  124.6 8.0 %collective-permute-done.19 = bf16[2,384,512]{2,1,0:T(8,128)(2,1)S(1)} collective-permute-done((bf16[2,384,512]{2,1,0:T(8,128)(2,1)S(1)}, bf16[2,384,512]{2,1,0:T(8,128)(2,1)S(1)}, u32[]{:S(2)}, u32[]{:S(2)}) %collective-permute-start.19) | collective-permute-done | bytes 786464 | tf_op jit(solution)/shard_map/ppermute | solution.py:71
  133.8 1.6 collective-permute-start.23
  137.4 9.6 %collective-permute-done.25.refs_8_ = bf16[1,1,384,512]{3,2,1,0:T(8,128)(2,1)S(1)} collective-permute-done((bf16[1,1,384,512]{3,2,1,0:T(8,128)(2,1)S(1)}, bf16[1,1,384,512]{3,2,1,0:T(8,128)(2,1)S(1)}, u32[]{:S(2)}, u32[]{:S(2)}) %collective-permute-start.25) | collective-permute-done | bytes 393248 | tf_op jit(solution)/shard_map/ppermute | solution.py:71
  150.8 15.4 %collective-permute-done.30 = bf16[2,512,384]{2,1,0:T(8,128)(2,1)S(1)} collective-permute-done((bf16[2,512,384]{2,1,0:T(8,128)(2,1)S(1)}, bf16[2,512,384]{2,1,0:T(8,128)(2,1)S(1)}, u32[]{:S(2)}, u32[]{:S(2)}) %collective-permute-start.30) | collective-permute-done | bytes 786464 | tf_op jit(solution)/shard_map/ppermute | solution.py:71
  167.6 1.6 collective-permute-done.29
  169.9 2.2 collective-permute-done.23.refs_2_
  175.5 2.2 collective-permute-done.27.refs_13_
  177.7 6.5 %collective-permute-done.31.refs_18_ = bf16[1,1,512,384]{3,2,1,0:T(8,128)(2,1)} collective-permute-done((bf16[1,1,512,384]{3,2,1,0:T(8,128)(2,1)S(1)}, bf16[1,1,512,384]{3,2,1,0:T(8,128)(2,1)}, u32[]{:S(2)}, u32[]{:S(2)}) %collective-permute-start.31) | collective-permute-done | bytes 393248 | tf_op jit(solution)/shard_map/ppermute | solution.py:71
  184.3 31.7 %expert_chunk.4 = (bf16[528,1536]{1,0:T(8,128)(2,1)}, bf16[528,1536]{1,0:T(8,128)(2,1)}, bf16[4096,1536]{1,0:T(8,128)(2,1)}, bf16[4096,1536]{1,0:T(8,128)(2,1)},...) custom-call(s32[6]{0:T(128)} %copy-done.18, s32[3]{0:T(128)} %get-tuple-element.516.refs_1_, ...), custom_call_target="tpu_custom_call" | custom-call | flops 80999997440 | bytes 8000000 | tf_op jit(solution)/shard_map/expert_chunk/pallas_call | solution.py:844
  217.6 32.1 %expert_chunk.5 = (bf16[528,1536]{1,0:T(8,128)(2,1)}, bf16[528,1536]{1,0:T(8,128)(2,1)}, bf16[4096,1536]{1,0:T(8,128)(2,1)}, bf16[4096,1536]{1,0:T(8,128)(2,1)},...) custom-call(s32[6]{0:T(128)} %copy-done.18, ...), custom_call_target="tpu_custom_call", output_to_operand_aliasing={{2}: (20, {}), {3}: (21, {}), {4}: (22, {}), {5}: (23, {})} | custom-call | flops 80999997440 | bytes 8000000 | tf_op jit(solution)/shard_map/expert_chunk/pallas_call | solution.py:844
  249.7 4.1 collective-permute-done.36.refs_2_
  255.1 4.1 collective-permute-done.38
  259.2 1.8 add_convert_fusion.2
  261.1 31.7 %expert_chunk.6 = (bf16[528,1536]{1,0:T(8,128)(2,1)}, bf16[528,1536]{1,0:T(8,128)(2,1)}, bf16[4096,1536]{1,0:T(8,128)(2,1)}, bf16[4096,1536]{1,0:T(8,128)(2,1)},...) custom-call(s32[6]{0:T(128)} %copy-done.18, ...), custom_call_target="tpu_custom_call", output_to_operand_aliasing={{2}: (20, {}), {3}: (21, {}), {4}: (22, {}), {5}: (23, {})} | custom-call | flops 80999997440 | bytes 8000000 | tf_op jit(solution)/shard_map/expert_chunk/pallas_call | solution.py:844
  292.8 7.6 %collective-permute-done.40 = bf16[528,1536]{1,0:T(8,128)(2,1)S(1)} collective-permute-done((bf16[528,1536]{1,0:T(8,128)(2,1)S(1)}, bf16[528,1536]{1,0:T(8,128)(2,1)S(1)}, u32[]{:S(2)}, u32[]{:S(2)}) %collective-permute-start.40) | collective-permute-done | bytes 1622048 | tf_op jit(solution)/shard_map/ppermute | solution.py:67
  300.4 3.7 collective-permute-done.41
  304.0 2.0 add_convert_fusion.1
  306.1 31.9 %expert_chunk.7 = (bf16[528,1536]{1,0:T(8,128)(2,1)}, bf16[528,1536]{1,0:T(8,128)(2,1)}, bf16[4096,1536]{1,0:T(8,128)(2,1)}, bf16[4096,1536]{1,0:T(8,128)(2,1)},...) custom-call(s32[6]{0:T(128)} %copy-done.18, ...), custom_call_target="tpu_custom_call", output_to_operand_aliasing={{2}: (20, {}), {3}: (21, {}), {4}: (22, {}), {5}: (23, {})} | custom-call | flops 80999997440 | bytes 8000000 | tf_op jit(solution)/shard_map/expert_chunk/pallas_call | solution.py:844
  338.0 7.4 %collective-permute-done.42 = bf16[528,1536]{1,0:T(8,128)(2,1)S(1)} collective-permute-done((bf16[528,1536]{1,0:T(8,128)(2,1)S(1)}, bf16[528,1536]{1,0:T(8,128)(2,1)S(1)}, u32[]{:S(2)}, u32[]{:S(2)}) %collective-permute-start.42) | collective-permute-done | bytes 1622048 | tf_op jit(solution)/shard_map/ppermute | solution.py:67
  345.9 3.2 collective-permute-done.43
  349.1 2.0 add_convert_fusion
  351.2 20.4 %weight_grad.3 = (bf16[2,384,512]{2,1,0:T(8,128)(2,1)S(1)}, bf16[1,384,512]{2,1,0:T(8,128)(2,1)S(1)}, bf16[1,384,512]{2,1,0:T(8,128)(2,1)S(1)}, bf16[2,1,384,512...) custom-call(s32[6]{0:T(128)S(1)} %copy-done.19, bf16[4096,1536]{1,0:T(8,128)(2,1)} %get-tuple-element.352.refs_1_, ...), custom_call_target="tpu_custom_call" | custom-call | flops 60000002048 | bytes 8000000 | tf_op jit(solution)/shard_map/weight_grad/pallas_call | solution.py:972
  373.6 20.4 %weight_grad.4 = (bf16[2,384,512]{2,1,0:T(8,128)(2,1)S(1)}, bf16[1,384,512]{2,1,0:T(8,128)(2,1)S(1)}, bf16[1,384,512]{2,1,0:T(8,128)(2,1)S(1)}, bf16[2,1,384,512...) custom-call(s32[6]{0:T(128)S(1)} %copy-done.19, bf16[4096,1536]{1,0:T(8,128)(2,1)} %get-tuple-element.352.refs_1_, ...), custom_call_target="tpu_custom_call" | custom-call | flops 60000002048 | bytes 8000000 | tf_op jit(solution)/shard_map/weight_grad/pallas_call | solution.py:972
  397.9 14.6 %turn.1 = (bf16[512,1536]{1,0:T(8,128)(2,1)}, f32[512,1536]{1,0:T(8,128)}, bf16[1536,896]{1,0:T(8,128)(2,1)}, bf16[1536,896]{1,0:T(8,128)(2,1)}) custom-call(s32[6]{0:T(128)} %copy-done.18, bf16[528,1536]{1,0:T(8,128)(2,1)} %get-tuple-element.298.refs_1_, bf16[528,1536]{1,0:T(8,128)(2,1)} %copy-done.74, bf16[528,1536]{1,0:T(8,128)(2,1)} %copy-done.75, ...), custom_call_target="tpu_custom_call" | custom-call | flops 30000001024 | bytes 8000000 | tf_op jit(solution)/shard_map/turn/pallas_call | solution.py:606
  417.8 1.8 add_convert_fusion.10
  420.9 1.8 add_convert_fusion.9
  423.3 26.2 %attend_back.2 = (bf16[1536,640]{1,0:T(8,128)(2,1)}, bf16[1536,640]{1,0:T(8,128)(2,1)}, f32[512,1536]{1,0:T(8,128)}) custom-call(s32[2]{0:T(128)} %copy-done.27, s32[6]{0:T(128)} %copy-done.18, bf16[512,1536]{1,0:T(8,128)(2,1)} %get-tuple-element.395.refs_2_, bf16[512,1536]{1,0:T(8,128)(2,1)} %fusion.2.refs_2_.refs_3_, ...), custom_call_target="tpu_custom_call" | custom-call | flops 60000002048 | bytes 8000000 | tf_op jit(solution)/shard_map/attend_back/pallas_call | solution.py:428
  451.2 3.6 collective-permute-done.54.refs_2_
  456.1 10.0 %fold.2 = (bf16[384,1536]{1,0:T(8,128)(2,1)}, bf16[384,1536]{1,0:T(8,128)(2,1)}, bf16[384,1536]{1,0:T(8,128)(2,1)}, bf16[192,1536]{1,0:T(8,128)(2,1)}, bf16[192,1536]{1,0:T(8,128)(2,1)}) custom-call(s32[8]{0:T(128)} %stack.121.refs_0_, bf16[1536,640]{1,0:T(8,128)(2,1)} %get-tuple-element.390.refs_1_, bf16[1536,640]{1,0:T(8,128)(2,1)} %copy-done.34, ...), custom_call_target="tpu_custom_call" | custom-call | flops 1000000000 | bytes 4000000 | tf_op jit(solution)/shard_map/fold/pallas_call | solution.py:661
  468.4 30.7 %attend_back.3 = (bf16[1536,768]{1,0:T(8,128)(2,1)}, bf16[1536,768]{1,0:T(8,128)(2,1)}, bf16[512,1536]{1,0:T(8,128)(2,1)}) custom-call(s32[2]{0:T(128)} %copy-done.26, s32[6]{0:T(128)} %copy-done.18, bf16[512,1536]{1,0:T(8,128)(2,1)} %get-tuple-element.395.refs_2_, bf16[512,1536]{1,0:T(8,128)(2,1)} %fusion.2.refs_2_.refs_3_, ...), custom_call_target="tpu_custom_call" | custom-call | flops 60000002048 | bytes 8000000 | tf_op jit(solution)/shard_map/attend_back/pallas_call | solution.py:428
  501.5 21.8 %weight_grad.5 = (bf16[2,512,384]{2,1,0:T(8,128)(2,1)S(1)}, bf16[1,512,384]{2,1,0:T(8,128)(2,1)S(1)}, bf16[1,512,384]{2,1,0:T(8,128)(2,1)S(1)}, bf16[2,1,512,384...) custom-call(s32[6]{0:T(128)S(1)} %copy-done.20, bf16[2,4096,512]{2,1,0:T(8,128)(2,1)} %get-tuple-element.408.refs_1_, ...), custom_call_target="tpu_custom_call" | custom-call | flops 60000002048 | bytes 8000000 | tf_op jit(solution)/shard_map/weight_grad/pallas_call | solution.py:972
  528.9 7.7 %fold.3 = (bf16[384,768]{1,0:T(8,128)(2,1)}, bf16[384,768]{1,0:T(8,128)(2,1)}, bf16[384,768]{1,0:T(8,128)(2,1)}, bf16[192,768]{1,0:T(8,128)(2,1)}, bf16[192,768]{1,0:T(8,128)(2,1)}) custom-call(s32[8]{0:T(128)} %stack.121.refs_0_, bf16[1536,768]{1,0:T(8,128)(2,1)} %get-tuple-element.431.refs_1_, bf16[1536,768]{1,0:T(8,128)(2,1)} %copy-done.33), custom_call_target="tpu_custom_call" | custom-call | flops 1000000000 | bytes 4000000 | tf_op jit(solution)/shard_map/fold/pallas_call | solution.py:661
  541.5 1.6 fusion.12
  547.0 9.3 %collective-permute-done.60 = bf16[384,768]{1,0:T(8,128)(2,1)S(1)} collective-permute-done((bf16[384,768]{1,0:T(8,128)(2,1)S(1)}, bf16[384,768]{1,0:T(8,128)(2,1)S(1)}, u32[]{:S(2)}, u32[]{:S(2)}) %collective-permute-start.60) | collective-permute-done | bytes 589856 | tf_op jit(solution)/shard_map/ppermute | solution.py:71
  558.6 4.3 collective-permute-done.70
  563.1 2.1 collective-permute-start.71
  566.7 11.8 %collective-permute-done.71 = bf16[96,1536]{1,0:T(8,128)(2,1)S(1)} collective-permute-done((bf16[96,1536]{1,0:T(8,128)(2,1)S(1)}, bf16[96,1536]{1,0:T(8,128)(2,1)S(1)}, u32[]{:S(2)}, u32[]{:S(2)}) %collective-permute-start.71) | collective-permute-done | bytes 294944 | tf_op jit(solution)/shard_map/ppermute | solution.py:160
  578.7 1.8 add_convert_fusion.8
  580.5 1.7 collective-permute-start.76
  582.3 3.0 collective-permute-start.67
  585.3 11.2 %collective-permute-done.72 = bf16[96,1536]{1,0:T(8,128)(2,1)S(1)} collective-permute-done((bf16[96,1536]{1,0:T(8,128)(2,1)S(1)}, bf16[96,1536]{1,0:T(8,128)(2,1)S(1)}, u32[]{:S(2)}, u32[]{:S(2)}) %collective-permute-start.72) | collective-permute-done | bytes 294944 | tf_op jit(solution)/shard_map/ppermute | solution.py:160
  596.8 2.9 collective-permute-done.67
  600.1 1.8 add_convert_fusion.7
  601.9 1.7 collective-permute-start.77
  603.6 9.3 %collective-permute-done.68 = bf16[96,768]{1,0:T(8,128)(2,1)S(1)} collective-permute-done((bf16[96,768]{1,0:T(8,128)(2,1)S(1)}, bf16[96,768]{1,0:T(8,128)(2,1)S(1)}, u32[]{:S(2)}, u32[]{:S(2)}) %collective-permute-start.68) | collective-permute-done | bytes 147488 | tf_op jit(solution)/shard_map/ppermute | solution.py:160
  612.9 3.7 collective-permute-start.69
  618.0 5.2 collective-permute-done.69
  624.2 3.1 add_convert_fusion.3
  631.1 5.8 finish.1
  (393 shorter events, 99.8 us)
Async XLA Ops:
  7.2 177.1 %all-gather.2.cloned.1.call-start = ((), (), s32[]{:S(2)}) async-start(), calls=%async_computation.1 | async-start | bytes 14155776 | tf_op jit(solution)/shard_map/all_gather | solution.py:1045
  7.9 616.3 %reduce-scatter.2.cloned.1.call-start = ((), (), s32[]{:S(2)}) async-start(), calls=%async_computation.2 | async-start | bytes 14155776 | tf_op jit(solution)/shard_map/reduce_scatter | solution.py:1104
  19.3 31.1 %collective-permute-start = (bf16[384,1280]{1,0:T(8,128)(2,1)}, bf16[384,1280]{1,0:T(8,128)(2,1)}, u32[]{:S(2)}, u32[]{:S(2)}) collective-permute-start(bf16[384,1280]{1,0:T(8,128)(2,1)} %broadcast_select_fusion), channel_id=1, source_target_pairs={{0,1},{1,0},{2,3},{3,2},{4,5},{5,4},{6,7},{7,6},{8,9},{9,8},{10,11... | collective-permute-start | bytes 2949128 | tf_op jit(solution)/shard_map/ppermute | solution.py:71
  22.4 28.1 %collective-permute-start.1 = (bf16[384,1280]{1,0:T(8,128)(2,1)}, bf16[384,1280]{1,0:T(8,128)(2,1)}, u32[]{:S(2)}, u32[]{:S(2)}) collective-permute-start(bf16[384,1280]{1,0:T(8,128)(2,1)} %broadcast_select_fusion), channel_id=1, source_target_pairs={{0,2},{1,3},{2,0},{3,1},{4,6},{5,7},{6,4},{7,5},{8,10},{9,11},{10,... | collective-permute-start | bytes 2949128 | tf_op jit(solution)/shard_map/ppermute | solution.py:71
  24.6 21.8 %collective-permute-start.2 = (bf16[18,384]{1,0:T(8,128)(2,1)}, bf16[18,384]{1,0:T(8,128)(2,1)}, u32[]{:S(2)}, u32[]{:S(2)}) collective-permute-start(bf16[18,384]{1,0:T(8,128)(2,1)} %maximum_bitcast_fusion), channel_id=1, source_target_pairs={{0,3},{1,2},{2,1},{3,0},{4,7},{5,6},{6,5},{7,4},{8,11},{9,10},{10,... | collective-permute-start | bytes 41480 | tf_op jit(solution)/shard_map/ppermute | solution.py:71
  24.6 22.1 %collective-permute-start.3 = (bf16[18,384]{1,0:T(8,128)(2,1)}, bf16[18,384]{1,0:T(8,128)(2,1)}, u32[]{:S(2)}, u32[]{:S(2)}) collective-permute-start(bf16[18,384]{1,0:T(8,128)(2,1)} %maximum_bitcast_fusion), channel_id=1, source_target_pairs={{0,2},{1,3},{2,0},{3,1},{4,6},{5,7},{6,4},{7,5},{8,10},{9,11},{10,... | collective-permute-start | bytes 41480 | tf_op jit(solution)/shard_map/ppermute | solution.py:71
  26.6 20.1 %collective-permute-start.4 = (bf16[18,384]{1,0:T(8,128)(2,1)}, bf16[18,384]{1,0:T(8,128)(2,1)}, u32[]{:S(2)}, u32[]{:S(2)}) collective-permute-start(bf16[18,384]{1,0:T(8,128)(2,1)} %maximum_bitcast_fusion), channel_id=1, source_target_pairs={{0,1},{1,0},{2,3},{3,2},{4,5},{5,4},{6,7},{7,6},{8,9},{9,8},{10,11... | collective-permute-start | bytes 41480 | tf_op jit(solution)/shard_map/ppermute | solution.py:71
  51.5 16.9 %collective-permute-start.9 = (bf16[1,384,1280]{2,1,0:T(8,128)(2,1)}, bf16[1,384,1280]{2,1,0:T(8,128)(2,1)}, u32[]{:S(2)}, u32[]{:S(2)}) collective-permute-start(bf16[1,384,1280]{2,1,0:T(8,128)(2,1)} %broadcast_select_fusion.1.refs_6_.refs_19_), channel_id=1, source_target_pairs={{0,4},{4,0},{8,12},{12,8},{16,20},{20,16},{24,28},{28,24},{1,5},{5... | collective-permute-start | bytes 2949128 | tf_op jit(solution)/shard_map/ppermute | solution.py:62
  51.6 17.9 %collective-permute-start.10 = (bf16[1,384,1280]{2,1,0:T(8,128)(2,1)}, bf16[1,384,1280]{2,1,0:T(8,128)(2,1)}, u32[]{:S(2)}, u32[]{:S(2)}) collective-permute-start(bf16[1,384,1280]{2,1,0:T(8,128)(2,1)} %bitcast.30.refs_7_.refs_20_), channel_id=1, source_target_pairs={{0,4},{4,0},{8,12},{12,8},{16,20},{20,16},{24,28},{28,24},{1,5},{5... | collective-permute-start | bytes 2949128 | tf_op jit(solution)/shard_map/ppermute | solution.py:62
  53.2 13.4 %collective-permute-start.5 = (bf16[1,192,1280]{2,1,0:T(8,128)(2,1)S(1)}, bf16[1,192,1280]{2,1,0:T(8,128)(2,1)}, u32[]{:S(2)}, u32[]{:S(2)}) collective-permute-start(bf16[1,192,1280]{2,1,0:T(8,128)(2,1)S(1)} %slice.240), channel_id=1, source_target_pairs={{0,1},{1,0},{2,3},{3,2},{4,5},{5,4},{6,7},{7,6},{8,9},{9,8},{10,11... | collective-permute-start | bytes 1474568 | tf_op jit(solution)/shard_map/ppermute | solution.py:71
  54.3 16.8 %collective-permute-start.11 = (bf16[1,384,1280]{2,1,0:T(8,128)(2,1)}, bf16[1,384,1280]{2,1,0:T(8,128)(2,1)}, u32[]{:S(2)}, u32[]{:S(2)}) collective-permute-start(bf16[1,384,1280]{2,1,0:T(8,128)(2,1)} %bitcast.31.refs_8_.refs_21_), channel_id=1, source_target_pairs={{0,4},{4,0},{8,12},{12,8},{16,20},{20,16},{24,28},{28,24},{1,5},{5... | collective-permute-start | bytes 2949128 | tf_op jit(solution)/shard_map/ppermute | solution.py:62
  54.3 13.7 %collective-permute-start.6 = (bf16[1,192,1280]{2,1,0:T(8,128)(2,1)S(1)}, bf16[1,192,1280]{2,1,0:T(8,128)(2,1)}, u32[]{:S(2)}, u32[]{:S(2)}) collective-permute-start(bf16[1,192,1280]{2,1,0:T(8,128)(2,1)S(1)} %slice.241), channel_id=1, source_target_pairs={{0,2},{1,3},{2,0},{3,1},{4,6},{5,7},{6,4},{7,5},{8,10},{9,11},{10,... | collective-permute-start | bytes 1474568 | tf_op jit(solution)/shard_map/ppermute | solution.py:71
  68.5 17.7 %collective-permute-start.7 = (bf16[192,1536]{1,0:T(8,128)(2,1)S(1)}, bf16[192,1536]{1,0:T(8,128)(2,1)S(1)}, u32[]{:S(2)}, u32[]{:S(2)}) collective-permute-start(bf16[192,1536]{1,0:T(8,128)(2,1)S(1)} %constant_dynamic-slice_fusion), channel_id=1, source_target_pairs={{0,1},{1,0},{2,3},{3,2},{4,5},{5,4},{6,7},{7,6},{8,9},{9,8},{10,11... | collective-permute-start | bytes 1769480 | tf_op jit(solution)/shard_map/ppermute | solution.py:71
  69.6 16.6 %collective-permute-start.8 = (bf16[192,1536]{1,0:T(8,128)(2,1)S(1)}, bf16[192,1536]{1,0:T(8,128)(2,1)S(1)}, u32[]{:S(2)}, u32[]{:S(2)}) collective-permute-start(bf16[192,1536]{1,0:T(8,128)(2,1)S(1)} %constant_dynamic-slice_fusion), channel_id=1, source_target_pairs={{0,2},{1,3},{2,0},{3,1},{4,6},{5,7},{6,4},{7,5},{8,10},{9,11},{10,... | collective-permute-start | bytes 1769480 | tf_op jit(solution)/shard_map/ppermute | solution.py:71
  86.3 26.0 %collective-permute-start.17 = (bf16[2,384,512]{2,1,0:T(8,128)(2,1)S(1)}, bf16[2,384,512]{2,1,0:T(8,128)(2,1)S(1)}, u32[]{:S(2)}, u32[]{:S(2)}) collective-permute-start(bf16[2,384,512]{2,1,0:T(8,128)(2,1)S(1)} %copy-done.77), channel_id=1, source_target_pairs={{0,1},{1,0},{2,3},{3,2},{4,5},{5,4},{6,7},{7,6},{8,9},{9,8},{10,11... | collective-permute-start | bytes 2359304 | tf_op jit(solution)/shard_map/ppermute | solution.py:71
  86.8 25.4 %collective-permute-start.18 = (bf16[2,384,512]{2,1,0:T(8,128)(2,1)S(1)}, bf16[2,384,512]{2,1,0:T(8,128)(2,1)S(1)}, u32[]{:S(2)}, u32[]{:S(2)}) collective-permute-start(bf16[2,384,512]{2,1,0:T(8,128)(2,1)S(1)} %copy-done.77), channel_id=1, source_target_pairs={{0,2},{1,3},{2,0},{3,1},{4,6},{5,7},{6,4},{7,5},{8,10},{9,11},{10,... | collective-permute-start | bytes 2359304 | tf_op jit(solution)/shard_map/ppermute | solution.py:71
  88.0 24.0 %collective-permute-start.14 = (bf16[1,96,1536]{2,1,0:T(8,128)(2,1)S(1)}, bf16[1,96,1536]{2,1,0:T(8,128)(2,1)S(1)}, u32[]{:S(2)}, u32[]{:S(2)}) collective-permute-start(bf16[1,96,1536]{2,1,0:T(8,128)(2,1)S(1)} %slice.242), channel_id=1, source_target_pairs={{0,1},{1,0},{2,3},{3,2},{4,5},{5,4},{6,7},{7,6},{8,9},{9,8},{10,11... | collective-permute-start | bytes 884744 | tf_op jit(solution)/shard_map/ppermute | solution.py:71
  88.8 23.4 %collective-permute-start.15 = (bf16[1,96,1536]{2,1,0:T(8,128)(2,1)S(1)}, bf16[1,96,1536]{2,1,0:T(8,128)(2,1)S(1)}, u32[]{:S(2)}, u32[]{:S(2)}) collective-permute-start(bf16[1,96,1536]{2,1,0:T(8,128)(2,1)S(1)} %slice.243), channel_id=1, source_target_pairs={{0,2},{1,3},{2,0},{3,1},{4,6},{5,7},{6,4},{7,5},{8,10},{9,11},{10,... | collective-permute-start | bytes 884744 | tf_op jit(solution)/shard_map/ppermute | solution.py:71
  90.7 21.6 %collective-permute-start.16 = (bf16[3,192,1536]{2,1,0:T(8,128)(2,1)S(1)}, bf16[3,192,1536]{2,1,0:T(8,128)(2,1)S(1)}, u32[]{:S(2)}, u32[]{:S(2)}) collective-permute-start(bf16[3,192,1536]{2,1,0:T(8,128)(2,1)S(1)} %pad_maximum_fusion), channel_id=1, source_target_pairs={{0,4},{4,0},{8,12},{12,8},{16,20},{20,16},{24,28},{28,24},{1,5},{5... | collective-permute-start | bytes 5308424 | tf_op jit(solution)/shard_map/ppermute | solution.py:62
  113.0 19.6 %collective-permute-start.19 = (bf16[2,384,512]{2,1,0:T(8,128)(2,1)S(1)}, bf16[2,384,512]{2,1,0:T(8,128)(2,1)S(1)}, u32[]{:S(2)}, u32[]{:S(2)}) collective-permute-start(bf16[2,384,512]{2,1,0:T(8,128)(2,1)S(1)} %copy-done.78), channel_id=1, source_target_pairs={{0,1},{1,0},{2,3},{3,2},{4,5},{5,4},{6,7},{7,6},{8,9},{9,8},{10,11... | collective-permute-start | bytes 2359304 | tf_op jit(solution)/shard_map/ppermute | solution.py:71
  114.5 19.2 %collective-permute-start.20 = (bf16[2,384,512]{2,1,0:T(8,128)(2,1)S(1)}, bf16[2,384,512]{2,1,0:T(8,128)(2,1)S(1)}, u32[]{:S(2)}, u32[]{:S(2)}) collective-permute-start(bf16[2,384,512]{2,1,0:T(8,128)(2,1)S(1)} %copy-done.78), channel_id=1, source_target_pairs={{0,2},{1,3},{2,0},{3,1},{4,6},{5,7},{6,4},{7,5},{8,10},{9,11},{10,... | collective-permute-start | bytes 2359304 | tf_op jit(solution)/shard_map/ppermute | solution.py:71
  133.8 38.3 %collective-permute-start.23 = (bf16[528,1536]{1,0:T(8,128)(2,1)}, bf16[528,1536]{1,0:T(8,128)(2,1)S(1)}, u32[]{:S(2)}, u32[]{:S(2)}) collective-permute-start(bf16[528,1536]{1,0:T(8,128)(2,1)} %get-tuple-element.278.refs_2_.refs_4_), channel_id=1, source_target_pairs={{0,8},{4,12},{8,16},{12,20},{16,24},{20,28},{24,0},{28,4},{1,9},{5... | collective-permute-start | bytes 4866056 | tf_op jit(solution)/shard_map/ppermute | solution.py:67
  135.4 39.8 %collective-permute-start.24 = (bf16[528,1536]{1,0:T(8,128)(2,1)}, bf16[528,1536]{1,0:T(8,128)(2,1)}, u32[]{:S(2)}, u32[]{:S(2)}) collective-permute-start(bf16[528,1536]{1,0:T(8,128)(2,1)} %get-tuple-element.278.refs_2_.refs_4_), channel_id=1, source_target_pairs={{0,4},{4,0},{8,12},{12,8},{16,20},{20,16},{24,28},{28,24},{1,5},{5... | collective-permute-start | bytes 4866056 | tf_op jit(solution)/shard_map/ppermute | solution.py:62
  147.4 18.9 %collective-permute-start.30 = (bf16[2,512,384]{2,1,0:T(8,128)(2,1)S(1)}, bf16[2,512,384]{2,1,0:T(8,128)(2,1)S(1)}, u32[]{:S(2)}, u32[]{:S(2)}) collective-permute-start(bf16[2,512,384]{2,1,0:T(8,128)(2,1)S(1)} %copy-done.79), channel_id=1, source_target_pairs={{0,2},{1,3},{2,0},{3,1},{4,6},{5,7},{6,4},{7,5},{8,10},{9,11},{10,... | collective-permute-start | bytes 2359304 | tf_op jit(solution)/shard_map/ppermute | solution.py:71
  148.7 20.5 %collective-permute-start.29 = (bf16[2,512,384]{2,1,0:T(8,128)(2,1)S(1)}, bf16[2,512,384]{2,1,0:T(8,128)(2,1)S(1)}, u32[]{:S(2)}, u32[]{:S(2)}) collective-permute-start(bf16[2,512,384]{2,1,0:T(8,128)(2,1)S(1)} %copy-done.79), channel_id=1, source_target_pairs={{0,1},{1,0},{2,3},{3,2},{4,5},{5,4},{6,7},{7,6},{8,9},{9,8},{10,11... | collective-permute-start | bytes 2359304 | tf_op jit(solution)/shard_map/ppermute | solution.py:71
  149.4 28.3 %collective-permute-start.27 = (bf16[1,1,384,512]{3,2,1,0:T(8,128)(2,1)S(1)}, bf16[1,1,384,512]{3,2,1,0:T(8,128)(2,1)}, u32[]{:S(2)}, u32[]{:S(2)}) collective-permute-start(bf16[1,1,384,512]{3,2,1,0:T(8,128)(2,1)S(1)} %slice.248), channel_id=1, source_target_pairs={{0,1},{1,0},{2,3},{3,2},{4,5},{5,4},{6,7},{7,6},{8,9},{9,8},{10,11... | collective-permute-start | bytes 1179656 | tf_op jit(solution)/shard_map/ppermute | solution.py:71
  169.1 15.1 %collective-permute-start.31 = (bf16[1,1,512,384]{3,2,1,0:T(8,128)(2,1)S(1)}, bf16[1,1,512,384]{3,2,1,0:T(8,128)(2,1)}, u32[]{:S(2)}, u32[]{:S(2)}) collective-permute-start(bf16[1,1,512,384]{3,2,1,0:T(8,128)(2,1)S(1)} %slice.300), channel_id=1, source_target_pairs={{0,1},{1,0},{2,3},{3,2},{4,5},{5,4},{6,7},{7,6},{8,9},{9,8},{10,11... | collective-permute-start | bytes 1179656 | tf_op jit(solution)/shard_map/ppermute | solution.py:71
  175.1 41.0 %collective-permute-start.33 = (bf16[528,1536]{1,0:T(8,128)(2,1)}, bf16[528,1536]{1,0:T(8,128)(2,1)}, u32[]{:S(2)}, u32[]{:S(2)}) collective-permute-start(bf16[528,1536]{1,0:T(8,128)(2,1)} %copy-done.72), channel_id=1, source_target_pairs={{0,8},{4,12},{8,16},{12,20},{16,24},{20,28},{24,0},{28,4},{1,9},{5... | collective-permute-start | bytes 4866056 | tf_op jit(solution)/shard_map/ppermute | solution.py:67
  177.7 38.4 %collective-permute-start.34 = (bf16[528,1536]{1,0:T(8,128)(2,1)}, bf16[528,1536]{1,0:T(8,128)(2,1)}, u32[]{:S(2)}, u32[]{:S(2)}) collective-permute-start(bf16[528,1536]{1,0:T(8,128)(2,1)} %copy-done.72), channel_id=1, source_target_pairs={{0,4},{4,0},{8,12},{12,8},{16,20},{20,16},{24,28},{28,24},{1,5},{5... | collective-permute-start | bytes 4866056 | tf_op jit(solution)/shard_map/ppermute | solution.py:62
  216.1 37.8 %collective-permute-start.36 = (bf16[528,1536]{1,0:T(8,128)(2,1)}, bf16[528,1536]{1,0:T(8,128)(2,1)S(1)}, u32[]{:S(2)}, u32[]{:S(2)}) collective-permute-start(bf16[528,1536]{1,0:T(8,128)(2,1)} %collective-permute-done.33.refs_2_), channel_id=1, source_target_pairs={{0,8},{4,12},{8,16},{12,20},{16,24},{20,28},{24,0},{28,4},{1,9},{5... | collective-permute-start | bytes 4866056 | tf_op jit(solution)/shard_map/ppermute | solution.py:67
  217.6 36.3 %collective-permute-start.37 = (bf16[528,1536]{1,0:T(8,128)(2,1)}, bf16[528,1536]{1,0:T(8,128)(2,1)S(1)}, u32[]{:S(2)}, u32[]{:S(2)}) collective-permute-start(bf16[528,1536]{1,0:T(8,128)(2,1)} %collective-permute-done.33.refs_2_), channel_id=1, source_target_pairs={{0,4},{4,0},{8,12},{12,8},{16,20},{20,16},{24,28},{28,24},{1,5},{5... | collective-permute-start | bytes 4866056 | tf_op jit(solution)/shard_map/ppermute | solution.py:62
  253.9 38.8 %collective-permute-start.39 = (bf16[528,1536]{1,0:T(8,128)(2,1)S(1)}, bf16[528,1536]{1,0:T(8,128)(2,1)}, u32[]{:S(2)}, u32[]{:S(2)}) collective-permute-start(bf16[528,1536]{1,0:T(8,128)(2,1)S(1)} %collective-permute-done.36.refs_2_), channel_id=1, source_target_pairs={{0,4},{4,0},{8,12},{12,8},{16,20},{20,16},{24,28},{28,24},{1,5},{5... | collective-permute-start | bytes 4866056 | tf_op jit(solution)/shard_map/ppermute | solution.py:62
  261.0 39.3 %collective-permute-start.40 = (bf16[528,1536]{1,0:T(8,128)(2,1)S(1)}, bf16[528,1536]{1,0:T(8,128)(2,1)S(1)}, u32[]{:S(2)}, u32[]{:S(2)}) collective-permute-start(bf16[528,1536]{1,0:T(8,128)(2,1)S(1)} %add_convert_fusion.2), channel_id=1, source_target_pairs={{0,8},{4,12},{8,16},{12,20},{16,24},{20,28},{24,0},{28,4},{1,9},{5... | collective-permute-start | bytes 4866056 | tf_op jit(solution)/shard_map/ppermute | solution.py:67
  306.1 39.3 %collective-permute-start.42 = (bf16[528,1536]{1,0:T(8,128)(2,1)S(1)}, bf16[528,1536]{1,0:T(8,128)(2,1)S(1)}, u32[]{:S(2)}, u32[]{:S(2)}) collective-permute-start(bf16[528,1536]{1,0:T(8,128)(2,1)S(1)} %add_convert_fusion.1), channel_id=1, source_target_pairs={{0,8},{4,12},{8,16},{12,20},{16,24},{20,28},{24,0},{28,4},{1,9},{5... | collective-permute-start | bytes 4866056 | tf_op jit(solution)/shard_map/ppermute | solution.py:67
  345.4 50.8 %collective-permute-start.35 = (bf16[528,1536]{1,0:T(8,128)(2,1)}, bf16[528,1536]{1,0:T(8,128)(2,1)S(1)}, u32[]{:S(2)}, u32[]{:S(2)}) collective-permute-start(bf16[528,1536]{1,0:T(8,128)(2,1)} %get-tuple-element.299), channel_id=1, source_target_pairs={{0,4},{4,0},{8,12},{12,8},{16,20},{20,16},{24,28},{28,24},{1,5},{5... | collective-permute-start | bytes 4866056 | tf_op jit(solution)/shard_map/ppermute | solution.py:62
  351.1 45.0 %collective-permute-start.44 = (bf16[528,1536]{1,0:T(8,128)(2,1)S(1)}, bf16[528,1536]{1,0:T(8,128)(2,1)S(1)}, u32[]{:S(2)}, u32[]{:S(2)}) collective-permute-start(bf16[528,1536]{1,0:T(8,128)(2,1)S(1)} %add_convert_fusion), channel_id=1, source_target_pairs={{0,8},{4,12},{8,16},{12,20},{16,24},{20,28},{24,0},{28,4},{1,9},{5... | collective-permute-start | bytes 4866056 | tf_op jit(solution)/shard_map/ppermute | solution.py:67
  371.6 23.1 %collective-permute-start.45 = (bf16[2,384,512]{2,1,0:T(8,128)(2,1)S(1)}, bf16[2,384,512]{2,1,0:T(8,128)(2,1)S(1)}, u32[]{:S(2)}, u32[]{:S(2)}) collective-permute-start(bf16[2,384,512]{2,1,0:T(8,128)(2,1)S(1)} %bitcast.104), channel_id=1, source_target_pairs={{0,1},{1,0},{2,3},{3,2},{4,5},{5,4},{6,7},{7,6},{8,9},{9,8},{10,11... | collective-permute-start | bytes 2359304 | tf_op jit(solution)/shard_map/ppermute | solution.py:71
  372.4 23.7 %collective-permute-start.46 = (bf16[2,384,512]{2,1,0:T(8,128)(2,1)S(1)}, bf16[2,384,512]{2,1,0:T(8,128)(2,1)}, u32[]{:S(2)}, u32[]{:S(2)}) collective-permute-start(bf16[2,384,512]{2,1,0:T(8,128)(2,1)S(1)} %bitcast.103), channel_id=1, source_target_pairs={{0,2},{1,3},{2,0},{3,1},{4,6},{5,7},{6,4},{7,5},{8,10},{9,11},{10,... | collective-permute-start | bytes 2359304 | tf_op jit(solution)/shard_map/ppermute | solution.py:71
  394.0 19.2 %collective-permute-start.47 = (bf16[2,384,512]{2,1,0:T(8,128)(2,1)S(1)}, bf16[2,384,512]{2,1,0:T(8,128)(2,1)}, u32[]{:S(2)}, u32[]{:S(2)}) collective-permute-start(bf16[2,384,512]{2,1,0:T(8,128)(2,1)S(1)} %bitcast.102), channel_id=1, source_target_pairs={{0,1},{1,0},{2,3},{3,2},{4,5},{5,4},{6,7},{7,6},{8,9},{9,8},{10,11... | collective-permute-start | bytes 2359304 | tf_op jit(solution)/shard_map/ppermute | solution.py:71
  394.7 18.8 %collective-permute-start.48 = (bf16[2,384,512]{2,1,0:T(8,128)(2,1)S(1)}, bf16[2,384,512]{2,1,0:T(8,128)(2,1)}, u32[]{:S(2)}, u32[]{:S(2)}) collective-permute-start(bf16[2,384,512]{2,1,0:T(8,128)(2,1)S(1)} %bitcast.101), channel_id=1, source_target_pairs={{0,2},{1,3},{2,0},{3,1},{4,6},{5,7},{6,4},{7,5},{8,10},{9,11},{10,... | collective-permute-start | bytes 2359304 | tf_op jit(solution)/shard_map/ppermute | solution.py:71
  413.5 36.0 %collective-permute-start.49 = (bf16[1536,896]{1,0:T(8,128)(2,1)}, bf16[1536,896]{1,0:T(8,128)(2,1)}, u32[]{:S(2)}, u32[]{:S(2)}) collective-permute-start(bf16[1536,896]{1,0:T(8,128)(2,1)} %get-tuple-element.378), channel_id=1, source_target_pairs={{0,4},{4,0},{8,12},{12,8},{16,20},{20,16},{24,28},{28,24},{1,5},{5... | collective-permute-start | bytes 8257544 | tf_op jit(solution)/shard_map/ppermute | solution.py:62
  414.6 34.8 %collective-permute-start.50 = (bf16[1,384,512]{2,1,0:T(8,128)(2,1)S(1)}, bf16[1,384,512]{2,1,0:T(8,128)(2,1)S(1)}, u32[]{:S(2)}, u32[]{:S(2)}) collective-permute-start(bf16[1,384,512]{2,1,0:T(8,128)(2,1)S(1)} %add_convert_fusion.12), channel_id=1, source_target_pairs={{0,1},{1,0},{2,3},{3,2},{4,5},{5,4},{6,7},{7,6},{8,9},{9,8},{10,11... | collective-permute-start | bytes 1179656 | tf_op jit(solution)/shard_map/ppermute | solution.py:71
  416.9 32.5 %collective-permute-start.51 = (bf16[1,384,512]{2,1,0:T(8,128)(2,1)}, bf16[1,384,512]{2,1,0:T(8,128)(2,1)S(1)}, u32[]{:S(2)}, u32[]{:S(2)}) collective-permute-start(bf16[1,384,512]{2,1,0:T(8,128)(2,1)} %add_convert_fusion.11), channel_id=1, source_target_pairs={{0,2},{1,3},{2,0},{3,1},{4,6},{5,7},{6,4},{7,5},{8,10},{9,11},{10,... | collective-permute-start | bytes 1179656 | tf_op jit(solution)/shard_map/ppermute | solution.py:71
  419.6 29.9 %collective-permute-start.52 = (bf16[1,384,512]{2,1,0:T(8,128)(2,1)}, bf16[1,384,512]{2,1,0:T(8,128)(2,1)S(1)}, u32[]{:S(2)}, u32[]{:S(2)}) collective-permute-start(bf16[1,384,512]{2,1,0:T(8,128)(2,1)} %add_convert_fusion.10), channel_id=1, source_target_pairs={{0,1},{1,0},{2,3},{3,2},{4,5},{5,4},{6,7},{7,6},{8,9},{9,8},{10,11... | collective-permute-start | bytes 1179656 | tf_op jit(solution)/shard_map/ppermute | solution.py:71
  422.7 26.8 %collective-permute-start.53 = (bf16[1,384,512]{2,1,0:T(8,128)(2,1)}, bf16[1,384,512]{2,1,0:T(8,128)(2,1)S(1)}, u32[]{:S(2)}, u32[]{:S(2)}) collective-permute-start(bf16[1,384,512]{2,1,0:T(8,128)(2,1)} %add_convert_fusion.9), channel_id=1, source_target_pairs={{0,2},{1,3},{2,0},{3,1},{4,6},{5,7},{6,4},{7,5},{8,10},{9,11},{10,... | collective-permute-start | bytes 1179656 | tf_op jit(solution)/shard_map/ppermute | solution.py:71
  466.1 33.1 %collective-permute-start.55 = (bf16[384,1536]{1,0:T(8,128)(2,1)}, bf16[384,1536]{1,0:T(8,128)(2,1)S(1)}, u32[]{:S(2)}, u32[]{:S(2)}) collective-permute-start(bf16[384,1536]{1,0:T(8,128)(2,1)} %get-tuple-element.404), channel_id=1, source_target_pairs={{0,1},{1,0},{2,3},{3,2},{4,5},{5,4},{6,7},{7,6},{8,9},{9,8},{10,11... | collective-permute-start | bytes 3538952 | tf_op jit(solution)/shard_map/ppermute | solution.py:71
  467.5 31.7 %collective-permute-start.56 = (bf16[384,1536]{1,0:T(8,128)(2,1)}, bf16[384,1536]{1,0:T(8,128)(2,1)S(1)}, u32[]{:S(2)}, u32[]{:S(2)}) collective-permute-start(bf16[384,1536]{1,0:T(8,128)(2,1)} %get-tuple-element.405), channel_id=1, source_target_pairs={{0,2},{1,3},{2,0},{3,1},{4,6},{5,7},{6,4},{7,5},{8,10},{9,11},{10,... | collective-permute-start | bytes 3538952 | tf_op jit(solution)/shard_map/ppermute | solution.py:71
  499.4 26.2 %collective-permute-start.57 = (bf16[192,1536]{1,0:T(8,128)(2,1)S(1)}, bf16[192,1536]{1,0:T(8,128)(2,1)S(1)}, u32[]{:S(2)}, u32[]{:S(2)}) collective-permute-start(bf16[192,1536]{1,0:T(8,128)(2,1)S(1)} %add_convert_fusion.6), channel_id=1, source_target_pairs={{0,1},{1,0},{2,3},{3,2},{4,5},{5,4},{6,7},{7,6},{8,9},{9,8},{10,11... | collective-permute-start | bytes 1769480 | tf_op jit(solution)/shard_map/ppermute | solution.py:71
  500.7 24.8 %collective-permute-start.58 = (bf16[192,1536]{1,0:T(8,128)(2,1)S(1)}, bf16[192,1536]{1,0:T(8,128)(2,1)S(1)}, u32[]{:S(2)}, u32[]{:S(2)}) collective-permute-start(bf16[192,1536]{1,0:T(8,128)(2,1)S(1)} %add_convert_fusion.5), channel_id=1, source_target_pairs={{0,2},{1,3},{2,0},{3,1},{4,6},{5,7},{6,4},{7,5},{8,10},{9,11},{10,... | collective-permute-start | bytes 1769480 | tf_op jit(solution)/shard_map/ppermute | solution.py:71
  501.5 24.0 %collective-permute-start.59 = (bf16[1536,768]{1,0:T(8,128)(2,1)S(1)}, bf16[1536,768]{1,0:T(8,128)(2,1)S(1)}, u32[]{:S(2)}, u32[]{:S(2)}) collective-permute-start(bf16[1536,768]{1,0:T(8,128)(2,1)S(1)} %copy-done.71), channel_id=1, source_target_pairs={{0,4},{4,0},{8,12},{12,8},{16,20},{20,16},{24,28},{28,24},{1,5},{5... | collective-permute-start | bytes 7077896 | tf_op jit(solution)/shard_map/ppermute | solution.py:62
  523.3 43.2 %collective-permute-start.64 = (bf16[2,512,384]{2,1,0:T(8,128)(2,1)}, bf16[2,512,384]{2,1,0:T(8,128)(2,1)}, u32[]{:S(2)}, u32[]{:S(2)}) collective-permute-start(bf16[2,512,384]{2,1,0:T(8,128)(2,1)} %bitcast.58), channel_id=1, source_target_pairs={{0,1},{1,0},{2,3},{3,2},{4,5},{5,4},{6,7},{7,6},{8,9},{9,8},{10,11... | collective-permute-start | bytes 2359304 | tf_op jit(solution)/shard_map/ppermute | solution.py:71
  524.6 42.0 %collective-permute-start.65 = (bf16[2,512,384]{2,1,0:T(8,128)(2,1)S(1)}, bf16[2,512,384]{2,1,0:T(8,128)(2,1)}, u32[]{:S(2)}, u32[]{:S(2)}) collective-permute-start(bf16[2,512,384]{2,1,0:T(8,128)(2,1)S(1)} %bitcast.100), channel_id=1, source_target_pairs={{0,2},{1,3},{2,0},{3,1},{4,6},{5,7},{6,4},{7,5},{8,10},{9,11},{10,... | collective-permute-start | bytes 2359304 | tf_op jit(solution)/shard_map/ppermute | solution.py:71
  537.9 18.4 %collective-permute-start.60 = (bf16[384,768]{1,0:T(8,128)(2,1)S(1)}, bf16[384,768]{1,0:T(8,128)(2,1)S(1)}, u32[]{:S(2)}, u32[]{:S(2)}) collective-permute-start(bf16[384,768]{1,0:T(8,128)(2,1)S(1)} %copy-done.81), channel_id=1, source_target_pairs={{0,1},{1,0},{2,3},{3,2},{4,5},{5,4},{6,7},{7,6},{8,9},{9,8},{10,11... | collective-permute-start | bytes 1769480 | tf_op jit(solution)/shard_map/ppermute | solution.py:71
  539.1 18.6 %collective-permute-start.62 = (bf16[384,768]{1,0:T(8,128)(2,1)S(1)}, bf16[384,768]{1,0:T(8,128)(2,1)S(1)}, u32[]{:S(2)}, u32[]{:S(2)}) collective-permute-start(bf16[384,768]{1,0:T(8,128)(2,1)S(1)} %copy-done.80), channel_id=1, source_target_pairs={{0,2},{1,3},{2,0},{3,1},{4,6},{5,7},{6,4},{7,5},{8,10},{9,11},{10,... | collective-permute-start | bytes 1769480 | tf_op jit(solution)/shard_map/ppermute | solution.py:71
  541.4 21.4 %collective-permute-start.70 = (bf16[192,1536]{1,0:T(8,128)(2,1)S(1)}, bf16[192,1536]{1,0:T(8,128)(2,1)S(1)}, u32[]{:S(2)}, u32[]{:S(2)}) collective-permute-start(bf16[192,1536]{1,0:T(8,128)(2,1)S(1)} %broadcast_select_fusion.4), channel_id=1, source_target_pairs={{0,8},{4,12},{8,0},{12,4},{16,24},{20,28},{24,16},{28,20},{1,9},{5... | collective-permute-start | bytes 1769480 | tf_op jit(solution)/shard_map/ppermute | solution.py:160
  563.1 15.4 %collective-permute-start.71 = (bf16[96,1536]{1,0:T(8,128)(2,1)S(1)}, bf16[96,1536]{1,0:T(8,128)(2,1)S(1)}, u32[]{:S(2)}, u32[]{:S(2)}) collective-permute-start(bf16[96,1536]{1,0:T(8,128)(2,1)S(1)} %broadcast_select_fusion.7), channel_id=1, source_target_pairs={{0,16},{4,20},{8,24},{12,28},{16,0},{20,4},{24,8},{28,12},{1,17},{... | collective-permute-start | bytes 884744 | tf_op jit(solution)/shard_map/ppermute | solution.py:160
  566.6 15.6 %collective-permute-start.66 = (bf16[192,768]{1,0:T(8,128)(2,1)S(1)}, bf16[192,768]{1,0:T(8,128)(2,1)S(1)}, u32[]{:S(2)}, u32[]{:S(2)}) collective-permute-start(bf16[192,768]{1,0:T(8,128)(2,1)S(1)} %broadcast_select_fusion.10), channel_id=1, source_target_pairs={{0,8},{4,12},{8,0},{12,4},{16,24},{20,28},{24,16},{28,20},{1,9},{5... | collective-permute-start | bytes 884744 | tf_op jit(solution)/shard_map/ppermute | solution.py:160
  578.6 18.0 %collective-permute-start.72 = (bf16[96,1536]{1,0:T(8,128)(2,1)S(1)}, bf16[96,1536]{1,0:T(8,128)(2,1)S(1)}, u32[]{:S(2)}, u32[]{:S(2)}) collective-permute-start(bf16[96,1536]{1,0:T(8,128)(2,1)S(1)} %add_convert_fusion.13), channel_id=1, source_target_pairs={{0,16},{4,20},{8,24},{12,28},{16,0},{20,4},{24,8},{28,12},{1,17},{... | collective-permute-start | bytes 884744 | tf_op jit(solution)/shard_map/ppermute | solution.py:160
  580.5 46.9 %collective-permute-start.76 = (bf16[1,512,384]{2,1,0:T(8,128)(2,1)}, bf16[1,512,384]{2,1,0:T(8,128)(2,1)S(1)}, u32[]{:S(2)}, u32[]{:S(2)}) collective-permute-start(bf16[1,512,384]{2,1,0:T(8,128)(2,1)} %add_convert_fusion.8), channel_id=1, source_target_pairs={{0,2},{1,3},{2,0},{3,1},{4,6},{5,7},{6,4},{7,5},{8,10},{9,11},{10,... | collective-permute-start | bytes 1179656 | tf_op jit(solution)/shard_map/ppermute | solution.py:71
  582.3 17.3 %collective-permute-start.67 = (bf16[96,768]{1,0:T(8,128)(2,1)S(1)}, bf16[96,768]{1,0:T(8,128)(2,1)S(1)}, u32[]{:S(2)}, u32[]{:S(2)}) collective-permute-start(bf16[96,768]{1,0:T(8,128)(2,1)S(1)} %broadcast_select_fusion.13), channel_id=1, source_target_pairs={{0,16},{4,20},{8,24},{12,28},{16,0},{20,4},{24,8},{28,12},{1,17},{... | collective-permute-start | bytes 442376 | tf_op jit(solution)/shard_map/ppermute | solution.py:160
  596.7 20.0 %collective-permute-start.73 = (bf16[192,1536]{1,0:T(8,128)(2,1)S(1)}, bf16[192,1536]{1,0:T(8,128)(2,1)S(1)}, u32[]{:S(2)}, u32[]{:S(2)}) collective-permute-start(bf16[192,1536]{1,0:T(8,128)(2,1)S(1)} %pad_maximum_fusion.8), channel_id=1, source_target_pairs={{0,8},{4,12},{8,0},{12,4},{16,24},{20,28},{24,16},{28,20},{1,9},{5... | collective-permute-start | bytes 1769480 | tf_op jit(solution)/shard_map/ppermute | solution.py:160
  599.7 13.1 %collective-permute-start.68 = (bf16[96,768]{1,0:T(8,128)(2,1)S(1)}, bf16[96,768]{1,0:T(8,128)(2,1)S(1)}, u32[]{:S(2)}, u32[]{:S(2)}) collective-permute-start(bf16[96,768]{1,0:T(8,128)(2,1)S(1)} %add_convert_fusion.17), channel_id=1, source_target_pairs={{0,16},{4,20},{8,24},{12,28},{16,0},{20,4},{24,8},{28,12},{1,17},{... | collective-permute-start | bytes 442376 | tf_op jit(solution)/shard_map/ppermute | solution.py:160
  601.9 25.6 %collective-permute-start.77 = (bf16[1,512,384]{2,1,0:T(8,128)(2,1)}, bf16[1,512,384]{2,1,0:T(8,128)(2,1)}, u32[]{:S(2)}, u32[]{:S(2)}) collective-permute-start(bf16[1,512,384]{2,1,0:T(8,128)(2,1)} %add_convert_fusion.7), channel_id=1, source_target_pairs={{0,1},{1,0},{2,3},{3,2},{4,5},{5,4},{6,7},{7,6},{8,9},{9,8},{10,11... | collective-permute-start | bytes 1179656 | tf_op jit(solution)/shard_map/ppermute | solution.py:71
  618.0 12.3 %collective-permute-start.74 = (bf16[384,1536]{1,0:T(8,128)(2,1)}, bf16[384,1536]{1,0:T(8,128)(2,1)}, u32[]{:S(2)}, u32[]{:S(2)}) collective-permute-start(bf16[384,1536]{1,0:T(8,128)(2,1)} %pad_maximum_fusion.5.one_mine), channel_id=1, source_target_pairs={{0,4},{4,0},{8,12},{12,8},{16,20},{20,16},{24,28},{28,24},{1,5},{5... | collective-permute-start | bytes 3538952 | tf_op jit(solution)/shard_map/ppermute | solution.py:62
  (102 other events, 1285.0 us)
Sparse Core Ops, SparseCore 0:
  9.7 119.4 all-gather.1
  423.4 135.2 reduce-scatter.1

commit v3 on v2

--- a/solution.py
+++ b/solution.py
@@ -97,12 +97,39 @@
     if lax.axis_size("shard") != 4:
         return lax.all_gather(value, "shard", axis=1, tiled=True)
     me = lax.axis_index("shard")
-    parts = [value, across(value, 1), across(value, 2), across(value, 3)]
+    rows = value.shape[0]
+    near = jnp.concatenate([value, across(value, 1)])
+    far = across(near, 2)
+    parts = [near[:rows], near[rows:], far[:rows], far[rows:]]
     odd = me % 2 == 1
     parts = [jnp.where(odd, parts[i ^ 1], parts[i]) for i in range(4)]
     high = me >= 2
     parts = [jnp.where(high, parts[i ^ 2], parts[i]) for i in range(4)]
     return jnp.concatenate(parts, axis=1)
+
+
+def own_groups_kernel(order_ref, query_ref, key_ref, value_ref, out_ref):
+    out_ref[:, :384] = query_ref[...]
+    out_ref[:, 384:512] = key_ref[...]
+    out_ref[:, 512:] = value_ref[...]
+
+
+def own_groups(weight, order):
+    rows = weight.shape[0]
+    last = order.shape[0] - 1
+    spec = lambda w, at: pl.BlockSpec((rows, w), lambda j, o: (0, at + 2 * j + o[last]))
+    return pl.pallas_call(
+        own_groups_kernel,
+        grid_spec=pltpu.PrefetchScalarGridSpec(
+            num_scalar_prefetch=1,
+            grid=(2,),
+            in_specs=[spec(384, 0), spec(128, 12), spec(128, 16)],
+            out_specs=pl.BlockSpec((rows, 640), lambda j, o: (0, j)),
+        ),
+        out_shape=pltpu.HBM((rows, 1280), weight.dtype),
+        cost_estimate=pl.CostEstimate(flops=10**8, bytes_accessed=10**6, transcendentals=0),
+        name="own_groups",
+    )(order, weight, weight, weight)
 
 
 def shard_order():
@@ -153,22 +180,32 @@
     return jnp.concatenate([low_half, high_half]).astype(dtype)
 
 
-def reduce_chips(value):
+def chip_ahead(value, distance):
     count = lax.axis_size("expert")
-    me = lax.axis_index("expert")
-    masks = [1 << i for i in range(1, count.bit_length() - 1)]
-    swap = lambda v, mask: lax.ppermute(v, "expert", [(i, i ^ mask) for i in range(count)])
-    for mask in masks:
-        half = value.shape[0] // 2
-        upper = (me & mask) != 0
-        keep = jnp.where(upper, value[half:], value[:half])
-        send = jnp.where(upper, value[:half], value[half:])
-        value = add_low(keep, swap(send, mask))
-    for mask in reversed(masks):
-        other = swap(value, mask)
-        upper = (me & mask) != 0
-        value = jnp.concatenate([jnp.where(upper, other, value), jnp.where(upper, value, other)])
-    return value
+    return lax.ppermute(value, "expert", [(i, (i + 2 * distance) % count) for i in range(count)])
+
+
+def chips_send(value):
+    chips = lax.axis_size("expert") // 2
+    z = lax.axis_index("expert") // 2
+    size = value.shape[0] // chips
+    part = lambda d: lax.dynamic_slice_in_dim(value, (z + d) % chips * size, size, 0)
+    return [part(0)] + [chip_ahead(part(d), d) for d in range(1, chips)]
+
+
+def chips_gather(parts):
+    mine = add_low(*parts)
+    return [mine] + [chip_ahead(mine, d) for d in range(1, len(parts))]
+
+
+def chips_order(parts):
+    chips = len(parts)
+    z = lax.axis_index("expert") // 2
+    size = parts[0].shape[0]
+    onward = [parts[-j % chips] for j in range(chips)]
+    return lax.dynamic_slice_in_dim(
+        jnp.concatenate(onward + onward[:-1]), (chips - z) % chips * size, chips * size, 0
+    )
 
 
 def piece_copies(pieces, order_ref, target, sem, axis, split, base=0, stride=None, window=None):
@@ -629,47 +666,51 @@
     )(order, a, b, c, rows, gates, resid, cots, left, gain, router)
 
 
-def fold_kernel(pairs, table_ref, *refs):
+def fold_kernel(pairs, order_ref, *refs):
     x_ref, y_ref, own_ref, beside_ref, above_ref = refs[2 * pairs :]
-    places = ((x_ref, 0, 2), (y_ref, 2, 4), (own_ref, 4, 6), (beside_ref, 6, 7), (above_ref, 7, 8))
     step = pl.program_id(0)
+    half = x_ref.shape[0] // 2
+    low, high = slice(0, half), slice(half, 2 * half)
+    places = (
+        ((own_ref, low), (own_ref, high)),
+        ((x_ref, high), (beside_ref, low)),
+        ((above_ref, low), (y_ref, high)),
+        ((x_ref, low), (y_ref, low)),
+    )
     at = 0
     for i in range(pairs):
-        left, right = refs[2 * i][...], refs[2 * i + 1][...]
-        value = (left.astype(jnp.float32) + right.astype(jnp.float32)).astype(jnp.bfloat16)
+        value = refs[2 * i][...] + refs[2 * i + 1][...]
         columns = slice(at, at + value.shape[1])
         at += value.shape[1]
-        for ref, low, high in places:
-
-            @pl.when((step >= low) & (step < high))
+        for r, ((first, first_rows), (second, second_rows)) in enumerate(places):
+
+            @pl.when(step == r)
             def _():
-                ref[:, columns] = value
-
-
-def fold(*operands):
+                first[first_rows, columns] = value[low]
+                second[second_rows, columns] = value[high]
+
+
+def fold(order, *operands):
     if lax.axis_size("shard") != 4:
         parts = [add_low(operands[i], operands[i + 1]) for i in range(0, len(operands), 2)]
         blocks = jnp.concatenate(parts, axis=1)
         return reduce_first(blocks.reshape(lax.axis_size("shard"), -1, blocks.shape[1]))
-    me = lax.axis_index("shard")
-    rows = operands[0].shape[0] // 8
-    where = [(3, 0), (1, 0), (3, 1), (2, 1), (0, 0), (0, 1), (1, 1), (2, 0)]
-    table = jnp.stack([(me ^ r) * 2 + half for r, half in where]).astype(jnp.int32)
+    rows = operands[0].shape[0] // 4
     columns = sum(v.shape[1] for v in operands[::2])
-    given = lambda n: jax.ShapeDtypeStruct((n * rows, columns), jnp.bfloat16)
-    place = lambda low, count: pl.BlockSpec((rows, columns), lambda i, t: (jnp.clip(i - low, 0, count - 1), 0))
+    given = [jax.ShapeDtypeStruct((n * rows // 2, columns), jnp.bfloat16) for n in (2, 2, 2, 1, 1)]
     x, y, own, beside, above = pl.pallas_call(
         lambda *refs: fold_kernel(len(operands) // 2, *refs),
         grid_spec=pltpu.PrefetchScalarGridSpec(
             num_scalar_prefetch=1,
-            grid=(8,),
-            in_specs=[pl.BlockSpec((rows, v.shape[1]), lambda i, t: (t[i], 0)) for v in operands],
-            out_specs=[place(0, 2), place(2, 2), place(4, 2), place(6, 1), place(7, 1)],
+            grid=(4,),
+            in_specs=[pl.BlockSpec((rows, v.shape[1]), lambda i, o: (o[i], 0)) for v in operands],
+            out_specs=[pl.BlockSpec(v.shape, lambda i, o: (0, 0)) for v in given],
         ),
-        out_shape=[given(2), given(2), given(2), given(1), given(1)],
-        cost_estimate=pl.CostEstimate(flops=10**9, bytes_accessed=4 * 10**6, transcendentals=0),
+        out_shape=given,
+        compiler_params=pltpu.CompilerParams(vmem_limit_bytes=40 * 2**20),
+        cost_estimate=pl.CostEstimate(flops=3 * 10**9, bytes_accessed=4 * 10**6, transcendentals=0),
         name="fold",
-    )(table, *operands)
+    )(order, *operands)
     return own, beside, above, across(x, 1), across(y, 2)
 
 
@@ -949,10 +990,17 @@
         beside_ref[...] = block(1)
 
 
+def exchange_first(state):
+    if len(state) == 1:
+        return reduce_first(state[0])
+    own, beside, above, x, y = state
+    return own, beside, above, across(x, 1), across(y, 2)
+
+
 def grad_exchange(left, right, order, on_rows, pick=0, stride=1):
     shards = lax.axis_size("shard")
     if shards != 4:
-        return reduce_first(weight_grad(left, right[pick::stride] if right.ndim == 3 else right, shards, on_rows))
+        return (weight_grad(left, right[pick::stride] if right.ndim == 3 else right, shards, on_rows),)
     count = left.shape[0] if left.ndim == 3 else right.shape[0] // stride
     half = count // 2
     total, size_m = left.shape[-2:]
@@ -984,7 +1032,7 @@
         name="weight_grad",
     )(order, left, right)
     merged = lambda v: v.reshape((2 * half,) + shape)
-    return own, beside, above, across(merged(x), 1), across(merged(y), 2)
+    return own, beside, above, merged(x), merged(y)
 
 
 def per_device(
@@ -1012,19 +1060,7 @@
     order = shard_order()
     queries = HEADS * HEAD_DIM
 
-    by_group = [
-        jnp.concatenate(
-            [
-                qkv_weight[:, 384 * g : 384 * (g + 1)],
-                qkv_weight[:, queries + 128 * g : queries + 128 * (g + 1)],
-                qkv_weight[:, queries + 512 + 128 * g : queries + 512 + 128 * (g + 1)],
-            ],
-            axis=1,
-        )
-        for g in range(4)
-    ]
-    half_columns = lambda g, h: jnp.concatenate([by_group[g], by_group[h]], axis=1)
-    block = jnp.where(core == 0, half_columns(0, 2), half_columns(1, 3))
+    block = own_groups(qkv_weight, order)
     small = jnp.concatenate([router_weight, norm1_gain[:, None], norm2_gain[:, None]], axis=1).T
     small = gather_small(small)
     mixer_first = gather_first(block)
@@ -1034,10 +1070,11 @@
     activity = layer_input.astype(jnp.float32)
     hidden_one = (activity * inverse_rms(activity) * gain_one).astype(low)
     bias, cosine, sine = tree_tables(parents)
-    mixer_first, hidden_one, bias, cosine, sine = lax.optimization_barrier(
-        (mixer_first, hidden_one, bias, cosine, sine)
-    )
     mine = gather_second(mixer_first, 0)
+    last_pieces, hidden_one, bias, cosine, sine = lax.optimization_barrier(
+        (mine[3:], hidden_one, bias, cosine, sine)
+    )
+    mine = mine[:3] + last_pieces
     mixer_p = mine + [swap_core(p) for p in mine]
     block = lax.dynamic_slice_in_dim(out_weight, core * (out_weight.shape[0] // 2), out_weight.shape[0] // 2, 0)
     project_first = gather_first(after(block, *mine))
@@ -1062,6 +1099,7 @@
     resid, gates, sent_rows = project(
         attended, layer_input, routes, gain_two, router, expert_count, proj, len(mixer_p) // 2, order
     )
+    onward = next_chip(sent_rows)
     ups_first, sent_rows = lax.optimization_barrier((ups_first, sent_rows))
     gates_p = gather_second(gates_first, 0)
     ups_first, down_block = lax.optimization_barrier((ups_first, after(down_weight, *gates_p)))
@@ -1069,7 +1107,7 @@
     ups_p = gather_second(ups_first, 0)
     downs_p = gather_second(downs_first, 0)
     rows = [sent_rows]
-    rows.append(next_chip(rows[0]))
+    rows.append(onward)
     beside = swap_core(rows[0])
     rows[0], rows[1], beside = lax.optimization_barrier((rows[0], rows[1], beside))
     kept = total = None
@@ -1097,10 +1135,10 @@
     sent = next_chip(total)
     gate_state = grad_exchange(all_rows, all_sides, order, True, 0, 2)
     gate_done, all_rows = lax.optimization_barrier((gate_state[0], all_rows))
-    gate_state = (gate_done,) + gate_state[1:]
+    gate_state = exchange_first((gate_done,) + gate_state[1:])
     up_state = grad_exchange(all_rows, all_sides, order, True, 1, 2)
     sent, up_done, gate_state = lax.optimization_barrier((sent, up_state[0], gate_state))
-    up_state = (up_done,) + up_state[1:]
+    up_state = exchange_first((up_done,) + up_state[1:])
     branch_out = lax.psum_scatter(after(out_all, sent), "expert", scatter_dimension=0, tiled=True)
     grad_branch, grad_resid, out_mine, out_other = turn(
         expert_count, order, *last, sent, sent_rows, gates, resid, out_cotangent, attended, gain_two, router
@@ -1116,7 +1154,7 @@
     grad_branch, wide, other, part, out_mine, out_sent, gate_state, up_state = lax.optimization_barrier(
         (grad_branch, wide, other, part, out_mine, out_sent, gate_state, up_state)
     )
-    state_one = fold(wide, swap_core(other), out_mine, out_sent)
+    state_one = fold(order, wide, swap_core(other), out_mine, out_sent)
     grad_branch, folded = lax.optimization_barrier((grad_branch, state_one[0]))
     state_one = (folded,) + state_one[1:]
     wide, other, grad_input = backward(1, grad_branch, part, layer_input, grad_resid, gain_one)
@@ -1124,28 +1162,37 @@
         (wide, other, grad_input, state_one, all_mid)
     )
     state_one = reduce_second(state_one)
-    sent = swap_core(other)
+    state_two = fold(order, wide, swap_core(other))
+    folded, state_one = lax.optimization_barrier((state_two[0], state_one))
+    state_two = (folded,) + state_two[1:]
+    one = reduce_last(state_one)
+    all_mid, one, folded = lax.optimization_barrier((all_mid, one, state_two[0]))
+    state_two = (folded,) + state_two[1:]
+    one = chips_send(one)
     down_state = grad_exchange(all_mid, cots, order, False)
-    kernel_done, state_one, sent, gate_state, up_state = lax.optimization_barrier(
-        (down_state[0], state_one, sent, gate_state, up_state)
+    kernel_done, state_two, one, gate_state, up_state = lax.optimization_barrier(
+        (down_state[0], state_two, one, gate_state, up_state)
     )
     down_state = (kernel_done,) + down_state[1:]
-    one = reduce_last(state_one)
-    wide, one = lax.optimization_barrier((wide, one))
-    state_two = fold(wide, sent)
     state_two = reduce_second(state_two)
-    two = reduce_last(state_two)
-    two, down_state = lax.optimization_barrier((two, down_state))
+    one = chips_gather(one)
+    state_two, one, down_state = lax.optimization_barrier((state_two, one, down_state))
+    two = chips_send(reduce_last(state_two))
+    down_state = exchange_first(down_state)
+    one = chips_order(one)
+    two, down_state, one = lax.optimization_barrier((two, down_state, one))
+    two = chips_gather(two)
     down_state = reduce_second(down_state)
-    one = reduce_chips(one)
-    two = reduce_chips(two)
+    two, down_state, one = lax.optimization_barrier((two, down_state, one))
+    two = chips_order(two)
+    one = (one, swap_core(one))
+    two = (two, swap_core(two))
     grad_gate = reduce_last(gate_state, jnp.float32)
     grad_up = reduce_last(up_state, jnp.float32)
     grad_down = reduce_last(down_state, jnp.float32)
     output = (resid + branch_out.astype(jnp.float32)).astype(low)
-    two, output, grad_gate, grad_up = lax.optimization_barrier((two, output, grad_gate, grad_up))
     grad_mixer, grad_projector, grad_router, grad_gain_two, grad_gain_one = finish(
-        expert_count, order, (one, swap_core(one)), (two, swap_core(two))
+        expert_count, order, one, two
     )
     return (
         output,

time: 651 us -> 645 us (level)
  starting transfers between devices: 64.4 us -> 83.8 us
  other arithmetic: 50.1 us -> 37 us
  Pallas kernels: 318 us -> 311 us
    ppermute x8 -> x12, waiting for transfers between devices: 44.7 us -> 22.6 us  [chip_ahead(): lax.ppermute(value, 'expert', [(i, (i + 2 * distance) % count) for i in r...]
    ppermute x43 -> x42, waiting for transfers between devices: 88.6 us -> 106 us  [across(): return lax.ppermute(value, 'shard', [(i, i ^ mask) for i in range(4)])]
    ppermute x8 -> x12, starting transfers between devices: 9.36 us -> 26.3 us  [chip_ahead(): lax.ppermute(value, 'expert', [(i, (i + 2 * distance) % count) for i in r...]
    pallas_call x2, Pallas kernels: 17.7 us -> 8.02 us  [fold(): pl.pallas_call(lambda *refs: fold_kernel(len(operands) // 2, *refs), grid...]
    convert_element_type x17 -> x15, other arithmetic: 16.1 us -> 12.9 us  [add_low(): return total.astype(jnp.bfloat16)]
    unnamed x186 -> x159, local copies, waits for them, and re-layouts: 20.7 us -> 18.6 us
    ppermute x43 -> x42, starting transfers between devices: 49.1 us -> 50.5 us  [across(): return lax.ppermute(value, 'shard', [(i, i ^ mask) for i in range(4)])]
  transfers between devices with their start and end apart: 80 -> 83, of which waited for: 34 -> 38; matrix products, arithmetic and copies ran while one was open for 9% -> 6% of each run, Pallas kernels for 48% -> 49%
where the time goes in v3:
time: 645 us; the launch traced here: 637 us
  Pallas kernels  311 us (48%)
  waiting for transfers between devices  166 us (26%)
  starting transfers between devices  83.8 us (13%)
  other arithmetic  37 us (6%)
  local copies, waits for them, and re-layouts  23.5 us (4%)
  between operations  15.9 us (2%)
    pallas_call x4, Pallas kernels, expert_chunk(): pl.pallas_call(lambda *refs: expert_kernel((len(gates), more), expert_cou...  127 us
    ppermute x42, waiting for transfers between devices, across(): return lax.ppermute(value, 'shard', [(i, i ^ mask) for i in range(4)])  106 us
    pallas_call x3, Pallas kernels, grad_exchange(): pl.pallas_call(lambda *refs: sorted_grad_kernel(on_rows, half, *refs), gr...  63 us
    pallas_call x2, Pallas kernels, attend_back(): pl.pallas_call(lambda *refs: attend_back_kernel(mine, (len(proj), len(mix...  56.9 us
    ppermute x42, starting transfers between devices, across(): return lax.ppermute(value, 'shard', [(i, i ^ mask) for i in range(4)])  50.5 us
    ppermute x12, starting transfers between devices, chip_ahead(): lax.ppermute(value, 'expert', [(i, (i + 2 * distance) % count) for i in r...  26.3 us
    pallas_call x2, Pallas kernels, attend(): pl.pallas_call(lambda *refs: attend_kernel(len(mixer_p) // 2, call, *refs...  25.3 us
    ppermute x12, waiting for transfers between devices, chip_ahead(): lax.ppermute(value, 'expert', [(i, (i + 2 * distance) % count) for i in r...  22.6 us
  transfers between devices with their start and end apart: 83, of which 38 were waited for; matrix products, arithmetic and copies ran while one was open for 6% of the time, Pallas kernels for 49%

profile of v3, /device:TPU:0, one launch (start us, length us, event | category | flops | bytes accessed | tf_op | source)
XLA Modules:
  0.0 637.3 jit_solution(5354737935827668622)
XLA Ops:
  8.7 2.9 own_groups.1
  11.6 2.9 collective-permute-start
  18.9 1.6 broadcast_in_dim.114
  21.7 15.2 %collective-permute-done.4 = bf16[18,384]{1,0:T(8,128)(2,1)S(1)} collective-permute-done((bf16[18,384]{1,0:T(8,128)(2,1)S(1)}, bf16[18,384]{1,0:T(8,128)(2,1)S(1)}, u32[]{:S(2)}, u32[]{:S(2)}) %collective-permute-start.4) | collective-permute-done | bytes 13856 | tf_op jit(solution)/shard_map/ppermute | solution.py:71
  36.9 1.8 collective-permute-start.5
  39.3 1.6 collective-permute-done.5
  44.4 1.8 collective-permute-start.2
  49.3 8.5 %collective-permute-done.2.refs_9_.refs_22_ = bf16[1,192,1280]{2,1,0:T(8,128)(2,1)} collective-permute-done((bf16[1,192,1280]{2,1,0:T(8,128)(2,1)S(1)}, bf16[1,192,1280]{2,1,0:T(8,128)(2,1)}, u32[]{:S(2)}, u32[]{:S(2)}) %collective-permute-start.2) | collective-permute-done | bytes 491552 | tf_op jit(solution)/shard_map/ppermute | solution.py:71
  61.2 1.7 collective-permute-start.7
  66.8 12.3 %attend.2 = (bf16[512,1536]{1,0:T(8,128)(2,1)}, bf16[512,1536]{1,0:T(8,128)(2,1)}, bf16[512,512]{1,0:T(8,128)(2,1)}, bf16[512,512]{1,0:T(8,128)(2,1)}, f32[4,512,8]{2,1,0:T(8,128)}) custom-call(s32[6]{0:T(128)S(1)} %copy-done.14, s32[2]{0:T(128)S(1)} %get-tuple-element.565.refs_1_.refs_0_, bf16[512,1536]{1,0:T(8,128)(2,1)S(1)} %copy-done.5, ...), custom_call_target="tpu_custom_call" | custom-call | flops 48000000000 | bytes 8000000 | tf_op jit(solution)/shard_map/attend/pallas_call | solution.py:301
  83.7 13.0 %attend.3 = (bf16[512,1536]{1,0:T(8,128)(2,1)}, bf16[512,1536]{1,0:T(8,128)(2,1)}, bf16[512,512]{1,0:T(8,128)(2,1)}, bf16[512,512]{1,0:T(8,128)(2,1)}, f32[4,512,8]{2,1,0:T(8,128)}) custom-call(s32[6]{0:T(128)S(1)} %copy-done.14, ...), custom_call_target="tpu_custom_call", output_to_operand_aliasing={{0}: (16, {}), {1}: (17, {}), {2}: (18, {}), {3}: (19, {}),... | custom-call | flops 48000000000 | bytes 8000000 | tf_op jit(solution)/shard_map/attend/pallas_call | solution.py:301
  96.7 8.0 %collective-permute-done.13.refs_9_.refs_14_ = bf16[1,96,1536]{2,1,0:T(8,128)(2,1)S(1)} collective-permute-done((bf16[1,96,1536]{2,1,0:T(8,128)(2,1)S(1)}, bf16[1,96,1536]{2,1,0:T(8,128)(2,1)S(1)}, u32[]{:S(2)}, u32[]{:S(2)}) %collective-permute-start.13) | collective-permute-done | bytes 294944 | tf_op jit(solution)/shard_map/ppermute | solution.py:71
  110.3 7.8 %project.1 = (f32[512,1536]{1,0:T(8,128)S(1)}, f32[512,128]{1,0:T(8,128)S(1)}, bf16[528,1536]{1,0:T(8,128)(2,1)}) custom-call(s32[6]{0:T(128)S(1)} %copy-done.14, bf16[512,1536]{1,0:T(8,128)(2,1)S(1)} %copy-done.28, bf16[512,1536]{1,0:T(8,128)(2,1)S(1)} %copy-done.2, s32[512,8]{1,0:T(8,128)S(1)} %copy.39.refs_3_, ...), custom_call_target="tpu_custom_call" | custom-call | flops 30000001024 | bytes 8000000 | tf_op jit(solution)/shard_map/project/pallas_call | solution.py:567
  119.5 6.6 %collective-permute-done.20 = bf16[2,384,512]{2,1,0:T(8,128)(2,1)S(1)} collective-permute-done((bf16[2,384,512]{2,1,0:T(8,128)(2,1)S(1)}, bf16[2,384,512]{2,1,0:T(8,128)(2,1)S(1)}, u32[]{:S(2)}, u32[]{:S(2)}) %collective-permute-start.20) | collective-permute-done | bytes 786464 | tf_op jit(solution)/shard_map/ppermute | solution.py:71
  128.6 9.5 %collective-permute-done.24.refs_8_ = bf16[1,1,384,512]{3,2,1,0:T(8,128)(2,1)S(1)} collective-permute-done((bf16[1,1,384,512]{3,2,1,0:T(8,128)(2,1)S(1)}, bf16[1,1,384,512]{3,2,1,0:T(8,128)(2,1)S(1)}, u32[]{:S(2)}, u32[]{:S(2)}) %collective-permute-start.24) | collective-permute-done | bytes 393248 | tf_op jit(solution)/shard_map/ppermute | solution.py:71
  139.8 1.7 collective-permute-start.28
  142.0 16.2 %collective-permute-done.29 = bf16[2,512,384]{2,1,0:T(8,128)(2,1)S(1)} collective-permute-done((bf16[2,512,384]{2,1,0:T(8,128)(2,1)S(1)}, bf16[2,512,384]{2,1,0:T(8,128)(2,1)S(1)}, u32[]{:S(2)}, u32[]{:S(2)}) %collective-permute-start.29) | collective-permute-done | bytes 786464 | tf_op jit(solution)/shard_map/ppermute | solution.py:71
  160.3 1.7 collective-permute-start.30
  166.5 2.3 collective-permute-done.26.refs_13_
  169.6 5.8 collective-permute-done.30.refs_18_
  176.2 31.9 %expert_chunk.4 = (bf16[528,1536]{1,0:T(8,128)(2,1)}, bf16[528,1536]{1,0:T(8,128)(2,1)}, bf16[4096,1536]{1,0:T(8,128)(2,1)}, bf16[4096,1536]{1,0:T(8,128)(2,1)},...) custom-call(s32[6]{0:T(128)} %stack.82.order_ref.refs_0_.refs_1_, s32[3]{0:T(128)} %get-tuple-element.569.refs_1_, ...), custom_call_target="tpu_custom_call" | custom-call | flops 80999997440 | bytes 8000000 | tf_op jit(solution)/shard_map/expert_chunk/pallas_call | solution.py:885
  209.5 31.6 %expert_chunk.5 = (bf16[528,1536]{1,0:T(8,128)(2,1)}, bf16[528,1536]{1,0:T(8,128)(2,1)}, bf16[4096,1536]{1,0:T(8,128)(2,1)}, bf16[4096,1536]{1,0:T(8,128)(2,1)},...) custom-call(s32[6]{0:T(128)} %stack.82.order_ref.refs_0_.refs_1_, ...), custom_call_target="tpu_custom_call", output_to_operand_aliasing={{2}: (20, {}), {3}: (21, {}), {4}: (22, {}), {5}: (23, {})} | custom-call | flops 80999997440 | bytes 8000000 | tf_op jit(solution)/shard_map/expert_chunk/pallas_call | solution.py:885
  241.1 4.8 collective-permute-done.34.refs_2_
  247.2 4.1 collective-permute-done.36
  251.3 1.8 add_convert_fusion.2
  253.2 31.9 %expert_chunk.6 = (bf16[528,1536]{1,0:T(8,128)(2,1)}, bf16[528,1536]{1,0:T(8,128)(2,1)}, bf16[4096,1536]{1,0:T(8,128)(2,1)}, bf16[4096,1536]{1,0:T(8,128)(2,1)},...) custom-call(s32[6]{0:T(128)} %stack.82.order_ref.refs_0_.refs_1_, ...), custom_call_target="tpu_custom_call", output_to_operand_aliasing={{2}: (20, {}), {3}: (21, {}), {4}: (22, {}), {5}: (23, {})} | custom-call | flops 80999997440 | bytes 8000000 | tf_op jit(solution)/shard_map/expert_chunk/pallas_call | solution.py:885
  285.1 7.4 %collective-permute-done.38 = bf16[528,1536]{1,0:T(8,128)(2,1)S(1)} collective-permute-done((bf16[528,1536]{1,0:T(8,128)(2,1)S(1)}, bf16[528,1536]{1,0:T(8,128)(2,1)S(1)}, u32[]{:S(2)}, u32[]{:S(2)}) %collective-permute-start.38) | collective-permute-done | bytes 1622048 | tf_op jit(solution)/shard_map/ppermute | solution.py:67
  292.5 3.7 collective-permute-done.39
  296.2 2.0 add_convert_fusion.1
  298.3 31.6 %expert_chunk.7 = (bf16[528,1536]{1,0:T(8,128)(2,1)}, bf16[528,1536]{1,0:T(8,128)(2,1)}, bf16[4096,1536]{1,0:T(8,128)(2,1)}, bf16[4096,1536]{1,0:T(8,128)(2,1)},...) custom-call(s32[6]{0:T(128)} %stack.82.order_ref.refs_0_.refs_1_, ...), custom_call_target="tpu_custom_call", output_to_operand_aliasing={{2}: (20, {}), {3}: (21, {}), {4}: (22, {}), {5}: (23, {})} | custom-call | flops 80999997440 | bytes 8000000 | tf_op jit(solution)/shard_map/expert_chunk/pallas_call | solution.py:885
  329.9 7.6 %collective-permute-done.40 = bf16[528,1536]{1,0:T(8,128)(2,1)S(1)} collective-permute-done((bf16[528,1536]{1,0:T(8,128)(2,1)S(1)}, bf16[528,1536]{1,0:T(8,128)(2,1)S(1)}, u32[]{:S(2)}, u32[]{:S(2)}) %collective-permute-start.40) | collective-permute-done | bytes 1622048 | tf_op jit(solution)/shard_map/ppermute | solution.py:67
  338.0 5.5 collective-permute-done.41
  343.5 2.0 add_convert_fusion
  345.6 20.8 %weight_grad.3 = (bf16[2,384,512]{2,1,0:T(8,128)(2,1)S(1)}, bf16[1,384,512]{2,1,0:T(8,128)(2,1)S(1)}, bf16[1,384,512]{2,1,0:T(8,128)(2,1)S(1)}, bf16[2,1,384,512...) custom-call(s32[6]{0:T(128)S(1)} %copy-done.15, bf16[4096,1536]{1,0:T(8,128)(2,1)} %get-tuple-element.384.refs_1_, ...), custom_call_target="tpu_custom_call" | custom-call | flops 60000002048 | bytes 8000000 | tf_op jit(solution)/shard_map/weight_grad/pallas_call | solution.py:1020
  369.1 21.7 %weight_grad.4 = (bf16[2,384,512]{2,1,0:T(8,128)(2,1)S(1)}, bf16[1,384,512]{2,1,0:T(8,128)(2,1)S(1)}, bf16[1,384,512]{2,1,0:T(8,128)(2,1)S(1)}, bf16[2,1,384,512]{3,2,1,0:T(8,128)(2,1)}, bf16[2,1,384,512]{3,2,1,0:T(8,128)(2,1)}) custom-call(s32[6]{0:T(128)S(1)} %copy-done.15, bf16[4096,1536]{1,0:T(8,128)(2,1)} %get-tuple-element.384.refs_1_, ...), custom_call_target="tpu_custom_call" | custom-call | flops 60000002048 | bytes 8000000 | tf_op jit(solution)/shard_map/weight_grad/pallas_call | solution.py:1020
  393.7 14.5 %turn.1 = (bf16[512,1536]{1,0:T(8,128)(2,1)}, f32[512,1536]{1,0:T(8,128)}, bf16[1536,896]{1,0:T(8,128)(2,1)}, bf16[1536,896]{1,0:T(8,128)(2,1)}) custom-call(s32[6]{0:T(128)} %stack.82.order_ref.refs_0_.refs_1_, bf16[528,1536]{1,0:T(8,128)(2,1)} %get-tuple-element.393.refs_1_, bf16[528,1536]{1,0:T(8,128)(2,1)} %collective-permute-done.45.refs_2_, ...), custom_call_target="tpu_custom_call" | custom-call | flops 30000001024 | bytes 8000000 | tf_op jit(solution)/shard_map/turn/pallas_call | solution.py:643
  408.2 1.9 collective-permute-done.46
  417.1 26.1 %attend_back.2 = (bf16[1536,640]{1,0:T(8,128)(2,1)}, bf16[1536,640]{1,0:T(8,128)(2,1)}, f32[512,1536]{1,0:T(8,128)}) custom-call(s32[2]{0:T(128)} %copy-done.19, s32[6]{0:T(128)} %stack.82.order_ref.refs_0_.refs_1_, bf16[512,1536]{1,0:T(8,128)(2,1)} %get-tuple-element.429.refs_2_, bf16[512,1536]{1,0:T(8,128)(2,1)} %fusion.2.refs_2_.refs_3_, ...), custom_call_target="tpu_custom_call" | custom-call | flops 60000002048 | bytes 8000000 | tf_op jit(solution)/shard_map/attend_back/pallas_call | solution.py:465
  444.3 3.3 collective-permute-done.53.refs_2_
  447.6 1.9 copy-done.25
  451.0 4.6 fold.2
  457.6 30.8 %attend_back.3 = (bf16[1536,768]{1,0:T(8,128)(2,1)}, bf16[1536,768]{1,0:T(8,128)(2,1)}, bf16[512,1536]{1,0:T(8,128)(2,1)}) custom-call(s32[2]{0:T(128)} %copy-done.18, s32[6]{0:T(128)} %stack.82.order_ref.refs_0_.refs_1_, bf16[512,1536]{1,0:T(8,128)(2,1)} %get-tuple-element.429.refs_2_, bf16[512,1536]{1,0:T(8,128)(2,1)} %fusion.2.refs_2_.refs_3_, ...), custom_call_target="tpu_custom_call" | custom-call | flops 60000002048 | bytes 8000000 | tf_op jit(solution)/shard_map/attend_back/pallas_call | solution.py:465
  488.5 2.0 add_convert_fusion.5
  491.2 2.0 add_convert_fusion.4
  494.4 1.7 copy-done.27
  496.1 3.4 fold.3
  499.5 7.0 %collective-permute-done.57 = bf16[192,1536]{1,0:T(8,128)(2,1)} collective-permute-done((bf16[192,1536]{1,0:T(8,128)(2,1)}, bf16[192,1536]{1,0:T(8,128)(2,1)}, u32[]{:S(2)}, u32[]{:S(2)}) %collective-permute-start.57) | collective-permute-done | bytes 589856 | tf_op jit(solution)/shard_map/ppermute | solution.py:71
  506.6 2.4 collective-permute-done.58
  509.3 2.1 fusion.6
  514.4 4.0 collective-permute-start.62
  518.4 20.6 %weight_grad.5 = (bf16[2,512,384]{2,1,0:T(8,128)(2,1)S(1)}, bf16[1,512,384]{2,1,0:T(8,128)(2,1)S(1)}, bf16[1,512,384]{2,1,0:T(8,128)(2,1)S(1)}, bf16[2,1,512,384...) custom-call(s32[6]{0:T(128)S(1)} %copy-done.17, bf16[2,4096,512]{2,1,0:T(8,128)(2,1)} %get-tuple-element.457.refs_1_, ...), custom_call_target="tpu_custom_call" | custom-call | flops 60000002048 | bytes 8000000 | tf_op jit(solution)/shard_map/weight_grad/pallas_call | solution.py:1020
  539.0 2.4 collective-permute-done.62
  541.6 6.6 %collective-permute-start.66 = (bf16[96,1536]{1,0:T(8,128)(2,1)S(1)}, bf16[96,1536]{1,0:T(8,128)(2,1)S(1)}, u32[]{:S(2)}, u32[]{:S(2)}) collective-permute-start(bf16[96,1536]{1,0:T(8,128)(2,1)S(1)} %add_convert_fusion.12), channel_id=1, source_target_pairs={{0,8},{4,12},{8,16},{12,20},{16,24},{20,28},{24,0},{28,4},{1,9},{5... | collective-permute-start | bytes 884744 | tf_op jit(solution)/shard_map/ppermute | solution.py:185
  560.3 7.9 %collective-permute-done.67 = bf16[96,1536]{1,0:T(8,128)(2,1)S(1)} collective-permute-done((bf16[96,1536]{1,0:T(8,128)(2,1)S(1)}, bf16[96,1536]{1,0:T(8,128)(2,1)S(1)}, u32[]{:S(2)}, u32[]{:S(2)}) %collective-permute-start.67) | collective-permute-done | bytes 294944 | tf_op jit(solution)/shard_map/ppermute | solution.py:185
  569.2 6.8 %collective-permute-start.69 = (bf16[96,768]{1,0:T(8,128)(2,1)S(1)}, bf16[96,768]{1,0:T(8,128)(2,1)S(1)}, u32[]{:S(2)}, u32[]{:S(2)}) collective-permute-start(bf16[96,768]{1,0:T(8,128)(2,1)S(1)} %get-tuple-element.558), channel_id=1, source_target_pairs={{0,8},{4,12},{8,16},{12,20},{16,24},{20,28},{24,0},{28,4},{1,9},{5... | collective-permute-start | bytes 442376 | tf_op jit(solution)/shard_map/ppermute | solution.py:185
  576.1 2.1 collective-permute-start.70
  582.5 4.8 collective-permute-done.70
  587.3 10.1 %collective-permute-done.72 = bf16[2,512,384]{2,1,0:T(8,128)(2,1)S(1)} collective-permute-done((bf16[2,512,384]{2,1,0:T(8,128)(2,1)S(1)}, bf16[2,512,384]{2,1,0:T(8,128)(2,1)S(1)}, u32[]{:S(2)}, u32[]{:S(2)}) %collective-permute-start.72) | collective-permute-done | bytes 786464 | tf_op jit(solution)/shard_map/ppermute | solution.py:71
  601.7 1.6 collective-permute-start.75
  603.4 1.6 collective-permute-start.76
  606.2 3.4 collective-permute-done.74
  609.6 3.3 collective-permute-done.75
  617.6 5.8 finish.1
  626.1 4.0 add_convert_fusion.3
  (359 shorter events, 101.2 us)
Async XLA Ops:
  7.2 169.0 %all-gather.2.cloned.1.call-start = ((), (), s32[]{:S(2)}) async-start(), calls=%async_computation.1 | async-start | bytes 14155776 | tf_op jit(solution)/shard_map/all_gather | solution.py:1082
  7.9 618.1 %reduce-scatter.2.cloned.1.call-start = ((), (), s32[]{:S(2)}) async-start(), calls=%async_computation.2 | async-start | bytes 14155776 | tf_op jit(solution)/shard_map/reduce_scatter | solution.py:1142
  11.6 30.0 %collective-permute-start = (bf16[384,1280]{1,0:T(8,128)(2,1)}, bf16[384,1280]{1,0:T(8,128)(2,1)}, u32[]{:S(2)}, u32[]{:S(2)}) collective-permute-start(bf16[384,1280]{1,0:T(8,128)(2,1)} %own_groups.1), channel_id=1, source_target_pairs={{0,1},{1,0},{2,3},{3,2},{4,5},{5,4},{6,7},{7,6},{8,9},{9,8},{10,11... | collective-permute-start | bytes 2949128 | tf_op jit(solution)/shard_map/ppermute | solution.py:71
  14.6 28.2 %collective-permute-start.1 = (bf16[384,1280]{1,0:T(8,128)(2,1)}, bf16[384,1280]{1,0:T(8,128)(2,1)}, u32[]{:S(2)}, u32[]{:S(2)}) collective-permute-start(bf16[384,1280]{1,0:T(8,128)(2,1)} %own_groups.1), channel_id=1, source_target_pairs={{0,2},{1,3},{2,0},{3,1},{4,6},{5,7},{6,4},{7,5},{8,10},{9,11},{10,... | collective-permute-start | bytes 2949128 | tf_op jit(solution)/shard_map/ppermute | solution.py:71
  16.1 20.8 %collective-permute-start.4 = (bf16[18,384]{1,0:T(8,128)(2,1)S(1)}, bf16[18,384]{1,0:T(8,128)(2,1)S(1)}, u32[]{:S(2)}, u32[]{:S(2)}) collective-permute-start(bf16[18,384]{1,0:T(8,128)(2,1)S(1)} %maximum_bitcast_fusion), channel_id=1, source_target_pairs={{0,1},{1,0},{2,3},{3,2},{4,5},{5,4},{6,7},{7,6},{8,9},{9,8},{10,11... | collective-permute-start | bytes 41480 | tf_op jit(solution)/shard_map/ppermute | solution.py:71
  16.7 44.0 %collective-permute-start.8 = (bf16[1,384,1280]{2,1,0:T(8,128)(2,1)}, bf16[1,384,1280]{2,1,0:T(8,128)(2,1)}, u32[]{:S(2)}, u32[]{:S(2)}) collective-permute-start(bf16[1,384,1280]{2,1,0:T(8,128)(2,1)} %bitcast.69), channel_id=1, source_target_pairs={{0,4},{4,0},{8,12},{12,8},{16,20},{20,16},{24,28},{28,24},{1,5},{5... | collective-permute-start | bytes 2949128 | tf_op jit(solution)/shard_map/ppermute | solution.py:62
  42.7 18.5 %collective-permute-start.9 = (bf16[1,384,1280]{2,1,0:T(8,128)(2,1)}, bf16[1,384,1280]{2,1,0:T(8,128)(2,1)}, u32[]{:S(2)}, u32[]{:S(2)}) collective-permute-start(bf16[1,384,1280]{2,1,0:T(8,128)(2,1)} %bitcast.6.refs_7_.refs_20_), channel_id=1, source_target_pairs={{0,4},{4,0},{8,12},{12,8},{16,20},{20,16},{24,28},{28,24},{1,5},{5... | collective-permute-start | bytes 2949128 | tf_op jit(solution)/shard_map/ppermute | solution.py:62
  43.9 19.0 %collective-permute-start.10 = (bf16[1,384,1280]{2,1,0:T(8,128)(2,1)}, bf16[1,384,1280]{2,1,0:T(8,128)(2,1)}, u32[]{:S(2)}, u32[]{:S(2)}) collective-permute-start(bf16[1,384,1280]{2,1,0:T(8,128)(2,1)} %bitcast.7.refs_8_.refs_21_), channel_id=1, source_target_pairs={{0,4},{4,0},{8,12},{12,8},{16,20},{20,16},{24,28},{28,24},{1,5},{5... | collective-permute-start | bytes 2949128 | tf_op jit(solution)/shard_map/ppermute | solution.py:62
  44.4 13.4 %collective-permute-start.2 = (bf16[1,192,1280]{2,1,0:T(8,128)(2,1)S(1)}, bf16[1,192,1280]{2,1,0:T(8,128)(2,1)}, u32[]{:S(2)}, u32[]{:S(2)}) collective-permute-start(bf16[1,192,1280]{2,1,0:T(8,128)(2,1)S(1)} %slice.220), channel_id=1, source_target_pairs={{0,1},{1,0},{2,3},{3,2},{4,5},{5,4},{6,7},{7,6},{8,9},{9,8},{10,11... | collective-permute-start | bytes 1474568 | tf_op jit(solution)/shard_map/ppermute | solution.py:71
  46.2 13.0 %collective-permute-start.3 = (bf16[1,192,1280]{2,1,0:T(8,128)(2,1)S(1)}, bf16[1,192,1280]{2,1,0:T(8,128)(2,1)}, u32[]{:S(2)}, u32[]{:S(2)}) collective-permute-start(bf16[1,192,1280]{2,1,0:T(8,128)(2,1)S(1)} %slice.221), channel_id=1, source_target_pairs={{0,2},{1,3},{2,0},{3,1},{4,6},{5,7},{6,4},{7,5},{8,10},{9,11},{10,... | collective-permute-start | bytes 1474568 | tf_op jit(solution)/shard_map/ppermute | solution.py:71
  60.8 18.4 %collective-permute-start.6 = (bf16[192,1536]{1,0:T(8,128)(2,1)S(1)}, bf16[192,1536]{1,0:T(8,128)(2,1)S(1)}, u32[]{:S(2)}, u32[]{:S(2)}) collective-permute-start(bf16[192,1536]{1,0:T(8,128)(2,1)S(1)} %constant_dynamic-slice_fusion.6), channel_id=1, source_target_pairs={{0,1},{1,0},{2,3},{3,2},{4,5},{5,4},{6,7},{7,6},{8,9},{9,8},{10,11... | collective-permute-start | bytes 1769480 | tf_op jit(solution)/shard_map/ppermute | solution.py:71
  61.2 17.9 %collective-permute-start.7 = (bf16[192,1536]{1,0:T(8,128)(2,1)S(1)}, bf16[192,1536]{1,0:T(8,128)(2,1)S(1)}, u32[]{:S(2)}, u32[]{:S(2)}) collective-permute-start(bf16[192,1536]{1,0:T(8,128)(2,1)S(1)} %constant_dynamic-slice_fusion.6), channel_id=1, source_target_pairs={{0,2},{1,3},{2,0},{3,1},{4,6},{5,7},{6,4},{7,5},{8,10},{9,11},{10,... | collective-permute-start | bytes 1769480 | tf_op jit(solution)/shard_map/ppermute | solution.py:71
  79.2 26.5 %collective-permute-start.16 = (bf16[2,384,512]{2,1,0:T(8,128)(2,1)S(1)}, bf16[2,384,512]{2,1,0:T(8,128)(2,1)S(1)}, u32[]{:S(2)}, u32[]{:S(2)}) collective-permute-start(bf16[2,384,512]{2,1,0:T(8,128)(2,1)S(1)} %copy-done.65), channel_id=1, source_target_pairs={{0,1},{1,0},{2,3},{3,2},{4,5},{5,4},{6,7},{7,6},{8,9},{9,8},{10,11... | collective-permute-start | bytes 2359304 | tf_op jit(solution)/shard_map/ppermute | solution.py:71
  80.8 25.0 %collective-permute-start.17 = (bf16[2,384,512]{2,1,0:T(8,128)(2,1)S(1)}, bf16[2,384,512]{2,1,0:T(8,128)(2,1)S(1)}, u32[]{:S(2)}, u32[]{:S(2)}) collective-permute-start(bf16[2,384,512]{2,1,0:T(8,128)(2,1)S(1)} %copy-done.65), channel_id=1, source_target_pairs={{0,2},{1,3},{2,0},{3,1},{4,6},{5,7},{6,4},{7,5},{8,10},{9,11},{10,... | collective-permute-start | bytes 2359304 | tf_op jit(solution)/shard_map/ppermute | solution.py:71
  81.3 23.4 %collective-permute-start.13 = (bf16[1,96,1536]{2,1,0:T(8,128)(2,1)S(1)}, bf16[1,96,1536]{2,1,0:T(8,128)(2,1)S(1)}, u32[]{:S(2)}, u32[]{:S(2)}) collective-permute-start(bf16[1,96,1536]{2,1,0:T(8,128)(2,1)S(1)} %slice.170), channel_id=1, source_target_pairs={{0,1},{1,0},{2,3},{3,2},{4,5},{5,4},{6,7},{7,6},{8,9},{9,8},{10,11... | collective-permute-start | bytes 884744 | tf_op jit(solution)/shard_map/ppermute | solution.py:71
  82.4 23.4 %collective-permute-start.14 = (bf16[1,96,1536]{2,1,0:T(8,128)(2,1)S(1)}, bf16[1,96,1536]{2,1,0:T(8,128)(2,1)S(1)}, u32[]{:S(2)}, u32[]{:S(2)}) collective-permute-start(bf16[1,96,1536]{2,1,0:T(8,128)(2,1)S(1)} %slice.171), channel_id=1, source_target_pairs={{0,2},{1,3},{2,0},{3,1},{4,6},{5,7},{6,4},{7,5},{8,10},{9,11},{10,... | collective-permute-start | bytes 884744 | tf_op jit(solution)/shard_map/ppermute | solution.py:71
  83.6 22.3 %collective-permute-start.15 = (bf16[3,192,1536]{2,1,0:T(8,128)(2,1)S(1)}, bf16[3,192,1536]{2,1,0:T(8,128)(2,1)S(1)}, u32[]{:S(2)}, u32[]{:S(2)}) collective-permute-start(bf16[3,192,1536]{2,1,0:T(8,128)(2,1)S(1)} %pad_maximum_fusion), channel_id=1, source_target_pairs={{0,4},{4,0},{8,12},{12,8},{16,20},{20,16},{24,28},{28,24},{1,5},{5... | collective-permute-start | bytes 5308424 | tf_op jit(solution)/shard_map/ppermute | solution.py:62
  106.5 19.6 %collective-permute-start.20 = (bf16[2,384,512]{2,1,0:T(8,128)(2,1)S(1)}, bf16[2,384,512]{2,1,0:T(8,128)(2,1)S(1)}, u32[]{:S(2)}, u32[]{:S(2)}) collective-permute-start(bf16[2,384,512]{2,1,0:T(8,128)(2,1)S(1)} %copy-done.66), channel_id=1, source_target_pairs={{0,1},{1,0},{2,3},{3,2},{4,5},{5,4},{6,7},{7,6},{8,9},{9,8},{10,11... | collective-permute-start | bytes 2359304 | tf_op jit(solution)/shard_map/ppermute | solution.py:71
  107.2 19.2 %collective-permute-start.21 = (bf16[2,384,512]{2,1,0:T(8,128)(2,1)S(1)}, bf16[2,384,512]{2,1,0:T(8,128)(2,1)S(1)}, u32[]{:S(2)}, u32[]{:S(2)}) collective-permute-start(bf16[2,384,512]{2,1,0:T(8,128)(2,1)S(1)} %copy-done.66), channel_id=1, source_target_pairs={{0,2},{1,3},{2,0},{3,1},{4,6},{5,7},{6,4},{7,5},{8,10},{9,11},{10,... | collective-permute-start | bytes 2359304 | tf_op jit(solution)/shard_map/ppermute | solution.py:71
  118.2 44.1 %collective-permute-start.22 = (bf16[528,1536]{1,0:T(8,128)(2,1)}, bf16[528,1536]{1,0:T(8,128)(2,1)S(1)}, u32[]{:S(2)}, u32[]{:S(2)}) collective-permute-start(bf16[528,1536]{1,0:T(8,128)(2,1)} %get-tuple-element.312.refs_2_.refs_4_), channel_id=1, source_target_pairs={{0,8},{4,12},{8,16},{12,20},{16,24},{20,28},{24,0},{28,4},{1,9},{5... | collective-permute-start | bytes 4866056 | tf_op jit(solution)/shard_map/ppermute | solution.py:67
  126.5 39.6 %collective-permute-start.23 = (bf16[528,1536]{1,0:T(8,128)(2,1)}, bf16[528,1536]{1,0:T(8,128)(2,1)}, u32[]{:S(2)}, u32[]{:S(2)}) collective-permute-start(bf16[528,1536]{1,0:T(8,128)(2,1)} %get-tuple-element.312.refs_2_.refs_4_), channel_id=1, source_target_pairs={{0,4},{4,0},{8,12},{12,8},{16,20},{20,16},{24,28},{28,24},{1,5},{5... | collective-permute-start | bytes 4866056 | tf_op jit(solution)/shard_map/ppermute | solution.py:62
  126.5 11.6 %collective-permute-start.24 = (bf16[1,1,384,512]{3,2,1,0:T(8,128)(2,1)S(1)}, bf16[1,1,384,512]{3,2,1,0:T(8,128)(2,1)S(1)}, u32[]{:S(2)}, u32[]{:S(2)}) collective-permute-start(bf16[1,1,384,512]{3,2,1,0:T(8,128)(2,1)S(1)} %slice.174), channel_id=1, source_target_pairs={{0,1},{1,0},{2,3},{3,2},{4,5},{5,4},{6,7},{7,6},{8,9},{9,8},{10,11... | collective-permute-start | bytes 1179656 | tf_op jit(solution)/shard_map/ppermute | solution.py:71
  128.0 11.3 %collective-permute-start.25 = (bf16[1,1,384,512]{3,2,1,0:T(8,128)(2,1)S(1)}, bf16[1,1,384,512]{3,2,1,0:T(8,128)(2,1)S(1)}, u32[]{:S(2)}, u32[]{:S(2)}) collective-permute-start(bf16[1,1,384,512]{3,2,1,0:T(8,128)(2,1)S(1)} %slice.175), channel_id=1, source_target_pairs={{0,2},{1,3},{2,0},{3,1},{4,6},{5,7},{6,4},{7,5},{8,10},{9,11},{10,... | collective-permute-start | bytes 1179656 | tf_op jit(solution)/shard_map/ppermute | solution.py:71
  139.3 18.8 %collective-permute-start.29 = (bf16[2,512,384]{2,1,0:T(8,128)(2,1)S(1)}, bf16[2,512,384]{2,1,0:T(8,128)(2,1)S(1)}, u32[]{:S(2)}, u32[]{:S(2)}) collective-permute-start(bf16[2,512,384]{2,1,0:T(8,128)(2,1)S(1)} %copy-done.67), channel_id=1, source_target_pairs={{0,2},{1,3},{2,0},{3,1},{4,6},{5,7},{6,4},{7,5},{8,10},{9,11},{10,... | collective-permute-start | bytes 2359304 | tf_op jit(solution)/shard_map/ppermute | solution.py:71
  139.8 20.5 %collective-permute-start.28 = (bf16[2,512,384]{2,1,0:T(8,128)(2,1)S(1)}, bf16[2,512,384]{2,1,0:T(8,128)(2,1)S(1)}, u32[]{:S(2)}, u32[]{:S(2)}) collective-permute-start(bf16[2,512,384]{2,1,0:T(8,128)(2,1)S(1)} %copy-done.67), channel_id=1, source_target_pairs={{0,1},{1,0},{2,3},{3,2},{4,5},{5,4},{6,7},{7,6},{8,9},{9,8},{10,11... | collective-permute-start | bytes 2359304 | tf_op jit(solution)/shard_map/ppermute | solution.py:71
  141.5 27.3 %collective-permute-start.26 = (bf16[1,1,384,512]{3,2,1,0:T(8,128)(2,1)S(1)}, bf16[1,1,384,512]{3,2,1,0:T(8,128)(2,1)}, u32[]{:S(2)}, u32[]{:S(2)}) collective-permute-start(bf16[1,1,384,512]{3,2,1,0:T(8,128)(2,1)S(1)} %slice.176), channel_id=1, source_target_pairs={{0,1},{1,0},{2,3},{3,2},{4,5},{5,4},{6,7},{7,6},{8,9},{9,8},{10,11... | collective-permute-start | bytes 1179656 | tf_op jit(solution)/shard_map/ppermute | solution.py:71
  158.1 11.5 %collective-permute-start.27 = (bf16[1,1,384,512]{3,2,1,0:T(8,128)(2,1)S(1)}, bf16[1,1,384,512]{3,2,1,0:T(8,128)(2,1)}, u32[]{:S(2)}, u32[]{:S(2)}) collective-permute-start(bf16[1,1,384,512]{3,2,1,0:T(8,128)(2,1)S(1)} %slice.177), channel_id=1, source_target_pairs={{0,2},{1,3},{2,0},{3,1},{4,6},{5,7},{6,4},{7,5},{8,10},{9,11},{10,... | collective-permute-start | bytes 1179656 | tf_op jit(solution)/shard_map/ppermute | solution.py:71
  160.3 15.2 %collective-permute-start.30 = (bf16[1,1,512,384]{3,2,1,0:T(8,128)(2,1)S(1)}, bf16[1,1,512,384]{3,2,1,0:T(8,128)(2,1)S(1)}, u32[]{:S(2)}, u32[]{:S(2)}) collective-permute-start(bf16[1,1,512,384]{3,2,1,0:T(8,128)(2,1)S(1)} %slice.224), channel_id=1, source_target_pairs={{0,1},{1,0},{2,3},{3,2},{4,5},{5,4},{6,7},{7,6},{8,9},{9,8},{10,11... | collective-permute-start | bytes 1179656 | tf_op jit(solution)/shard_map/ppermute | solution.py:71
  163.5 12.7 %collective-permute-start.31 = (bf16[1,1,512,384]{3,2,1,0:T(8,128)(2,1)S(1)}, bf16[1,1,512,384]{3,2,1,0:T(8,128)(2,1)}, u32[]{:S(2)}, u32[]{:S(2)}) collective-permute-start(bf16[1,1,512,384]{3,2,1,0:T(8,128)(2,1)S(1)} %slice.225), channel_id=1, source_target_pairs={{0,2},{1,3},{2,0},{3,1},{4,6},{5,7},{6,4},{7,5},{8,10},{9,11},{10,... | collective-permute-start | bytes 1179656 | tf_op jit(solution)/shard_map/ppermute | solution.py:71
  166.1 41.9 %collective-permute-start.32 = (bf16[528,1536]{1,0:T(8,128)(2,1)}, bf16[528,1536]{1,0:T(8,128)(2,1)}, u32[]{:S(2)}, u32[]{:S(2)}) collective-permute-start(bf16[528,1536]{1,0:T(8,128)(2,1)} %copy-done.61), channel_id=1, source_target_pairs={{0,8},{4,12},{8,16},{12,20},{16,24},{20,28},{24,0},{28,4},{1,9},{5... | collective-permute-start | bytes 4866056 | tf_op jit(solution)/shard_map/ppermute | solution.py:67
  168.8 39.2 %collective-permute-start.33 = (bf16[528,1536]{1,0:T(8,128)(2,1)}, bf16[528,1536]{1,0:T(8,128)(2,1)}, u32[]{:S(2)}, u32[]{:S(2)}) collective-permute-start(bf16[528,1536]{1,0:T(8,128)(2,1)} %copy-done.61), channel_id=1, source_target_pairs={{0,4},{4,0},{8,12},{12,8},{16,20},{20,16},{24,28},{28,24},{1,5},{5... | collective-permute-start | bytes 4866056 | tf_op jit(solution)/shard_map/ppermute | solution.py:62
  208.1 37.9 %collective-permute-start.34 = (bf16[528,1536]{1,0:T(8,128)(2,1)}, bf16[528,1536]{1,0:T(8,128)(2,1)S(1)}, u32[]{:S(2)}, u32[]{:S(2)}) collective-permute-start(bf16[528,1536]{1,0:T(8,128)(2,1)} %collective-permute-done.32.refs_2_), channel_id=1, source_target_pairs={{0,8},{4,12},{8,16},{12,20},{16,24},{20,28},{24,0},{28,4},{1,9},{5... | collective-permute-start | bytes 4866056 | tf_op jit(solution)/shard_map/ppermute | solution.py:67
  209.5 36.5 %collective-permute-start.35 = (bf16[528,1536]{1,0:T(8,128)(2,1)}, bf16[528,1536]{1,0:T(8,128)(2,1)S(1)}, u32[]{:S(2)}, u32[]{:S(2)}) collective-permute-start(bf16[528,1536]{1,0:T(8,128)(2,1)} %collective-permute-done.32.refs_2_), channel_id=1, source_target_pairs={{0,4},{4,0},{8,12},{12,8},{16,20},{20,16},{24,28},{28,24},{1,5},{5... | collective-permute-start | bytes 4866056 | tf_op jit(solution)/shard_map/ppermute | solution.py:62
  246.1 39.0 %collective-permute-start.37 = (bf16[528,1536]{1,0:T(8,128)(2,1)S(1)}, bf16[528,1536]{1,0:T(8,128)(2,1)}, u32[]{:S(2)}, u32[]{:S(2)}) collective-permute-start(bf16[528,1536]{1,0:T(8,128)(2,1)S(1)} %collective-permute-done.34.refs_2_), channel_id=1, source_target_pairs={{0,4},{4,0},{8,12},{12,8},{16,20},{20,16},{24,28},{28,24},{1,5},{5... | collective-permute-start | bytes 4866056 | tf_op jit(solution)/shard_map/ppermute | solution.py:62
  253.1 39.3 %collective-permute-start.38 = (bf16[528,1536]{1,0:T(8,128)(2,1)S(1)}, bf16[528,1536]{1,0:T(8,128)(2,1)S(1)}, u32[]{:S(2)}, u32[]{:S(2)}) collective-permute-start(bf16[528,1536]{1,0:T(8,128)(2,1)S(1)} %add_convert_fusion.2), channel_id=1, source_target_pairs={{0,8},{4,12},{8,16},{12,20},{16,24},{20,28},{24,0},{28,4},{1,9},{5... | collective-permute-start | bytes 4866056 | tf_op jit(solution)/shard_map/ppermute | solution.py:67
  298.2 39.3 %collective-permute-start.40 = (bf16[528,1536]{1,0:T(8,128)(2,1)S(1)}, bf16[528,1536]{1,0:T(8,128)(2,1)S(1)}, u32[]{:S(2)}, u32[]{:S(2)}) collective-permute-start(bf16[528,1536]{1,0:T(8,128)(2,1)S(1)} %add_convert_fusion.1), channel_id=1, source_target_pairs={{0,8},{4,12},{8,16},{12,20},{16,24},{20,28},{24,0},{28,4},{1,9},{5... | collective-permute-start | bytes 4866056 | tf_op jit(solution)/shard_map/ppermute | solution.py:67
  337.5 56.1 %collective-permute-start.45 = (bf16[528,1536]{1,0:T(8,128)(2,1)}, bf16[528,1536]{1,0:T(8,128)(2,1)}, u32[]{:S(2)}, u32[]{:S(2)}) collective-permute-start(bf16[528,1536]{1,0:T(8,128)(2,1)} %get-tuple-element.394), channel_id=1, source_target_pairs={{0,4},{4,0},{8,12},{12,8},{16,20},{20,16},{24,28},{28,24},{1,5},{5... | collective-permute-start | bytes 4866056 | tf_op jit(solution)/shard_map/ppermute | solution.py:62
  345.5 46.7 %collective-permute-start.42 = (bf16[528,1536]{1,0:T(8,128)(2,1)S(1)}, bf16[528,1536]{1,0:T(8,128)(2,1)S(1)}, u32[]{:S(2)}, u32[]{:S(2)}) collective-permute-start(bf16[528,1536]{1,0:T(8,128)(2,1)S(1)} %add_convert_fusion), channel_id=1, source_target_pairs={{0,8},{4,12},{8,16},{12,20},{16,24},{20,28},{24,0},{28,4},{1,9},{5... | collective-permute-start | bytes 4866056 | tf_op jit(solution)/shard_map/ppermute | solution.py:67
  366.4 24.9 %collective-permute-start.43 = (bf16[2,384,512]{2,1,0:T(8,128)(2,1)S(1)}, bf16[2,384,512]{2,1,0:T(8,128)(2,1)S(1)}, u32[]{:S(2)}, u32[]{:S(2)}) collective-permute-start(bf16[2,384,512]{2,1,0:T(8,128)(2,1)S(1)} %bitcast.77), channel_id=1, source_target_pairs={{0,1},{1,0},{2,3},{3,2},{4,5},{5,4},{6,7},{7,6},{8,9},{9,8},{10,11... | collective-permute-start | bytes 2359304 | tf_op jit(solution)/shard_map/ppermute | solution.py:71
  367.7 24.5 %collective-permute-start.44 = (bf16[2,384,512]{2,1,0:T(8,128)(2,1)S(1)}, bf16[2,384,512]{2,1,0:T(8,128)(2,1)S(1)}, u32[]{:S(2)}, u32[]{:S(2)}) collective-permute-start(bf16[2,384,512]{2,1,0:T(8,128)(2,1)S(1)} %bitcast.76), channel_id=1, source_target_pairs={{0,2},{1,3},{2,0},{3,1},{4,6},{5,7},{6,4},{7,5},{8,10},{9,11},{10,... | collective-permute-start | bytes 2359304 | tf_op jit(solution)/shard_map/ppermute | solution.py:71
  390.8 19.3 %collective-permute-start.46 = (bf16[2,384,512]{2,1,0:T(8,128)(2,1)}, bf16[2,384,512]{2,1,0:T(8,128)(2,1)}, u32[]{:S(2)}, u32[]{:S(2)}) collective-permute-start(bf16[2,384,512]{2,1,0:T(8,128)(2,1)} %bitcast.37), channel_id=1, source_target_pairs={{0,1},{1,0},{2,3},{3,2},{4,5},{5,4},{6,7},{7,6},{8,9},{9,8},{10,11... | collective-permute-start | bytes 2359304 | tf_op jit(solution)/shard_map/ppermute | solution.py:71
  391.3 19.1 %collective-permute-start.47 = (bf16[2,384,512]{2,1,0:T(8,128)(2,1)}, bf16[2,384,512]{2,1,0:T(8,128)(2,1)}, u32[]{:S(2)}, u32[]{:S(2)}) collective-permute-start(bf16[2,384,512]{2,1,0:T(8,128)(2,1)} %bitcast.38), channel_id=1, source_target_pairs={{0,2},{1,3},{2,0},{3,1},{4,6},{5,7},{6,4},{7,5},{8,10},{9,11},{10,... | collective-permute-start | bytes 2359304 | tf_op jit(solution)/shard_map/ppermute | solution.py:71
  410.4 32.9 %collective-permute-start.48 = (bf16[1536,896]{1,0:T(8,128)(2,1)}, bf16[1536,896]{1,0:T(8,128)(2,1)}, u32[]{:S(2)}, u32[]{:S(2)}) collective-permute-start(bf16[1536,896]{1,0:T(8,128)(2,1)} %get-tuple-element.412), channel_id=1, source_target_pairs={{0,4},{4,0},{8,12},{12,8},{16,20},{20,16},{24,28},{28,24},{1,5},{5... | collective-permute-start | bytes 8257544 | tf_op jit(solution)/shard_map/ppermute | solution.py:62
  410.5 32.7 %collective-permute-start.49 = (bf16[1,384,512]{2,1,0:T(8,128)(2,1)S(1)}, bf16[1,384,512]{2,1,0:T(8,128)(2,1)S(1)}, u32[]{:S(2)}, u32[]{:S(2)}) collective-permute-start(bf16[1,384,512]{2,1,0:T(8,128)(2,1)S(1)} %add_convert_fusion.11), channel_id=1, source_target_pairs={{0,1},{1,0},{2,3},{3,2},{4,5},{5,4},{6,7},{7,6},{8,9},{9,8},{10,11... | collective-permute-start | bytes 1179656 | tf_op jit(solution)/shard_map/ppermute | solution.py:71
  412.1 31.1 %collective-permute-start.50 = (bf16[1,384,512]{2,1,0:T(8,128)(2,1)S(1)}, bf16[1,384,512]{2,1,0:T(8,128)(2,1)S(1)}, u32[]{:S(2)}, u32[]{:S(2)}) collective-permute-start(bf16[1,384,512]{2,1,0:T(8,128)(2,1)S(1)} %add_convert_fusion.10), channel_id=1, source_target_pairs={{0,2},{1,3},{2,0},{3,1},{4,6},{5,7},{6,4},{7,5},{8,10},{9,11},{10,... | collective-permute-start | bytes 1179656 | tf_op jit(solution)/shard_map/ppermute | solution.py:71
  413.9 29.3 %collective-permute-start.51 = (bf16[1,384,512]{2,1,0:T(8,128)(2,1)S(1)}, bf16[1,384,512]{2,1,0:T(8,128)(2,1)S(1)}, u32[]{:S(2)}, u32[]{:S(2)}) collective-permute-start(bf16[1,384,512]{2,1,0:T(8,128)(2,1)S(1)} %add_convert_fusion.9), channel_id=1, source_target_pairs={{0,1},{1,0},{2,3},{3,2},{4,5},{5,4},{6,7},{7,6},{8,9},{9,8},{10,11... | collective-permute-start | bytes 1179656 | tf_op jit(solution)/shard_map/ppermute | solution.py:71
  415.9 27.4 %collective-permute-start.52 = (bf16[1,384,512]{2,1,0:T(8,128)(2,1)S(1)}, bf16[1,384,512]{2,1,0:T(8,128)(2,1)S(1)}, u32[]{:S(2)}, u32[]{:S(2)}) collective-permute-start(bf16[1,384,512]{2,1,0:T(8,128)(2,1)S(1)} %add_convert_fusion.8), channel_id=1, source_target_pairs={{0,2},{1,3},{2,0},{3,1},{4,6},{5,7},{6,4},{7,5},{8,10},{9,11},{10,... | collective-permute-start | bytes 1179656 | tf_op jit(solution)/shard_map/ppermute | solution.py:71
  455.6 32.8 %collective-permute-start.54 = (bf16[384,1536]{1,0:T(8,128)(2,1)}, bf16[384,1536]{1,0:T(8,128)(2,1)}, u32[]{:S(2)}, u32[]{:S(2)}) collective-permute-start(bf16[384,1536]{1,0:T(8,128)(2,1)} %get-tuple-element.438), channel_id=1, source_target_pairs={{0,1},{1,0},{2,3},{3,2},{4,5},{5,4},{6,7},{7,6},{8,9},{9,8},{10,11... | collective-permute-start | bytes 3538952 | tf_op jit(solution)/shard_map/ppermute | solution.py:71
  457.0 31.4 %collective-permute-start.55 = (bf16[384,1536]{1,0:T(8,128)(2,1)S(1)}, bf16[384,1536]{1,0:T(8,128)(2,1)}, u32[]{:S(2)}, u32[]{:S(2)}) collective-permute-start(bf16[384,1536]{1,0:T(8,128)(2,1)S(1)} %get-tuple-element.439), channel_id=1, source_target_pairs={{0,2},{1,3},{2,0},{3,1},{4,6},{5,7},{6,4},{7,5},{8,10},{9,11},{10,... | collective-permute-start | bytes 3538952 | tf_op jit(solution)/shard_map/ppermute | solution.py:71
  490.5 16.0 %collective-permute-start.57 = (bf16[192,1536]{1,0:T(8,128)(2,1)}, bf16[192,1536]{1,0:T(8,128)(2,1)}, u32[]{:S(2)}, u32[]{:S(2)}) collective-permute-start(bf16[192,1536]{1,0:T(8,128)(2,1)} %add_convert_fusion.5), channel_id=1, source_target_pairs={{0,1},{1,0},{2,3},{3,2},{4,5},{5,4},{6,7},{7,6},{8,9},{9,8},{10,11... | collective-permute-start | bytes 1769480 | tf_op jit(solution)/shard_map/ppermute | solution.py:71
  493.2 15.8 %collective-permute-start.58 = (bf16[192,1536]{1,0:T(8,128)(2,1)}, bf16[192,1536]{1,0:T(8,128)(2,1)}, u32[]{:S(2)}, u32[]{:S(2)}) collective-permute-start(bf16[192,1536]{1,0:T(8,128)(2,1)} %add_convert_fusion.4), channel_id=1, source_target_pairs={{0,2},{1,3},{2,0},{3,1},{4,6},{5,7},{6,4},{7,5},{8,10},{9,11},{10,... | collective-permute-start | bytes 1769480 | tf_op jit(solution)/shard_map/ppermute | solution.py:71
  511.4 30.0 %collective-permute-start.59 = (bf16[384,768]{1,0:T(8,128)(2,1)S(1)}, bf16[384,768]{1,0:T(8,128)(2,1)S(1)}, u32[]{:S(2)}, u32[]{:S(2)}) collective-permute-start(bf16[384,768]{1,0:T(8,128)(2,1)S(1)} %get-tuple-element.462), channel_id=1, source_target_pairs={{0,1},{1,0},{2,3},{3,2},{4,5},{5,4},{6,7},{7,6},{8,9},{9,8},{10,11... | collective-permute-start | bytes 1769480 | tf_op jit(solution)/shard_map/ppermute | solution.py:71
  512.8 28.6 %collective-permute-start.60 = (bf16[384,768]{1,0:T(8,128)(2,1)S(1)}, bf16[384,768]{1,0:T(8,128)(2,1)S(1)}, u32[]{:S(2)}, u32[]{:S(2)}) collective-permute-start(bf16[384,768]{1,0:T(8,128)(2,1)S(1)} %get-tuple-element.463), channel_id=1, source_target_pairs={{0,2},{1,3},{2,0},{3,1},{4,6},{5,7},{6,4},{7,5},{8,10},{9,11},{10,... | collective-permute-start | bytes 1769480 | tf_op jit(solution)/shard_map/ppermute | solution.py:71
  514.3 24.7 %collective-permute-start.61 = (bf16[96,1536]{1,0:T(8,128)(2,1)S(1)}, bf16[96,1536]{1,0:T(8,128)(2,1)S(1)}, u32[]{:S(2)}, u32[]{:S(2)}) collective-permute-start(bf16[96,1536]{1,0:T(8,128)(2,1)S(1)} %get-tuple-element.554), channel_id=1, source_target_pairs={{0,8},{4,12},{8,16},{12,20},{16,24},{20,28},{24,0},{28,4},{1,9},{5... | collective-permute-start | bytes 884744 | tf_op jit(solution)/shard_map/ppermute | solution.py:185
  514.4 27.0 %collective-permute-start.62 = (bf16[96,1536]{1,0:T(8,128)(2,1)S(1)}, bf16[96,1536]{1,0:T(8,128)(2,1)S(1)}, u32[]{:S(2)}, u32[]{:S(2)}) collective-permute-start(bf16[96,1536]{1,0:T(8,128)(2,1)S(1)} %get-tuple-element.553), channel_id=1, source_target_pairs={{0,16},{4,20},{8,24},{12,28},{16,0},{20,4},{24,8},{28,12},{1,17},{... | collective-permute-start | bytes 884744 | tf_op jit(solution)/shard_map/ppermute | solution.py:185
  518.4 23.0 %collective-permute-start.63 = (bf16[96,1536]{1,0:T(8,128)(2,1)S(1)}, bf16[96,1536]{1,0:T(8,128)(2,1)S(1)}, u32[]{:S(2)}, u32[]{:S(2)}) collective-permute-start(bf16[96,1536]{1,0:T(8,128)(2,1)S(1)} %get-tuple-element.552), channel_id=1, source_target_pairs={{0,24},{4,28},{8,0},{12,4},{16,8},{20,12},{24,16},{28,20},{1,25},{... | collective-permute-start | bytes 884744 | tf_op jit(solution)/shard_map/ppermute | solution.py:185
  541.6 18.7 %collective-permute-start.66 = (bf16[96,1536]{1,0:T(8,128)(2,1)S(1)}, bf16[96,1536]{1,0:T(8,128)(2,1)S(1)}, u32[]{:S(2)}, u32[]{:S(2)}) collective-permute-start(bf16[96,1536]{1,0:T(8,128)(2,1)S(1)} %add_convert_fusion.12), channel_id=1, source_target_pairs={{0,8},{4,12},{8,16},{12,20},{16,24},{20,28},{24,0},{28,4},{1,9},{5... | collective-permute-start | bytes 884744 | tf_op jit(solution)/shard_map/ppermute | solution.py:185
  548.2 20.0 %collective-permute-start.67 = (bf16[96,1536]{1,0:T(8,128)(2,1)S(1)}, bf16[96,1536]{1,0:T(8,128)(2,1)S(1)}, u32[]{:S(2)}, u32[]{:S(2)}) collective-permute-start(bf16[96,1536]{1,0:T(8,128)(2,1)S(1)} %add_convert_fusion.12), channel_id=1, source_target_pairs={{0,16},{4,20},{8,24},{12,28},{16,0},{20,4},{24,8},{28,12},{1,17},{... | collective-permute-start | bytes 884744 | tf_op jit(solution)/shard_map/ppermute | solution.py:185
  549.2 18.9 %collective-permute-start.68 = (bf16[96,1536]{1,0:T(8,128)(2,1)S(1)}, bf16[96,1536]{1,0:T(8,128)(2,1)S(1)}, u32[]{:S(2)}, u32[]{:S(2)}) collective-permute-start(bf16[96,1536]{1,0:T(8,128)(2,1)S(1)} %add_convert_fusion.12), channel_id=1, source_target_pairs={{0,24},{4,28},{8,0},{12,4},{16,8},{20,12},{24,16},{28,20},{1,25},{... | collective-permute-start | bytes 884744 | tf_op jit(solution)/shard_map/ppermute | solution.py:185
  569.2 13.3 %collective-permute-start.69 = (bf16[96,768]{1,0:T(8,128)(2,1)S(1)}, bf16[96,768]{1,0:T(8,128)(2,1)S(1)}, u32[]{:S(2)}, u32[]{:S(2)}) collective-permute-start(bf16[96,768]{1,0:T(8,128)(2,1)S(1)} %get-tuple-element.558), channel_id=1, source_target_pairs={{0,8},{4,12},{8,16},{12,20},{16,24},{20,28},{24,0},{28,4},{1,9},{5... | collective-permute-start | bytes 442376 | tf_op jit(solution)/shard_map/ppermute | solution.py:185
  578.5 18.9 %collective-permute-start.72 = (bf16[2,512,384]{2,1,0:T(8,128)(2,1)S(1)}, bf16[2,512,384]{2,1,0:T(8,128)(2,1)S(1)}, u32[]{:S(2)}, u32[]{:S(2)}) collective-permute-start(bf16[2,512,384]{2,1,0:T(8,128)(2,1)S(1)} %bitcast.75), channel_id=1, source_target_pairs={{0,1},{1,0},{2,3},{3,2},{4,5},{5,4},{6,7},{7,6},{8,9},{9,8},{10,11... | collective-permute-start | bytes 2359304 | tf_op jit(solution)/shard_map/ppermute | solution.py:71
  580.0 18.6 %collective-permute-start.73 = (bf16[2,512,384]{2,1,0:T(8,128)(2,1)S(1)}, bf16[2,512,384]{2,1,0:T(8,128)(2,1)S(1)}, u32[]{:S(2)}, u32[]{:S(2)}) collective-permute-start(bf16[2,512,384]{2,1,0:T(8,128)(2,1)S(1)} %bitcast.74), channel_id=1, source_target_pairs={{0,2},{1,3},{2,0},{3,1},{4,6},{5,7},{6,4},{7,5},{8,10},{9,11},{10,... | collective-permute-start | bytes 2359304 | tf_op jit(solution)/shard_map/ppermute | solution.py:71
  598.7 14.2 %collective-permute-start.77 = (bf16[1,512,384]{2,1,0:T(8,128)(2,1)S(1)}, bf16[1,512,384]{2,1,0:T(8,128)(2,1)S(1)}, u32[]{:S(2)}, u32[]{:S(2)}) collective-permute-start(bf16[1,512,384]{2,1,0:T(8,128)(2,1)S(1)} %add_convert_fusion.7), channel_id=1, source_target_pairs={{0,1},{1,0},{2,3},{3,2},{4,5},{5,4},{6,7},{7,6},{8,9},{9,8},{10,11... | collective-permute-start | bytes 1179656 | tf_op jit(solution)/shard_map/ppermute | solution.py:71
  599.4 13.5 %collective-permute-start.78 = (bf16[1,512,384]{2,1,0:T(8,128)(2,1)S(1)}, bf16[1,512,384]{2,1,0:T(8,128)(2,1)S(1)}, u32[]{:S(2)}, u32[]{:S(2)}) collective-permute-start(bf16[1,512,384]{2,1,0:T(8,128)(2,1)S(1)} %add_convert_fusion.6), channel_id=1, source_target_pairs={{0,2},{1,3},{2,0},{3,1},{4,6},{5,7},{6,4},{7,5},{8,10},{9,11},{10,... | collective-permute-start | bytes 1179656 | tf_op jit(solution)/shard_map/ppermute | solution.py:71
  (92 other events, 1112.4 us)
Sparse Core Ops, SparseCore 0:
  9.7 124.3 all-gather.1
  393.8 134.2 reduce-scatter.1

commit v4 on v3

--- a/solution.py
+++ b/solution.py
@@ -761,61 +761,53 @@
     )(order, *operands)
 
 
-def expert_kernel(counts, expert_count, order_ref, place_ref, xa_ref, xb_ref, u_ref, *rest):
+def expert_kernel(counts, expert_count, order_ref, place_ref, xa_ref, u_ref, *rest):
     pieces, more = counts
     gates_p, ups_p, downs_p = (rest[i * pieces : (i + 1) * pieces] for i in range(3))
     rest = rest[3 * pieces + more :]
-    (gta_ref, gtb_ref, out_ref, x_ref, mid_ref, sides_ref, wg_ref, wu_ref, wd_ref, sems) = rest
+    (gt_ref, out_ref, x_ref, mid_ref, sides_ref, wg_ref, wu_ref, wd_ref, sems) = rest
     low = jnp.bfloat16
     extra = extra_rows(expert_count)
     step = pl.program_id(0)
-    half = pl.num_programs(0) // 2
-    load = piece_copies(gates_p, order_ref, wg_ref, sems.at[0], 1, 0)
-    load += piece_copies(ups_p, order_ref, wu_ref, sems.at[0], 1, 0)
-    load_down = piece_copies(downs_p, order_ref, wd_ref, sems.at[1], 2, 0)
+    loads = [
+        piece_copies(gates_p, order_ref, wg_ref, sems.at[0], 1, 0),
+        piece_copies(ups_p, order_ref, wu_ref, sems.at[1], 1, 0),
+        piece_copies(downs_p, order_ref, wd_ref, sems.at[2], 2, 0),
+    ]
 
     @pl.when(step == 0)
     def _():
-        for copy in load + load_down:
-            copy.start()
-
-    first = step < half
-    table = jnp.where(first, xa_ref[TILE:, :], xb_ref[TILE:, :])
-
-    @pl.when(first)
-    def _():
-        x_ref[...] = xa_ref[:TILE, :]
-
-    @pl.when(jnp.logical_not(first))
-    def _():
-        x_ref[...] = xb_ref[:TILE, :]
-
-    @pl.when(step == 0)
-    def _():
-        for copy in load + load_down:
-            copy.wait()
-
-    rows, cots = x_ref[...], u_ref[...]
+        for load in loads:
+            for copy in load:
+                copy.start()
+
+    def arrive(number):
+        @pl.when(step == 0)
+        def _():
+            for copy in loads[number]:
+                copy.wait()
+
+    rows, table, cots = xa_ref[:TILE, :], xa_ref[TILE:, :], u_ref[...]
+    x_ref[...] = rows
     row = lax.broadcasted_iota(jnp.int32, (extra, 128), 0)
     lane = lax.broadcasted_iota(jnp.int32, (extra, 128), 1)
-    expert = place_ref[2] * 2 + lane
+    expert = place_ref[1] * 2 + lane
     picks = []
     for block in range(expert_count // extra):
         hit = (lane < 2) & (row == expert - block * extra)
         picks.append(jnp.where(hit, 1.0, 0.0).astype(low))
-    gates_wide = None
-    for block, pick in enumerate(picks):
-        for part in range(2):
-            at = (2 * block + part) * TILE
-            value = dot(table[:, at : at + TILE], pick, TN)
-            gates_wide = value if gates_wide is None else gates_wide + value
+    gates_wide = table_values(table, picks)
+    arrive(0)
+    gate_ins = [dot(rows, wg_ref[l], NN) for l in range(2)]
+    arrive(1)
+    up_ins = [dot(rows, wu_ref[l], NN) for l in range(2)]
+    arrive(2)
     out = None
     taken = None
     sums = []
     for l in range(2):
         gates = gates_wide[:, l : l + 1]
-        gate_in = dot(rows, wg_ref[l], NN)
-        up_in = dot(rows, wu_ref[l], NN)
+        gate_in, up_in = gate_ins[l], up_ins[l]
         back = dot(cots, wd_ref[l], NT)
         sigma = 1.0 / (1.0 + jnp.exp(-gate_in))
         active = gate_in * sigma
@@ -833,53 +825,34 @@
         part = dot(grad_gate, wg_ref[l], NT) + dot(grad_up, wu_ref[l], NT)
         taken = part if taken is None else taken + part
     out_ref[...] = out.astype(low)
-    taken_low = taken.astype(low)
+    gt_ref[:TILE, :] = taken.astype(low)
     wide = lax.broadcasted_iota(jnp.int32, (TILE, 128), 1)
     sums = jnp.where(wide == 0, sums[0], jnp.where(wide == 1, sums[1], 0.0))
-    high = sums.astype(low)
-    parts = (high, (sums - high.astype(jnp.float32)).astype(low))
-    columns = [dot(pick, value, NT).astype(low) for pick in picks for value in parts]
-    left = rows.shape[1] - TILE * len(columns)
-    if left:
-        columns.append(jnp.zeros((extra, left), low))
-    columns = jnp.concatenate(columns, axis=1)
-
-    @pl.when(first)
-    def _():
-        gta_ref[:TILE, :] = taken_low
-        gta_ref[TILE:, :] = columns
-
-    @pl.when(jnp.logical_not(first))
-    def _():
-        gtb_ref[:TILE, :] = taken_low
-        gtb_ref[TILE:, :] = columns
-
-
-def expert_chunk(order, place, xa, xb, cots, gates, ups, downs, expert_count, kept):
+    gt_ref[TILE:, :] = table_rows(sums, picks, rows.shape[1])
+
+
+def expert_chunk(order, place, xa, cots, gates, ups, downs, expert_count, kept):
     total, width = cots.shape
     devices = lax.axis_size("expert")
     tokens = total // devices
     hidden = gates[0].shape[-1]
-    half = tokens // TILE
-    steps = 2 * half
+    steps = tokens // TILE
     low = jnp.bfloat16
     tall = TILE + extra_rows(expert_count)
-    first = pl.BlockSpec((tall, width), lambda i, o, p: (jnp.minimum(i, half - 1), 0))
-    second = pl.BlockSpec((tall, width), lambda i, o, p: (jnp.maximum(i - half, 0), 0))
-    where = lambda i, p: jnp.where(i < half, p[0] * half + i, p[1] * half + i - half)
+    own = pl.BlockSpec((tall, width), lambda i, o, p: (i, 0))
     anywhere = pl.BlockSpec(memory_space=pltpu.HBM)
-    big_row = pl.BlockSpec((TILE, width), lambda i, o, p: (where(i, p), 0))
-    big = lambda n: pl.BlockSpec((n, TILE, hidden), lambda i, o, p: (0, where(i, p), 0))
-    single = jax.ShapeDtypeStruct((half * tall, width), low)
+    big_row = pl.BlockSpec((TILE, width), lambda i, o, p: (p[0] * steps + i, 0))
+    big = lambda n: pl.BlockSpec((n, TILE, hidden), lambda i, o, p: (0, p[0] * steps + i, 0))
+    single = jax.ShapeDtypeStruct((steps * tall, width), low)
     shapes = [jax.ShapeDtypeStruct((total, width), low)] * 2
     shapes += [jax.ShapeDtypeStruct((n, total, hidden), low) for n in (2, 4)]
-    operands = [order, place, xa, xb, cots, *gates, *ups, *downs]
-    in_specs = [first, second, big_row] + [anywhere] * (3 * len(gates))
+    operands = [order, place, xa, cots, *gates, *ups, *downs]
+    in_specs = [own, big_row] + [anywhere] * (3 * len(gates))
     aliases = {}
     more = 0
     if kept is not None:
         more = len(shapes)
-        aliases = {len(operands) + i: 2 + i for i in range(more)}
+        aliases = {len(operands) + i: 1 + i for i in range(more)}
         operands += list(kept)
         in_specs += [anywhere] * more
     res = pl.pallas_call(
@@ -888,21 +861,21 @@
             num_scalar_prefetch=2,
             grid=(steps,),
             in_specs=in_specs,
-            out_specs=[first, second, big_row, big_row, big(2), big(4)],
+            out_specs=[own, big_row, big_row, big(2), big(4)],
             scratch_shapes=[
                 pltpu.VMEM((2, width, hidden), low),
                 pltpu.VMEM((2, width, hidden), low),
                 pltpu.VMEM((2, hidden, width), low),
-                pltpu.SemaphoreType.DMA((2,)),
+                pltpu.SemaphoreType.DMA((3,)),
             ],
         ),
-        out_shape=[single] * 2 + shapes,
+        out_shape=[single] + shapes,
         input_output_aliases=aliases,
         compiler_params=pltpu.CompilerParams(vmem_limit_bytes=58 * 2**20),
-        cost_estimate=pl.CostEstimate(flops=81 * 10**9, bytes_accessed=8 * 10**6, transcendentals=0),
+        cost_estimate=pl.CostEstimate(flops=50 * 10**9, bytes_accessed=4 * 10**6, transcendentals=0),
         name="expert_chunk",
     )(*operands)
-    return res[:2], res[2:]
+    return res[0], res[1:]
 
 
 def wide_grad_kernel(on_rows, left_ref, right_ref, out_ref, acc_ref):
@@ -1116,16 +1089,22 @@
         beside_next = swap_core(rows[step + 1]) if step + 1 < chips else None
         here = rows[step]
         if step > 1:
-            here, total = lax.optimization_barrier((here, total))
+            here, beside, total = lax.optimization_barrier((here, beside, total))
         sent = next_chip(total) if step > 1 else None
-        place = jnp.stack([(me - 2 * step) % (2 * chips), (me - 2 * step) % (2 * chips) ^ 1, me])
-        parts, kept = expert_chunk(
-            order, place.astype(jnp.int32), here, beside, cots, gates_p, ups_p, downs_p, expert_count, kept
+        source = (me - 2 * step) % (2 * chips)
+        place = lambda at: jnp.stack([at, me]).astype(jnp.int32)
+        run = lambda at, value, kept: expert_chunk(
+            order, place(at), value, cots, gates_p, ups_p, downs_p, expert_count, kept
         )
-        parts, kept, ahead, beside, sent = lax.optimization_barrier((parts, kept, ahead, beside_next, sent))
+        other, kept = run(source ^ 1, beside, kept)
+        other = swap_core(other)
+        mine, kept = run(source, here, kept)
+        mine, kept, ahead, beside, sent, other = lax.optimization_barrier(
+            (mine, kept, ahead, beside_next, sent, other)
+        )
         if ahead is not None:
             rows.append(ahead)
-        pair = (parts[0], swap_core(parts[1]))
+        pair = (mine, other)
         if step == 0:
             last = pair
         else:

time: 645 us -> 636 us (0.986)
  waiting for transfers between devices: 166 us -> 129 us
  Pallas kernels: 311 us -> 327 us
    pallas_call x4 -> x8, Pallas kernels: 127 us -> 144 us  [expert_chunk(): pl.pallas_call(lambda *refs: expert_kernel((len(gates), more), expert_cou...]
    ppermute x42, waiting for transfers between devices: 106 us -> 91.9 us  [across(): return lax.ppermute(value, 'shard', [(i, i ^ mask) for i in range(4)])]
    ppermute x21, waiting for transfers between devices: 16.6 us -> 3.22 us  [swap_core(): return lax.ppermute(value, 'expert', [(i, i ^ 1) for i in range(count)])]
    ppermute x6, waiting for transfers between devices: 20.2 us -> 10.6 us  [next_chip(): lax.ppermute(value, 'expert', [(i, (i + 2) % count) for i in range(count)])]
    unnamed x159 -> x169, local copies, waits for them, and re-layouts: 18.6 us -> 20.9 us
  transfers between devices with their start and end apart: 83 -> 83, of which waited for: 38 -> 31; matrix products, arithmetic and copies ran while one was open for 6% -> 6% of each run, Pallas kernels for 49% -> 52%
where the time goes in v4:
time: 636 us; the launch traced here: 628 us
  Pallas kernels  327 us (51%)
  waiting for transfers between devices  129 us (20%)
  starting transfers between devices  85.4 us (13%)
  other arithmetic  42.1 us (7%)
  local copies, waits for them, and re-layouts  27.8 us (4%)
  between operations  16 us (3%)
    pallas_call x8, Pallas kernels, expert_chunk(): pl.pallas_call(lambda *refs: expert_kernel((len(gates), more), expert_cou...  144 us
    ppermute x42, waiting for transfers between devices, across(): return lax.ppermute(value, 'shard', [(i, i ^ mask) for i in range(4)])  91.9 us
    pallas_call x3, Pallas kernels, grad_exchange(): pl.pallas_call(lambda *refs: sorted_grad_kernel(on_rows, half, *refs), gr...  63 us
    pallas_call x2, Pallas kernels, attend_back(): pl.pallas_call(lambda *refs: attend_back_kernel(mine, (len(proj), len(mix...  56.8 us
    ppermute x42, starting transfers between devices, across(): return lax.ppermute(value, 'shard', [(i, i ^ mask) for i in range(4)])  50.3 us
    ppermute x12, starting transfers between devices, chip_ahead(): lax.ppermute(value, 'expert', [(i, (i + 2 * distance) % count) for i in r...  28.3 us
    pallas_call x2, Pallas kernels, attend(): pl.pallas_call(lambda *refs: attend_kernel(len(mixer_p) // 2, call, *refs...  24.7 us
    ppermute x12, waiting for transfers between devices, chip_ahead(): lax.ppermute(value, 'expert', [(i, (i + 2 * distance) % count) for i in r...  23 us
  transfers between devices with their start and end apart: 83, of which 31 were waited for; matrix products, arithmetic and copies ran while one was open for 6% of the time, Pallas kernels for 52%

profile of v4, /device:TPU:0, one launch (start us, length us, event | category | flops | bytes accessed | tf_op | source)
XLA Modules:
  0.0 627.7 jit_solution(1446022183352651151)
XLA Ops:
  8.6 2.9 own_groups.1
  11.6 2.9 collective-permute-start
  18.9 1.6 broadcast_in_dim.114
  22.2 14.6 %collective-permute-done.4 = bf16[18,384]{1,0:T(8,128)(2,1)S(1)} collective-permute-done((bf16[18,384]{1,0:T(8,128)(2,1)S(1)}, bf16[18,384]{1,0:T(8,128)(2,1)S(1)}, u32[]{:S(2)}, u32[]{:S(2)}) %collective-permute-start.4) | collective-permute-done | bytes 13856 | tf_op jit(solution)/shard_map/ppermute | solution.py:71
  37.5 1.8 collective-permute-start.5
  39.8 1.9 collective-permute-done.5
  46.8 1.7 collective-permute-start.2
  51.6 8.5 %collective-permute-done.2.refs_9_.refs_22_ = bf16[1,192,1280]{2,1,0:T(8,128)(2,1)} collective-permute-done((bf16[1,192,1280]{2,1,0:T(8,128)(2,1)S(1)}, bf16[1,192,1280]{2,1,0:T(8,128)(2,1)}, u32[]{:S(2)}, u32[]{:S(2)}) %collective-permute-start.2) | collective-permute-done | bytes 491552 | tf_op jit(solution)/shard_map/ppermute | solution.py:71
  63.5 1.7 collective-permute-start.7
  69.1 12.2 %attend.2 = (bf16[512,1536]{1,0:T(8,128)(2,1)}, bf16[512,1536]{1,0:T(8,128)(2,1)}, bf16[512,512]{1,0:T(8,128)(2,1)}, bf16[512,512]{1,0:T(8,128)(2,1)}, f32[4,512,8]{2,1,0:T(8,128)}) custom-call(s32[6]{0:T(128)S(1)} %copy-done.14, s32[2]{0:T(128)S(1)} %get-tuple-element.601.refs_1_.refs_0_, bf16[512,1536]{1,0:T(8,128)(2,1)S(1)} %copy-done.5, ...), custom_call_target="tpu_custom_call" | custom-call | flops 48000000000 | bytes 8000000 | tf_op jit(solution)/shard_map/attend/pallas_call | solution.py:301
  85.9 12.5 %attend.3 = (bf16[512,1536]{1,0:T(8,128)(2,1)}, bf16[512,1536]{1,0:T(8,128)(2,1)}, bf16[512,512]{1,0:T(8,128)(2,1)}, bf16[512,512]{1,0:T(8,128)(2,1)}, f32[4,512,8]{2,1,0:T(8,128)}) custom-call(s32[6]{0:T(128)S(1)} %copy-done.14, ...), custom_call_target="tpu_custom_call", output_to_operand_aliasing={{0}: (16, {}), {1}: (17, {}), {2}: (18, {}), {3}: (19, {}),... | custom-call | flops 48000000000 | bytes 8000000 | tf_op jit(solution)/shard_map/attend/pallas_call | solution.py:301
  98.4 8.4 %collective-permute-done.13.refs_9_.refs_14_ = bf16[1,96,1536]{2,1,0:T(8,128)(2,1)S(1)} collective-permute-done((bf16[1,96,1536]{2,1,0:T(8,128)(2,1)S(1)}, bf16[1,96,1536]{2,1,0:T(8,128)(2,1)S(1)}, u32[]{:S(2)}, u32[]{:S(2)}) %collective-permute-start.13) | collective-permute-done | bytes 294944 | tf_op jit(solution)/shard_map/ppermute | solution.py:71
  112.5 7.7 %project.1 = (f32[512,1536]{1,0:T(8,128)S(1)}, f32[512,128]{1,0:T(8,128)S(1)}, bf16[528,1536]{1,0:T(8,128)(2,1)}) custom-call(s32[6]{0:T(128)S(1)} %copy-done.14, bf16[512,1536]{1,0:T(8,128)(2,1)S(1)} %copy-done.28, bf16[512,1536]{1,0:T(8,128)(2,1)S(1)} %copy-done.2, s32[512,8]{1,0:T(8,128)S(1)} %copy.55.refs_3_, ...), custom_call_target="tpu_custom_call" | custom-call | flops 30000001024 | bytes 8000000 | tf_op jit(solution)/shard_map/project/pallas_call | solution.py:567
  120.3 1.7 copy-done.3
  126.1 2.9 collective-permute-done.20
  129.8 6.8 %collective-permute-done.24.refs_7_ = bf16[1,1,384,512]{3,2,1,0:T(8,128)(2,1)S(1)} collective-permute-done((bf16[1,1,384,512]{3,2,1,0:T(8,128)(2,1)S(1)}, bf16[1,1,384,512]{3,2,1,0:T(8,128)(2,1)S(1)}, u32[]{:S(2)}, u32[]{:S(2)}) %collective-permute-start.24) | collective-permute-done | bytes 393248 | tf_op jit(solution)/shard_map/ppermute | solution.py:71
  140.0 1.7 collective-permute-start.26
  142.7 13.0 %collective-permute-done.29 = bf16[2,512,384]{2,1,0:T(8,128)(2,1)S(1)} collective-permute-done((bf16[2,512,384]{2,1,0:T(8,128)(2,1)}, bf16[2,512,384]{2,1,0:T(8,128)(2,1)S(1)}, u32[]{:S(2)}, u32[]{:S(2)}) %collective-permute-start.29) | collective-permute-done | bytes 786464 | tf_op jit(solution)/shard_map/ppermute | solution.py:71
  157.3 2.0 collective-permute-done.28
  159.7 2.7 collective-permute-done.22.refs_2_
  167.7 6.1 collective-permute-done.30.refs_17_
  174.6 18.1 %expert_chunk.8 = (bf16[528,1536]{1,0:T(8,128)(2,1)}, bf16[4096,1536]{1,0:T(8,128)(2,1)}, bf16[4096,1536]{1,0:T(8,128)(2,1)}, bf16[2,4096,512]{2,1,0:T(8,128)(2,1)}, bf16[4,4096,512]{2,1,0:T(8,128)(2,1)}) custom-call(s32[6]{0:T(128)} %stack.98.order_ref.refs_0_.refs_1_, s32[2]{0:T(128)} %get-tuple-element.607.refs_1_, ...), custom_call_target="tpu_custom_call" | custom-call | flops 49999998976 | bytes 4000000 | tf_op jit(solution)/shard_map/expert_chunk/pallas_call | solution.py:858
  192.8 17.8 %expert_chunk.9 = (bf16[528,1536]{1,0:T(8,128)(2,1)}, bf16[4096,1536]{1,0:T(8,128)(2,1)}, bf16[4096,1536]{1,0:T(8,128)(2,1)}, bf16[2,4096,512]{2,1,0:T(8,128)(2,1)}, bf16[4,4096,512]{2,1,0:T(8,128)(2,1)}) custom-call(s32[6]{0:T(128)} %stack.98.order_ref.refs_0_.refs_1_, ...), custom_call_target="tpu_custom_call", output_to_operand_aliasing={{1}: (19, {}), {2}: (20, {}), {3}: (21, {}), {4}: (22, {})} | custom-call | flops 49999998976 | bytes 4000000 | tf_op jit(solution)/shard_map/expert_chunk/pallas_call | solution.py:858
  212.3 18.2 %expert_chunk.10 = (bf16[528,1536]{1,0:T(8,128)(2,1)}, bf16[4096,1536]{1,0:T(8,128)(2,1)}, bf16[4096,1536]{1,0:T(8,128)(2,1)}, bf16[2,4096,512]{2,1,0:T(8,128)(2,1)}, bf16[4,4096,512]{2,1,0:T(8,128)(2,1)}) custom-call(s32[6]{0:T(128)} %stack.98.order_ref.refs_0_.refs_1_, ...), custom_call_target="tpu_custom_call", output_to_operand_aliasing={{1}: (19, {}), {2}: (20, {}), {3}: (21, {}), {4}: (22, {})} | custom-call | flops 49999998976 | bytes 4000000 | tf_op jit(solution)/shard_map/expert_chunk/pallas_call | solution.py:858
  230.9 17.8 %expert_chunk.11 = (bf16[528,1536]{1,0:T(8,128)(2,1)}, bf16[4096,1536]{1,0:T(8,128)(2,1)}, bf16[4096,1536]{1,0:T(8,128)(2,1)}, bf16[2,4096,512]{2,1,0:T(8,128)(2,1)}, bf16[4,4096,512]{2,1,0:T(8,128)(2,1)}) custom-call(s32[6]{0:T(128)} %stack.98.order_ref.refs_0_.refs_1_, ...), custom_call_target="tpu_custom_call", output_to_operand_aliasing={{1}: (19, {}), {2}: (20, {}), {3}: (21, {}), {4}: (22, {})} | custom-call | flops 49999998976 | bytes 4000000 | tf_op jit(solution)/shard_map/expert_chunk/pallas_call | solution.py:858
  248.7 2.0 collective-permute-done.35.refs_2_
  250.7 2.4 add_convert_fusion.2
  253.3 18.0 %expert_chunk.12 = (bf16[528,1536]{1,0:T(8,128)(2,1)}, bf16[4096,1536]{1,0:T(8,128)(2,1)}, bf16[4096,1536]{1,0:T(8,128)(2,1)}, bf16[2,4096,512]{2,1,0:T(8,128)(2,1)}, bf16[4,4096,512]{2,1,0:T(8,128)(2,1)}) custom-call(s32[6]{0:T(128)} %stack.98.order_ref.refs_0_.refs_1_, ...), custom_call_target="tpu_custom_call", output_to_operand_aliasing={{1}: (19, {}), {2}: (20, {}), {3}: (21, {}), {4}: (22, {})} | custom-call | flops 49999998976 | bytes 4000000 | tf_op jit(solution)/shard_map/expert_chunk/pallas_call | solution.py:858
  271.8 17.9 %expert_chunk.13 = (bf16[528,1536]{1,0:T(8,128)(2,1)}, bf16[4096,1536]{1,0:T(8,128)(2,1)}, bf16[4096,1536]{1,0:T(8,128)(2,1)}, bf16[2,4096,512]{2,1,0:T(8,128)(2,1)}, bf16[4,4096,512]{2,1,0:T(8,128)(2,1)}) custom-call(s32[6]{0:T(128)} %stack.98.order_ref.refs_0_.refs_1_, ...), custom_call_target="tpu_custom_call", output_to_operand_aliasing={{1}: (19, {}), {2}: (20, {}), {3}: (21, {}), {4}: (22, {})} | custom-call | flops 49999998976 | bytes 4000000 | tf_op jit(solution)/shard_map/expert_chunk/pallas_call | solution.py:858
  289.7 3.2 collective-permute-done.39
  292.9 2.0 add_convert_fusion.1
  295.0 18.1 %expert_chunk.14 = (bf16[528,1536]{1,0:T(8,128)(2,1)}, bf16[4096,1536]{1,0:T(8,128)(2,1)}, bf16[4096,1536]{1,0:T(8,128)(2,1)}, bf16[2,4096,512]{2,1,0:T(8,128)(2,1)}, bf16[4,4096,512]{2,1,0:T(8,128)(2,1)}) custom-call(s32[6]{0:T(128)} %stack.98.order_ref.refs_0_.refs_1_, ...), custom_call_target="tpu_custom_call", output_to_operand_aliasing={{1}: (19, {}), {2}: (20, {}), {3}: (21, {}), {4}: (22, {})} | custom-call | flops 49999998976 | bytes 4000000 | tf_op jit(solution)/shard_map/expert_chunk/pallas_call | solution.py:858
  313.2 17.8 %expert_chunk.15 = (bf16[528,1536]{1,0:T(8,128)(2,1)}, bf16[4096,1536]{1,0:T(8,128)(2,1)}, bf16[4096,1536]{1,0:T(8,128)(2,1)}, bf16[2,4096,512]{2,1,0:T(8,128)(2,1)}, bf16[4,4096,512]{2,1,0:T(8,128)(2,1)}) custom-call(s32[6]{0:T(128)} %stack.98.order_ref.refs_0_.refs_1_, ...), custom_call_target="tpu_custom_call", output_to_operand_aliasing={{1}: (19, {}), {2}: (20, {}), {3}: (21, {}), {4}: (22, {})} | custom-call | flops 49999998976 | bytes 4000000 | tf_op jit(solution)/shard_map/expert_chunk/pallas_call | solution.py:858
  331.0 2.8 collective-permute-done.41
  333.8 2.5 add_convert_fusion
  336.4 20.8 %weight_grad.3 = (bf16[2,384,512]{2,1,0:T(8,128)(2,1)S(1)}, bf16[1,384,512]{2,1,0:T(8,128)(2,1)S(1)}, bf16[1,384,512]{2,1,0:T(8,128)(2,1)S(1)}, bf16[2,1,384,512...) custom-call(s32[6]{0:T(128)S(1)} %copy-done.15, bf16[4096,1536]{1,0:T(8,128)(2,1)} %get-tuple-element.420.refs_1_, ...), custom_call_target="tpu_custom_call" | custom-call | flops 60000002048 | bytes 8000000 | tf_op jit(solution)/shard_map/weight_grad/pallas_call | solution.py:993
  359.1 21.7 %weight_grad.4 = (bf16[2,384,512]{2,1,0:T(8,128)(2,1)S(1)}, bf16[1,384,512]{2,1,0:T(8,128)(2,1)S(1)}, bf16[1,384,512]{2,1,0:T(8,128)(2,1)S(1)}, bf16[2,1,384,512]{3,2,1,0:T(8,128)(2,1)}, bf16[2,1,384,512]{3,2,1,0:T(8,128)(2,1)}) custom-call(s32[6]{0:T(128)S(1)} %copy-done.15, bf16[4096,1536]{1,0:T(8,128)(2,1)} %get-tuple-element.420.refs_1_, ...), custom_call_target="tpu_custom_call" | custom-call | flops 60000002048 | bytes 8000000 | tf_op jit(solution)/shard_map/weight_grad/pallas_call | solution.py:993
  385.1 14.5 %turn.1 = (bf16[512,1536]{1,0:T(8,128)(2,1)}, f32[512,1536]{1,0:T(8,128)}, bf16[1536,896]{1,0:T(8,128)(2,1)}, bf16[1536,896]{1,0:T(8,128)(2,1)}) custom-call(s32[6]{0:T(128)} %stack.98.order_ref.refs_0_.refs_1_, bf16[528,1536]{1,0:T(8,128)(2,1)} %get-tuple-element.429.refs_1_, bf16[528,1536]{1,0:T(8,128)(2,1)} %copy-done.66, bf16[528,1536]{1,0:T(8,128)(2,1)} %copy-done.67, ...), custom_call_target="tpu_custom_call" | custom-call | flops 30000001024 | bytes 8000000 | tf_op jit(solution)/shard_map/turn/pallas_call | solution.py:643
  406.4 26.1 %attend_back.2 = (bf16[1536,640]{1,0:T(8,128)(2,1)}, bf16[1536,640]{1,0:T(8,128)(2,1)}, f32[512,1536]{1,0:T(8,128)}) custom-call(s32[2]{0:T(128)} %copy-done.19, s32[6]{0:T(128)} %stack.98.order_ref.refs_0_.refs_1_, bf16[512,1536]{1,0:T(8,128)(2,1)} %get-tuple-element.465.refs_2_, bf16[512,1536]{1,0:T(8,128)(2,1)} %fusion.2.refs_2_.refs_3_, ...), custom_call_target="tpu_custom_call" | custom-call | flops 60000002048 | bytes 8000000 | tf_op jit(solution)/shard_map/attend_back/pallas_call | solution.py:465
  433.7 3.2 collective-permute-done.53.refs_2_
  436.9 1.8 copy-done.25
  440.2 4.6 fold.2
  446.6 30.6 %attend_back.3 = (bf16[1536,768]{1,0:T(8,128)(2,1)}, bf16[1536,768]{1,0:T(8,128)(2,1)}, bf16[512,1536]{1,0:T(8,128)(2,1)}) custom-call(s32[2]{0:T(128)} %copy-done.18, s32[6]{0:T(128)} %stack.98.order_ref.refs_0_.refs_1_, bf16[512,1536]{1,0:T(8,128)(2,1)} %get-tuple-element.465.refs_2_, bf16[512,1536]{1,0:T(8,128)(2,1)} %fusion.2.refs_2_.refs_3_, ...), custom_call_target="tpu_custom_call" | custom-call | flops 60000002048 | bytes 8000000 | tf_op jit(solution)/shard_map/attend_back/pallas_call | solution.py:465
  477.4 2.0 add_convert_fusion.5
  480.5 2.0 add_convert_fusion.4
  483.7 1.7 copy-done.27
  485.4 3.4 fold.3
  488.8 6.6 %collective-permute-done.57 = bf16[192,1536]{1,0:T(8,128)(2,1)S(1)} collective-permute-done((bf16[192,1536]{1,0:T(8,128)(2,1)}, bf16[192,1536]{1,0:T(8,128)(2,1)S(1)}, u32[]{:S(2)}, u32[]{:S(2)}) %collective-permute-start.57) | collective-permute-done | bytes 589856 | tf_op jit(solution)/shard_map/ppermute | solution.py:71
  495.4 3.0 collective-permute-done.58
  498.6 2.0 fusion.6
  502.9 4.0 collective-permute-start.62
  507.0 1.8 collective-permute-start.63
  508.7 20.5 %weight_grad.5 = (bf16[2,512,384]{2,1,0:T(8,128)(2,1)S(1)}, bf16[1,512,384]{2,1,0:T(8,128)(2,1)S(1)}, bf16[1,512,384]{2,1,0:T(8,128)(2,1)S(1)}, bf16[2,1,512,384...) custom-call(s32[6]{0:T(128)S(1)} %copy-done.17, bf16[2,4096,512]{2,1,0:T(8,128)(2,1)} %get-tuple-element.493.refs_1_, ...), custom_call_target="tpu_custom_call" | custom-call | flops 60000002048 | bytes 8000000 | tf_op jit(solution)/shard_map/weight_grad/pallas_call | solution.py:993
  529.3 2.8 collective-permute-done.62
  532.3 6.6 %collective-permute-start.66 = (bf16[96,1536]{1,0:T(8,128)(2,1)S(1)}, bf16[96,1536]{1,0:T(8,128)(2,1)S(1)}, u32[]{:S(2)}, u32[]{:S(2)}) collective-permute-start(bf16[96,1536]{1,0:T(8,128)(2,1)S(1)} %add_convert_fusion.12), channel_id=1, source_target_pairs={{0,8},{4,12},{8,16},{12,20},{16,24},{20,28},{24,0},{28,4},{1,9},{5... | collective-permute-start | bytes 884744 | tf_op jit(solution)/shard_map/ppermute | solution.py:185
  551.0 7.6 %collective-permute-done.67 = bf16[96,1536]{1,0:T(8,128)(2,1)S(1)} collective-permute-done((bf16[96,1536]{1,0:T(8,128)(2,1)S(1)}, bf16[96,1536]{1,0:T(8,128)(2,1)S(1)}, u32[]{:S(2)}, u32[]{:S(2)}) %collective-permute-start.67) | collective-permute-done | bytes 294944 | tf_op jit(solution)/shard_map/ppermute | solution.py:185
  559.7 6.8 %collective-permute-start.69 = (bf16[96,768]{1,0:T(8,128)(2,1)S(1)}, bf16[96,768]{1,0:T(8,128)(2,1)S(1)}, u32[]{:S(2)}, u32[]{:S(2)}) collective-permute-start(bf16[96,768]{1,0:T(8,128)(2,1)S(1)} %get-tuple-element.594), channel_id=1, source_target_pairs={{0,8},{4,12},{8,16},{12,20},{16,24},{20,28},{24,0},{28,4},{1,9},{5... | collective-permute-start | bytes 442376 | tf_op jit(solution)/shard_map/ppermute | solution.py:185
  566.6 2.4 collective-permute-start.70
  573.2 4.8 collective-permute-done.70
  578.1 9.8 %collective-permute-done.72 = bf16[2,512,384]{2,1,0:T(8,128)(2,1)S(1)} collective-permute-done((bf16[2,512,384]{2,1,0:T(8,128)(2,1)S(1)}, bf16[2,512,384]{2,1,0:T(8,128)(2,1)S(1)}, u32[]{:S(2)}, u32[]{:S(2)}) %collective-permute-start.72) | collective-permute-done | bytes 786464 | tf_op jit(solution)/shard_map/ppermute | solution.py:71
  596.7 3.4 collective-permute-done.74
  600.1 3.3 collective-permute-done.75
  608.1 5.8 finish.1
  616.5 4.0 add_convert_fusion.3
  (375 shorter events, 110.1 us)
Async XLA Ops:
  7.2 167.4 %all-gather.2.cloned.1.call-start = ((), (), s32[]{:S(2)}) async-start(), calls=%async_computation.1 | async-start | bytes 14155776 | tf_op jit(solution)/shard_map/all_gather | solution.py:1055
  7.9 608.6 %reduce-scatter.2.cloned.1.call-start = ((), (), s32[]{:S(2)}) async-start(), calls=%async_computation.2 | async-start | bytes 14155776 | tf_op jit(solution)/shard_map/reduce_scatter | solution.py:1121
  11.6 32.4 %collective-permute-start = (bf16[384,1280]{1,0:T(8,128)(2,1)}, bf16[384,1280]{1,0:T(8,128)(2,1)}, u32[]{:S(2)}, u32[]{:S(2)}) collective-permute-start(bf16[384,1280]{1,0:T(8,128)(2,1)} %own_groups.1), channel_id=1, source_target_pairs={{0,1},{1,0},{2,3},{3,2},{4,5},{5,4},{6,7},{7,6},{8,9},{9,8},{10,11... | collective-permute-start | bytes 2949128 | tf_op jit(solution)/shard_map/ppermute | solution.py:71
  14.5 30.6 %collective-permute-start.1 = (bf16[384,1280]{1,0:T(8,128)(2,1)}, bf16[384,1280]{1,0:T(8,128)(2,1)}, u32[]{:S(2)}, u32[]{:S(2)}) collective-permute-start(bf16[384,1280]{1,0:T(8,128)(2,1)} %own_groups.1), channel_id=1, source_target_pairs={{0,2},{1,3},{2,0},{3,1},{4,6},{5,7},{6,4},{7,5},{8,10},{9,11},{10,... | collective-permute-start | bytes 2949128 | tf_op jit(solution)/shard_map/ppermute | solution.py:71
  16.1 20.8 %collective-permute-start.4 = (bf16[18,384]{1,0:T(8,128)(2,1)S(1)}, bf16[18,384]{1,0:T(8,128)(2,1)S(1)}, u32[]{:S(2)}, u32[]{:S(2)}) collective-permute-start(bf16[18,384]{1,0:T(8,128)(2,1)S(1)} %maximum_bitcast_fusion), channel_id=1, source_target_pairs={{0,1},{1,0},{2,3},{3,2},{4,5},{5,4},{6,7},{7,6},{8,9},{9,8},{10,11... | collective-permute-start | bytes 41480 | tf_op jit(solution)/shard_map/ppermute | solution.py:71
  16.7 46.4 %collective-permute-start.8 = (bf16[1,384,1280]{2,1,0:T(8,128)(2,1)}, bf16[1,384,1280]{2,1,0:T(8,128)(2,1)}, u32[]{:S(2)}, u32[]{:S(2)}) collective-permute-start(bf16[1,384,1280]{2,1,0:T(8,128)(2,1)} %bitcast.69), channel_id=1, source_target_pairs={{0,4},{4,0},{8,12},{12,8},{16,20},{20,16},{24,28},{28,24},{1,5},{5... | collective-permute-start | bytes 2949128 | tf_op jit(solution)/shard_map/ppermute | solution.py:62
  45.1 18.4 %collective-permute-start.9 = (bf16[1,384,1280]{2,1,0:T(8,128)(2,1)}, bf16[1,384,1280]{2,1,0:T(8,128)(2,1)}, u32[]{:S(2)}, u32[]{:S(2)}) collective-permute-start(bf16[1,384,1280]{2,1,0:T(8,128)(2,1)} %bitcast.6.refs_7_.refs_20_), channel_id=1, source_target_pairs={{0,4},{4,0},{8,12},{12,8},{16,20},{20,16},{24,28},{28,24},{1,5},{5... | collective-permute-start | bytes 2949128 | tf_op jit(solution)/shard_map/ppermute | solution.py:62
  46.2 19.0 %collective-permute-start.10 = (bf16[1,384,1280]{2,1,0:T(8,128)(2,1)}, bf16[1,384,1280]{2,1,0:T(8,128)(2,1)}, u32[]{:S(2)}, u32[]{:S(2)}) collective-permute-start(bf16[1,384,1280]{2,1,0:T(8,128)(2,1)} %bitcast.7.refs_8_.refs_21_), channel_id=1, source_target_pairs={{0,4},{4,0},{8,12},{12,8},{16,20},{20,16},{24,28},{28,24},{1,5},{5... | collective-permute-start | bytes 2949128 | tf_op jit(solution)/shard_map/ppermute | solution.py:62
  46.8 13.3 %collective-permute-start.2 = (bf16[1,192,1280]{2,1,0:T(8,128)(2,1)S(1)}, bf16[1,192,1280]{2,1,0:T(8,128)(2,1)}, u32[]{:S(2)}, u32[]{:S(2)}) collective-permute-start(bf16[1,192,1280]{2,1,0:T(8,128)(2,1)S(1)} %slice.220), channel_id=1, source_target_pairs={{0,1},{1,0},{2,3},{3,2},{4,5},{5,4},{6,7},{7,6},{8,9},{9,8},{10,11... | collective-permute-start | bytes 1474568 | tf_op jit(solution)/shard_map/ppermute | solution.py:71
  48.5 13.0 %collective-permute-start.3 = (bf16[1,192,1280]{2,1,0:T(8,128)(2,1)S(1)}, bf16[1,192,1280]{2,1,0:T(8,128)(2,1)}, u32[]{:S(2)}, u32[]{:S(2)}) collective-permute-start(bf16[1,192,1280]{2,1,0:T(8,128)(2,1)S(1)} %slice.221), channel_id=1, source_target_pairs={{0,2},{1,3},{2,0},{3,1},{4,6},{5,7},{6,4},{7,5},{8,10},{9,11},{10,... | collective-permute-start | bytes 1474568 | tf_op jit(solution)/shard_map/ppermute | solution.py:71
  63.1 18.2 %collective-permute-start.6 = (bf16[192,1536]{1,0:T(8,128)(2,1)S(1)}, bf16[192,1536]{1,0:T(8,128)(2,1)S(1)}, u32[]{:S(2)}, u32[]{:S(2)}) collective-permute-start(bf16[192,1536]{1,0:T(8,128)(2,1)S(1)} %constant_dynamic-slice_fusion.6), channel_id=1, source_target_pairs={{0,1},{1,0},{2,3},{3,2},{4,5},{5,4},{6,7},{7,6},{8,9},{9,8},{10,11... | collective-permute-start | bytes 1769480 | tf_op jit(solution)/shard_map/ppermute | solution.py:71
  63.5 17.8 %collective-permute-start.7 = (bf16[192,1536]{1,0:T(8,128)(2,1)S(1)}, bf16[192,1536]{1,0:T(8,128)(2,1)S(1)}, u32[]{:S(2)}, u32[]{:S(2)}) collective-permute-start(bf16[192,1536]{1,0:T(8,128)(2,1)S(1)} %constant_dynamic-slice_fusion.6), channel_id=1, source_target_pairs={{0,2},{1,3},{2,0},{3,1},{4,6},{5,7},{6,4},{7,5},{8,10},{9,11},{10,... | collective-permute-start | bytes 1769480 | tf_op jit(solution)/shard_map/ppermute | solution.py:71
  81.4 26.5 %collective-permute-start.16 = (bf16[2,384,512]{2,1,0:T(8,128)(2,1)S(1)}, bf16[2,384,512]{2,1,0:T(8,128)(2,1)S(1)}, u32[]{:S(2)}, u32[]{:S(2)}) collective-permute-start(bf16[2,384,512]{2,1,0:T(8,128)(2,1)S(1)} %copy-done.69), channel_id=1, source_target_pairs={{0,1},{1,0},{2,3},{3,2},{4,5},{5,4},{6,7},{7,6},{8,9},{9,8},{10,11... | collective-permute-start | bytes 2359304 | tf_op jit(solution)/shard_map/ppermute | solution.py:71
  82.9 24.9 %collective-permute-start.17 = (bf16[2,384,512]{2,1,0:T(8,128)(2,1)S(1)}, bf16[2,384,512]{2,1,0:T(8,128)(2,1)S(1)}, u32[]{:S(2)}, u32[]{:S(2)}) collective-permute-start(bf16[2,384,512]{2,1,0:T(8,128)(2,1)S(1)} %copy-done.69), channel_id=1, source_target_pairs={{0,2},{1,3},{2,0},{3,1},{4,6},{5,7},{6,4},{7,5},{8,10},{9,11},{10,... | collective-permute-start | bytes 2359304 | tf_op jit(solution)/shard_map/ppermute | solution.py:71
  83.5 23.3 %collective-permute-start.13 = (bf16[1,96,1536]{2,1,0:T(8,128)(2,1)S(1)}, bf16[1,96,1536]{2,1,0:T(8,128)(2,1)S(1)}, u32[]{:S(2)}, u32[]{:S(2)}) collective-permute-start(bf16[1,96,1536]{2,1,0:T(8,128)(2,1)S(1)} %slice.170), channel_id=1, source_target_pairs={{0,1},{1,0},{2,3},{3,2},{4,5},{5,4},{6,7},{7,6},{8,9},{9,8},{10,11... | collective-permute-start | bytes 884744 | tf_op jit(solution)/shard_map/ppermute | solution.py:71
  84.5 23.4 %collective-permute-start.14 = (bf16[1,96,1536]{2,1,0:T(8,128)(2,1)S(1)}, bf16[1,96,1536]{2,1,0:T(8,128)(2,1)S(1)}, u32[]{:S(2)}, u32[]{:S(2)}) collective-permute-start(bf16[1,96,1536]{2,1,0:T(8,128)(2,1)S(1)} %slice.171), channel_id=1, source_target_pairs={{0,2},{1,3},{2,0},{3,1},{4,6},{5,7},{6,4},{7,5},{8,10},{9,11},{10,... | collective-permute-start | bytes 884744 | tf_op jit(solution)/shard_map/ppermute | solution.py:71
  85.7 22.2 %collective-permute-start.15 = (bf16[3,192,1536]{2,1,0:T(8,128)(2,1)S(1)}, bf16[3,192,1536]{2,1,0:T(8,128)(2,1)S(1)}, u32[]{:S(2)}, u32[]{:S(2)}) collective-permute-start(bf16[3,192,1536]{2,1,0:T(8,128)(2,1)S(1)} %pad_maximum_fusion), channel_id=1, source_target_pairs={{0,4},{4,0},{8,12},{12,8},{16,20},{20,16},{24,28},{28,24},{1,5},{5... | collective-permute-start | bytes 5308424 | tf_op jit(solution)/shard_map/ppermute | solution.py:62
  108.6 20.5 %collective-permute-start.20 = (bf16[2,384,512]{2,1,0:T(8,128)(2,1)S(1)}, bf16[2,384,512]{2,1,0:T(8,128)(2,1)S(1)}, u32[]{:S(2)}, u32[]{:S(2)}) collective-permute-start(bf16[2,384,512]{2,1,0:T(8,128)(2,1)S(1)} %copy-done.70), channel_id=1, source_target_pairs={{0,1},{1,0},{2,3},{3,2},{4,5},{5,4},{6,7},{7,6},{8,9},{9,8},{10,11... | collective-permute-start | bytes 2359304 | tf_op jit(solution)/shard_map/ppermute | solution.py:71
  109.4 20.4 %collective-permute-start.21 = (bf16[2,384,512]{2,1,0:T(8,128)(2,1)S(1)}, bf16[2,384,512]{2,1,0:T(8,128)(2,1)S(1)}, u32[]{:S(2)}, u32[]{:S(2)}) collective-permute-start(bf16[2,384,512]{2,1,0:T(8,128)(2,1)S(1)} %copy-done.70), channel_id=1, source_target_pairs={{0,2},{1,3},{2,0},{3,1},{4,6},{5,7},{6,4},{7,5},{8,10},{9,11},{10,... | collective-permute-start | bytes 2359304 | tf_op jit(solution)/shard_map/ppermute | solution.py:71
  122.6 39.7 %collective-permute-start.22 = (bf16[528,1536]{1,0:T(8,128)(2,1)}, bf16[528,1536]{1,0:T(8,128)(2,1)}, u32[]{:S(2)}, u32[]{:S(2)}) collective-permute-start(bf16[528,1536]{1,0:T(8,128)(2,1)} %get-tuple-element.341.refs_2_.refs_4_), channel_id=1, source_target_pairs={{0,8},{4,12},{8,16},{12,20},{16,24},{20,28},{24,0},{28,4},{1,9},{5... | collective-permute-start | bytes 4866056 | tf_op jit(solution)/shard_map/ppermute | solution.py:67
  123.9 12.7 %collective-permute-start.24 = (bf16[1,1,384,512]{3,2,1,0:T(8,128)(2,1)S(1)}, bf16[1,1,384,512]{3,2,1,0:T(8,128)(2,1)S(1)}, u32[]{:S(2)}, u32[]{:S(2)}) collective-permute-start(bf16[1,1,384,512]{3,2,1,0:T(8,128)(2,1)S(1)} %slice.174), channel_id=1, source_target_pairs={{0,1},{1,0},{2,3},{3,2},{4,5},{5,4},{6,7},{7,6},{8,9},{9,8},{10,11... | collective-permute-start | bytes 1179656 | tf_op jit(solution)/shard_map/ppermute | solution.py:71
  129.8 36.6 %collective-permute-start.23 = (bf16[528,1536]{1,0:T(8,128)(2,1)}, bf16[528,1536]{1,0:T(8,128)(2,1)}, u32[]{:S(2)}, u32[]{:S(2)}) collective-permute-start(bf16[528,1536]{1,0:T(8,128)(2,1)} %get-tuple-element.341.refs_2_.refs_4_), channel_id=1, source_target_pairs={{0,4},{4,0},{8,12},{12,8},{16,20},{20,16},{24,28},{28,24},{1,5},{5... | collective-permute-start | bytes 4866056 | tf_op jit(solution)/shard_map/ppermute | solution.py:62
  137.1 18.7 %collective-permute-start.29 = (bf16[2,512,384]{2,1,0:T(8,128)(2,1)}, bf16[2,512,384]{2,1,0:T(8,128)(2,1)S(1)}, u32[]{:S(2)}, u32[]{:S(2)}) collective-permute-start(bf16[2,512,384]{2,1,0:T(8,128)(2,1)} %param.23), channel_id=1, source_target_pairs={{0,2},{1,3},{2,0},{3,1},{4,6},{5,7},{6,4},{7,5},{8,10},{9,11},{10,... | collective-permute-start | bytes 2359304 | tf_op jit(solution)/shard_map/ppermute | solution.py:71
  138.6 20.7 %collective-permute-start.28 = (bf16[2,512,384]{2,1,0:T(8,128)(2,1)}, bf16[2,512,384]{2,1,0:T(8,128)(2,1)S(1)}, u32[]{:S(2)}, u32[]{:S(2)}) collective-permute-start(bf16[2,512,384]{2,1,0:T(8,128)(2,1)} %param.23), channel_id=1, source_target_pairs={{0,1},{1,0},{2,3},{3,2},{4,5},{5,4},{6,7},{7,6},{8,9},{9,8},{10,11... | collective-permute-start | bytes 2359304 | tf_op jit(solution)/shard_map/ppermute | solution.py:71
  140.0 27.7 %collective-permute-start.26 = (bf16[1,1,384,512]{3,2,1,0:T(8,128)(2,1)S(1)}, bf16[1,1,384,512]{3,2,1,0:T(8,128)(2,1)S(1)}, u32[]{:S(2)}, u32[]{:S(2)}) collective-permute-start(bf16[1,1,384,512]{3,2,1,0:T(8,128)(2,1)S(1)} %slice.176), channel_id=1, source_target_pairs={{0,1},{1,0},{2,3},{3,2},{4,5},{5,4},{6,7},{7,6},{8,9},{9,8},{10,11... | collective-permute-start | bytes 1179656 | tf_op jit(solution)/shard_map/ppermute | solution.py:71
  159.3 14.6 %collective-permute-start.30 = (bf16[1,1,512,384]{3,2,1,0:T(8,128)(2,1)S(1)}, bf16[1,1,512,384]{3,2,1,0:T(8,128)(2,1)S(1)}, u32[]{:S(2)}, u32[]{:S(2)}) collective-permute-start(bf16[1,1,512,384]{3,2,1,0:T(8,128)(2,1)S(1)} %slice.224), channel_id=1, source_target_pairs={{0,1},{1,0},{2,3},{3,2},{4,5},{5,4},{6,7},{7,6},{8,9},{9,8},{10,11... | collective-permute-start | bytes 1179656 | tf_op jit(solution)/shard_map/ppermute | solution.py:71
  166.4 44.2 %collective-permute-start.32 = (bf16[528,1536]{1,0:T(8,128)(2,1)}, bf16[528,1536]{1,0:T(8,128)(2,1)}, u32[]{:S(2)}, u32[]{:S(2)}) collective-permute-start(bf16[528,1536]{1,0:T(8,128)(2,1)} %collective-permute-done.22.refs_2_), channel_id=1, source_target_pairs={{0,8},{4,12},{8,16},{12,20},{16,24},{20,28},{24,0},{28,4},{1,9},{5... | collective-permute-start | bytes 4866056 | tf_op jit(solution)/shard_map/ppermute | solution.py:67
  167.7 42.9 %collective-permute-start.33 = (bf16[528,1536]{1,0:T(8,128)(2,1)}, bf16[528,1536]{1,0:T(8,128)(2,1)}, u32[]{:S(2)}, u32[]{:S(2)}) collective-permute-start(bf16[528,1536]{1,0:T(8,128)(2,1)} %collective-permute-done.22.refs_2_), channel_id=1, source_target_pairs={{0,4},{4,0},{8,12},{12,8},{16,20},{20,16},{24,28},{28,24},{1,5},{5... | collective-permute-start | bytes 4866056 | tf_op jit(solution)/shard_map/ppermute | solution.py:62
  192.7 17.9 %collective-permute-start.34 = (bf16[528,1536]{1,0:T(8,128)(2,1)}, bf16[528,1536]{1,0:T(8,128)(2,1)S(1)}, u32[]{:S(2)}, u32[]{:S(2)}) collective-permute-start(bf16[528,1536]{1,0:T(8,128)(2,1)} %get-tuple-element.352), channel_id=1, source_target_pairs={{0,4},{4,0},{8,12},{12,8},{16,20},{20,16},{24,28},{28,24},{1,5},{5... | collective-permute-start | bytes 4866056 | tf_op jit(solution)/shard_map/ppermute | solution.py:62
  210.7 40.0 %collective-permute-start.35 = (bf16[528,1536]{1,0:T(8,128)(2,1)}, bf16[528,1536]{1,0:T(8,128)(2,1)}, u32[]{:S(2)}, u32[]{:S(2)}) collective-permute-start(bf16[528,1536]{1,0:T(8,128)(2,1)} %collective-permute-done.32.refs_2_), channel_id=1, source_target_pairs={{0,8},{4,12},{8,16},{12,20},{16,24},{20,28},{24,0},{28,4},{1,9},{5... | collective-permute-start | bytes 4866056 | tf_op jit(solution)/shard_map/ppermute | solution.py:67
  212.1 38.6 %collective-permute-start.36 = (bf16[528,1536]{1,0:T(8,128)(2,1)}, bf16[528,1536]{1,0:T(8,128)(2,1)S(1)}, u32[]{:S(2)}, u32[]{:S(2)}) collective-permute-start(bf16[528,1536]{1,0:T(8,128)(2,1)} %collective-permute-done.32.refs_2_), channel_id=1, source_target_pairs={{0,4},{4,0},{8,12},{12,8},{16,20},{20,16},{24,28},{28,24},{1,5},{5... | collective-permute-start | bytes 4866056 | tf_op jit(solution)/shard_map/ppermute | solution.py:62
  230.5 20.2 %collective-permute-start.37 = (bf16[528,1536]{1,0:T(8,128)(2,1)}, bf16[528,1536]{1,0:T(8,128)(2,1)S(1)}, u32[]{:S(2)}, u32[]{:S(2)}) collective-permute-start(bf16[528,1536]{1,0:T(8,128)(2,1)} %get-tuple-element.368), channel_id=1, source_target_pairs={{0,4},{4,0},{8,12},{12,8},{16,20},{20,16},{24,28},{28,24},{1,5},{5... | collective-permute-start | bytes 4866056 | tf_op jit(solution)/shard_map/ppermute | solution.py:62
  253.1 36.5 %collective-permute-start.38 = (bf16[528,1536]{1,0:T(8,128)(2,1)}, bf16[528,1536]{1,0:T(8,128)(2,1)}, u32[]{:S(2)}, u32[]{:S(2)}) collective-permute-start(bf16[528,1536]{1,0:T(8,128)(2,1)} %collective-permute-done.35.refs_2_), channel_id=1, source_target_pairs={{0,4},{4,0},{8,12},{12,8},{16,20},{20,16},{24,28},{28,24},{1,5},{5... | collective-permute-start | bytes 4866056 | tf_op jit(solution)/shard_map/ppermute | solution.py:62
  253.2 39.6 %collective-permute-start.39 = (bf16[528,1536]{1,0:T(8,128)(2,1)S(1)}, bf16[528,1536]{1,0:T(8,128)(2,1)S(1)}, u32[]{:S(2)}, u32[]{:S(2)}) collective-permute-start(bf16[528,1536]{1,0:T(8,128)(2,1)S(1)} %add_convert_fusion.2), channel_id=1, source_target_pairs={{0,8},{4,12},{8,16},{12,20},{16,24},{20,28},{24,0},{28,4},{1,9},{5... | collective-permute-start | bytes 4866056 | tf_op jit(solution)/shard_map/ppermute | solution.py:67
  271.3 21.6 %collective-permute-start.40 = (bf16[528,1536]{1,0:T(8,128)(2,1)}, bf16[528,1536]{1,0:T(8,128)(2,1)S(1)}, u32[]{:S(2)}, u32[]{:S(2)}) collective-permute-start(bf16[528,1536]{1,0:T(8,128)(2,1)} %get-tuple-element.389), channel_id=1, source_target_pairs={{0,4},{4,0},{8,12},{12,8},{16,20},{20,16},{24,28},{28,24},{1,5},{5... | collective-permute-start | bytes 4866056 | tf_op jit(solution)/shard_map/ppermute | solution.py:62
  294.9 38.9 %collective-permute-start.41 = (bf16[528,1536]{1,0:T(8,128)(2,1)S(1)}, bf16[528,1536]{1,0:T(8,128)(2,1)S(1)}, u32[]{:S(2)}, u32[]{:S(2)}) collective-permute-start(bf16[528,1536]{1,0:T(8,128)(2,1)S(1)} %add_convert_fusion.1), channel_id=1, source_target_pairs={{0,8},{4,12},{8,16},{12,20},{16,24},{20,28},{24,0},{28,4},{1,9},{5... | collective-permute-start | bytes 4866056 | tf_op jit(solution)/shard_map/ppermute | solution.py:67
  313.1 20.7 %collective-permute-start.42 = (bf16[528,1536]{1,0:T(8,128)(2,1)}, bf16[528,1536]{1,0:T(8,128)(2,1)}, u32[]{:S(2)}, u32[]{:S(2)}) collective-permute-start(bf16[528,1536]{1,0:T(8,128)(2,1)} %get-tuple-element.410), channel_id=1, source_target_pairs={{0,4},{4,0},{8,12},{12,8},{16,20},{20,16},{24,28},{28,24},{1,5},{5... | collective-permute-start | bytes 4866056 | tf_op jit(solution)/shard_map/ppermute | solution.py:62
  336.3 46.7 %collective-permute-start.43 = (bf16[528,1536]{1,0:T(8,128)(2,1)S(1)}, bf16[528,1536]{1,0:T(8,128)(2,1)S(1)}, u32[]{:S(2)}, u32[]{:S(2)}) collective-permute-start(bf16[528,1536]{1,0:T(8,128)(2,1)S(1)} %add_convert_fusion), channel_id=1, source_target_pairs={{0,8},{4,12},{8,16},{12,20},{16,24},{20,28},{24,0},{28,4},{1,9},{5... | collective-permute-start | bytes 4866056 | tf_op jit(solution)/shard_map/ppermute | solution.py:67
  357.1 25.8 %collective-permute-start.44 = (bf16[2,384,512]{2,1,0:T(8,128)(2,1)S(1)}, bf16[2,384,512]{2,1,0:T(8,128)(2,1)S(1)}, u32[]{:S(2)}, u32[]{:S(2)}) collective-permute-start(bf16[2,384,512]{2,1,0:T(8,128)(2,1)S(1)} %bitcast.77), channel_id=1, source_target_pairs={{0,1},{1,0},{2,3},{3,2},{4,5},{5,4},{6,7},{7,6},{8,9},{9,8},{10,11... | collective-permute-start | bytes 2359304 | tf_op jit(solution)/shard_map/ppermute | solution.py:71
  357.9 25.1 %collective-permute-start.45 = (bf16[2,384,512]{2,1,0:T(8,128)(2,1)S(1)}, bf16[2,384,512]{2,1,0:T(8,128)(2,1)S(1)}, u32[]{:S(2)}, u32[]{:S(2)}) collective-permute-start(bf16[2,384,512]{2,1,0:T(8,128)(2,1)S(1)} %bitcast.76), channel_id=1, source_target_pairs={{0,2},{1,3},{2,0},{3,1},{4,6},{5,7},{6,4},{7,5},{8,10},{9,11},{10,... | collective-permute-start | bytes 2359304 | tf_op jit(solution)/shard_map/ppermute | solution.py:71
  380.8 18.8 %collective-permute-start.46 = (bf16[2,384,512]{2,1,0:T(8,128)(2,1)}, bf16[2,384,512]{2,1,0:T(8,128)(2,1)}, u32[]{:S(2)}, u32[]{:S(2)}) collective-permute-start(bf16[2,384,512]{2,1,0:T(8,128)(2,1)} %bitcast.37), channel_id=1, source_target_pairs={{0,1},{1,0},{2,3},{3,2},{4,5},{5,4},{6,7},{7,6},{8,9},{9,8},{10,11... | collective-permute-start | bytes 2359304 | tf_op jit(solution)/shard_map/ppermute | solution.py:71
  381.5 18.1 %collective-permute-start.47 = (bf16[2,384,512]{2,1,0:T(8,128)(2,1)}, bf16[2,384,512]{2,1,0:T(8,128)(2,1)}, u32[]{:S(2)}, u32[]{:S(2)}) collective-permute-start(bf16[2,384,512]{2,1,0:T(8,128)(2,1)} %bitcast.38), channel_id=1, source_target_pairs={{0,2},{1,3},{2,0},{3,1},{4,6},{5,7},{6,4},{7,5},{8,10},{9,11},{10,... | collective-permute-start | bytes 2359304 | tf_op jit(solution)/shard_map/ppermute | solution.py:71
  399.6 33.0 %collective-permute-start.48 = (bf16[1536,896]{1,0:T(8,128)(2,1)}, bf16[1536,896]{1,0:T(8,128)(2,1)}, u32[]{:S(2)}, u32[]{:S(2)}) collective-permute-start(bf16[1536,896]{1,0:T(8,128)(2,1)} %get-tuple-element.448), channel_id=1, source_target_pairs={{0,4},{4,0},{8,12},{12,8},{16,20},{20,16},{24,28},{28,24},{1,5},{5... | collective-permute-start | bytes 8257544 | tf_op jit(solution)/shard_map/ppermute | solution.py:62
  399.8 32.7 %collective-permute-start.49 = (bf16[1,384,512]{2,1,0:T(8,128)(2,1)S(1)}, bf16[1,384,512]{2,1,0:T(8,128)(2,1)S(1)}, u32[]{:S(2)}, u32[]{:S(2)}) collective-permute-start(bf16[1,384,512]{2,1,0:T(8,128)(2,1)S(1)} %add_convert_fusion.11), channel_id=1, source_target_pairs={{0,1},{1,0},{2,3},{3,2},{4,5},{5,4},{6,7},{7,6},{8,9},{9,8},{10,11... | collective-permute-start | bytes 1179656 | tf_op jit(solution)/shard_map/ppermute | solution.py:71
  400.8 31.8 %collective-permute-start.50 = (bf16[1,384,512]{2,1,0:T(8,128)(2,1)S(1)}, bf16[1,384,512]{2,1,0:T(8,128)(2,1)S(1)}, u32[]{:S(2)}, u32[]{:S(2)}) collective-permute-start(bf16[1,384,512]{2,1,0:T(8,128)(2,1)S(1)} %add_convert_fusion.10), channel_id=1, source_target_pairs={{0,2},{1,3},{2,0},{3,1},{4,6},{5,7},{6,4},{7,5},{8,10},{9,11},{10,... | collective-permute-start | bytes 1179656 | tf_op jit(solution)/shard_map/ppermute | solution.py:71
  403.0 29.5 %collective-permute-start.51 = (bf16[1,384,512]{2,1,0:T(8,128)(2,1)S(1)}, bf16[1,384,512]{2,1,0:T(8,128)(2,1)S(1)}, u32[]{:S(2)}, u32[]{:S(2)}) collective-permute-start(bf16[1,384,512]{2,1,0:T(8,128)(2,1)S(1)} %add_convert_fusion.9), channel_id=1, source_target_pairs={{0,1},{1,0},{2,3},{3,2},{4,5},{5,4},{6,7},{7,6},{8,9},{9,8},{10,11... | collective-permute-start | bytes 1179656 | tf_op jit(solution)/shard_map/ppermute | solution.py:71
  405.3 27.3 %collective-permute-start.52 = (bf16[1,384,512]{2,1,0:T(8,128)(2,1)S(1)}, bf16[1,384,512]{2,1,0:T(8,128)(2,1)S(1)}, u32[]{:S(2)}, u32[]{:S(2)}) collective-permute-start(bf16[1,384,512]{2,1,0:T(8,128)(2,1)S(1)} %add_convert_fusion.8), channel_id=1, source_target_pairs={{0,2},{1,3},{2,0},{3,1},{4,6},{5,7},{6,4},{7,5},{8,10},{9,11},{10,... | collective-permute-start | bytes 1179656 | tf_op jit(solution)/shard_map/ppermute | solution.py:71
  444.8 32.5 %collective-permute-start.54 = (bf16[384,1536]{1,0:T(8,128)(2,1)}, bf16[384,1536]{1,0:T(8,128)(2,1)}, u32[]{:S(2)}, u32[]{:S(2)}) collective-permute-start(bf16[384,1536]{1,0:T(8,128)(2,1)} %get-tuple-element.474), channel_id=1, source_target_pairs={{0,1},{1,0},{2,3},{3,2},{4,5},{5,4},{6,7},{7,6},{8,9},{9,8},{10,11... | collective-permute-start | bytes 3538952 | tf_op jit(solution)/shard_map/ppermute | solution.py:71
  445.5 31.8 %collective-permute-start.55 = (bf16[384,1536]{1,0:T(8,128)(2,1)S(1)}, bf16[384,1536]{1,0:T(8,128)(2,1)}, u32[]{:S(2)}, u32[]{:S(2)}) collective-permute-start(bf16[384,1536]{1,0:T(8,128)(2,1)S(1)} %get-tuple-element.475), channel_id=1, source_target_pairs={{0,2},{1,3},{2,0},{3,1},{4,6},{5,7},{6,4},{7,5},{8,10},{9,11},{10,... | collective-permute-start | bytes 3538952 | tf_op jit(solution)/shard_map/ppermute | solution.py:71
  479.4 15.9 %collective-permute-start.57 = (bf16[192,1536]{1,0:T(8,128)(2,1)}, bf16[192,1536]{1,0:T(8,128)(2,1)S(1)}, u32[]{:S(2)}, u32[]{:S(2)}) collective-permute-start(bf16[192,1536]{1,0:T(8,128)(2,1)} %add_convert_fusion.5), channel_id=1, source_target_pairs={{0,1},{1,0},{2,3},{3,2},{4,5},{5,4},{6,7},{7,6},{8,9},{9,8},{10,11... | collective-permute-start | bytes 1769480 | tf_op jit(solution)/shard_map/ppermute | solution.py:71
  482.6 15.7 %collective-permute-start.58 = (bf16[192,1536]{1,0:T(8,128)(2,1)}, bf16[192,1536]{1,0:T(8,128)(2,1)}, u32[]{:S(2)}, u32[]{:S(2)}) collective-permute-start(bf16[192,1536]{1,0:T(8,128)(2,1)} %add_convert_fusion.4), channel_id=1, source_target_pairs={{0,2},{1,3},{2,0},{3,1},{4,6},{5,7},{6,4},{7,5},{8,10},{9,11},{10,... | collective-permute-start | bytes 1769480 | tf_op jit(solution)/shard_map/ppermute | solution.py:71
  500.7 31.4 %collective-permute-start.59 = (bf16[384,768]{1,0:T(8,128)(2,1)S(1)}, bf16[384,768]{1,0:T(8,128)(2,1)S(1)}, u32[]{:S(2)}, u32[]{:S(2)}) collective-permute-start(bf16[384,768]{1,0:T(8,128)(2,1)S(1)} %get-tuple-element.498), channel_id=1, source_target_pairs={{0,1},{1,0},{2,3},{3,2},{4,5},{5,4},{6,7},{7,6},{8,9},{9,8},{10,11... | collective-permute-start | bytes 1769480 | tf_op jit(solution)/shard_map/ppermute | solution.py:71
  501.7 30.4 %collective-permute-start.60 = (bf16[384,768]{1,0:T(8,128)(2,1)S(1)}, bf16[384,768]{1,0:T(8,128)(2,1)S(1)}, u32[]{:S(2)}, u32[]{:S(2)}) collective-permute-start(bf16[384,768]{1,0:T(8,128)(2,1)S(1)} %get-tuple-element.499), channel_id=1, source_target_pairs={{0,2},{1,3},{2,0},{3,1},{4,6},{5,7},{6,4},{7,5},{8,10},{9,11},{10,... | collective-permute-start | bytes 1769480 | tf_op jit(solution)/shard_map/ppermute | solution.py:71
  502.6 26.6 %collective-permute-start.61 = (bf16[96,1536]{1,0:T(8,128)(2,1)S(1)}, bf16[96,1536]{1,0:T(8,128)(2,1)S(1)}, u32[]{:S(2)}, u32[]{:S(2)}) collective-permute-start(bf16[96,1536]{1,0:T(8,128)(2,1)S(1)} %get-tuple-element.590), channel_id=1, source_target_pairs={{0,8},{4,12},{8,16},{12,20},{16,24},{20,28},{24,0},{28,4},{1,9},{5... | collective-permute-start | bytes 884744 | tf_op jit(solution)/shard_map/ppermute | solution.py:185
  502.9 29.2 %collective-permute-start.62 = (bf16[96,1536]{1,0:T(8,128)(2,1)S(1)}, bf16[96,1536]{1,0:T(8,128)(2,1)S(1)}, u32[]{:S(2)}, u32[]{:S(2)}) collective-permute-start(bf16[96,1536]{1,0:T(8,128)(2,1)S(1)} %get-tuple-element.589), channel_id=1, source_target_pairs={{0,16},{4,20},{8,24},{12,28},{16,0},{20,4},{24,8},{28,12},{1,17},{... | collective-permute-start | bytes 884744 | tf_op jit(solution)/shard_map/ppermute | solution.py:185
  507.0 25.1 %collective-permute-start.63 = (bf16[96,1536]{1,0:T(8,128)(2,1)S(1)}, bf16[96,1536]{1,0:T(8,128)(2,1)S(1)}, u32[]{:S(2)}, u32[]{:S(2)}) collective-permute-start(bf16[96,1536]{1,0:T(8,128)(2,1)S(1)} %get-tuple-element.588), channel_id=1, source_target_pairs={{0,24},{4,28},{8,0},{12,4},{16,8},{20,12},{24,16},{28,20},{1,25},{... | collective-permute-start | bytes 884744 | tf_op jit(solution)/shard_map/ppermute | solution.py:185
  532.3 18.7 %collective-permute-start.66 = (bf16[96,1536]{1,0:T(8,128)(2,1)S(1)}, bf16[96,1536]{1,0:T(8,128)(2,1)S(1)}, u32[]{:S(2)}, u32[]{:S(2)}) collective-permute-start(bf16[96,1536]{1,0:T(8,128)(2,1)S(1)} %add_convert_fusion.12), channel_id=1, source_target_pairs={{0,8},{4,12},{8,16},{12,20},{16,24},{20,28},{24,0},{28,4},{1,9},{5... | collective-permute-start | bytes 884744 | tf_op jit(solution)/shard_map/ppermute | solution.py:185
  538.9 19.7 %collective-permute-start.67 = (bf16[96,1536]{1,0:T(8,128)(2,1)S(1)}, bf16[96,1536]{1,0:T(8,128)(2,1)S(1)}, u32[]{:S(2)}, u32[]{:S(2)}) collective-permute-start(bf16[96,1536]{1,0:T(8,128)(2,1)S(1)} %add_convert_fusion.12), channel_id=1, source_target_pairs={{0,16},{4,20},{8,24},{12,28},{16,0},{20,4},{24,8},{28,12},{1,17},{... | collective-permute-start | bytes 884744 | tf_op jit(solution)/shard_map/ppermute | solution.py:185
  539.9 18.7 %collective-permute-start.68 = (bf16[96,1536]{1,0:T(8,128)(2,1)S(1)}, bf16[96,1536]{1,0:T(8,128)(2,1)S(1)}, u32[]{:S(2)}, u32[]{:S(2)}) collective-permute-start(bf16[96,1536]{1,0:T(8,128)(2,1)S(1)} %add_convert_fusion.12), channel_id=1, source_target_pairs={{0,24},{4,28},{8,0},{12,4},{16,8},{20,12},{24,16},{28,20},{1,25},{... | collective-permute-start | bytes 884744 | tf_op jit(solution)/shard_map/ppermute | solution.py:185
  559.7 13.5 %collective-permute-start.69 = (bf16[96,768]{1,0:T(8,128)(2,1)S(1)}, bf16[96,768]{1,0:T(8,128)(2,1)S(1)}, u32[]{:S(2)}, u32[]{:S(2)}) collective-permute-start(bf16[96,768]{1,0:T(8,128)(2,1)S(1)} %get-tuple-element.594), channel_id=1, source_target_pairs={{0,8},{4,12},{8,16},{12,20},{16,24},{20,28},{24,0},{28,4},{1,9},{5... | collective-permute-start | bytes 442376 | tf_op jit(solution)/shard_map/ppermute | solution.py:185
  569.0 18.9 %collective-permute-start.72 = (bf16[2,512,384]{2,1,0:T(8,128)(2,1)S(1)}, bf16[2,512,384]{2,1,0:T(8,128)(2,1)S(1)}, u32[]{:S(2)}, u32[]{:S(2)}) collective-permute-start(bf16[2,512,384]{2,1,0:T(8,128)(2,1)S(1)} %bitcast.75), channel_id=1, source_target_pairs={{0,1},{1,0},{2,3},{3,2},{4,5},{5,4},{6,7},{7,6},{8,9},{9,8},{10,11... | collective-permute-start | bytes 2359304 | tf_op jit(solution)/shard_map/ppermute | solution.py:71
  570.5 18.6 %collective-permute-start.73 = (bf16[2,512,384]{2,1,0:T(8,128)(2,1)S(1)}, bf16[2,512,384]{2,1,0:T(8,128)(2,1)S(1)}, u32[]{:S(2)}, u32[]{:S(2)}) collective-permute-start(bf16[2,512,384]{2,1,0:T(8,128)(2,1)S(1)} %bitcast.74), channel_id=1, source_target_pairs={{0,2},{1,3},{2,0},{3,1},{4,6},{5,7},{6,4},{7,5},{8,10},{9,11},{10,... | collective-permute-start | bytes 2359304 | tf_op jit(solution)/shard_map/ppermute | solution.py:71
  589.2 14.2 %collective-permute-start.77 = (bf16[1,512,384]{2,1,0:T(8,128)(2,1)S(1)}, bf16[1,512,384]{2,1,0:T(8,128)(2,1)S(1)}, u32[]{:S(2)}, u32[]{:S(2)}) collective-permute-start(bf16[1,512,384]{2,1,0:T(8,128)(2,1)S(1)} %add_convert_fusion.7), channel_id=1, source_target_pairs={{0,1},{1,0},{2,3},{3,2},{4,5},{5,4},{6,7},{7,6},{8,9},{9,8},{10,11... | collective-permute-start | bytes 1179656 | tf_op jit(solution)/shard_map/ppermute | solution.py:71
  589.9 13.5 %collective-permute-start.78 = (bf16[1,512,384]{2,1,0:T(8,128)(2,1)S(1)}, bf16[1,512,384]{2,1,0:T(8,128)(2,1)S(1)}, u32[]{:S(2)}, u32[]{:S(2)}) collective-permute-start(bf16[1,512,384]{2,1,0:T(8,128)(2,1)S(1)} %add_convert_fusion.6), channel_id=1, source_target_pairs={{0,2},{1,3},{2,0},{3,1},{4,6},{5,7},{6,4},{7,5},{8,10},{9,11},{10,... | collective-permute-start | bytes 1179656 | tf_op jit(solution)/shard_map/ppermute | solution.py:71
  (97 other events, 1044.4 us)
Sparse Core Ops, SparseCore 0:
  9.7 119.9 all-gather.1
  385.2 135.7 reduce-scatter.1

commit v5 on v4

--- a/solution.py
+++ b/solution.py
@@ -1064,9 +1064,10 @@
             proj = gather_second(project_first, 0)
             near = swap_core(jnp.concatenate(proj[:3], axis=0))
             gates_first = gather_first(after(gate_weight, project_first))
-    proj, near, gates_first, saved = lax.optimization_barrier((proj, near, gates_first, saved))
+    proj, near, saved = lax.optimization_barrier((proj, near, saved))
     far = [swap_core(p) for p in proj[3:]]
     ups_first = gather_first(after(up_weight, proj))
+    far, gates_first, saved = lax.optimization_barrier((far, gates_first, saved))
     proj = proj + [near] + far
     attended, query, keys, values, log_total = saved
     resid, gates, sent_rows = project(

time: 636 us -> 636 us (level)
  no operation moved by 1% of the time
where the time goes in v5:
time: 636 us; the launch traced here: 628 us
  Pallas kernels  327 us (51%)
  waiting for transfers between devices  129 us (20%)
  starting transfers between devices  85.6 us (13%)
  other arithmetic  42.1 us (7%)
  local copies, waits for them, and re-layouts  28.1 us (4%)
  between operations  16 us (3%)
    pallas_call x8, Pallas kernels, expert_chunk(): pl.pallas_call(lambda *refs: expert_kernel((len(gates), more), expert_cou...  144 us
    ppermute x42, waiting for transfers between devices, across(): return lax.ppermute(value, 'shard', [(i, i ^ mask) for i in range(4)])  91.5 us
    pallas_call x3, Pallas kernels, grad_exchange(): pl.pallas_call(lambda *refs: sorted_grad_kernel(on_rows, half, *refs), gr...  63 us
    pallas_call x2, Pallas kernels, attend_back(): pl.pallas_call(lambda *refs: attend_back_kernel(mine, (len(proj), len(mix...  56.7 us
    ppermute x42, starting transfers between devices, across(): return lax.ppermute(value, 'shard', [(i, i ^ mask) for i in range(4)])  50.3 us
    ppermute x12, starting transfers between devices, chip_ahead(): lax.ppermute(value, 'expert', [(i, (i + 2 * distance) % count) for i in r...  28.4 us
    pallas_call x2, Pallas kernels, attend(): pl.pallas_call(lambda *refs: attend_kernel(len(mixer_p) // 2, call, *refs...  24.7 us
    ppermute x12, waiting for transfers between devices, chip_ahead(): lax.ppermute(value, 'expert', [(i, (i + 2 * distance) % count) for i in r...  23 us
  transfers between devices with their start and end apart: 83, of which 31 were waited for; matrix products, arithmetic and copies ran while one was open for 6% of the time, Pallas kernels for 52%

profile of v5, /device:TPU:0, one launch (start us, length us, event | category | flops | bytes accessed | tf_op | source)
XLA Modules:
  0.0 627.7 jit_solution(11330742256016661096)
XLA Ops:
  8.6 2.9 own_groups.1
  11.6 2.9 collective-permute-start
  22.2 14.6 %collective-permute-done.4 = bf16[18,384]{1,0:T(8,128)(2,1)S(1)} collective-permute-done((bf16[18,384]{1,0:T(8,128)(2,1)S(1)}, bf16[18,384]{1,0:T(8,128)(2,1)S(1)}, u32[]{:S(2)}, u32[]{:S(2)}) %collective-permute-start.4) | collective-permute-done | bytes 13856 | tf_op jit(solution)/shard_map/ppermute | solution.py:71
  37.5 1.8 collective-permute-start.5
  39.8 1.9 collective-permute-done.5
  46.8 1.7 collective-permute-start.2
  51.6 8.5 %collective-permute-done.2.refs_9_.refs_22_ = bf16[1,192,1280]{2,1,0:T(8,128)(2,1)} collective-permute-done((bf16[1,192,1280]{2,1,0:T(8,128)(2,1)S(1)}, bf16[1,192,1280]{2,1,0:T(8,128)(2,1)}, u32[]{:S(2)}, u32[]{:S(2)}) %collective-permute-start.2) | collective-permute-done | bytes 491552 | tf_op jit(solution)/shard_map/ppermute | solution.py:71
  63.5 1.7 collective-permute-start.7
  69.1 12.2 %attend.2 = (bf16[512,1536]{1,0:T(8,128)(2,1)}, bf16[512,1536]{1,0:T(8,128)(2,1)}, bf16[512,512]{1,0:T(8,128)(2,1)}, bf16[512,512]{1,0:T(8,128)(2,1)}, f32[4,512,8]{2,1,0:T(8,128)}) custom-call(s32[6]{0:T(128)S(1)} %copy-done.14, s32[2]{0:T(128)S(1)} %get-tuple-element.615.refs_1_.refs_0_, bf16[512,1536]{1,0:T(8,128)(2,1)S(1)} %copy-done.5, ...), custom_call_target="tpu_custom_call" | custom-call | flops 48000000000 | bytes 8000000 | tf_op jit(solution)/shard_map/attend/pallas_call | solution.py:301
  85.9 12.5 %attend.3 = (bf16[512,1536]{1,0:T(8,128)(2,1)}, bf16[512,1536]{1,0:T(8,128)(2,1)}, bf16[512,512]{1,0:T(8,128)(2,1)}, bf16[512,512]{1,0:T(8,128)(2,1)}, f32[4,512,8]{2,1,0:T(8,128)}) custom-call(s32[6]{0:T(128)S(1)} %copy-done.14, ...), custom_call_target="tpu_custom_call", output_to_operand_aliasing={{0}: (16, {}), {1}: (17, {}), {2}: (18, {}), {3}: (19, {}),... | custom-call | flops 48000000000 | bytes 8000000 | tf_op jit(solution)/shard_map/attend/pallas_call | solution.py:301
  98.4 8.4 %collective-permute-done.13.refs_9_.refs_14_ = bf16[1,96,1536]{2,1,0:T(8,128)(2,1)S(1)} collective-permute-done((bf16[1,96,1536]{2,1,0:T(8,128)(2,1)S(1)}, bf16[1,96,1536]{2,1,0:T(8,128)(2,1)S(1)}, u32[]{:S(2)}, u32[]{:S(2)}) %collective-permute-start.13) | collective-permute-done | bytes 294944 | tf_op jit(solution)/shard_map/ppermute | solution.py:71
  111.0 1.9 copy-done.28
  112.8 7.7 %project.1 = (f32[512,1536]{1,0:T(8,128)S(1)}, f32[512,128]{1,0:T(8,128)S(1)}, bf16[528,1536]{1,0:T(8,128)(2,1)}) custom-call(s32[6]{0:T(128)S(1)} %copy-done.14, bf16[512,1536]{1,0:T(8,128)(2,1)S(1)} %copy-done.28, bf16[512,1536]{1,0:T(8,128)(2,1)S(1)} %copy-done.2, s32[512,8]{1,0:T(8,128)S(1)} %copy.55.refs_3_, ...), custom_call_target="tpu_custom_call" | custom-call | flops 30000001024 | bytes 8000000 | tf_op jit(solution)/shard_map/project/pallas_call | solution.py:567
  120.5 1.7 copy-done.3
  126.5 2.5 collective-permute-done.20
  129.8 6.8 %collective-permute-done.24.refs_7_ = bf16[1,1,384,512]{3,2,1,0:T(8,128)(2,1)S(1)} collective-permute-done((bf16[1,1,384,512]{3,2,1,0:T(8,128)(2,1)S(1)}, bf16[1,1,384,512]{3,2,1,0:T(8,128)(2,1)S(1)}, u32[]{:S(2)}, u32[]{:S(2)}) %collective-permute-start.24) | collective-permute-done | bytes 393248 | tf_op jit(solution)/shard_map/ppermute | solution.py:71
  140.0 1.7 collective-permute-start.26
  142.7 13.0 %collective-permute-done.29 = bf16[2,512,384]{2,1,0:T(8,128)(2,1)S(1)} collective-permute-done((bf16[2,512,384]{2,1,0:T(8,128)(2,1)}, bf16[2,512,384]{2,1,0:T(8,128)(2,1)S(1)}, u32[]{:S(2)}, u32[]{:S(2)}) %collective-permute-start.29) | collective-permute-done | bytes 786464 | tf_op jit(solution)/shard_map/ppermute | solution.py:71
  157.3 2.0 collective-permute-done.28
  159.7 2.7 collective-permute-done.22.refs_2_
  167.7 6.1 collective-permute-done.30.refs_17_
  174.6 18.1 %expert_chunk.8 = (bf16[528,1536]{1,0:T(8,128)(2,1)}, bf16[4096,1536]{1,0:T(8,128)(2,1)}, bf16[4096,1536]{1,0:T(8,128)(2,1)}, bf16[2,4096,512]{2,1,0:T(8,128)(2,1)}, bf16[4,4096,512]{2,1,0:T(8,128)(2,1)}) custom-call(s32[6]{0:T(128)} %stack.98.order_ref.refs_0_.refs_1_, s32[2]{0:T(128)} %get-tuple-element.621.refs_1_, ...), custom_call_target="tpu_custom_call" | custom-call | flops 49999998976 | bytes 4000000 | tf_op jit(solution)/shard_map/expert_chunk/pallas_call | solution.py:858
  192.7 17.8 %expert_chunk.9 = (bf16[528,1536]{1,0:T(8,128)(2,1)}, bf16[4096,1536]{1,0:T(8,128)(2,1)}, bf16[4096,1536]{1,0:T(8,128)(2,1)}, bf16[2,4096,512]{2,1,0:T(8,128)(2,1)}, bf16[4,4096,512]{2,1,0:T(8,128)(2,1)}) custom-call(s32[6]{0:T(128)} %stack.98.order_ref.refs_0_.refs_1_, ...), custom_call_target="tpu_custom_call", output_to_operand_aliasing={{1}: (19, {}), {2}: (20, {}), {3}: (21, {}), {4}: (22, {})} | custom-call | flops 49999998976 | bytes 4000000 | tf_op jit(solution)/shard_map/expert_chunk/pallas_call | solution.py:858
  212.2 18.2 %expert_chunk.10 = (bf16[528,1536]{1,0:T(8,128)(2,1)}, bf16[4096,1536]{1,0:T(8,128)(2,1)}, bf16[4096,1536]{1,0:T(8,128)(2,1)}, bf16[2,4096,512]{2,1,0:T(8,128)(2,1)}, bf16[4,4096,512]{2,1,0:T(8,128)(2,1)}) custom-call(s32[6]{0:T(128)} %stack.98.order_ref.refs_0_.refs_1_, ...), custom_call_target="tpu_custom_call", output_to_operand_aliasing={{1}: (19, {}), {2}: (20, {}), {3}: (21, {}), {4}: (22, {})} | custom-call | flops 49999998976 | bytes 4000000 | tf_op jit(solution)/shard_map/expert_chunk/pallas_call | solution.py:858
  230.9 17.8 %expert_chunk.11 = (bf16[528,1536]{1,0:T(8,128)(2,1)}, bf16[4096,1536]{1,0:T(8,128)(2,1)}, bf16[4096,1536]{1,0:T(8,128)(2,1)}, bf16[2,4096,512]{2,1,0:T(8,128)(2,1)}, bf16[4,4096,512]{2,1,0:T(8,128)(2,1)}) custom-call(s32[6]{0:T(128)} %stack.98.order_ref.refs_0_.refs_1_, ...), custom_call_target="tpu_custom_call", output_to_operand_aliasing={{1}: (19, {}), {2}: (20, {}), {3}: (21, {}), {4}: (22, {})} | custom-call | flops 49999998976 | bytes 4000000 | tf_op jit(solution)/shard_map/expert_chunk/pallas_call | solution.py:858
  248.7 2.0 collective-permute-done.35.refs_2_
  250.7 2.4 add_convert_fusion.2
  253.2 18.0 %expert_chunk.12 = (bf16[528,1536]{1,0:T(8,128)(2,1)}, bf16[4096,1536]{1,0:T(8,128)(2,1)}, bf16[4096,1536]{1,0:T(8,128)(2,1)}, bf16[2,4096,512]{2,1,0:T(8,128)(2,1)}, bf16[4,4096,512]{2,1,0:T(8,128)(2,1)}) custom-call(s32[6]{0:T(128)} %stack.98.order_ref.refs_0_.refs_1_, ...), custom_call_target="tpu_custom_call", output_to_operand_aliasing={{1}: (19, {}), {2}: (20, {}), {3}: (21, {}), {4}: (22, {})} | custom-call | flops 49999998976 | bytes 4000000 | tf_op jit(solution)/shard_map/expert_chunk/pallas_call | solution.py:858
  271.8 17.9 %expert_chunk.13 = (bf16[528,1536]{1,0:T(8,128)(2,1)}, bf16[4096,1536]{1,0:T(8,128)(2,1)}, bf16[4096,1536]{1,0:T(8,128)(2,1)}, bf16[2,4096,512]{2,1,0:T(8,128)(2,1)}, bf16[4,4096,512]{2,1,0:T(8,128)(2,1)}) custom-call(s32[6]{0:T(128)} %stack.98.order_ref.refs_0_.refs_1_, ...), custom_call_target="tpu_custom_call", output_to_operand_aliasing={{1}: (19, {}), {2}: (20, {}), {3}: (21, {}), {4}: (22, {})} | custom-call | flops 49999998976 | bytes 4000000 | tf_op jit(solution)/shard_map/expert_chunk/pallas_call | solution.py:858
  289.7 3.2 collective-permute-done.39
  292.8 2.0 add_convert_fusion.1
  294.9 18.1 %expert_chunk.14 = (bf16[528,1536]{1,0:T(8,128)(2,1)}, bf16[4096,1536]{1,0:T(8,128)(2,1)}, bf16[4096,1536]{1,0:T(8,128)(2,1)}, bf16[2,4096,512]{2,1,0:T(8,128)(2,1)}, bf16[4,4096,512]{2,1,0:T(8,128)(2,1)}) custom-call(s32[6]{0:T(128)} %stack.98.order_ref.refs_0_.refs_1_, ...), custom_call_target="tpu_custom_call", output_to_operand_aliasing={{1}: (19, {}), {2}: (20, {}), {3}: (21, {}), {4}: (22, {})} | custom-call | flops 49999998976 | bytes 4000000 | tf_op jit(solution)/shard_map/expert_chunk/pallas_call | solution.py:858
  313.1 17.8 %expert_chunk.15 = (bf16[528,1536]{1,0:T(8,128)(2,1)}, bf16[4096,1536]{1,0:T(8,128)(2,1)}, bf16[4096,1536]{1,0:T(8,128)(2,1)}, bf16[2,4096,512]{2,1,0:T(8,128)(2,1)}, bf16[4,4096,512]{2,1,0:T(8,128)(2,1)}) custom-call(s32[6]{0:T(128)} %stack.98.order_ref.refs_0_.refs_1_, ...), custom_call_target="tpu_custom_call", output_to_operand_aliasing={{1}: (19, {}), {2}: (20, {}), {3}: (21, {}), {4}: (22, {})} | custom-call | flops 49999998976 | bytes 4000000 | tf_op jit(solution)/shard_map/expert_chunk/pallas_call | solution.py:858
  331.0 2.8 collective-permute-done.41
  333.7 2.5 add_convert_fusion
  336.3 20.8 %weight_grad.3 = (bf16[2,384,512]{2,1,0:T(8,128)(2,1)S(1)}, bf16[1,384,512]{2,1,0:T(8,128)(2,1)S(1)}, bf16[1,384,512]{2,1,0:T(8,128)(2,1)S(1)}, bf16[2,1,384,512...) custom-call(s32[6]{0:T(128)S(1)} %copy-done.15, bf16[4096,1536]{1,0:T(8,128)(2,1)} %get-tuple-element.434.refs_1_, ...), custom_call_target="tpu_custom_call" | custom-call | flops 60000002048 | bytes 8000000 | tf_op jit(solution)/shard_map/weight_grad/pallas_call | solution.py:993
  359.1 21.7 %weight_grad.4 = (bf16[2,384,512]{2,1,0:T(8,128)(2,1)S(1)}, bf16[1,384,512]{2,1,0:T(8,128)(2,1)S(1)}, bf16[1,384,512]{2,1,0:T(8,128)(2,1)S(1)}, bf16[2,1,384,512]{3,2,1,0:T(8,128)(2,1)}, bf16[2,1,384,512]{3,2,1,0:T(8,128)(2,1)}) custom-call(s32[6]{0:T(128)S(1)} %copy-done.15, bf16[4096,1536]{1,0:T(8,128)(2,1)} %get-tuple-element.434.refs_1_, ...), custom_call_target="tpu_custom_call" | custom-call | flops 60000002048 | bytes 8000000 | tf_op jit(solution)/shard_map/weight_grad/pallas_call | solution.py:993
  385.0 14.5 %turn.1 = (bf16[512,1536]{1,0:T(8,128)(2,1)}, f32[512,1536]{1,0:T(8,128)}, bf16[1536,896]{1,0:T(8,128)(2,1)}, bf16[1536,896]{1,0:T(8,128)(2,1)}) custom-call(s32[6]{0:T(128)} %stack.98.order_ref.refs_0_.refs_1_, bf16[528,1536]{1,0:T(8,128)(2,1)} %get-tuple-element.443.refs_1_, bf16[528,1536]{1,0:T(8,128)(2,1)} %copy-done.66, bf16[528,1536]{1,0:T(8,128)(2,1)} %copy-done.67, ...), custom_call_target="tpu_custom_call" | custom-call | flops 30000001024 | bytes 8000000 | tf_op jit(solution)/shard_map/turn/pallas_call | solution.py:643
  406.4 26.1 %attend_back.2 = (bf16[1536,640]{1,0:T(8,128)(2,1)}, bf16[1536,640]{1,0:T(8,128)(2,1)}, f32[512,1536]{1,0:T(8,128)}) custom-call(s32[2]{0:T(128)} %copy-done.19, s32[6]{0:T(128)} %stack.98.order_ref.refs_0_.refs_1_, bf16[512,1536]{1,0:T(8,128)(2,1)} %get-tuple-element.479.refs_2_, bf16[512,1536]{1,0:T(8,128)(2,1)} %fusion.2.refs_2_.refs_3_, ...), custom_call_target="tpu_custom_call" | custom-call | flops 60000002048 | bytes 8000000 | tf_op jit(solution)/shard_map/attend_back/pallas_call | solution.py:465
  433.6 3.2 collective-permute-done.53.refs_2_
  436.8 1.8 copy-done.25
  440.2 4.6 fold.2
  446.6 30.6 %attend_back.3 = (bf16[1536,768]{1,0:T(8,128)(2,1)}, bf16[1536,768]{1,0:T(8,128)(2,1)}, bf16[512,1536]{1,0:T(8,128)(2,1)}) custom-call(s32[2]{0:T(128)} %copy-done.18, s32[6]{0:T(128)} %stack.98.order_ref.refs_0_.refs_1_, bf16[512,1536]{1,0:T(8,128)(2,1)} %get-tuple-element.479.refs_2_, bf16[512,1536]{1,0:T(8,128)(2,1)} %fusion.2.refs_2_.refs_3_, ...), custom_call_target="tpu_custom_call" | custom-call | flops 60000002048 | bytes 8000000 | tf_op jit(solution)/shard_map/attend_back/pallas_call | solution.py:465
  477.3 2.0 add_convert_fusion.5
  480.4 2.0 add_convert_fusion.4
  483.6 1.7 copy-done.27
  485.3 3.4 fold.3
  488.7 6.6 %collective-permute-done.57 = bf16[192,1536]{1,0:T(8,128)(2,1)S(1)} collective-permute-done((bf16[192,1536]{1,0:T(8,128)(2,1)}, bf16[192,1536]{1,0:T(8,128)(2,1)S(1)}, u32[]{:S(2)}, u32[]{:S(2)}) %collective-permute-start.57) | collective-permute-done | bytes 589856 | tf_op jit(solution)/shard_map/ppermute | solution.py:71
  495.3 2.9 collective-permute-done.58
  498.5 2.0 fusion.6
  502.9 4.0 collective-permute-start.62
  506.9 1.9 collective-permute-start.63
  508.7 20.5 %weight_grad.5 = (bf16[2,512,384]{2,1,0:T(8,128)(2,1)S(1)}, bf16[1,512,384]{2,1,0:T(8,128)(2,1)S(1)}, bf16[1,512,384]{2,1,0:T(8,128)(2,1)S(1)}, bf16[2,1,512,384...) custom-call(s32[6]{0:T(128)S(1)} %copy-done.17, bf16[2,4096,512]{2,1,0:T(8,128)(2,1)} %get-tuple-element.507.refs_1_, ...), custom_call_target="tpu_custom_call" | custom-call | flops 60000002048 | bytes 8000000 | tf_op jit(solution)/shard_map/weight_grad/pallas_call | solution.py:993
  529.3 2.8 collective-permute-done.62
  532.2 6.6 %collective-permute-start.66 = (bf16[96,1536]{1,0:T(8,128)(2,1)S(1)}, bf16[96,1536]{1,0:T(8,128)(2,1)S(1)}, u32[]{:S(2)}, u32[]{:S(2)}) collective-permute-start(bf16[96,1536]{1,0:T(8,128)(2,1)S(1)} %add_convert_fusion.12), channel_id=1, source_target_pairs={{0,8},{4,12},{8,16},{12,20},{16,24},{20,28},{24,0},{28,4},{1,9},{5... | collective-permute-start | bytes 884744 | tf_op jit(solution)/shard_map/ppermute | solution.py:185
  550.9 7.6 %collective-permute-done.67 = bf16[96,1536]{1,0:T(8,128)(2,1)S(1)} collective-permute-done((bf16[96,1536]{1,0:T(8,128)(2,1)S(1)}, bf16[96,1536]{1,0:T(8,128)(2,1)S(1)}, u32[]{:S(2)}, u32[]{:S(2)}) %collective-permute-start.67) | collective-permute-done | bytes 294944 | tf_op jit(solution)/shard_map/ppermute | solution.py:185
  559.7 6.8 %collective-permute-start.69 = (bf16[96,768]{1,0:T(8,128)(2,1)S(1)}, bf16[96,768]{1,0:T(8,128)(2,1)S(1)}, u32[]{:S(2)}, u32[]{:S(2)}) collective-permute-start(bf16[96,768]{1,0:T(8,128)(2,1)S(1)} %get-tuple-element.608), channel_id=1, source_target_pairs={{0,8},{4,12},{8,16},{12,20},{16,24},{20,28},{24,0},{28,4},{1,9},{5... | collective-permute-start | bytes 442376 | tf_op jit(solution)/shard_map/ppermute | solution.py:185
  566.5 2.4 collective-permute-start.70
  573.2 4.8 collective-permute-done.70
  578.0 9.9 %collective-permute-done.72 = bf16[2,512,384]{2,1,0:T(8,128)(2,1)S(1)} collective-permute-done((bf16[2,512,384]{2,1,0:T(8,128)(2,1)S(1)}, bf16[2,512,384]{2,1,0:T(8,128)(2,1)S(1)}, u32[]{:S(2)}, u32[]{:S(2)}) %collective-permute-start.72) | collective-permute-done | bytes 786464 | tf_op jit(solution)/shard_map/ppermute | solution.py:71
  596.6 3.4 collective-permute-done.74
  600.0 3.3 collective-permute-done.75
  608.0 5.8 finish.1
  616.5 4.0 add_convert_fusion.3
  (375 shorter events, 110.3 us)
Async XLA Ops:
  7.2 167.4 %all-gather.2.cloned.1.call-start = ((), (), s32[]{:S(2)}) async-start(), calls=%async_computation.1 | async-start | bytes 14155776 | tf_op jit(solution)/shard_map/all_gather | solution.py:1055
  7.9 608.5 %reduce-scatter.2.cloned.1.call-start = ((), (), s32[]{:S(2)}) async-start(), calls=%async_computation.2 | async-start | bytes 14155776 | tf_op jit(solution)/shard_map/reduce_scatter | solution.py:1122
  11.6 32.4 %collective-permute-start = (bf16[384,1280]{1,0:T(8,128)(2,1)}, bf16[384,1280]{1,0:T(8,128)(2,1)}, u32[]{:S(2)}, u32[]{:S(2)}) collective-permute-start(bf16[384,1280]{1,0:T(8,128)(2,1)} %own_groups.1), channel_id=1, source_target_pairs={{0,1},{1,0},{2,3},{3,2},{4,5},{5,4},{6,7},{7,6},{8,9},{9,8},{10,11... | collective-permute-start | bytes 2949128 | tf_op jit(solution)/shard_map/ppermute | solution.py:71
  14.5 30.7 %collective-permute-start.1 = (bf16[384,1280]{1,0:T(8,128)(2,1)}, bf16[384,1280]{1,0:T(8,128)(2,1)}, u32[]{:S(2)}, u32[]{:S(2)}) collective-permute-start(bf16[384,1280]{1,0:T(8,128)(2,1)} %own_groups.1), channel_id=1, source_target_pairs={{0,2},{1,3},{2,0},{3,1},{4,6},{5,7},{6,4},{7,5},{8,10},{9,11},{10,... | collective-permute-start | bytes 2949128 | tf_op jit(solution)/shard_map/ppermute | solution.py:71
  16.1 20.8 %collective-permute-start.4 = (bf16[18,384]{1,0:T(8,128)(2,1)S(1)}, bf16[18,384]{1,0:T(8,128)(2,1)S(1)}, u32[]{:S(2)}, u32[]{:S(2)}) collective-permute-start(bf16[18,384]{1,0:T(8,128)(2,1)S(1)} %maximum_bitcast_fusion), channel_id=1, source_target_pairs={{0,1},{1,0},{2,3},{3,2},{4,5},{5,4},{6,7},{7,6},{8,9},{9,8},{10,11... | collective-permute-start | bytes 41480 | tf_op jit(solution)/shard_map/ppermute | solution.py:71
  16.7 46.4 %collective-permute-start.8 = (bf16[1,384,1280]{2,1,0:T(8,128)(2,1)}, bf16[1,384,1280]{2,1,0:T(8,128)(2,1)}, u32[]{:S(2)}, u32[]{:S(2)}) collective-permute-start(bf16[1,384,1280]{2,1,0:T(8,128)(2,1)} %bitcast.69), channel_id=1, source_target_pairs={{0,4},{4,0},{8,12},{12,8},{16,20},{20,16},{24,28},{28,24},{1,5},{5... | collective-permute-start | bytes 2949128 | tf_op jit(solution)/shard_map/ppermute | solution.py:62
  45.1 18.4 %collective-permute-start.9 = (bf16[1,384,1280]{2,1,0:T(8,128)(2,1)}, bf16[1,384,1280]{2,1,0:T(8,128)(2,1)}, u32[]{:S(2)}, u32[]{:S(2)}) collective-permute-start(bf16[1,384,1280]{2,1,0:T(8,128)(2,1)} %bitcast.6.refs_7_.refs_20_), channel_id=1, source_target_pairs={{0,4},{4,0},{8,12},{12,8},{16,20},{20,16},{24,28},{28,24},{1,5},{5... | collective-permute-start | bytes 2949128 | tf_op jit(solution)/shard_map/ppermute | solution.py:62
  46.2 19.0 %collective-permute-start.10 = (bf16[1,384,1280]{2,1,0:T(8,128)(2,1)}, bf16[1,384,1280]{2,1,0:T(8,128)(2,1)}, u32[]{:S(2)}, u32[]{:S(2)}) collective-permute-start(bf16[1,384,1280]{2,1,0:T(8,128)(2,1)} %bitcast.7.refs_8_.refs_21_), channel_id=1, source_target_pairs={{0,4},{4,0},{8,12},{12,8},{16,20},{20,16},{24,28},{28,24},{1,5},{5... | collective-permute-start | bytes 2949128 | tf_op jit(solution)/shard_map/ppermute | solution.py:62
  46.8 13.3 %collective-permute-start.2 = (bf16[1,192,1280]{2,1,0:T(8,128)(2,1)S(1)}, bf16[1,192,1280]{2,1,0:T(8,128)(2,1)}, u32[]{:S(2)}, u32[]{:S(2)}) collective-permute-start(bf16[1,192,1280]{2,1,0:T(8,128)(2,1)S(1)} %slice.220), channel_id=1, source_target_pairs={{0,1},{1,0},{2,3},{3,2},{4,5},{5,4},{6,7},{7,6},{8,9},{9,8},{10,11... | collective-permute-start | bytes 1474568 | tf_op jit(solution)/shard_map/ppermute | solution.py:71
  48.5 13.0 %collective-permute-start.3 = (bf16[1,192,1280]{2,1,0:T(8,128)(2,1)S(1)}, bf16[1,192,1280]{2,1,0:T(8,128)(2,1)}, u32[]{:S(2)}, u32[]{:S(2)}) collective-permute-start(bf16[1,192,1280]{2,1,0:T(8,128)(2,1)S(1)} %slice.221), channel_id=1, source_target_pairs={{0,2},{1,3},{2,0},{3,1},{4,6},{5,7},{6,4},{7,5},{8,10},{9,11},{10,... | collective-permute-start | bytes 1474568 | tf_op jit(solution)/shard_map/ppermute | solution.py:71
  63.1 18.2 %collective-permute-start.6 = (bf16[192,1536]{1,0:T(8,128)(2,1)S(1)}, bf16[192,1536]{1,0:T(8,128)(2,1)S(1)}, u32[]{:S(2)}, u32[]{:S(2)}) collective-permute-start(bf16[192,1536]{1,0:T(8,128)(2,1)S(1)} %constant_dynamic-slice_fusion.6), channel_id=1, source_target_pairs={{0,1},{1,0},{2,3},{3,2},{4,5},{5,4},{6,7},{7,6},{8,9},{9,8},{10,11... | collective-permute-start | bytes 1769480 | tf_op jit(solution)/shard_map/ppermute | solution.py:71
  63.5 17.8 %collective-permute-start.7 = (bf16[192,1536]{1,0:T(8,128)(2,1)S(1)}, bf16[192,1536]{1,0:T(8,128)(2,1)S(1)}, u32[]{:S(2)}, u32[]{:S(2)}) collective-permute-start(bf16[192,1536]{1,0:T(8,128)(2,1)S(1)} %constant_dynamic-slice_fusion.6), channel_id=1, source_target_pairs={{0,2},{1,3},{2,0},{3,1},{4,6},{5,7},{6,4},{7,5},{8,10},{9,11},{10,... | collective-permute-start | bytes 1769480 | tf_op jit(solution)/shard_map/ppermute | solution.py:71
  81.4 28.0 %collective-permute-start.18 = (bf16[2,384,512]{2,1,0:T(8,128)(2,1)S(1)}, bf16[2,384,512]{2,1,0:T(8,128)(2,1)S(1)}, u32[]{:S(2)}, u32[]{:S(2)}) collective-permute-start(bf16[2,384,512]{2,1,0:T(8,128)(2,1)S(1)} %copy-done.69), channel_id=1, source_target_pairs={{0,1},{1,0},{2,3},{3,2},{4,5},{5,4},{6,7},{7,6},{8,9},{9,8},{10,11... | collective-permute-start | bytes 2359304 | tf_op jit(solution)/shard_map/ppermute | solution.py:71
  82.9 27.9 %collective-permute-start.19 = (bf16[2,384,512]{2,1,0:T(8,128)(2,1)S(1)}, bf16[2,384,512]{2,1,0:T(8,128)(2,1)S(1)}, u32[]{:S(2)}, u32[]{:S(2)}) collective-permute-start(bf16[2,384,512]{2,1,0:T(8,128)(2,1)S(1)} %copy-done.69), channel_id=1, source_target_pairs={{0,2},{1,3},{2,0},{3,1},{4,6},{5,7},{6,4},{7,5},{8,10},{9,11},{10,... | collective-permute-start | bytes 2359304 | tf_op jit(solution)/shard_map/ppermute | solution.py:71
  83.5 23.3 %collective-permute-start.13 = (bf16[1,96,1536]{2,1,0:T(8,128)(2,1)S(1)}, bf16[1,96,1536]{2,1,0:T(8,128)(2,1)S(1)}, u32[]{:S(2)}, u32[]{:S(2)}) collective-permute-start(bf16[1,96,1536]{2,1,0:T(8,128)(2,1)S(1)} %slice.170), channel_id=1, source_target_pairs={{0,1},{1,0},{2,3},{3,2},{4,5},{5,4},{6,7},{7,6},{8,9},{9,8},{10,11... | collective-permute-start | bytes 884744 | tf_op jit(solution)/shard_map/ppermute | solution.py:71
  84.5 23.4 %collective-permute-start.14 = (bf16[1,96,1536]{2,1,0:T(8,128)(2,1)S(1)}, bf16[1,96,1536]{2,1,0:T(8,128)(2,1)S(1)}, u32[]{:S(2)}, u32[]{:S(2)}) collective-permute-start(bf16[1,96,1536]{2,1,0:T(8,128)(2,1)S(1)} %slice.171), channel_id=1, source_target_pairs={{0,2},{1,3},{2,0},{3,1},{4,6},{5,7},{6,4},{7,5},{8,10},{9,11},{10,... | collective-permute-start | bytes 884744 | tf_op jit(solution)/shard_map/ppermute | solution.py:71
  85.7 22.2 %collective-permute-start.15 = (bf16[3,192,1536]{2,1,0:T(8,128)(2,1)S(1)}, bf16[3,192,1536]{2,1,0:T(8,128)(2,1)S(1)}, u32[]{:S(2)}, u32[]{:S(2)}) collective-permute-start(bf16[3,192,1536]{2,1,0:T(8,128)(2,1)S(1)} %pad_maximum_fusion), channel_id=1, source_target_pairs={{0,4},{4,0},{8,12},{12,8},{16,20},{20,16},{24,28},{28,24},{1,5},{5... | collective-permute-start | bytes 5308424 | tf_op jit(solution)/shard_map/ppermute | solution.py:62
  108.5 20.5 %collective-permute-start.20 = (bf16[2,384,512]{2,1,0:T(8,128)(2,1)S(1)}, bf16[2,384,512]{2,1,0:T(8,128)(2,1)S(1)}, u32[]{:S(2)}, u32[]{:S(2)}) collective-permute-start(bf16[2,384,512]{2,1,0:T(8,128)(2,1)S(1)} %copy-done.70), channel_id=1, source_target_pairs={{0,1},{1,0},{2,3},{3,2},{4,5},{5,4},{6,7},{7,6},{8,9},{9,8},{10,11... | collective-permute-start | bytes 2359304 | tf_op jit(solution)/shard_map/ppermute | solution.py:71
  109.4 20.4 %collective-permute-start.21 = (bf16[2,384,512]{2,1,0:T(8,128)(2,1)S(1)}, bf16[2,384,512]{2,1,0:T(8,128)(2,1)S(1)}, u32[]{:S(2)}, u32[]{:S(2)}) collective-permute-start(bf16[2,384,512]{2,1,0:T(8,128)(2,1)S(1)} %copy-done.70), channel_id=1, source_target_pairs={{0,2},{1,3},{2,0},{3,1},{4,6},{5,7},{6,4},{7,5},{8,10},{9,11},{10,... | collective-permute-start | bytes 2359304 | tf_op jit(solution)/shard_map/ppermute | solution.py:71
  122.9 39.5 %collective-permute-start.22 = (bf16[528,1536]{1,0:T(8,128)(2,1)}, bf16[528,1536]{1,0:T(8,128)(2,1)}, u32[]{:S(2)}, u32[]{:S(2)}) collective-permute-start(bf16[528,1536]{1,0:T(8,128)(2,1)} %get-tuple-element.355.refs_2_.refs_4_), channel_id=1, source_target_pairs={{0,8},{4,12},{8,16},{12,20},{16,24},{20,28},{24,0},{28,4},{1,9},{5... | collective-permute-start | bytes 4866056 | tf_op jit(solution)/shard_map/ppermute | solution.py:67
  124.2 12.3 %collective-permute-start.24 = (bf16[1,1,384,512]{3,2,1,0:T(8,128)(2,1)S(1)}, bf16[1,1,384,512]{3,2,1,0:T(8,128)(2,1)S(1)}, u32[]{:S(2)}, u32[]{:S(2)}) collective-permute-start(bf16[1,1,384,512]{3,2,1,0:T(8,128)(2,1)S(1)} %slice.174), channel_id=1, source_target_pairs={{0,1},{1,0},{2,3},{3,2},{4,5},{5,4},{6,7},{7,6},{8,9},{9,8},{10,11... | collective-permute-start | bytes 1179656 | tf_op jit(solution)/shard_map/ppermute | solution.py:71
  129.8 36.6 %collective-permute-start.23 = (bf16[528,1536]{1,0:T(8,128)(2,1)}, bf16[528,1536]{1,0:T(8,128)(2,1)}, u32[]{:S(2)}, u32[]{:S(2)}) collective-permute-start(bf16[528,1536]{1,0:T(8,128)(2,1)} %get-tuple-element.355.refs_2_.refs_4_), channel_id=1, source_target_pairs={{0,4},{4,0},{8,12},{12,8},{16,20},{20,16},{24,28},{28,24},{1,5},{5... | collective-permute-start | bytes 4866056 | tf_op jit(solution)/shard_map/ppermute | solution.py:62
  137.0 18.7 %collective-permute-start.29 = (bf16[2,512,384]{2,1,0:T(8,128)(2,1)}, bf16[2,512,384]{2,1,0:T(8,128)(2,1)S(1)}, u32[]{:S(2)}, u32[]{:S(2)}) collective-permute-start(bf16[2,512,384]{2,1,0:T(8,128)(2,1)} %param.23), channel_id=1, source_target_pairs={{0,2},{1,3},{2,0},{3,1},{4,6},{5,7},{6,4},{7,5},{8,10},{9,11},{10,... | collective-permute-start | bytes 2359304 | tf_op jit(solution)/shard_map/ppermute | solution.py:71
  138.6 20.7 %collective-permute-start.28 = (bf16[2,512,384]{2,1,0:T(8,128)(2,1)}, bf16[2,512,384]{2,1,0:T(8,128)(2,1)S(1)}, u32[]{:S(2)}, u32[]{:S(2)}) collective-permute-start(bf16[2,512,384]{2,1,0:T(8,128)(2,1)} %param.23), channel_id=1, source_target_pairs={{0,1},{1,0},{2,3},{3,2},{4,5},{5,4},{6,7},{7,6},{8,9},{9,8},{10,11... | collective-permute-start | bytes 2359304 | tf_op jit(solution)/shard_map/ppermute | solution.py:71
  140.0 27.7 %collective-permute-start.26 = (bf16[1,1,384,512]{3,2,1,0:T(8,128)(2,1)S(1)}, bf16[1,1,384,512]{3,2,1,0:T(8,128)(2,1)S(1)}, u32[]{:S(2)}, u32[]{:S(2)}) collective-permute-start(bf16[1,1,384,512]{3,2,1,0:T(8,128)(2,1)S(1)} %slice.176), channel_id=1, source_target_pairs={{0,1},{1,0},{2,3},{3,2},{4,5},{5,4},{6,7},{7,6},{8,9},{9,8},{10,11... | collective-permute-start | bytes 1179656 | tf_op jit(solution)/shard_map/ppermute | solution.py:71
  159.2 14.6 %collective-permute-start.30 = (bf16[1,1,512,384]{3,2,1,0:T(8,128)(2,1)S(1)}, bf16[1,1,512,384]{3,2,1,0:T(8,128)(2,1)S(1)}, u32[]{:S(2)}, u32[]{:S(2)}) collective-permute-start(bf16[1,1,512,384]{3,2,1,0:T(8,128)(2,1)S(1)} %slice.224), channel_id=1, source_target_pairs={{0,1},{1,0},{2,3},{3,2},{4,5},{5,4},{6,7},{7,6},{8,9},{9,8},{10,11... | collective-permute-start | bytes 1179656 | tf_op jit(solution)/shard_map/ppermute | solution.py:71
  166.4 44.2 %collective-permute-start.32 = (bf16[528,1536]{1,0:T(8,128)(2,1)}, bf16[528,1536]{1,0:T(8,128)(2,1)}, u32[]{:S(2)}, u32[]{:S(2)}) collective-permute-start(bf16[528,1536]{1,0:T(8,128)(2,1)} %collective-permute-done.22.refs_2_), channel_id=1, source_target_pairs={{0,8},{4,12},{8,16},{12,20},{16,24},{20,28},{24,0},{28,4},{1,9},{5... | collective-permute-start | bytes 4866056 | tf_op jit(solution)/shard_map/ppermute | solution.py:67
  167.7 42.9 %collective-permute-start.33 = (bf16[528,1536]{1,0:T(8,128)(2,1)}, bf16[528,1536]{1,0:T(8,128)(2,1)}, u32[]{:S(2)}, u32[]{:S(2)}) collective-permute-start(bf16[528,1536]{1,0:T(8,128)(2,1)} %collective-permute-done.22.refs_2_), channel_id=1, source_target_pairs={{0,4},{4,0},{8,12},{12,8},{16,20},{20,16},{24,28},{28,24},{1,5},{5... | collective-permute-start | bytes 4866056 | tf_op jit(solution)/shard_map/ppermute | solution.py:62
  192.7 17.9 %collective-permute-start.34 = (bf16[528,1536]{1,0:T(8,128)(2,1)}, bf16[528,1536]{1,0:T(8,128)(2,1)S(1)}, u32[]{:S(2)}, u32[]{:S(2)}) collective-permute-start(bf16[528,1536]{1,0:T(8,128)(2,1)} %get-tuple-element.366), channel_id=1, source_target_pairs={{0,4},{4,0},{8,12},{12,8},{16,20},{20,16},{24,28},{28,24},{1,5},{5... | collective-permute-start | bytes 4866056 | tf_op jit(solution)/shard_map/ppermute | solution.py:62
  210.6 40.0 %collective-permute-start.35 = (bf16[528,1536]{1,0:T(8,128)(2,1)}, bf16[528,1536]{1,0:T(8,128)(2,1)}, u32[]{:S(2)}, u32[]{:S(2)}) collective-permute-start(bf16[528,1536]{1,0:T(8,128)(2,1)} %collective-permute-done.32.refs_2_), channel_id=1, source_target_pairs={{0,8},{4,12},{8,16},{12,20},{16,24},{20,28},{24,0},{28,4},{1,9},{5... | collective-permute-start | bytes 4866056 | tf_op jit(solution)/shard_map/ppermute | solution.py:67
  212.0 38.7 %collective-permute-start.36 = (bf16[528,1536]{1,0:T(8,128)(2,1)}, bf16[528,1536]{1,0:T(8,128)(2,1)S(1)}, u32[]{:S(2)}, u32[]{:S(2)}) collective-permute-start(bf16[528,1536]{1,0:T(8,128)(2,1)} %collective-permute-done.32.refs_2_), channel_id=1, source_target_pairs={{0,4},{4,0},{8,12},{12,8},{16,20},{20,16},{24,28},{28,24},{1,5},{5... | collective-permute-start | bytes 4866056 | tf_op jit(solution)/shard_map/ppermute | solution.py:62
  230.5 20.2 %collective-permute-start.37 = (bf16[528,1536]{1,0:T(8,128)(2,1)}, bf16[528,1536]{1,0:T(8,128)(2,1)S(1)}, u32[]{:S(2)}, u32[]{:S(2)}) collective-permute-start(bf16[528,1536]{1,0:T(8,128)(2,1)} %get-tuple-element.382), channel_id=1, source_target_pairs={{0,4},{4,0},{8,12},{12,8},{16,20},{20,16},{24,28},{28,24},{1,5},{5... | collective-permute-start | bytes 4866056 | tf_op jit(solution)/shard_map/ppermute | solution.py:62
  253.1 36.5 %collective-permute-start.38 = (bf16[528,1536]{1,0:T(8,128)(2,1)}, bf16[528,1536]{1,0:T(8,128)(2,1)}, u32[]{:S(2)}, u32[]{:S(2)}) collective-permute-start(bf16[528,1536]{1,0:T(8,128)(2,1)} %collective-permute-done.35.refs_2_), channel_id=1, source_target_pairs={{0,4},{4,0},{8,12},{12,8},{16,20},{20,16},{24,28},{28,24},{1,5},{5... | collective-permute-start | bytes 4866056 | tf_op jit(solution)/shard_map/ppermute | solution.py:62
  253.2 39.6 %collective-permute-start.39 = (bf16[528,1536]{1,0:T(8,128)(2,1)S(1)}, bf16[528,1536]{1,0:T(8,128)(2,1)S(1)}, u32[]{:S(2)}, u32[]{:S(2)}) collective-permute-start(bf16[528,1536]{1,0:T(8,128)(2,1)S(1)} %add_convert_fusion.2), channel_id=1, source_target_pairs={{0,8},{4,12},{8,16},{12,20},{16,24},{20,28},{24,0},{28,4},{1,9},{5... | collective-permute-start | bytes 4866056 | tf_op jit(solution)/shard_map/ppermute | solution.py:67
  271.3 21.6 %collective-permute-start.40 = (bf16[528,1536]{1,0:T(8,128)(2,1)}, bf16[528,1536]{1,0:T(8,128)(2,1)S(1)}, u32[]{:S(2)}, u32[]{:S(2)}) collective-permute-start(bf16[528,1536]{1,0:T(8,128)(2,1)} %get-tuple-element.403), channel_id=1, source_target_pairs={{0,4},{4,0},{8,12},{12,8},{16,20},{20,16},{24,28},{28,24},{1,5},{5... | collective-permute-start | bytes 4866056 | tf_op jit(solution)/shard_map/ppermute | solution.py:62
  294.9 38.9 %collective-permute-start.41 = (bf16[528,1536]{1,0:T(8,128)(2,1)S(1)}, bf16[528,1536]{1,0:T(8,128)(2,1)S(1)}, u32[]{:S(2)}, u32[]{:S(2)}) collective-permute-start(bf16[528,1536]{1,0:T(8,128)(2,1)S(1)} %add_convert_fusion.1), channel_id=1, source_target_pairs={{0,8},{4,12},{8,16},{12,20},{16,24},{20,28},{24,0},{28,4},{1,9},{5... | collective-permute-start | bytes 4866056 | tf_op jit(solution)/shard_map/ppermute | solution.py:67
  313.0 20.7 %collective-permute-start.42 = (bf16[528,1536]{1,0:T(8,128)(2,1)}, bf16[528,1536]{1,0:T(8,128)(2,1)}, u32[]{:S(2)}, u32[]{:S(2)}) collective-permute-start(bf16[528,1536]{1,0:T(8,128)(2,1)} %get-tuple-element.424), channel_id=1, source_target_pairs={{0,4},{4,0},{8,12},{12,8},{16,20},{20,16},{24,28},{28,24},{1,5},{5... | collective-permute-start | bytes 4866056 | tf_op jit(solution)/shard_map/ppermute | solution.py:62
  336.3 46.7 %collective-permute-start.43 = (bf16[528,1536]{1,0:T(8,128)(2,1)S(1)}, bf16[528,1536]{1,0:T(8,128)(2,1)S(1)}, u32[]{:S(2)}, u32[]{:S(2)}) collective-permute-start(bf16[528,1536]{1,0:T(8,128)(2,1)S(1)} %add_convert_fusion), channel_id=1, source_target_pairs={{0,8},{4,12},{8,16},{12,20},{16,24},{20,28},{24,0},{28,4},{1,9},{5... | collective-permute-start | bytes 4866056 | tf_op jit(solution)/shard_map/ppermute | solution.py:67
  357.1 25.8 %collective-permute-start.44 = (bf16[2,384,512]{2,1,0:T(8,128)(2,1)S(1)}, bf16[2,384,512]{2,1,0:T(8,128)(2,1)S(1)}, u32[]{:S(2)}, u32[]{:S(2)}) collective-permute-start(bf16[2,384,512]{2,1,0:T(8,128)(2,1)S(1)} %bitcast.77), channel_id=1, source_target_pairs={{0,1},{1,0},{2,3},{3,2},{4,5},{5,4},{6,7},{7,6},{8,9},{9,8},{10,11... | collective-permute-start | bytes 2359304 | tf_op jit(solution)/shard_map/ppermute | solution.py:71
  357.8 25.1 %collective-permute-start.45 = (bf16[2,384,512]{2,1,0:T(8,128)(2,1)S(1)}, bf16[2,384,512]{2,1,0:T(8,128)(2,1)S(1)}, u32[]{:S(2)}, u32[]{:S(2)}) collective-permute-start(bf16[2,384,512]{2,1,0:T(8,128)(2,1)S(1)} %bitcast.76), channel_id=1, source_target_pairs={{0,2},{1,3},{2,0},{3,1},{4,6},{5,7},{6,4},{7,5},{8,10},{9,11},{10,... | collective-permute-start | bytes 2359304 | tf_op jit(solution)/shard_map/ppermute | solution.py:71
  380.8 18.8 %collective-permute-start.46 = (bf16[2,384,512]{2,1,0:T(8,128)(2,1)}, bf16[2,384,512]{2,1,0:T(8,128)(2,1)}, u32[]{:S(2)}, u32[]{:S(2)}) collective-permute-start(bf16[2,384,512]{2,1,0:T(8,128)(2,1)} %bitcast.37), channel_id=1, source_target_pairs={{0,1},{1,0},{2,3},{3,2},{4,5},{5,4},{6,7},{7,6},{8,9},{9,8},{10,11... | collective-permute-start | bytes 2359304 | tf_op jit(solution)/shard_map/ppermute | solution.py:71
  381.5 18.1 %collective-permute-start.47 = (bf16[2,384,512]{2,1,0:T(8,128)(2,1)}, bf16[2,384,512]{2,1,0:T(8,128)(2,1)}, u32[]{:S(2)}, u32[]{:S(2)}) collective-permute-start(bf16[2,384,512]{2,1,0:T(8,128)(2,1)} %bitcast.38), channel_id=1, source_target_pairs={{0,2},{1,3},{2,0},{3,1},{4,6},{5,7},{6,4},{7,5},{8,10},{9,11},{10,... | collective-permute-start | bytes 2359304 | tf_op jit(solution)/shard_map/ppermute | solution.py:71
  399.6 33.0 %collective-permute-start.48 = (bf16[1536,896]{1,0:T(8,128)(2,1)}, bf16[1536,896]{1,0:T(8,128)(2,1)}, u32[]{:S(2)}, u32[]{:S(2)}) collective-permute-start(bf16[1536,896]{1,0:T(8,128)(2,1)} %get-tuple-element.462), channel_id=1, source_target_pairs={{0,4},{4,0},{8,12},{12,8},{16,20},{20,16},{24,28},{28,24},{1,5},{5... | collective-permute-start | bytes 8257544 | tf_op jit(solution)/shard_map/ppermute | solution.py:62
  399.8 32.7 %collective-permute-start.49 = (bf16[1,384,512]{2,1,0:T(8,128)(2,1)S(1)}, bf16[1,384,512]{2,1,0:T(8,128)(2,1)S(1)}, u32[]{:S(2)}, u32[]{:S(2)}) collective-permute-start(bf16[1,384,512]{2,1,0:T(8,128)(2,1)S(1)} %add_convert_fusion.11), channel_id=1, source_target_pairs={{0,1},{1,0},{2,3},{3,2},{4,5},{5,4},{6,7},{7,6},{8,9},{9,8},{10,11... | collective-permute-start | bytes 1179656 | tf_op jit(solution)/shard_map/ppermute | solution.py:71
  400.7 31.7 %collective-permute-start.50 = (bf16[1,384,512]{2,1,0:T(8,128)(2,1)S(1)}, bf16[1,384,512]{2,1,0:T(8,128)(2,1)S(1)}, u32[]{:S(2)}, u32[]{:S(2)}) collective-permute-start(bf16[1,384,512]{2,1,0:T(8,128)(2,1)S(1)} %add_convert_fusion.10), channel_id=1, source_target_pairs={{0,2},{1,3},{2,0},{3,1},{4,6},{5,7},{6,4},{7,5},{8,10},{9,11},{10,... | collective-permute-start | bytes 1179656 | tf_op jit(solution)/shard_map/ppermute | solution.py:71
  403.0 29.5 %collective-permute-start.51 = (bf16[1,384,512]{2,1,0:T(8,128)(2,1)S(1)}, bf16[1,384,512]{2,1,0:T(8,128)(2,1)S(1)}, u32[]{:S(2)}, u32[]{:S(2)}) collective-permute-start(bf16[1,384,512]{2,1,0:T(8,128)(2,1)S(1)} %add_convert_fusion.9), channel_id=1, source_target_pairs={{0,1},{1,0},{2,3},{3,2},{4,5},{5,4},{6,7},{7,6},{8,9},{9,8},{10,11... | collective-permute-start | bytes 1179656 | tf_op jit(solution)/shard_map/ppermute | solution.py:71
  405.2 27.3 %collective-permute-start.52 = (bf16[1,384,512]{2,1,0:T(8,128)(2,1)S(1)}, bf16[1,384,512]{2,1,0:T(8,128)(2,1)S(1)}, u32[]{:S(2)}, u32[]{:S(2)}) collective-permute-start(bf16[1,384,512]{2,1,0:T(8,128)(2,1)S(1)} %add_convert_fusion.8), channel_id=1, source_target_pairs={{0,2},{1,3},{2,0},{3,1},{4,6},{5,7},{6,4},{7,5},{8,10},{9,11},{10,... | collective-permute-start | bytes 1179656 | tf_op jit(solution)/shard_map/ppermute | solution.py:71
  444.8 32.5 %collective-permute-start.54 = (bf16[384,1536]{1,0:T(8,128)(2,1)}, bf16[384,1536]{1,0:T(8,128)(2,1)}, u32[]{:S(2)}, u32[]{:S(2)}) collective-permute-start(bf16[384,1536]{1,0:T(8,128)(2,1)} %get-tuple-element.488), channel_id=1, source_target_pairs={{0,1},{1,0},{2,3},{3,2},{4,5},{5,4},{6,7},{7,6},{8,9},{9,8},{10,11... | collective-permute-start | bytes 3538952 | tf_op jit(solution)/shard_map/ppermute | solution.py:71
  445.5 31.7 %collective-permute-start.55 = (bf16[384,1536]{1,0:T(8,128)(2,1)S(1)}, bf16[384,1536]{1,0:T(8,128)(2,1)}, u32[]{:S(2)}, u32[]{:S(2)}) collective-permute-start(bf16[384,1536]{1,0:T(8,128)(2,1)S(1)} %get-tuple-element.489), channel_id=1, source_target_pairs={{0,2},{1,3},{2,0},{3,1},{4,6},{5,7},{6,4},{7,5},{8,10},{9,11},{10,... | collective-permute-start | bytes 3538952 | tf_op jit(solution)/shard_map/ppermute | solution.py:71
  479.4 15.9 %collective-permute-start.57 = (bf16[192,1536]{1,0:T(8,128)(2,1)}, bf16[192,1536]{1,0:T(8,128)(2,1)S(1)}, u32[]{:S(2)}, u32[]{:S(2)}) collective-permute-start(bf16[192,1536]{1,0:T(8,128)(2,1)} %add_convert_fusion.5), channel_id=1, source_target_pairs={{0,1},{1,0},{2,3},{3,2},{4,5},{5,4},{6,7},{7,6},{8,9},{9,8},{10,11... | collective-permute-start | bytes 1769480 | tf_op jit(solution)/shard_map/ppermute | solution.py:71
  482.5 15.7 %collective-permute-start.58 = (bf16[192,1536]{1,0:T(8,128)(2,1)}, bf16[192,1536]{1,0:T(8,128)(2,1)}, u32[]{:S(2)}, u32[]{:S(2)}) collective-permute-start(bf16[192,1536]{1,0:T(8,128)(2,1)} %add_convert_fusion.4), channel_id=1, source_target_pairs={{0,2},{1,3},{2,0},{3,1},{4,6},{5,7},{6,4},{7,5},{8,10},{9,11},{10,... | collective-permute-start | bytes 1769480 | tf_op jit(solution)/shard_map/ppermute | solution.py:71
  500.6 31.5 %collective-permute-start.59 = (bf16[384,768]{1,0:T(8,128)(2,1)S(1)}, bf16[384,768]{1,0:T(8,128)(2,1)S(1)}, u32[]{:S(2)}, u32[]{:S(2)}) collective-permute-start(bf16[384,768]{1,0:T(8,128)(2,1)S(1)} %get-tuple-element.512), channel_id=1, source_target_pairs={{0,1},{1,0},{2,3},{3,2},{4,5},{5,4},{6,7},{7,6},{8,9},{9,8},{10,11... | collective-permute-start | bytes 1769480 | tf_op jit(solution)/shard_map/ppermute | solution.py:71
  501.6 30.5 %collective-permute-start.60 = (bf16[384,768]{1,0:T(8,128)(2,1)S(1)}, bf16[384,768]{1,0:T(8,128)(2,1)S(1)}, u32[]{:S(2)}, u32[]{:S(2)}) collective-permute-start(bf16[384,768]{1,0:T(8,128)(2,1)S(1)} %get-tuple-element.513), channel_id=1, source_target_pairs={{0,2},{1,3},{2,0},{3,1},{4,6},{5,7},{6,4},{7,5},{8,10},{9,11},{10,... | collective-permute-start | bytes 1769480 | tf_op jit(solution)/shard_map/ppermute | solution.py:71
  502.6 26.6 %collective-permute-start.61 = (bf16[96,1536]{1,0:T(8,128)(2,1)S(1)}, bf16[96,1536]{1,0:T(8,128)(2,1)S(1)}, u32[]{:S(2)}, u32[]{:S(2)}) collective-permute-start(bf16[96,1536]{1,0:T(8,128)(2,1)S(1)} %get-tuple-element.604), channel_id=1, source_target_pairs={{0,8},{4,12},{8,16},{12,20},{16,24},{20,28},{24,0},{28,4},{1,9},{5... | collective-permute-start | bytes 884744 | tf_op jit(solution)/shard_map/ppermute | solution.py:185
  502.9 29.2 %collective-permute-start.62 = (bf16[96,1536]{1,0:T(8,128)(2,1)S(1)}, bf16[96,1536]{1,0:T(8,128)(2,1)S(1)}, u32[]{:S(2)}, u32[]{:S(2)}) collective-permute-start(bf16[96,1536]{1,0:T(8,128)(2,1)S(1)} %get-tuple-element.603), channel_id=1, source_target_pairs={{0,16},{4,20},{8,24},{12,28},{16,0},{20,4},{24,8},{28,12},{1,17},{... | collective-permute-start | bytes 884744 | tf_op jit(solution)/shard_map/ppermute | solution.py:185
  506.9 25.2 %collective-permute-start.63 = (bf16[96,1536]{1,0:T(8,128)(2,1)S(1)}, bf16[96,1536]{1,0:T(8,128)(2,1)S(1)}, u32[]{:S(2)}, u32[]{:S(2)}) collective-permute-start(bf16[96,1536]{1,0:T(8,128)(2,1)S(1)} %get-tuple-element.602), channel_id=1, source_target_pairs={{0,24},{4,28},{8,0},{12,4},{16,8},{20,12},{24,16},{28,20},{1,25},{... | collective-permute-start | bytes 884744 | tf_op jit(solution)/shard_map/ppermute | solution.py:185
  532.2 18.7 %collective-permute-start.66 = (bf16[96,1536]{1,0:T(8,128)(2,1)S(1)}, bf16[96,1536]{1,0:T(8,128)(2,1)S(1)}, u32[]{:S(2)}, u32[]{:S(2)}) collective-permute-start(bf16[96,1536]{1,0:T(8,128)(2,1)S(1)} %add_convert_fusion.12), channel_id=1, source_target_pairs={{0,8},{4,12},{8,16},{12,20},{16,24},{20,28},{24,0},{28,4},{1,9},{5... | collective-permute-start | bytes 884744 | tf_op jit(solution)/shard_map/ppermute | solution.py:185
  538.9 19.7 %collective-permute-start.67 = (bf16[96,1536]{1,0:T(8,128)(2,1)S(1)}, bf16[96,1536]{1,0:T(8,128)(2,1)S(1)}, u32[]{:S(2)}, u32[]{:S(2)}) collective-permute-start(bf16[96,1536]{1,0:T(8,128)(2,1)S(1)} %add_convert_fusion.12), channel_id=1, source_target_pairs={{0,16},{4,20},{8,24},{12,28},{16,0},{20,4},{24,8},{28,12},{1,17},{... | collective-permute-start | bytes 884744 | tf_op jit(solution)/shard_map/ppermute | solution.py:185
  539.9 18.7 %collective-permute-start.68 = (bf16[96,1536]{1,0:T(8,128)(2,1)S(1)}, bf16[96,1536]{1,0:T(8,128)(2,1)S(1)}, u32[]{:S(2)}, u32[]{:S(2)}) collective-permute-start(bf16[96,1536]{1,0:T(8,128)(2,1)S(1)} %add_convert_fusion.12), channel_id=1, source_target_pairs={{0,24},{4,28},{8,0},{12,4},{16,8},{20,12},{24,16},{28,20},{1,25},{... | collective-permute-start | bytes 884744 | tf_op jit(solution)/shard_map/ppermute | solution.py:185
  559.7 13.5 %collective-permute-start.69 = (bf16[96,768]{1,0:T(8,128)(2,1)S(1)}, bf16[96,768]{1,0:T(8,128)(2,1)S(1)}, u32[]{:S(2)}, u32[]{:S(2)}) collective-permute-start(bf16[96,768]{1,0:T(8,128)(2,1)S(1)} %get-tuple-element.608), channel_id=1, source_target_pairs={{0,8},{4,12},{8,16},{12,20},{16,24},{20,28},{24,0},{28,4},{1,9},{5... | collective-permute-start | bytes 442376 | tf_op jit(solution)/shard_map/ppermute | solution.py:185
  569.0 18.9 %collective-permute-start.72 = (bf16[2,512,384]{2,1,0:T(8,128)(2,1)S(1)}, bf16[2,512,384]{2,1,0:T(8,128)(2,1)S(1)}, u32[]{:S(2)}, u32[]{:S(2)}) collective-permute-start(bf16[2,512,384]{2,1,0:T(8,128)(2,1)S(1)} %bitcast.75), channel_id=1, source_target_pairs={{0,1},{1,0},{2,3},{3,2},{4,5},{5,4},{6,7},{7,6},{8,9},{9,8},{10,11... | collective-permute-start | bytes 2359304 | tf_op jit(solution)/shard_map/ppermute | solution.py:71
  570.4 18.6 %collective-permute-start.73 = (bf16[2,512,384]{2,1,0:T(8,128)(2,1)S(1)}, bf16[2,512,384]{2,1,0:T(8,128)(2,1)S(1)}, u32[]{:S(2)}, u32[]{:S(2)}) collective-permute-start(bf16[2,512,384]{2,1,0:T(8,128)(2,1)S(1)} %bitcast.74), channel_id=1, source_target_pairs={{0,2},{1,3},{2,0},{3,1},{4,6},{5,7},{6,4},{7,5},{8,10},{9,11},{10,... | collective-permute-start | bytes 2359304 | tf_op jit(solution)/shard_map/ppermute | solution.py:71
  589.2 14.2 %collective-permute-start.77 = (bf16[1,512,384]{2,1,0:T(8,128)(2,1)S(1)}, bf16[1,512,384]{2,1,0:T(8,128)(2,1)S(1)}, u32[]{:S(2)}, u32[]{:S(2)}) collective-permute-start(bf16[1,512,384]{2,1,0:T(8,128)(2,1)S(1)} %add_convert_fusion.7), channel_id=1, source_target_pairs={{0,1},{1,0},{2,3},{3,2},{4,5},{5,4},{6,7},{7,6},{8,9},{9,8},{10,11... | collective-permute-start | bytes 1179656 | tf_op jit(solution)/shard_map/ppermute | solution.py:71
  589.9 13.5 %collective-permute-start.78 = (bf16[1,512,384]{2,1,0:T(8,128)(2,1)S(1)}, bf16[1,512,384]{2,1,0:T(8,128)(2,1)S(1)}, u32[]{:S(2)}, u32[]{:S(2)}) collective-permute-start(bf16[1,512,384]{2,1,0:T(8,128)(2,1)S(1)} %add_convert_fusion.6), channel_id=1, source_target_pairs={{0,2},{1,3},{2,0},{3,1},{4,6},{5,7},{6,4},{7,5},{8,10},{9,11},{10,... | collective-permute-start | bytes 1179656 | tf_op jit(solution)/shard_map/ppermute | solution.py:71
  (97 other events, 1044.0 us)
Sparse Core Ops, SparseCore 0:
  9.7 119.7 all-gather.1
  385.1 135.8 reduce-scatter.1
